TPU v7x, 256 devices: a whole 4x4x8 slice. The times are simulated.
256 devices in a mesh: lead: 16 (over z, core), grp: 16 (over x, y).
Axes of the slice: x: 4, y: 4, z: 8, core: 2. Of those that a mesh axis runs over, the one named last changes fastest.
Arguments:
- matrix_tiles: bfloat16 [512, 384, 384], P(('lead', 'grp')), may hold values from -0.0546875 to 0.0546875
- tile_slot: int32 [16, 32], P('lead'), may hold values from 0 to 31, each once within a row
- tile_cols: int32 [64, 8], P('lead'), may hold values from 0 to 7, as said below
- send_rows: int32 [16, 2, 2], replicated, may hold values from 0 to 3, as said below
- residual: float32 [24576, 128], P(('lead', 'grp')), may hold values from -6 to 6
- diag_inv: float32 [24576], P(('lead', 'grp')), may hold values from 0.25 to 1
Outputs:
- correction: float32 [24576, 128], P(('lead', 'grp'))
Inputs may be any that keep to these rules, and one draw needn't show every extreme that they name: `tile_cols`: entry 0 of every row is that row's own block row within its leader, r for row l * 4 + r; indices below 4 are the leader's own block rows, the next 2 are the rows received from leader l - 1, the last 2 those received from leader l + 1 (cyclic). `send_rows`: the 2 entries of each list are distinct block rows of the sending leader.
All inputs are finite; a program needn't handle non-finite values.
Results may differ from a plain program's by a relative error of at most 0.0013.
Values may be sent and summed in bfloat16 or wider, within the bound.
No kernel may reach another device: no remote copies, remote signals or barrier semaphores. Data moves between devices by JAX's collectives and lax.ppermute only.
A program may use at most 64 MiB of HBM per device.

v0:
```python
import jax
import jax.numpy as jnp
from jax import lax
from jax.sharding import PartitionSpec as P

TILES_ROW = 8


lower_bound = 0.5
upper_bound = 1.5


def from_behind(shard, axis, by):
    devices = lax.axis_size(axis)
    return lax.ppermute(shard, axis, [(i, (i + by) % devices) for i in range(devices)])


def one_sweep(start_residual, inverse, apply_operator):
    center_value = (upper_bound + lower_bound) / 2.0
    half_width = (upper_bound - lower_bound) / 2.0
    ratio_value = center_value / half_width
    update = inverse[:, None] * start_residual / center_value
    approx = update
    rho_now = 1.0 / ratio_value
    rho_next = 1.0 / (2.0 * ratio_value - rho_now)
    remaining = start_residual - apply_operator(approx)
    update = (
        rho_next * rho_now * update + 2.0 * rho_next / half_width * inverse[:, None] * remaining
    )
    approx = approx + update
    return approx


def smooth_twice(rhs_field, inverse, apply_operator):
    first_pass = one_sweep(rhs_field, inverse, apply_operator)
    remaining = rhs_field - apply_operator(first_pass)
    second_pass = one_sweep(remaining, inverse, apply_operator)
    return first_pass + second_pass


def extend(blocks, send_rows):
    position = lax.axis_index("lead")
    mine_up = jnp.take(blocks, send_rows[position, 0], axis=0)
    mine_down = jnp.take(blocks, send_rows[position, 1], axis=0)
    from_lower = from_behind(mine_up, "lead", 1)
    from_upper = from_behind(mine_down, "lead", -1)
    return jnp.concatenate([blocks, from_lower, from_upper], axis=0)


def local(matrix_tiles, tile_slot, tile_cols, send_rows, residual, diag_inv):
    block_rows = tile_cols.shape[0]
    tile_size = matrix_tiles.shape[1]
    member = lax.axis_index("grp")
    share_rows = residual.shape[0]
    group_slots = tile_slot[0]
    group_tiles = lax.all_gather(matrix_tiles, "grp", axis=0, tiled=True)
    full_residual, full_inverse = (
        lax.all_gather(residual, "grp", axis=0, tiled=True),
        lax.all_gather(diag_inv, "grp", axis=0, tiled=True),
    )
    placed = (
        jnp.zeros_like(group_slots)
        .at[group_slots]
        .set(jnp.arange(group_slots.shape[0], dtype=jnp.int32))
    )
    ordered = jnp.take(group_tiles, placed, axis=0)
    ordered = ordered.reshape(block_rows, TILES_ROW, tile_size, tile_size)
    flat_cols = tile_cols.reshape(-1)

    def apply_operator(approx):
        rounded = approx.astype(jnp.bfloat16).reshape(block_rows, tile_size, -1)
        extended = extend(rounded, send_rows)
        operand = jnp.take(extended, flat_cols, axis=0).reshape(
            block_rows, TILES_ROW, tile_size, -1
        )
        coupled = jnp.einsum("rkij,rkjn->rin", ordered, operand, preferred_element_type=jnp.float32)
        return approx / full_inverse[:, None] + coupled.reshape(block_rows * tile_size, -1)

    whole_result = smooth_twice(full_residual, full_inverse, apply_operator)
    correction = lax.dynamic_slice_in_dim(whole_result, member * share_rows, share_rows, 0)
    return correction


def solution(mesh):
    in_specs = (
        P(("lead", "grp"), None, None),
        P("lead", None),
        P("lead", None),
        P(),
        P(("lead", "grp"), None),
        P(("lead", "grp")),
    )
    out_specs = P(("lead", "grp"), None)
    return jax.shard_map(local, mesh=mesh, in_specs=in_specs, out_specs=out_specs, check_vma=False)
```

profile of v0, /device:TPU:97, one launch (start us, length us, event | category | flops | bytes accessed | tf_op | source)
XLA Modules:
  0.0 167.3 jit_solution(6383218233879301720)
XLA Ops:
  6.5 0.7 all-gather.2.cloned.1.call-update
  7.3 1.3 dynamic-slice
  9.2 0.9 dynamic-update-slice
  10.1 0.9 fusion.14
  11.0 34.7 %all-reduce = f32[1536]{0:T(1024)S(1)} all-reduce(f32[1536]{0:T(1024)S(1)} %dynamic-update-slice), channel_id=1, replica_groups=mesh['lead'=16,'grp'=16] {'grp'}, use_global_device_ids=true, to_apply=%add | all-reduce | flops 1536 | bytes 12288
  45.7 21.1 %all_gather.10 = f32[1536,128]{1,0:T(8,128)S(1)} all-gather(f32[96,128]{1,0:T(8,128)} %param.14), channel_id=1, replica_groups=mesh['lead'=16,'grp'=16] {'grp'}, dimensions={0}, use_global_device_ids=true | all-gather | bytes 835584 | tf_op jit(solution)/shard_map/all_gather | solution.py:58
  66.8 0.3 multiply_convert_fusion
  67.1 0.6 gather_fusion.1
  67.7 0.1 broadcast_select_fusion.12
  67.8 13.9 %collective-permute-start = (bf16[2,384,128]{2,1,0:T(8,128)(2,1)S(1)}, bf16[2,384,128]{2,1,0:T(8,128)(2,1)S(1)}, u32[]{:S(2)}, u32[]{:S(2)}) collective-permute-start(bf16[2,384,128]{2,1,0:T(8,128)(2,1)S(1)} %broadcast_select_fusion.12), channel_id=1, source_target_pairs={{0,16},{16,32},{32,48},{48,64},{64,80},{80,96},{96,112},{112,128},... | collective-permute-start | bytes 589832 | tf_op jit(solution)/shard_map/ppermute | solution.py:15
  81.8 0.6 gather_fusion.2
  82.4 0.1 broadcast_select_fusion.9
  82.6 0.7 scatter_custom_fusion
  83.3 0.1 broadcast_in_dim.40
  83.5 0.9 collective-permute-done
  84.4 4.8 %collective-permute-done.1 = bf16[2,384,128]{2,1,0:T(8,128)(2,1)S(1)} collective-permute-done((bf16[2,384,128]{2,1,0:T(8,128)(2,1)S(1)}, bf16[2,384,128]{2,1,0:T(8,128)(2,1)S(1)}, u32[]{:S(2)}, u32[]{:S(2)}) %collective-permute-start.1) | collective-permute-done | bytes 196640 | tf_op jit(solution)/shard_map/ppermute | solution.py:15
  89.2 0.1 pad_maximum_fusion
  89.3 2.6 %gather_fusion.3 = bf16[32,384,128]{2,1,0:T(8,128)(2,1)} fusion(bf16[8,384,128]{2,1,0:T(8,128)(2,1)S(1)} %pad_maximum_fusion, s32[1024]{0:T(1024)S(1)} %pad_clamp_fusion), kind=kCustom, calls=%fused_computation.1.clone | custom fusion | bytes 6291584 | tf_op jit(solution)/shard_map/jit(_take)/gather | solution.py:73
  91.9 3.9 %broadcast_select_fusion.6 = bf16[32,384,128]{2,1,0:T(8,128)(2,1)} fusion(bf16[32,384,128]{2,1,0:T(8,128)(2,1)} %gather_fusion.3, pred[32]{0:T(512)(128)(4,1)S(1)} %compare_and_fusion), kind=kLoop, calls=%fused_computation.20 | loop fusion | flops 1572864 | bytes 6291488 | tf_op jit(solution)/shard_map/jit(_take)/select_n | solution.py:73
  95.9 0.1 all-gather.2.cloned.1.call-done
  96.0 9.8 %gather_fusion = bf16[32,384,384]{2,1,0:T(8,128)(2,1)} fusion(bf16[32,384,384]{2,1,0:T(8,128)(2,1)} %all-gather.2.cloned.1.call-done, s32[1024]{0:T(1024)S(1)} %pad_clamp_fusion.3), kind=kCustom, calls=%fused_computation.9 | custom fusion | bytes 18874496 | tf_op jit(solution)/shard_map/jit(_take)/gather | solution.py:66
  105.7 7.3 %fusion.2 = f32[4,384,128,1]{2,1,3,0:T(8,128)S(1)} fusion(bf16[4,8,384,128]{3,2,1,0:T(8,128)(2,1)} %bitcast.54, bf16[4,8,384,384]{3,2,1,0:T(8,128)(2,1)} %bitcast.42, pred[4,8]{1,0:T(4,128)(4,1)S(1)} %broadcast_in_dim.40), kind=kOutput, calls=%fused_computation.14 | convolution fusion | flops 1212678144 | bytes 13369376 | tf_op jit(solution)/shard_map/rkij,rkjn->rin/dot_general | solution.py:76
  113.0 0.5 fusion.23
  113.5 0.6 gather_fusion.5
  114.1 0.6 gather_fusion.4
  114.7 0.1 broadcast_select_fusion.8
  114.8 0.1 broadcast_select_fusion.11
  114.9 3.2 %collective-permute-start.2 = (bf16[2,384,128]{2,1,0:T(8,128)(2,1)S(1)}, bf16[2,384,128]{2,1,0:T(8,128)(2,1)S(1)}, u32[]{:S(2)}, u32[]{:S(2)}) collective-permute-start(bf16[2,384,128]{2,1,0:T(8,128)(2,1)S(1)} %broadcast_select_fusion.11), channel_id=1, source_target_pairs={{0,16},{16,32},{32,48},{48,64},{64,80},{80,96},{96,112},{112,128},... | collective-permute-start | bytes 589832 | tf_op jit(solution)/shard_map/ppermute | solution.py:15
  118.2 2.6 %collective-permute-done.2 = bf16[2,384,128]{2,1,0:T(8,128)(2,1)S(1)} collective-permute-done((bf16[2,384,128]{2,1,0:T(8,128)(2,1)S(1)}, bf16[2,384,128]{2,1,0:T(8,128)(2,1)S(1)}, u32[]{:S(2)}, u32[]{:S(2)}) %collective-permute-start.2) | collective-permute-done | bytes 196640 | tf_op jit(solution)/shard_map/ppermute | solution.py:15
  120.8 3.7 %collective-permute-done.3 = bf16[2,384,128]{2,1,0:T(8,128)(2,1)S(1)} collective-permute-done((bf16[2,384,128]{2,1,0:T(8,128)(2,1)S(1)}, bf16[2,384,128]{2,1,0:T(8,128)(2,1)S(1)}, u32[]{:S(2)}, u32[]{:S(2)}) %collective-permute-start.3) | collective-permute-done | bytes 196640 | tf_op jit(solution)/shard_map/ppermute | solution.py:15
  124.5 0.1 pad_maximum_fusion.1
  124.6 2.6 %gather_fusion.6 = bf16[32,384,128]{2,1,0:T(8,128)(2,1)} fusion(bf16[8,384,128]{2,1,0:T(8,128)(2,1)S(1)} %pad_maximum_fusion.1, s32[1024]{0:T(1024)S(1)} %pad_clamp_fusion), kind=kCustom, calls=%fused_computation.7.clone | custom fusion | bytes 6291584 | tf_op jit(solution)/shard_map/jit(_take)/gather | solution.py:73
  127.2 2.3 %broadcast_select_fusion.5 = bf16[32,384,128]{2,1,0:T(8,128)(2,1)S(1)} fusion(bf16[32,384,128]{2,1,0:T(8,128)(2,1)} %gather_fusion.6, pred[32]{0:T(512)(128)(4,1)S(1)} %compare_and_fusion), kind=kLoop, calls=%fused_computation.19 | loop fusion | flops 1572864 | bytes 6291488 | tf_op jit(solution)/shard_map/jit(_take)/select_n | solution.py:73
  129.4 6.4 %fusion.1 = f32[4,384,128,1]{2,1,3,0:T(8,128)S(1)} fusion(bf16[4,8,384,128]{3,2,1,0:T(8,128)(2,1)S(1)} %bitcast.56, bf16[4,8,384,384]{3,2,1,0:T(8,128)(2,1)} %bitcast.43, pred[4,8]{1,0:T(4,128)(4,1)S(1)} %broadcast_in_dim.40), kind=kOutput, calls=%fused_computation.13 | convolution fusion | flops 1212678144 | bytes 13369376 | tf_op jit(solution)/shard_map/rkij,rkjn->rin/dot_general | solution.py:76
  135.8 1.3 broadcast_divide_fusion
  137.2 0.7 gather_fusion.8
  137.9 0.7 gather_fusion.7
  138.6 0.7 broadcast_select_fusion.7
  139.3 0.7 broadcast_select_fusion.10
  140.0 0.5 collective-permute-start.5
  140.6 2.0 %collective-permute-done.4 = bf16[2,384,128]{2,1,0:T(8,128)(2,1)S(1)} collective-permute-done((bf16[2,384,128]{2,1,0:T(8,128)(2,1)S(1)}, bf16[2,384,128]{2,1,0:T(8,128)(2,1)S(1)}, u32[]{:S(2)}, u32[]{:S(2)}) %collective-permute-start.4) | collective-permute-done | bytes 196640 | tf_op jit(solution)/shard_map/ppermute | solution.py:15
  142.7 0.7 copy-done
  143.3 3.1 %collective-permute-done.5 = bf16[2,384,128]{2,1,0:T(8,128)(2,1)} collective-permute-done((bf16[2,384,128]{2,1,0:T(8,128)(2,1)S(1)}, bf16[2,384,128]{2,1,0:T(8,128)(2,1)}, u32[]{:S(2)}, u32[]{:S(2)}) %collective-permute-start.5) | collective-permute-done | bytes 196640 | tf_op jit(solution)/shard_map/ppermute | solution.py:15
  146.5 1.1 pad_maximum_fusion.2
  147.6 2.7 %gather_fusion.9 = bf16[32,384,128]{2,1,0:T(8,128)(2,1)} fusion(bf16[8,384,128]{2,1,0:T(8,128)(2,1)S(1)} %pad_maximum_fusion.2, s32[1024]{0:T(1024)} %copy-done.1), kind=kCustom, calls=%fused_computation.8.clone | custom fusion | bytes 6291584 | tf_op jit(solution)/shard_map/jit(_take)/gather | solution.py:73
  150.3 2.3 %broadcast_select_fusion.4 = bf16[32,384,128]{2,1,0:T(8,128)(2,1)S(1)} fusion(bf16[32,384,128]{2,1,0:T(8,128)(2,1)} %gather_fusion.9, pred[32]{0:T(512)(128)(4,1)S(1)} %copy-done.5), kind=kLoop, calls=%fused_computation.18 | loop fusion | flops 1572864 | bytes 6291488 | tf_op jit(solution)/shard_map/jit(_take)/select_n | solution.py:73
  152.6 6.4 %fusion = f32[4,384,128,1]{2,1,3,0:T(8,128)S(1)} fusion(bf16[4,8,384,128]{3,2,1,0:T(8,128)(2,1)S(1)} %bitcast.55, bf16[4,8,384,384]{3,2,1,0:T(8,128)(2,1)} %bitcast.44, pred[4,8]{1,0:T(4,128)(4,1)S(1)} %copy-done.11), kind=kOutput, calls=%fused_computation.12 | convolution fusion | flops 1212678144 | bytes 13369376 | tf_op jit(solution)/shard_map/rkij,rkjn->rin/dot_general | solution.py:76
  159.0 1.5 dynamic-slice_add_fusion
  (46 shorter events, 0.4 us)
Async XLA Ops:
  6.5 76.0 %copy-start.8 = (s32[4,8]{1,0:T(4,128)S(1)}, s32[4,8]{1,0:T(4,128)}, u32[]{:S(2)}) copy-start(s32[4,8]{1,0:T(4,128)} %param.12) | copy-start | bytes 388
  6.5 76.1 %copy-start.9 = (s32[1,32]{1,0:T(1,128)S(1)}, s32[1,32]{1,0:T(1,128)}, u32[]{:S(2)}) copy-start(s32[1,32]{1,0:T(1,128)} %param.11) | copy-start | bytes 388
  6.5 89.4 %all-gather.2.cloned.1.call-start = ((), (), s32[]{:S(2)}) async-start(), calls=%async_computation | async-start | bytes 10027008 | tf_op jit(solution)/shard_map/all_gather | solution.py:56
  45.7 68.5 %copy-start.2 = (s32[1024]{0:T(1024)}, s32[1024]{0:T(1024)S(1)}, u32[]{:S(2)}) copy-start(s32[1024]{0:T(1024)S(1)} %pad_clamp_fusion.2) | copy-start | bytes 12292
  67.7 47.1 %copy-start.6 = (pred[2]{0:T(512)(128)(4,1)}, pred[2]{0:T(512)(128)(4,1)S(1)}, u32[]{:S(2)}) copy-start(pred[2]{0:T(512)(128)(4,1)S(1)} %compare_and_fusion.2) | copy-start | bytes 10
  67.8 16.6 %collective-permute-start = (bf16[2,384,128]{2,1,0:T(8,128)(2,1)S(1)}, bf16[2,384,128]{2,1,0:T(8,128)(2,1)S(1)}, u32[]{:S(2)}, u32[]{:S(2)}) collective-permute-start(bf16[2,384,128]{2,1,0:T(8,128)(2,1)S(1)} %broadcast_select_fusion.12), channel_id=1, source_target_pairs={{0,16},{16,32},{32,48},{48,64},{64,80},{80,96},{96,112},{112,128},... | collective-permute-start | bytes 589832 | tf_op jit(solution)/shard_map/ppermute | solution.py:15
  81.8 31.8 %copy-start.3 = (s32[1024]{0:T(1024)}, s32[1024]{0:T(1024)S(1)}, u32[]{:S(2)}) copy-start(s32[1024]{0:T(1024)S(1)} %pad_clamp_fusion.1) | copy-start | bytes 12292
  82.4 32.3 %copy-start.7 = (pred[2]{0:T(512)(128)(4,1)}, pred[2]{0:T(512)(128)(4,1)S(1)}, u32[]{:S(2)}) copy-start(pred[2]{0:T(512)(128)(4,1)S(1)} %compare_and_fusion.1) | copy-start | bytes 10
  82.5 6.7 %collective-permute-start.1 = (bf16[2,384,128]{2,1,0:T(8,128)(2,1)S(1)}, bf16[2,384,128]{2,1,0:T(8,128)(2,1)S(1)}, u32[]{:S(2)}, u32[]{:S(2)}) collective-permute-start(bf16[2,384,128]{2,1,0:T(8,128)(2,1)S(1)} %broadcast_select_fusion.9), channel_id=1, source_target_pairs={{0,240},{16,0},{32,16},{48,32},{64,48},{80,64},{96,80},{112,96},{1... | collective-permute-start | bytes 589832 | tf_op jit(solution)/shard_map/ppermute | solution.py:15
  83.4 46.0 %copy-start.10 = (pred[4,8]{1,0:T(4,128)(4,1)}, pred[4,8]{1,0:T(4,128)(4,1)S(1)}, u32[]{:S(2)}) copy-start(pred[4,8]{1,0:T(4,128)(4,1)S(1)} %broadcast_in_dim.40) | copy-start | bytes 100
  83.4 41.1 %copy-start.1 = (s32[1024]{0:T(1024)}, s32[1024]{0:T(1024)S(1)}, u32[]{:S(2)}) copy-start(s32[1024]{0:T(1024)S(1)} %pad_clamp_fusion) | copy-start | bytes 12292
  83.5 43.7 %copy-start.4 = (pred[32]{0:T(512)(128)(4,1)}, pred[32]{0:T(512)(128)(4,1)S(1)}, u32[]{:S(2)}) copy-start(pred[32]{0:T(512)(128)(4,1)S(1)} %compare_and_fusion) | copy-start | bytes 100
  114.9 5.8 %collective-permute-start.2 = (bf16[2,384,128]{2,1,0:T(8,128)(2,1)S(1)}, bf16[2,384,128]{2,1,0:T(8,128)(2,1)S(1)}, u32[]{:S(2)}, u32[]{:S(2)}) collective-permute-start(bf16[2,384,128]{2,1,0:T(8,128)(2,1)S(1)} %broadcast_select_fusion.11), channel_id=1, source_target_pairs={{0,16},{16,32},{32,48},{48,64},{64,80},{80,96},{96,112},{112,128},... | collective-permute-start | bytes 589832 | tf_op jit(solution)/shard_map/ppermute | solution.py:15
  118.2 6.3 %collective-permute-start.3 = (bf16[2,384,128]{2,1,0:T(8,128)(2,1)S(1)}, bf16[2,384,128]{2,1,0:T(8,128)(2,1)S(1)}, u32[]{:S(2)}, u32[]{:S(2)}) collective-permute-start(bf16[2,384,128]{2,1,0:T(8,128)(2,1)S(1)} %broadcast_select_fusion.8), channel_id=1, source_target_pairs={{0,240},{16,0},{32,16},{48,32},{64,48},{80,64},{96,80},{112,96},{1... | collective-permute-start | bytes 589832 | tf_op jit(solution)/shard_map/ppermute | solution.py:15
  140.0 2.6 %collective-permute-start.4 = (bf16[2,384,128]{2,1,0:T(8,128)(2,1)S(1)}, bf16[2,384,128]{2,1,0:T(8,128)(2,1)S(1)}, u32[]{:S(2)}, u32[]{:S(2)}) collective-permute-start(bf16[2,384,128]{2,1,0:T(8,128)(2,1)S(1)} %broadcast_select_fusion.10), channel_id=1, source_target_pairs={{0,16},{16,32},{32,48},{48,64},{64,80},{80,96},{96,112},{112,128},... | collective-permute-start | bytes 589832 | tf_op jit(solution)/shard_map/ppermute | solution.py:15
  140.0 6.4 %collective-permute-start.5 = (bf16[2,384,128]{2,1,0:T(8,128)(2,1)S(1)}, bf16[2,384,128]{2,1,0:T(8,128)(2,1)}, u32[]{:S(2)}, u32[]{:S(2)}) collective-permute-start(bf16[2,384,128]{2,1,0:T(8,128)(2,1)S(1)} %broadcast_select_fusion.7), channel_id=1, source_target_pairs={{0,240},{16,0},{32,16},{48,32},{64,48},{80,64},{96,80},{112,96},{1... | collective-permute-start | bytes 589832 | tf_op jit(solution)/shard_map/ppermute | solution.py:15
  142.7 0.7 copy-start
  147.6 2.7 %copy-start.5 = (pred[32]{0:T(512)(128)(4,1)S(1)}, pred[32]{0:T(512)(128)(4,1)}, u32[]{:S(2)}) copy-start(pred[32]{0:T(512)(128)(4,1)} %copy-done.4) | copy-start | bytes 100
  150.3 2.3 %copy-start.11 = (pred[4,8]{1,0:T(4,128)(4,1)S(1)}, pred[4,8]{1,0:T(4,128)(4,1)}, u32[]{:S(2)}) copy-start(pred[4,8]{1,0:T(4,128)(4,1)} %copy-done.10) | copy-start | bytes 100
Sparse Core Ops, SparseCore 0:
  9.8 86.1 all-gather.1
where the time goes:
time: 168 us; the launch traced here: 167 us
  blocking collectives  55.8 us (33%)
  local copies, waits for them, and re-layouts  26.2 us (16%)
  matrix products  20.1 us (12%)
  waiting for transfers between devices  18 us (11%)
  starting transfers between devices  17.7 us (11%)
  other arithmetic  15.2 us (9%)
  between operations  14.4 us (9%)
    unnamed x1, blocking collectives  34.7 us
    all_gather x1, blocking collectives, local(): lax.all_gather(residual, 'grp', axis=0, tiled=True)  21.1 us
    dot_general x3, matrix products, apply_operator(): jnp.einsum('rkij,rkjn->rin', ordered, operand, preferred_element_type=jnp...  20.1 us
    ppermute x6, starting transfers between devices, from_behind(): lax.ppermute(shard, axis, [(i, (i + by) % devices) for i in range(devices)])  17.7 us
    ppermute x6, waiting for transfers between devices, from_behind(): lax.ppermute(shard, axis, [(i, (i + by) % devices) for i in range(devices)])  17.2 us
    gather x1, local copies, waits for them, and re-layouts, local(): ordered = jnp.take(group_tiles, placed, axis=0)  9.76 us
    select_n x4, other arithmetic, apply_operator(): jnp.take(extended, flat_cols, axis=0)  8.43 us
    gather x3, local copies, waits for them, and re-layouts, apply_operator(): jnp.take(extended, flat_cols, axis=0)  7.96 us
  transfers between devices with their start and end apart: 7, of which 7 were waited for; matrix products, arithmetic and copies ran while one was open for 7% of the time, Pallas kernels for 0%

commit v1 on v0

v1 whole, which is shorter than its diff:
```python
import jax
import jax.numpy as jnp
from jax import lax
from jax.experimental import pallas as pl
from jax.experimental.pallas import tpu as pltpu
from jax.sharding import PartitionSpec as P

TILE = 384
NRHS = 128
SIDE = 4
GROUP = 16
SHARE = 96
SLAB = 24
TILES = 32
PIECE = 96
F32 = jnp.float32
BF16 = jnp.bfloat16
GAIN = 8.0 / 7.0

X_GROUPS = [[SIDE * x + y for x in range(SIDE)] for y in range(SIDE)]
VMEM = pl.BlockSpec(memory_space=pltpu.VMEM)
SMEM = pl.BlockSpec(memory_space=pltpu.SMEM)


def column_of(row, first, count):
    line = lax.broadcasted_iota(jnp.int32, (count, 128), 0) + first
    lane = lax.broadcasted_iota(jnp.int32, (count, 128), 1)
    return jnp.sum(jnp.where(line == lane, jnp.broadcast_to(row, (count, 128)), 0.0), axis=1, keepdims=True)


def pack_kernel(tiles_ref, residual_ref, diag_ref, out_ref):
    diag_row = jnp.concatenate([diag_ref[...], jnp.zeros((1, 128 - SHARE), F32)], axis=1)
    scaled = residual_ref[...] * column_of(diag_row, 0, SHARE)
    high = scaled.astype(BF16)
    low = scaled - high.astype(F32)
    high = high.astype(F32)
    wide = jnp.concatenate([high[32 * k:32 * k + 32] for k in range(3)], axis=1).astype(BF16)
    d_high = diag_row.astype(BF16).astype(F32)
    d_mid = (diag_row - d_high).astype(BF16).astype(F32)
    d_low = diag_row - d_high - d_mid
    d_rows = jnp.broadcast_to(jnp.concatenate([d_high, d_mid, d_low], axis=1), (8, 384))
    tiles = [tiles_ref[j].astype(F32) for j in range(2)]
    for x in range(SIDE):
        mine = low[SLAB * x:SLAB * (x + 1)]
        low_rows = jnp.concatenate([mine[8 * k:8 * k + 8] for k in range(3)], axis=1)
        tail = jnp.concatenate([low_rows, d_rows], axis=0).astype(BF16)
        for q in range(SIDE):
            at = SHARE * q + SLAB * x
            slab = jnp.concatenate([tile[at:at + SLAB] for tile in tiles], axis=0).astype(BF16)
            out_ref[SIDE * x + q, 0:48] = slab
            out_ref[SIDE * x + q, 48:80] = wide
            out_ref[SIDE * x + q, 80:96] = tail


def send_blocks(rows_ref, lead, own_ref, up_ref, down_ref):
    for h in range(2):
        up_ref[h] = own_ref[rows_ref[lead, 0, h]]
        down_ref[h] = own_ref[rows_ref[lead, 1, h]]


def first_pick_kernel(place_ref, rows_ref, got_ref, own_ref, up_ref, down_ref):
    for source in range(GROUP):
        for k in range(3):
            at = SHARE * (source % SIDE) + 32 * k
            own_ref[source // SIDE, at:at + 32] = got_ref[source, 48:80, 128 * k:128 * k + 128]
    send_blocks(rows_ref, place_ref[0], own_ref, up_ref, down_ref)


def pick_kernel(place_ref, rows_ref, got_ref, own_ref, up_ref, down_ref):
    for q in range(SIDE):
        parts = [got_ref[SIDE * x + q].astype(F32) for x in range(SIDE)]
        for r in range(SIDE):
            block = jnp.concatenate([p[SLAB * r:SLAB * (r + 1)] for p in parts], axis=0)
            own_ref[r, SHARE * q:SHARE * (q + 1)] = block.astype(BF16)
    send_blocks(rows_ref, place_ref[0], own_ref, up_ref, down_ref)


def coupled(slot_ref, cols_ref, got_ref, own_ref, low_ref, high_ref, product_ref, total_ref):
    slabs = jnp.concatenate([got_ref[m, 0:48] for m in range(GROUP)], axis=0)
    blocks = [own_ref[k] for k in range(4)] + [low_ref[k] for k in range(2)] + [high_ref[k] for k in range(2)]
    for pair in range(4):
        wide = jnp.concatenate(blocks[2 * pair:2 * pair + 2], axis=1)
        product = jnp.dot(slabs, wide, preferred_element_type=F32)
        product_ref[2 * pair] = product[:, :128]
        product_ref[2 * pair + 1] = product[:, 128:]
    total_ref[...] = jnp.zeros_like(total_ref)
    for t in range(TILES):
        slot = slot_ref[0, t]
        row = lax.shift_right_logical(slot, 3)
        col = cols_ref[row, lax.bitwise_and(slot, 7)]
        total_ref[row] += product_ref[col, SLAB * t:SLAB * (t + 1)]
    return total_ref[...].reshape(SHARE, NRHS)


def spread(value, out_ref):
    value = value.astype(BF16)
    for m in range(GROUP):
        out_ref[m] = value


def first_kernel(place_ref, slot_ref, cols_ref, got_ref, own_ref, low_ref, high_ref,
                 wide_ref, first_ref, start_ref, scale_ref, product_ref, total_ref, line_ref):
    x, q = place_ref[1], place_ref[2]
    for r in range(SIDE):
        source = SIDE * r + q
        tail = got_ref[source, 80:96].astype(F32)
        top = got_ref[source, 48:80].astype(F32)
        line_ref[...] = jnp.concatenate([top[:, 128 * k:128 * k + 128] for k in range(3)], axis=0)
        high = line_ref[pl.ds(pl.multiple_of(x * SLAB, 8), SLAB), :]
        low = jnp.concatenate([tail[0:8, 128 * k:128 * k + 128] for k in range(3)], axis=0)
        row = tail[8:9, 0:128] + (tail[8:9, 128:256] + tail[8:9, 256:384])
        start_ref[SLAB * r:SLAB * (r + 1)] = high + low
        scale_ref[SLAB * r:SLAB * (r + 1)] = jnp.broadcast_to(column_of(row, x * SLAB, SLAB), (SLAB, NRHS))
    total = coupled(slot_ref, cols_ref, got_ref, own_ref, low_ref, high_ref, product_ref, total_ref)
    first = GAIN * (start_ref[...] - scale_ref[...] * total)
    first_ref[...] = first
    spread(first, wide_ref)


def second_kernel(slot_ref, cols_ref, got_ref, own_ref, low_ref, high_ref, first_ref, start_ref, scale_ref,
                  wide_ref, second_ref, product_ref, total_ref):
    total = coupled(slot_ref, cols_ref, got_ref, own_ref, low_ref, high_ref, product_ref, total_ref)
    second = start_ref[...] - first_ref[...] - scale_ref[...] * total
    second_ref[...] = second
    spread(second, wide_ref)


def last_kernel(slot_ref, cols_ref, got_ref, own_ref, low_ref, high_ref, first_ref, second_ref, scale_ref,
                out_ref, product_ref, total_ref):
    total = coupled(slot_ref, cols_ref, got_ref, own_ref, low_ref, high_ref, product_ref, total_ref)
    out_ref[...] = first_ref[...] + GAIN * (second_ref[...] - scale_ref[...] * total)


def arr(shape, dtype):
    return jax.ShapeDtypeStruct(shape, dtype)


def call(kernel, name, specs, outs, scratch=()):
    return pl.pallas_call(kernel, name=name, in_specs=specs, out_specs=[VMEM] * len(outs),
                          out_shape=outs, scratch_shapes=list(scratch))


WORK = (pltpu.VMEM((8, TILES * SLAB, NRHS), F32), pltpu.VMEM((SIDE, SLAB, NRHS), F32))
PICKED = [arr((SIDE, TILE, NRHS), BF16), arr((2, TILE, NRHS), BF16), arr((2, TILE, NRHS), BF16)]
ROWS = arr((SHARE, NRHS), F32)
WIDE = arr((GROUP, SHARE, NRHS), BF16)


def local(matrix_tiles, tile_slot, tile_cols, send_rows, residual, diag_inv):
    leads = lax.axis_size("lead")
    lead, member = lax.axis_index("lead"), lax.axis_index("grp")
    place = jnp.stack([lead, member // SIDE, member % SIDE]).astype(jnp.int32)
    ahead = [(i, (i + 1) % leads) for i in range(leads)]
    behind = [(i, (i - 1) % leads) for i in range(leads)]

    def halo(up, down):
        return lax.ppermute(up, "lead", ahead), lax.ppermute(down, "lead", behind)

    def gather(wide):
        return lax.all_to_all(wide, "grp", 0, 0)

    packed, = call(pack_kernel, "pack", [VMEM] * 3, [arr((GROUP, PIECE, TILE), BF16)])(
        matrix_tiles, residual, diag_inv.reshape(1, SHARE))
    got = gather(packed)
    pick_specs = [SMEM, SMEM, VMEM]
    own, up, down = call(first_pick_kernel, "pick0", pick_specs, PICKED)(place, send_rows, got)
    low, high = halo(up, down)
    wide, first, start, scale = call(
        first_kernel, "apply0", [SMEM] * 3 + [VMEM] * 4, [WIDE, ROWS, ROWS, ROWS],
        WORK + (pltpu.VMEM((SHARE, NRHS), F32),))(place, tile_slot, tile_cols, got, own, low, high)
    own, up, down = call(pick_kernel, "pick1", pick_specs, PICKED)(place, send_rows, gather(wide))
    low, high = halo(up, down)
    wide, second = call(second_kernel, "apply1", [SMEM] * 2 + [VMEM] * 7, [WIDE, ROWS], WORK)(
        tile_slot, tile_cols, got, own, low, high, first, start, scale)
    own, up, down = call(pick_kernel, "pick2", pick_specs, PICKED)(place, send_rows, gather(wide))
    low, high = halo(up, down)
    result, = call(last_kernel, "apply2", [SMEM] * 2 + [VMEM] * 7, [ROWS], WORK)(
        tile_slot, tile_cols, got, own, low, high, first, second, scale)
    home = lax.all_to_all(result.reshape(SIDE, SLAB, NRHS), "grp", 0, 0, axis_index_groups=X_GROUPS)
    return home.reshape(SHARE, NRHS)


def solution(mesh):
    in_specs = (
        P(("lead", "grp"), None, None),
        P("lead", None),
        P("lead", None),
        P(),
        P(("lead", "grp"), None),
        P(("lead", "grp")),
    )
    out_specs = P(("lead", "grp"), None)
    return jax.shard_map(local, mesh=mesh, in_specs=in_specs, out_specs=out_specs, check_vma=False)
```

time: 168 us -> 109 us (0.65)
  blocking collectives: 55.8 us -> 32 us
  local copies, waits for them, and re-layouts: 26.2 us -> 4.41 us
  matrix products: 20.1 us -> 0 us
  Pallas kernels: 0 us -> 18.6 us
  waiting for transfers between devices: 18 us -> 35.2 us
  other arithmetic: 15.2 us -> 0.59 us
  between operations: 14.4 us -> 0.06 us
    unnamed x1 -> x0, blocking collectives: 34.7 us -> none
    all_to_all x0 -> x3, blocking collectives: none -> 32 us  [the longest x2 24.3 us: gather(): return lax.all_to_all(wide, 'grp', 0, 0)]
    gather x10 -> x0, local copies, waits for them, and re-layouts: 21.5 us -> none  [the longest x1 9.76 us: local(): ordered = jnp.take(group_tiles, placed, axis=0)]
    all_gather x1 -> x0, blocking collectives: 21.1 us -> none  [local(): lax.all_gather(residual, 'grp', axis=0, tiled=True)]
    dot_general x3 -> x0, matrix products: 20.1 us -> none  [apply_operator(): jnp.einsum('rkij,rkjn->rin', ordered, operand, preferred_element_type=jnp...]
    pallas_call x0 -> x7, Pallas kernels: none -> 18.6 us  [the longest x1 3.47 us: local(): call(second_kernel, 'apply1', [SMEM] * 2 + [VMEM] * 7, [WIDE, ROWS], WORK)]
    all_to_all x0 -> x1, waiting for transfers between devices: none -> 15.7 us  [gather(): return lax.all_to_all(wide, 'grp', 0, 0)]
    select_n x14 -> x0, other arithmetic: 10.2 us -> none  [the longest x4 8.43 us: apply_operator(): jnp.take(extended, flat_cols, axis=0)]
  transfers between devices with their start and end apart: 7 -> 7, of which waited for: 7 -> 7; matrix products, arithmetic and copies ran while one was open for 7% -> 1% of each run, Pallas kernels for 0% -> 0%
where the time goes in v1:
time: 109 us
  waiting for transfers between devices  35.2 us (32%)
  blocking collectives  32 us (29%)
  Pallas kernels  18.6 us (17%)
  starting transfers between devices  17.7 us (16%)
  local copies, waits for them, and re-layouts  4.41 us (4%)
    all_to_all x2, blocking collectives, gather(): return lax.all_to_all(wide, 'grp', 0, 0)  24.3 us
    ppermute x6, waiting for transfers between devices, halo(): return (lax.ppermute(up, 'lead', ahead), lax.ppermute(down, 'lead', behind))  19.5 us
    all_to_all x1, waiting for transfers between devices, gather(): return lax.all_to_all(wide, 'grp', 0, 0)  15.7 us
    ppermute x6, starting transfers between devices, halo(): return (lax.ppermute(up, 'lead', ahead), lax.ppermute(down, 'lead', behind))  10.8 us
    all_to_all x1, blocking collectives, local(): lax.all_to_all(result.reshape(SIDE, SLAB, NRHS), 'grp', 0, 0, axis_index_...  7.63 us
    all_to_all x1, starting transfers between devices, gather(): return lax.all_to_all(wide, 'grp', 0, 0)  6.89 us
    unnamed x18, local copies, waits for them, and re-layouts  4.41 us
    pallas_call x1, Pallas kernels, local(): call(second_kernel, 'apply1', [SMEM] * 2 + [VMEM] * 7, [WIDE, ROWS], WORK)  3.47 us
  transfers between devices with their start and end apart: 7, of which 7 were waited for; matrix products, arithmetic and copies ran while one was open for 1% of the time, Pallas kernels for 0%

profile of v1, /device:TPU:97, one launch (start us, length us, event | category | flops | bytes accessed | tf_op | source)
XLA Modules:
  0.0 108.6 jit_solution(5683372501975092242)
XLA Ops:
  0.0 2.3 %pack.1 = bf16[16,96,384]{2,1,0:T(8,128)(2,1)} custom-call(bf16[2,384,384]{2,1,0:T(8,128)(2,1)} %tiles_ref.1, f32[96,128]{1,0:T(8,128)} %residual_ref.1, f32[1,96]{1,0:T(1,128)} %bitcast.8), custom_call_target="tpu_custom_call" | custom-call | tf_op jit(solution)/shard_map/pack/pallas_call | solution.py:162
  2.3 0.0 copy-start.7
  2.3 6.9 %all-to-all-start = ((bf16[16,96,384]{2,1,0:T(8,128)(2,1)}), bf16[16,96,384]{2,1,0:T(8,128)(2,1)S(1)}, u32[]{:S(2)}, u32[]{:S(2)}) async-start(bf16[16,96,384]{2,1,0:T(8,128)(2,1)} %pack.1), calls=%async_computation | async-start | bytes 2359296 | tf_op jit(solution)/shard_map/all_to_all | solution.py:160
  9.2 0.0 copy-done.7
  9.2 0.7 copy.9.rows_ref
  9.9 0.6 pad_add_fusion.place_ref
  10.5 15.7 %all-to-all-done.got_ref = bf16[16,96,384]{2,1,0:T(8,128)(2,1)S(1)} async-done(((bf16[16,96,384]{2,1,0:T(8,128)(2,1)}), bf16[16,96,384]{2,1,0:T(8,128)(2,1)S(1)}, u32[]{:S(2)}, u32[]{:S(2)}) %all-to-all-start) | async-done | bytes 1179680 | tf_op jit(solution)/shard_map/all_to_all | solution.py:160
  26.2 0.0 copy-start
  26.2 1.0 copy-done
  27.2 2.2 %pick0.1 = (bf16[4,384,128]{2,1,0:T(8,128)(2,1)}, bf16[2,384,128]{2,1,0:T(8,128)(2,1)}, bf16[2,384,128]{2,1,0:T(8,128)(2,1)}) custom-call(s32[3]{0:T(128)} %pad_add_fusion.place_ref, s32[16,2,2]{2,1,0:T(2,128)} %copy.9.rows_ref, bf16[16,96,384]{2,1,0:T(8,128)(2,1)} %copy-done), custom_call_target="tpu_custom_call" | custom-call | tf_op jit(solution)/shard_map/pick0/pallas_call | solution.py:166
  29.4 6.0 %collective-permute-start = (bf16[2,384,128]{2,1,0:T(8,128)(2,1)}, bf16[2,384,128]{2,1,0:T(8,128)(2,1)S(1)}, u32[]{:S(2)}, u32[]{:S(2)}) collective-permute-start(bf16[2,384,128]{2,1,0:T(8,128)(2,1)} %get-tuple-element.21), channel_id=1, source_target_pairs={{0,16},{16,32},{32,48},{48,64},{64,80},{80,96},{96,112},{112,128},... | collective-permute-start | bytes 589832 | tf_op jit(solution)/shard_map/ppermute | solution.py:157
  35.4 0.0 collective-permute-start.1
  35.4 2.9 %collective-permute-done.low_ref = bf16[2,384,128]{2,1,0:T(8,128)(2,1)S(1)} collective-permute-done((bf16[2,384,128]{2,1,0:T(8,128)(2,1)}, bf16[2,384,128]{2,1,0:T(8,128)(2,1)S(1)}, u32[]{:S(2)}, u32[]{:S(2)}) %collective-permute-start) | collective-permute-done | bytes 196640 | tf_op jit(solution)/shard_map/ppermute | solution.py:157
  38.4 0.0 copy-start.1
  38.4 3.6 %collective-permute-done.1.high_ref = bf16[2,384,128]{2,1,0:T(8,128)(2,1)S(1)} collective-permute-done((bf16[2,384,128]{2,1,0:T(8,128)(2,1)}, bf16[2,384,128]{2,1,0:T(8,128)(2,1)S(1)}, u32[]{:S(2)}, u32[]{:S(2)}) %collective-permute-start.1) | collective-permute-done | bytes 196640 | tf_op jit(solution)/shard_map/ppermute | solution.py:157
  42.0 0.0 copy-start.2
  42.0 0.0 copy-done.1
  42.0 0.7 copy-done.2
  42.6 3.5 %apply0.1 = (bf16[16,96,128]{2,1,0:T(8,128)(2,1)}, f32[96,128]{1,0:T(8,128)}, f32[96,128]{1,0:T(8,128)}, f32[96,128]{1,0:T(8,128)}) custom-call(s32[3]{0:T(128)} %pad_add_fusion.place_ref, s32[1,32]{1,0:T(1,128)} %slot_ref.5, s32[4,8]{1,0:T(4,128)} %cols_ref.5, bf16[16,96,384]{2,1,0:T(8,128)(2,1)} %copy-done, ...), custom_call_target="tpu_custom_call" | custom-call | tf_op jit(solution)/shard_map/apply0/pallas_call | solution.py:168
  46.1 12.2 %all_to_all.20.got_ref = bf16[16,96,128]{2,1,0:T(8,128)(2,1)} all-to-all(bf16[16,96,128]{2,1,0:T(8,128)(2,1)} %get-tuple-element.23), channel_id=1, replica_groups=mesh['lead'=16,'grp'=16] {'grp'}, dimensions={0} | all-to-all | bytes 786432 | tf_op jit(solution)/shard_map/all_to_all | solution.py:160
  58.3 2.0 %pick1.1 = (bf16[4,384,128]{2,1,0:T(8,128)(2,1)}, bf16[2,384,128]{2,1,0:T(8,128)(2,1)}, bf16[2,384,128]{2,1,0:T(8,128)(2,1)}) custom-call(s32[3]{0:T(128)} %pad_add_fusion.place_ref, s32[16,2,2]{2,1,0:T(2,128)} %copy.9.rows_ref, bf16[16,96,128]{2,1,0:T(8,128)(2,1)} %all_to_all.20.got_ref), custom_call_target="tpu_custom_call" | custom-call | tf_op jit(solution)/shard_map/pick1/pallas_call | solution.py:171
  60.2 2.4 %collective-permute-start.2 = (bf16[2,384,128]{2,1,0:T(8,128)(2,1)}, bf16[2,384,128]{2,1,0:T(8,128)(2,1)S(1)}, u32[]{:S(2)}, u32[]{:S(2)}) collective-permute-start(bf16[2,384,128]{2,1,0:T(8,128)(2,1)} %get-tuple-element.25), channel_id=1, source_target_pairs={{0,16},{16,32},{32,48},{48,64},{64,80},{80,96},{96,112},{112,128},... | collective-permute-start | bytes 589832 | tf_op jit(solution)/shard_map/ppermute | solution.py:157
  62.6 0.0 collective-permute-start.3
  62.6 2.9 %collective-permute-done.2.low_ref = bf16[2,384,128]{2,1,0:T(8,128)(2,1)S(1)} collective-permute-done((bf16[2,384,128]{2,1,0:T(8,128)(2,1)}, bf16[2,384,128]{2,1,0:T(8,128)(2,1)S(1)}, u32[]{:S(2)}, u32[]{:S(2)}) %collective-permute-start.2) | collective-permute-done | bytes 196640 | tf_op jit(solution)/shard_map/ppermute | solution.py:157
  65.6 0.0 copy-start.4
  65.6 3.6 %collective-permute-done.3.high_ref = bf16[2,384,128]{2,1,0:T(8,128)(2,1)S(1)} collective-permute-done((bf16[2,384,128]{2,1,0:T(8,128)(2,1)}, bf16[2,384,128]{2,1,0:T(8,128)(2,1)S(1)}, u32[]{:S(2)}, u32[]{:S(2)}) %collective-permute-start.3) | collective-permute-done | bytes 196640 | tf_op jit(solution)/shard_map/ppermute | solution.py:157
  69.1 0.0 copy-start.6
  69.1 0.0 copy-done.4
  69.1 0.7 copy-done.6
  69.8 3.5 %apply1.1 = (bf16[16,96,128]{2,1,0:T(8,128)(2,1)}, f32[96,128]{1,0:T(8,128)}) custom-call(s32[1,32]{1,0:T(1,128)} %slot_ref.5, s32[4,8]{1,0:T(4,128)} %cols_ref.5, bf16[16,96,384]{2,1,0:T(8,128)(2,1)} %copy-done, bf16[4,384,128]{2,1,0:T(8,128)(2,1)} %get-tuple-element.24.own_ref, bf16[2,384,128]{2,1,0:T(8,128)(2,1)} %copy-done.4, ...), custom_call_target="tpu_custom_call" | custom-call | tf_op jit(solution)/shard_map/apply1/pallas_call | solution.py:173
  73.3 12.2 %all_to_all.21.got_ref = bf16[16,96,128]{2,1,0:T(8,128)(2,1)} all-to-all(bf16[16,96,128]{2,1,0:T(8,128)(2,1)} %get-tuple-element.30), channel_id=1, replica_groups=mesh['lead'=16,'grp'=16] {'grp'}, dimensions={0} | all-to-all | bytes 786432 | tf_op jit(solution)/shard_map/all_to_all | solution.py:160
  85.5 2.0 %pick2.1 = (bf16[4,384,128]{2,1,0:T(8,128)(2,1)}, bf16[2,384,128]{2,1,0:T(8,128)(2,1)}, bf16[2,384,128]{2,1,0:T(8,128)(2,1)}) custom-call(s32[3]{0:T(128)} %pad_add_fusion.place_ref, s32[16,2,2]{2,1,0:T(2,128)} %copy.9.rows_ref, bf16[16,96,128]{2,1,0:T(8,128)(2,1)} %all_to_all.21.got_ref), custom_call_target="tpu_custom_call" | custom-call | tf_op jit(solution)/shard_map/pick2/pallas_call | solution.py:175
  87.4 2.4 %collective-permute-start.4 = (bf16[2,384,128]{2,1,0:T(8,128)(2,1)}, bf16[2,384,128]{2,1,0:T(8,128)(2,1)S(1)}, u32[]{:S(2)}, u32[]{:S(2)}) collective-permute-start(bf16[2,384,128]{2,1,0:T(8,128)(2,1)} %get-tuple-element.32), channel_id=1, source_target_pairs={{0,16},{16,32},{32,48},{48,64},{64,80},{80,96},{96,112},{112,128},... | collective-permute-start | bytes 589832 | tf_op jit(solution)/shard_map/ppermute | solution.py:157
  89.8 0.0 collective-permute-start.5
  89.8 2.9 %collective-permute-done.4.low_ref = bf16[2,384,128]{2,1,0:T(8,128)(2,1)S(1)} collective-permute-done((bf16[2,384,128]{2,1,0:T(8,128)(2,1)}, bf16[2,384,128]{2,1,0:T(8,128)(2,1)S(1)}, u32[]{:S(2)}, u32[]{:S(2)}) %collective-permute-start.4) | collective-permute-done | bytes 196640 | tf_op jit(solution)/shard_map/ppermute | solution.py:157
  92.7 0.0 copy-start.3
  92.7 3.6 %collective-permute-done.5.high_ref = bf16[2,384,128]{2,1,0:T(8,128)(2,1)S(1)} collective-permute-done((bf16[2,384,128]{2,1,0:T(8,128)(2,1)}, bf16[2,384,128]{2,1,0:T(8,128)(2,1)S(1)}, u32[]{:S(2)}, u32[]{:S(2)}) %collective-permute-start.5) | collective-permute-done | bytes 196640 | tf_op jit(solution)/shard_map/ppermute | solution.py:157
  96.3 0.0 copy-start.5
  96.3 0.0 copy-done.3
  96.3 0.7 copy-done.5
  97.0 3.3 %apply2.1 = f32[96,128]{1,0:T(8,128)} custom-call(s32[1,32]{1,0:T(1,128)} %slot_ref.5, s32[4,8]{1,0:T(4,128)} %cols_ref.5, bf16[16,96,384]{2,1,0:T(8,128)(2,1)} %copy-done, bf16[4,384,128]{2,1,0:T(8,128)(2,1)} %get-tuple-element.31.own_ref, bf16[2,384,128]{2,1,0:T(8,128)(2,1)} %copy-done.3, bf16[2,384,128]{2,1,0:T(8,128)(2,1)} %copy-done.5, ...), custom_call_target="tpu_custom_call" | custom-call | tf_op jit(solution)/shard_map/apply2/pallas_call | solution.py:177
  100.3 7.6 %all_to_all.22 = f32[4,24,128]{2,1,0:T(8,128)S(1)} all-to-all(f32[4,24,128]{2,1,0:T(8,128)} %bitcast.7), channel_id=1, replica_groups={{0,4,8,12},{1,5,9,13},{2,6,10,14},{3,7,11,15},{16,20,24,28},{17,21,25,2..., dimensions={0} | all-to-all | bytes 98304 | tf_op jit(solution)/shard_map/all_to_all | solution.py:179
  107.9 0.6 copy.11
Async XLA Ops:
  2.3 6.9 %copy-start.7 = (s32[16,2,2]{0,2,1:T(2,128)S(1)}, s32[16,2,2]{0,2,1:T(2,128)}, u32[]{:S(2)}) copy-start(s32[16,2,2]{0,2,1:T(2,128)} %param.9) | copy-start | bytes 772
  2.3 23.9 %all-to-all-start = ((bf16[16,96,384]{2,1,0:T(8,128)(2,1)}), bf16[16,96,384]{2,1,0:T(8,128)(2,1)S(1)}, u32[]{:S(2)}, u32[]{:S(2)}) async-start(bf16[16,96,384]{2,1,0:T(8,128)(2,1)} %pack.1), calls=%async_computation | async-start | bytes 2359296 | tf_op jit(solution)/shard_map/all_to_all | solution.py:160
  26.2 1.0 copy-start
  29.4 8.9 %collective-permute-start = (bf16[2,384,128]{2,1,0:T(8,128)(2,1)}, bf16[2,384,128]{2,1,0:T(8,128)(2,1)S(1)}, u32[]{:S(2)}, u32[]{:S(2)}) collective-permute-start(bf16[2,384,128]{2,1,0:T(8,128)(2,1)} %get-tuple-element.21), channel_id=1, source_target_pairs={{0,16},{16,32},{32,48},{48,64},{64,80},{80,96},{96,112},{112,128},... | collective-permute-start | bytes 589832 | tf_op jit(solution)/shard_map/ppermute | solution.py:157
  35.4 6.5 %collective-permute-start.1 = (bf16[2,384,128]{2,1,0:T(8,128)(2,1)}, bf16[2,384,128]{2,1,0:T(8,128)(2,1)S(1)}, u32[]{:S(2)}, u32[]{:S(2)}) collective-permute-start(bf16[2,384,128]{2,1,0:T(8,128)(2,1)} %get-tuple-element.22), channel_id=1, source_target_pairs={{0,240},{16,0},{32,16},{48,32},{64,48},{80,64},{96,80},{112,96},{1... | collective-permute-start | bytes 589832 | tf_op jit(solution)/shard_map/ppermute | solution.py:157
  38.4 3.6 %copy-start.1 = (bf16[2,384,128]{2,1,0:T(8,128)(2,1)}, bf16[2,384,128]{2,1,0:T(8,128)(2,1)S(1)}, u32[]{:S(2)}) copy-start(bf16[2,384,128]{2,1,0:T(8,128)(2,1)S(1)} %collective-permute-done.low_ref) | copy-start | bytes 589828
  42.0 0.7 copy-start.2
  60.2 5.3 %collective-permute-start.2 = (bf16[2,384,128]{2,1,0:T(8,128)(2,1)}, bf16[2,384,128]{2,1,0:T(8,128)(2,1)S(1)}, u32[]{:S(2)}, u32[]{:S(2)}) collective-permute-start(bf16[2,384,128]{2,1,0:T(8,128)(2,1)} %get-tuple-element.25), channel_id=1, source_target_pairs={{0,16},{16,32},{32,48},{48,64},{64,80},{80,96},{96,112},{112,128},... | collective-permute-start | bytes 589832 | tf_op jit(solution)/shard_map/ppermute | solution.py:157
  62.6 6.5 %collective-permute-start.3 = (bf16[2,384,128]{2,1,0:T(8,128)(2,1)}, bf16[2,384,128]{2,1,0:T(8,128)(2,1)S(1)}, u32[]{:S(2)}, u32[]{:S(2)}) collective-permute-start(bf16[2,384,128]{2,1,0:T(8,128)(2,1)} %get-tuple-element.26), channel_id=1, source_target_pairs={{0,240},{16,0},{32,16},{48,32},{64,48},{80,64},{96,80},{112,96},{1... | collective-permute-start | bytes 589832 | tf_op jit(solution)/shard_map/ppermute | solution.py:157
  65.6 3.6 %copy-start.4 = (bf16[2,384,128]{2,1,0:T(8,128)(2,1)}, bf16[2,384,128]{2,1,0:T(8,128)(2,1)S(1)}, u32[]{:S(2)}) copy-start(bf16[2,384,128]{2,1,0:T(8,128)(2,1)S(1)} %collective-permute-done.2.low_ref) | copy-start | bytes 589828
  69.1 0.7 copy-start.6
  87.4 5.3 %collective-permute-start.4 = (bf16[2,384,128]{2,1,0:T(8,128)(2,1)}, bf16[2,384,128]{2,1,0:T(8,128)(2,1)S(1)}, u32[]{:S(2)}, u32[]{:S(2)}) collective-permute-start(bf16[2,384,128]{2,1,0:T(8,128)(2,1)} %get-tuple-element.32), channel_id=1, source_target_pairs={{0,16},{16,32},{32,48},{48,64},{64,80},{80,96},{96,112},{112,128},... | collective-permute-start | bytes 589832 | tf_op jit(solution)/shard_map/ppermute | solution.py:157
  89.8 6.5 %collective-permute-start.5 = (bf16[2,384,128]{2,1,0:T(8,128)(2,1)}, bf16[2,384,128]{2,1,0:T(8,128)(2,1)S(1)}, u32[]{:S(2)}, u32[]{:S(2)}) collective-permute-start(bf16[2,384,128]{2,1,0:T(8,128)(2,1)} %get-tuple-element.33), channel_id=1, source_target_pairs={{0,240},{16,0},{32,16},{48,32},{64,48},{80,64},{96,80},{112,96},{1... | collective-permute-start | bytes 589832 | tf_op jit(solution)/shard_map/ppermute | solution.py:157
  92.7 3.6 %copy-start.3 = (bf16[2,384,128]{2,1,0:T(8,128)(2,1)}, bf16[2,384,128]{2,1,0:T(8,128)(2,1)S(1)}, u32[]{:S(2)}) copy-start(bf16[2,384,128]{2,1,0:T(8,128)(2,1)S(1)} %collective-permute-done.4.low_ref) | copy-start | bytes 589828
  96.3 0.7 copy-start.5

commit v2 on v1

v2 whole, which is shorter than its diff:
```python
import jax
import jax.numpy as jnp
from jax import lax
from jax.experimental import pallas as pl
from jax.experimental.pallas import tpu as pltpu
from jax.sharding import PartitionSpec as P

TILE = 384
NRHS = 128
SIDE = 4
GROUP = 16
SHARE = 96
SLAB = 24
TILES = 32
F32 = jnp.float32
BF16 = jnp.bfloat16
GAIN = 8.0 / 7.0

X_GROUPS = [[SIDE * x + y for x in range(SIDE)] for y in range(SIDE)]
VMEM = pl.BlockSpec(memory_space=pltpu.VMEM)
SMEM = pl.BlockSpec(memory_space=pltpu.SMEM)


def column_of(row, first, count):
    line = lax.broadcasted_iota(jnp.int32, (count, 128), 0) + first
    lane = lax.broadcasted_iota(jnp.int32, (count, 128), 1)
    return jnp.sum(jnp.where(line == lane, jnp.broadcast_to(row, (count, 128)), 0.0), axis=1, keepdims=True)


def start_kernel(residual_ref, diag_ref, wide_ref, start_ref, scale_ref):
    diag_row = jnp.concatenate([diag_ref[...], jnp.zeros((1, 128 - SHARE), F32)], axis=1)
    scale = jnp.broadcast_to(column_of(diag_row, 0, SHARE), (SHARE, NRHS))
    scaled = residual_ref[...] * scale
    scale_ref[...] = scale
    start_ref[...] = scaled
    high = scaled.astype(BF16)
    low = scaled - high.astype(F32)
    d_high = diag_row.astype(BF16).astype(F32)
    d_mid = (diag_row - d_high).astype(BF16).astype(F32)
    d_low = diag_row - d_high - d_mid
    d_rows = jnp.concatenate([d_high, d_mid, d_low] + [d_low] * 5, axis=0)
    for x in range(SIDE):
        tail = jnp.concatenate([low[SLAB * x:SLAB * (x + 1)], d_rows], axis=0).astype(BF16)
        for q in range(SIDE):
            wide_ref[SIDE * x + q, 0:SHARE] = high
            wide_ref[SIDE * x + q, SHARE:128] = tail


def pack_kernel(tiles_ref, out_ref):
    tiles = [tiles_ref[j].astype(F32) for j in range(2)]
    for x in range(SIDE):
        for q in range(SIDE):
            at = SHARE * q + SLAB * x
            out_ref[SIDE * x + q] = jnp.concatenate([tile[at:at + SLAB] for tile in tiles], axis=0).astype(BF16)


def pick_home_kernel(place_ref, rows_ref, got_ref, up_ref, down_ref):
    lead = place_ref[0]
    for side, ref in ((0, up_ref), (1, down_ref)):
        for h in range(2):
            row = rows_ref[lead, side, h]
            for q in range(SIDE):
                ref[h, SHARE * q:SHARE * (q + 1)] = got_ref[SIDE * row + q, 0:SHARE]


def pick_slab_kernel(place_ref, rows_ref, got_ref, own_ref, up_ref, down_ref):
    lead = place_ref[0]
    for q in range(SIDE):
        parts = [got_ref[SIDE * x + q, 0:SHARE].astype(F32) for x in range(SIDE)]
        for r in range(SIDE):
            block = jnp.concatenate([p[SLAB * r:SLAB * (r + 1)] for p in parts], axis=0)
            own_ref[r, SHARE * q:SHARE * (q + 1)] = block.astype(BF16)
    for side, ref in ((0, up_ref), (1, down_ref)):
        for h in range(2):
            ref[h] = own_ref[rows_ref[lead, side, h]]


def order_kernel(slot_ref, slabs_ref, out_ref):
    for t in range(TILES):
        slot = slot_ref[0, t]
        piece = slabs_ref[t // 2].astype(F32)[SLAB * (t % 2):SLAB * (t % 2 + 1)]
        out_ref[slot] = piece.astype(BF16)


def first_kernel(place_ref, slot_ref, cols_ref, slabs_ref, got_ref, low_ref, high_ref,
                 wide_ref, product_ref, total_ref, line_ref):
    x, q = place_ref[1], place_ref[2]
    slabs = jnp.concatenate([slabs_ref[m] for m in range(GROUP)], axis=0)
    own = [jnp.concatenate([got_ref[SIDE * r + s, 0:SHARE] for s in range(SIDE)], axis=0) for r in range(SIDE)]
    blocks = own + [low_ref[0], low_ref[1], high_ref[0], high_ref[1]]
    for pair in range(4):
        wide = jnp.concatenate(blocks[2 * pair:2 * pair + 2], axis=1)
        product = jnp.dot(slabs, wide, preferred_element_type=F32)
        product_ref[2 * pair] = product[:, :128]
        product_ref[2 * pair + 1] = product[:, 128:]
    total_ref[...] = jnp.zeros_like(total_ref)
    for t in range(TILES):
        slot = slot_ref[0, t]
        row = lax.shift_right_logical(slot, 3)
        col = cols_ref[row, lax.bitwise_and(slot, 7)]
        total_ref[row] += product_ref[col, SLAB * t:SLAB * (t + 1)]
    firsts = []
    for r in range(SIDE):
        whole = got_ref[SIDE * r + q].astype(F32)
        line_ref[...] = whole
        high = line_ref[pl.ds(pl.multiple_of(x * SLAB, 8), SLAB), :]
        row = whole[120:121] + (whole[121:122] + whole[122:123])
        scale = column_of(row, x * SLAB, SLAB)
        firsts.append(GAIN * (high + whole[SHARE:120] - scale * total_ref[r]))
    first = jnp.concatenate(firsts, axis=0)
    high = first.astype(BF16)
    low = first - high.astype(F32)
    for r in range(SIDE):
        tail = jnp.concatenate([low[SLAB * r:SLAB * (r + 1)], jnp.zeros((8, NRHS), F32)], axis=0).astype(BF16)
        for s in range(SIDE):
            wide_ref[SIDE * r + s, 0:SHARE] = high
            wide_ref[SIDE * r + s, SHARE:128] = tail


def home_product(place_ref, cols_ref, matrix_ref, ext_ref):
    row = place_ref[1]
    total = jnp.zeros((SHARE, NRHS), F32)
    for k in range(8):
        left = jnp.concatenate([matrix_ref[s, k] for s in range(SIDE)], axis=0)
        total += jnp.dot(left, ext_ref[cols_ref[row, k]], preferred_element_type=F32)
    return total


def fill_halo(ext_ref, low_ref, high_ref):
    for h in range(2):
        ext_ref[4 + h] = low_ref[h]
        ext_ref[6 + h] = high_ref[h]


def second_kernel(place_ref, cols_ref, matrix_ref, got_ref, own_ref, low_ref, high_ref, start_ref, scale_ref,
                  wide_ref, sum_ref, ext_ref, line_ref):
    ext_ref[0:4] = own_ref[...]
    fill_halo(ext_ref, low_ref, high_ref)
    total = home_product(place_ref, cols_ref, matrix_ref, ext_ref)
    row, q = place_ref[1], place_ref[2]
    firsts = []
    for x in range(SIDE):
        line_ref[...] = got_ref[SIDE * x + q].astype(F32)
        firsts.append(line_ref[pl.ds(pl.multiple_of(row * SLAB, 8), SLAB), :] + line_ref[SHARE:120])
    first = jnp.concatenate(firsts, axis=0)
    second = start_ref[...] - first - scale_ref[...] * total
    sum_ref[...] = first + GAIN * second
    second = second.astype(BF16)
    for m in range(GROUP):
        wide_ref[m] = second


def last_kernel(place_ref, cols_ref, matrix_ref, got_ref, low_ref, high_ref, sum_ref, scale_ref, out_ref, ext_ref):
    for r in range(SIDE):
        for q in range(SIDE):
            ext_ref[r, SHARE * q:SHARE * (q + 1)] = got_ref[SIDE * r + q]
    fill_halo(ext_ref, low_ref, high_ref)
    total = home_product(place_ref, cols_ref, matrix_ref, ext_ref)
    out_ref[...] = sum_ref[...] - GAIN * (scale_ref[...] * total)


def arr(shape, dtype):
    return pltpu.VMEM(shape, dtype)


def call(kernel, name, specs, outs, scratch=()):
    return pl.pallas_call(kernel, name=name, in_specs=specs, out_specs=[VMEM] * len(outs),
                          out_shape=outs, scratch_shapes=list(scratch))


def near(*arrays):
    out = tuple(pltpu.with_memory_space_constraint(a, pltpu.VMEM) for a in arrays)
    return out if len(out) > 1 else out[0]


HALVES = [arr((2, TILE, NRHS), BF16), arr((2, TILE, NRHS), BF16)]
ROWS = arr((SHARE, NRHS), F32)
WIDE = arr((GROUP, 128, NRHS), BF16)
EXT = pltpu.VMEM((8, TILE, NRHS), BF16)
LINE = pltpu.VMEM((128, NRHS), F32)


def local(matrix_tiles, tile_slot, tile_cols, send_rows, residual, diag_inv):
    leads = lax.axis_size("lead")
    lead, member = lax.axis_index("lead"), lax.axis_index("grp")
    place = jnp.stack([lead, member // SIDE, member % SIDE]).astype(jnp.int32)
    ahead = [(i, (i + 1) % leads) for i in range(leads)]
    behind = [(i, (i - 1) % leads) for i in range(leads)]

    def halo(up, down):
        return near(lax.ppermute(up, "lead", ahead), lax.ppermute(down, "lead", behind))

    def gather(wide):
        return near(lax.all_to_all(wide, "grp", 0, 0))

    wide, start, scale = call(start_kernel, "start", [VMEM] * 2, [WIDE, ROWS, ROWS])(
        residual, diag_inv.reshape(1, SHARE))
    start, scale = near(start, scale)
    packed, = call(pack_kernel, "pack", [VMEM], [arr((GROUP, 2 * SLAB, TILE), BF16)])(matrix_tiles)
    got0 = gather(wide)
    slabs = gather(packed)
    up, down = call(pick_home_kernel, "pick0", [SMEM] * 2 + [VMEM], HALVES)(place, send_rows, got0)
    low, high = halo(up, down)
    wide, = call(
        first_kernel, "apply0", [SMEM] * 3 + [VMEM] * 4, [WIDE],
        (pltpu.VMEM((8, TILES * SLAB, NRHS), F32), pltpu.VMEM((SIDE, SLAB, NRHS), F32), LINE))(
        place, tile_slot, tile_cols, slabs, got0, low, high)
    got1 = gather(wide)
    ordered, = call(order_kernel, "order", [SMEM, VMEM], [arr((TILES, SLAB, TILE), BF16)])(tile_slot, slabs)
    matrix = near(lax.all_to_all(ordered.reshape(SIDE, 8, SLAB, TILE), "grp", 0, 0, axis_index_groups=X_GROUPS))
    own, up, down = call(pick_slab_kernel, "pick1", [SMEM] * 2 + [VMEM],
                         [arr((SIDE, TILE, NRHS), BF16)] + HALVES)(place, send_rows, got1)
    low, high = halo(up, down)
    own = near(own)
    wide, partial = call(second_kernel, "apply1", [SMEM] * 2 + [VMEM] * 7,
                         [arr((GROUP, SHARE, NRHS), BF16), ROWS], (EXT, LINE))(
        place, tile_cols, matrix, got1, own, low, high, start, scale)
    got2 = gather(wide)
    partial = near(partial)
    up, down = call(pick_home_kernel, "pick2", [SMEM] * 2 + [VMEM], HALVES)(place, send_rows, got2)
    low, high = halo(up, down)
    result, = call(last_kernel, "apply2", [SMEM] * 2 + [VMEM] * 6, [jax.ShapeDtypeStruct((SHARE, NRHS), F32)], (EXT,))(
        place, tile_cols, matrix, got2, low, high, partial, scale)
    return result


def solution(mesh):
    in_specs = (
        P(("lead", "grp"), None, None),
        P("lead", None),
        P("lead", None),
        P(),
        P(("lead", "grp"), None),
        P(("lead", "grp")),
    )
    out_specs = P(("lead", "grp"), None)
    return jax.shard_map(local, mesh=mesh, in_specs=in_specs, out_specs=out_specs, check_vma=False)
```

time: 109 us -> 95.1 us (0.87)
  blocking collectives: 32 us -> 12.9 us
  starting transfers between devices: 17.7 us -> 30.8 us
  Pallas kernels: 18.6 us -> 13.7 us
  local copies, waits for them, and re-layouts: 4.41 us -> 1.37 us
    all_to_all x3 -> x1, blocking collectives: 32 us -> 12.9 us  [gather(): return near(lax.all_to_all(wide, 'grp', 0, 0))]
    all_to_all x1 -> x4, starting transfers between devices: 6.89 us -> 20.7 us  [the longest x3 17.2 us: gather(): return near(lax.all_to_all(wide, 'grp', 0, 0))]
    ppermute x6, waiting for transfers between devices: 19.5 us -> 12.7 us  [the longest x3 9.37 us: halo(): lax.ppermute(down, 'lead', behind)]
    all_to_all x1 -> x4, waiting for transfers between devices: 15.7 us -> 22 us  [the longest x3 17.7 us: gather(): return near(lax.all_to_all(wide, 'grp', 0, 0))]
    pallas_call x7 -> x9, Pallas kernels: 18.6 us -> 13.7 us  [the longest x1 2.69 us: local(): call(first_kernel, 'apply0', [SMEM] * 3 + [VMEM] * 4, [WIDE], (pltpu.VMEM...]
    unnamed x18 -> x3, local copies, waits for them, and re-layouts: 4.41 us -> 1.37 us
  transfers between devices with their start and end apart: 7 -> 10, of which waited for: 7 -> 9; matrix products, arithmetic and copies ran while one was open for 1% -> 1% of each run, Pallas kernels for 0% -> 6%
where the time goes in v2:
time: 95.1 us; the launch traced here: 94.2 us
  waiting for transfers between devices  34.7 us (36%)
  starting transfers between devices  30.8 us (32%)
  Pallas kernels  13.7 us (14%)
  blocking collectives  12.9 us (14%)
  local copies, waits for them, and re-layouts  1.37 us (1%)
    all_to_all x3, waiting for transfers between devices, gather(): return near(lax.all_to_all(wide, 'grp', 0, 0))  17.7 us
    all_to_all x3, starting transfers between devices, gather(): return near(lax.all_to_all(wide, 'grp', 0, 0))  17.2 us
    all_to_all x1, blocking collectives, gather(): return near(lax.all_to_all(wide, 'grp', 0, 0))  12.9 us
    ppermute x3, starting transfers between devices, halo(): lax.ppermute(up, 'lead', ahead)  10.1 us
    ppermute x3, waiting for transfers between devices, halo(): lax.ppermute(down, 'lead', behind)  9.37 us
    all_to_all x1, waiting for transfers between devices, local(): lax.all_to_all(ordered.reshape(SIDE, 8, SLAB, TILE), 'grp', 0, 0, axis_in...  4.31 us
    all_to_all x1, starting transfers between devices, local(): lax.all_to_all(ordered.reshape(SIDE, 8, SLAB, TILE), 'grp', 0, 0, axis_in...  3.48 us
    ppermute x3, waiting for transfers between devices, halo(): lax.ppermute(up, 'lead', ahead)  3.38 us
  transfers between devices with their start and end apart: 10, of which 9 were waited for; matrix products, arithmetic and copies ran while one was open for 1% of the time, Pallas kernels for 6%

profile of v2, /device:TPU:97, one launch (start us, length us, event | category | flops | bytes accessed | tf_op | source)
XLA Modules:
  0.0 94.2 jit_solution(8391187514557770174)
XLA Ops:
  0.0 1.7 %start.1 = (bf16[16,128,128]{2,1,0:T(8,128)(2,1)}, f32[96,128]{1,0:T(8,128)S(1)}, f32[96,128]{1,0:T(8,128)S(1)}) custom-call(f32[96,128]{1,0:T(8,128)} %residual_ref.1, f32[1,96]{1,0:T(1,128)} %bitcast.5), custom_call_target="tpu_custom_call" | custom-call | tf_op jit(solution)/shard_map/start/pallas_call | solution.py:196
  1.7 6.8 %all-to-all-start.2 = ((bf16[16,128,128]{2,1,0:T(8,128)(2,1)}), bf16[16,128,128]{2,1,0:T(8,128)(2,1)S(1)}, u32[]{:S(2)}, u32[]{:S(2)}) async-start(bf16[16,128,128]{2,1,0:T(8,128)(2,1)} %get-tuple-element.17), calls=%async_computation.2 | async-start | bytes 1048576 | tf_op jit(solution)/shard_map/all_to_all | solution.py:194
  8.5 1.9 %pack.1 = bf16[16,48,384]{2,1,0:T(8,128)(2,1)} custom-call(bf16[2,384,384]{2,1,0:T(8,128)(2,1)} %tiles_ref.1), custom_call_target="tpu_custom_call" | custom-call | tf_op jit(solution)/shard_map/pack/pallas_call | solution.py:199
  10.4 8.4 %all-to-all-done.2.got_ref = bf16[16,128,128]{2,1,0:T(8,128)(2,1)S(1)} async-done(((bf16[16,128,128]{2,1,0:T(8,128)(2,1)}), bf16[16,128,128]{2,1,0:T(8,128)(2,1)S(1)}, u32[]{:S(2)}, u32[]{:S(2)}) %all-to-all-start.2) | async-done | bytes 524320 | tf_op jit(solution)/shard_map/all_to_all | solution.py:194
  18.9 3.6 %all-to-all-start = ((bf16[16,48,384]{2,1,0:T(8,128)(2,1)}), bf16[16,48,384]{2,1,0:T(8,128)(2,1)S(1)}, u32[]{:S(2)}, u32[]{:S(2)}) async-start(bf16[16,48,384]{2,1,0:T(8,128)(2,1)} %pack.1), calls=%async_computation | async-start | bytes 1179648 | tf_op jit(solution)/shard_map/all_to_all | solution.py:194
  22.5 0.0 copy-start
  22.5 0.7 copy-done
  23.2 0.7 copy.7.rows_ref
  23.8 0.6 pad_add_fusion.place_ref
  24.5 1.0 %pick0.1 = (bf16[2,384,128]{2,1,0:T(8,128)(2,1)S(1)}, bf16[2,384,128]{2,1,0:T(8,128)(2,1)S(1)}) custom-call(s32[3]{0:T(128)} %pad_add_fusion.place_ref, s32[16,2,2]{2,1,0:T(2,128)} %copy.7.rows_ref, bf16[16,128,128]{2,1,0:T(8,128)(2,1)S(1)} %all-to-all-done.2.got_ref), custom_call_target="tpu_custom_call" | custom-call | tf_op jit(solution)/shard_map/pick0/pallas_call | solution.py:202
  25.4 4.8 %collective-permute-start = (bf16[2,384,128]{2,1,0:T(8,128)(2,1)S(1)}, bf16[2,384,128]{2,1,0:T(8,128)(2,1)S(1)}, u32[]{:S(2)}, u32[]{:S(2)}) collective-permute-start(bf16[2,384,128]{2,1,0:T(8,128)(2,1)S(1)} %get-tuple-element.18), channel_id=1, source_target_pairs={{0,16},{16,32},{32,48},{48,64},{64,80},{80,96},{96,112},{112,128},... | collective-permute-start | bytes 589832 | tf_op jit(solution)/shard_map/ppermute | solution.py:191
  30.3 0.0 collective-permute-start.1
  30.3 1.8 %all-to-all-done.slabs_ref = bf16[16,48,384]{2,1,0:T(8,128)(2,1)S(1)} async-done(((bf16[16,48,384]{2,1,0:T(8,128)(2,1)}), bf16[16,48,384]{2,1,0:T(8,128)(2,1)S(1)}, u32[]{:S(2)}, u32[]{:S(2)}) %all-to-all-start) | async-done | bytes 589856 | tf_op jit(solution)/shard_map/all_to_all | solution.py:194
  32.1 0.8 collective-permute-done.low_ref
  32.9 3.7 %collective-permute-done.1.high_ref = bf16[2,384,128]{2,1,0:T(8,128)(2,1)S(1)} collective-permute-done((bf16[2,384,128]{2,1,0:T(8,128)(2,1)S(1)}, bf16[2,384,128]{2,1,0:T(8,128)(2,1)S(1)}, u32[]{:S(2)}, u32[]{:S(2)}) %collective-permute-start.1) | collective-permute-done | bytes 196640 | tf_op jit(solution)/shard_map/ppermute | solution.py:191
  36.6 2.7 %apply0.1 = bf16[16,128,128]{2,1,0:T(8,128)(2,1)} custom-call(s32[3]{0:T(128)} %pad_add_fusion.place_ref, s32[1,32]{1,0:T(1,128)} %slot_ref.3, s32[4,8]{1,0:T(4,128)} %cols_ref.5, bf16[16,48,384]{2,1,0:T(8,128)(2,1)S(1)} %all-to-all-done.slabs_ref, bf16[16,128,128]{2,1,0:T(8,128)(2,1)S(1)} %all-to-all-done.2.got_ref, ...), custom_call_target="tpu_custom_call" | custom-call | tf_op jit(solution)/shard_map/apply0/pallas_call | solution.py:204
  39.3 6.9 %all-to-all-start.3 = ((bf16[16,128,128]{2,1,0:T(8,128)(2,1)}), bf16[16,128,128]{2,1,0:T(8,128)(2,1)S(1)}, u32[]{:S(2)}, u32[]{:S(2)}) async-start(bf16[16,128,128]{2,1,0:T(8,128)(2,1)} %apply0.1), calls=%async_computation.3 | async-start | bytes 1048576 | tf_op jit(solution)/shard_map/all_to_all | solution.py:194
  46.1 1.5 %order.1 = bf16[32,24,384]{2,1,0:T(8,128)(2,1)} custom-call(s32[1,32]{1,0:T(1,128)} %slot_ref.3, bf16[16,48,384]{2,1,0:T(8,128)(2,1)S(1)} %all-to-all-done.slabs_ref), custom_call_target="tpu_custom_call" | custom-call | tf_op jit(solution)/shard_map/order/pallas_call | solution.py:209
  47.7 7.4 %all-to-all-done.3.got_ref = bf16[16,128,128]{2,1,0:T(8,128)(2,1)S(1)} async-done(((bf16[16,128,128]{2,1,0:T(8,128)(2,1)}), bf16[16,128,128]{2,1,0:T(8,128)(2,1)S(1)}, u32[]{:S(2)}, u32[]{:S(2)}) %all-to-all-start.3) | async-done | bytes 524320 | tf_op jit(solution)/shard_map/all_to_all | solution.py:194
  55.1 3.5 %all-to-all-start.1 = ((bf16[4,8,24,384]{3,2,1,0:T(8,128)(2,1)}), bf16[4,8,24,384]{3,2,1,0:T(8,128)(2,1)S(1)}, u32[]{:S(2)}, u32[]{:S(2)}) async-start(bf16[4,8,24,384]{3,2,1,0:T(8,128)(2,1)} %bitcast.3), calls=%async_computation.1 | async-start | bytes 1179648 | tf_op jit(solution)/shard_map/all_to_all | solution.py:210
  58.5 1.0 %pick1.1 = (bf16[4,384,128]{2,1,0:T(8,128)(2,1)S(1)}, bf16[2,384,128]{2,1,0:T(8,128)(2,1)S(1)}, bf16[2,384,128]{2,1,0:T(8,128)(2,1)S(1)}) custom-call(s32[3]{0:T(128)} %pad_add_fusion.place_ref, s32[16,2,2]{2,1,0:T(2,128)} %copy.7.rows_ref, bf16[16,128,128]{2,1,0:T(8,128)(2,1)S(1)} %all-to-all-done.3.got_ref), custom_call_target="tpu_custom_call" | custom-call | tf_op jit(solution)/shard_map/pick1/pallas_call | solution.py:211
  59.6 3.1 %collective-permute-start.2 = (bf16[2,384,128]{2,1,0:T(8,128)(2,1)S(1)}, bf16[2,384,128]{2,1,0:T(8,128)(2,1)S(1)}, u32[]{:S(2)}, u32[]{:S(2)}) collective-permute-start(bf16[2,384,128]{2,1,0:T(8,128)(2,1)S(1)} %get-tuple-element.21), channel_id=1, source_target_pairs={{0,16},{16,32},{32,48},{48,64},{64,80},{80,96},{96,112},{112,128},... | collective-permute-start | bytes 589832 | tf_op jit(solution)/shard_map/ppermute | solution.py:191
  62.7 0.0 collective-permute-start.3
  62.7 4.3 %all-to-all-done.1.matrix_ref = bf16[4,8,24,384]{3,2,1,0:T(8,128)(2,1)S(1)} async-done(((bf16[4,8,24,384]{3,2,1,0:T(8,128)(2,1)}), bf16[4,8,24,384]{3,2,1,0:T(8,128)(2,1)S(1)}, u32[]{:S(2)}, u32[]{:S(2)}) %all-to-all-start.1) | async-done | bytes 589856 | tf_op jit(solution)/shard_map/all_to_all | solution.py:210
  67.0 0.0 collective-permute-done.2.low_ref
  67.0 2.0 %collective-permute-done.3.high_ref = bf16[2,384,128]{2,1,0:T(8,128)(2,1)S(1)} collective-permute-done((bf16[2,384,128]{2,1,0:T(8,128)(2,1)S(1)}, bf16[2,384,128]{2,1,0:T(8,128)(2,1)S(1)}, u32[]{:S(2)}, u32[]{:S(2)}) %collective-permute-start.3) | collective-permute-done | bytes 196640 | tf_op jit(solution)/shard_map/ppermute | solution.py:191
  69.0 1.1 %apply1.1 = (bf16[16,96,128]{2,1,0:T(8,128)(2,1)S(1)}, f32[96,128]{1,0:T(8,128)S(1)}) custom-call(s32[3]{0:T(128)} %pad_add_fusion.place_ref, s32[4,8]{1,0:T(4,128)} %cols_ref.5, bf16[4,8,24,384]{3,2,1,0:T(8,128)(2,1)S(1)} %all-to-all-done.1.matrix_ref, bf16[16,128,128]{2,1,0:T(8,128)(2,1)S(1)} %all-to-all-done.3.got_ref, ...), custom_call_target="tpu_custom_call" | custom-call | tf_op jit(solution)/shard_map/apply1/pallas_call | solution.py:215
  70.1 12.9 %all_to_all.25.got_ref = bf16[16,96,128]{2,1,0:T(8,128)(2,1)S(1)} all-to-all(bf16[16,96,128]{2,1,0:T(8,128)(2,1)S(1)} %get-tuple-element.25), channel_id=1, replica_groups=mesh['lead'=16,'grp'=16] {'grp'}, dimensions={0} | all-to-all | bytes 786432 | tf_op jit(solution)/shard_map/all_to_all | solution.py:194
  83.0 1.0 %pick2.1 = (bf16[2,384,128]{2,1,0:T(8,128)(2,1)S(1)}, bf16[2,384,128]{2,1,0:T(8,128)(2,1)S(1)}) custom-call(s32[3]{0:T(128)} %pad_add_fusion.place_ref, s32[16,2,2]{2,1,0:T(2,128)} %copy.7.rows_ref, bf16[16,96,128]{2,1,0:T(8,128)(2,1)S(1)} %all_to_all.25.got_ref), custom_call_target="tpu_custom_call" | custom-call | tf_op jit(solution)/shard_map/pick2/pallas_call | solution.py:220
  84.0 2.2 %collective-permute-start.4 = (bf16[2,384,128]{2,1,0:T(8,128)(2,1)S(1)}, bf16[2,384,128]{2,1,0:T(8,128)(2,1)S(1)}, u32[]{:S(2)}, u32[]{:S(2)}) collective-permute-start(bf16[2,384,128]{2,1,0:T(8,128)(2,1)S(1)} %get-tuple-element.26), channel_id=1, source_target_pairs={{0,16},{16,32},{32,48},{48,64},{64,80},{80,96},{96,112},{112,128},... | collective-permute-start | bytes 589832 | tf_op jit(solution)/shard_map/ppermute | solution.py:191
  86.2 0.0 collective-permute-start.5
  86.2 2.6 %collective-permute-done.4.low_ref = bf16[2,384,128]{2,1,0:T(8,128)(2,1)S(1)} collective-permute-done((bf16[2,384,128]{2,1,0:T(8,128)(2,1)S(1)}, bf16[2,384,128]{2,1,0:T(8,128)(2,1)S(1)}, u32[]{:S(2)}, u32[]{:S(2)}) %collective-permute-start.4) | collective-permute-done | bytes 196640 | tf_op jit(solution)/shard_map/ppermute | solution.py:191
  88.8 3.7 %collective-permute-done.5.high_ref = bf16[2,384,128]{2,1,0:T(8,128)(2,1)S(1)} collective-permute-done((bf16[2,384,128]{2,1,0:T(8,128)(2,1)S(1)}, bf16[2,384,128]{2,1,0:T(8,128)(2,1)S(1)}, u32[]{:S(2)}, u32[]{:S(2)}) %collective-permute-start.5) | collective-permute-done | bytes 196640 | tf_op jit(solution)/shard_map/ppermute | solution.py:191
  92.5 1.7 %apply2.1 = f32[96,128]{1,0:T(8,128)} custom-call(s32[3]{0:T(128)} %pad_add_fusion.place_ref, s32[4,8]{1,0:T(4,128)} %cols_ref.5, bf16[4,8,24,384]{3,2,1,0:T(8,128)(2,1)S(1)} %all-to-all-done.1.matrix_ref, bf16[16,96,128]{2,1,0:T(8,128)(2,1)S(1)} %all_to_all.25.got_ref, bf16[2,384,128]{2,1,0:T(8,128)(2,1)S(1)} %collective-permute-done.4.low_ref, ...), custom_call_target="tpu_custom_call" | custom-call | tf_op jit(solution)/shard_map/apply2/pallas_call | solution.py:222
Async XLA Ops:
  1.7 17.1 %all-to-all-start.2 = ((bf16[16,128,128]{2,1,0:T(8,128)(2,1)}), bf16[16,128,128]{2,1,0:T(8,128)(2,1)S(1)}, u32[]{:S(2)}, u32[]{:S(2)}) async-start(bf16[16,128,128]{2,1,0:T(8,128)(2,1)} %get-tuple-element.17), calls=%async_computation.2 | async-start | bytes 1048576 | tf_op jit(solution)/shard_map/all_to_all | solution.py:194
  18.9 13.2 %all-to-all-start = ((bf16[16,48,384]{2,1,0:T(8,128)(2,1)}), bf16[16,48,384]{2,1,0:T(8,128)(2,1)S(1)}, u32[]{:S(2)}, u32[]{:S(2)}) async-start(bf16[16,48,384]{2,1,0:T(8,128)(2,1)} %pack.1), calls=%async_computation | async-start | bytes 1179648 | tf_op jit(solution)/shard_map/all_to_all | solution.py:194
  22.5 0.7 copy-start
  25.4 7.4 %collective-permute-start = (bf16[2,384,128]{2,1,0:T(8,128)(2,1)S(1)}, bf16[2,384,128]{2,1,0:T(8,128)(2,1)S(1)}, u32[]{:S(2)}, u32[]{:S(2)}) collective-permute-start(bf16[2,384,128]{2,1,0:T(8,128)(2,1)S(1)} %get-tuple-element.18), channel_id=1, source_target_pairs={{0,16},{16,32},{32,48},{48,64},{64,80},{80,96},{96,112},{112,128},... | collective-permute-start | bytes 589832 | tf_op jit(solution)/shard_map/ppermute | solution.py:191
  30.3 6.3 %collective-permute-start.1 = (bf16[2,384,128]{2,1,0:T(8,128)(2,1)S(1)}, bf16[2,384,128]{2,1,0:T(8,128)(2,1)S(1)}, u32[]{:S(2)}, u32[]{:S(2)}) collective-permute-start(bf16[2,384,128]{2,1,0:T(8,128)(2,1)S(1)} %get-tuple-element.19), channel_id=1, source_target_pairs={{0,240},{16,0},{32,16},{48,32},{64,48},{80,64},{96,80},{112,96},{1... | collective-permute-start | bytes 589832 | tf_op jit(solution)/shard_map/ppermute | solution.py:191
  39.3 15.8 %all-to-all-start.3 = ((bf16[16,128,128]{2,1,0:T(8,128)(2,1)}), bf16[16,128,128]{2,1,0:T(8,128)(2,1)S(1)}, u32[]{:S(2)}, u32[]{:S(2)}) async-start(bf16[16,128,128]{2,1,0:T(8,128)(2,1)} %apply0.1), calls=%async_computation.3 | async-start | bytes 1048576 | tf_op jit(solution)/shard_map/all_to_all | solution.py:194
  55.1 12.0 %all-to-all-start.1 = ((bf16[4,8,24,384]{3,2,1,0:T(8,128)(2,1)}), bf16[4,8,24,384]{3,2,1,0:T(8,128)(2,1)S(1)}, u32[]{:S(2)}, u32[]{:S(2)}) async-start(bf16[4,8,24,384]{3,2,1,0:T(8,128)(2,1)} %bitcast.3), calls=%async_computation.1 | async-start | bytes 1179648 | tf_op jit(solution)/shard_map/all_to_all | solution.py:210
  59.6 7.4 %collective-permute-start.2 = (bf16[2,384,128]{2,1,0:T(8,128)(2,1)S(1)}, bf16[2,384,128]{2,1,0:T(8,128)(2,1)S(1)}, u32[]{:S(2)}, u32[]{:S(2)}) collective-permute-start(bf16[2,384,128]{2,1,0:T(8,128)(2,1)S(1)} %get-tuple-element.21), channel_id=1, source_target_pairs={{0,16},{16,32},{32,48},{48,64},{64,80},{80,96},{96,112},{112,128},... | collective-permute-start | bytes 589832 | tf_op jit(solution)/shard_map/ppermute | solution.py:191
  62.7 6.3 %collective-permute-start.3 = (bf16[2,384,128]{2,1,0:T(8,128)(2,1)S(1)}, bf16[2,384,128]{2,1,0:T(8,128)(2,1)S(1)}, u32[]{:S(2)}, u32[]{:S(2)}) collective-permute-start(bf16[2,384,128]{2,1,0:T(8,128)(2,1)S(1)} %get-tuple-element.22), channel_id=1, source_target_pairs={{0,240},{16,0},{32,16},{48,32},{64,48},{80,64},{96,80},{112,96},{1... | collective-permute-start | bytes 589832 | tf_op jit(solution)/shard_map/ppermute | solution.py:191
  84.0 4.8 %collective-permute-start.4 = (bf16[2,384,128]{2,1,0:T(8,128)(2,1)S(1)}, bf16[2,384,128]{2,1,0:T(8,128)(2,1)S(1)}, u32[]{:S(2)}, u32[]{:S(2)}) collective-permute-start(bf16[2,384,128]{2,1,0:T(8,128)(2,1)S(1)} %get-tuple-element.26), channel_id=1, source_target_pairs={{0,16},{16,32},{32,48},{48,64},{64,80},{80,96},{96,112},{112,128},... | collective-permute-start | bytes 589832 | tf_op jit(solution)/shard_map/ppermute | solution.py:191
  86.2 6.3 %collective-permute-start.5 = (bf16[2,384,128]{2,1,0:T(8,128)(2,1)S(1)}, bf16[2,384,128]{2,1,0:T(8,128)(2,1)S(1)}, u32[]{:S(2)}, u32[]{:S(2)}) collective-permute-start(bf16[2,384,128]{2,1,0:T(8,128)(2,1)S(1)} %get-tuple-element.27), channel_id=1, source_target_pairs={{0,240},{16,0},{32,16},{48,32},{64,48},{80,64},{96,80},{112,96},{1... | collective-permute-start | bytes 589832 | tf_op jit(solution)/shard_map/ppermute | solution.py:191

commit v3 on v2

v3 whole, which is shorter than its diff:
```python
import jax
import jax.numpy as jnp
from jax import lax
from jax.experimental import pallas as pl
from jax.experimental.pallas import tpu as pltpu
from jax.sharding import PartitionSpec as P


TILE = 384
NRHS = 128
SIDE = 4
GROUP = 16
SHARE = 96
SLAB = 24
TILES = 32
PIECE = 64
F32 = jnp.float32
BF16 = jnp.bfloat16
GRANT = 20 << 20
GAIN = 8.0 / 7.0

VMEM = pl.BlockSpec(memory_space=pltpu.VMEM)
SMEM = pl.BlockSpec(memory_space=pltpu.SMEM)


def place():
    member = lax.axis_index("grp")
    return lax.shift_right_logical(member, 2), lax.bitwise_and(member, 3)


def wrap(index):
    return lax.bitwise_and(index, 3)


def column_of(row, first, count):
    line = lax.broadcasted_iota(jnp.int32, (count, 128), 0) + first
    lane = lax.broadcasted_iota(jnp.int32, (count, 128), 1)
    return jnp.sum(jnp.where(line == lane, jnp.broadcast_to(row, (count, 128)), 0.0), axis=1, keepdims=True)


def padded(diag_ref):
    return jnp.concatenate([diag_ref[...], jnp.zeros((1, 128 - SHARE), F32)], axis=1)


def start_kernel(residual_ref, diag_ref, high_ref, start_ref, scale_ref):
    scale = jnp.broadcast_to(column_of(padded(diag_ref), 0, SHARE), (SHARE, NRHS))
    scaled = residual_ref[...] * scale
    scale_ref[...] = scale
    start_ref[...] = scaled
    high_ref[...] = scaled.astype(BF16)


def pack_kernel(tiles_ref, start_ref, diag_ref, out_ref):
    scaled = start_ref[...]
    low = scaled - scaled.astype(BF16).astype(F32)
    row = padded(diag_ref)
    d_high = row.astype(BF16).astype(F32)
    d_mid = (row - d_high).astype(BF16).astype(F32)
    d_rows = jnp.broadcast_to(jnp.concatenate([d_high, d_mid, row - d_high - d_mid], axis=1), (8, TILE))
    tiles = [tiles_ref[j].astype(F32) for j in range(2)]
    for x in range(SIDE):
        mine = low[SLAB * x:SLAB * (x + 1)]
        tail = [jnp.concatenate([mine[8 * k:8 * k + 8] for k in range(3)], axis=1), d_rows]
        for q in range(SIDE):
            at = SHARE * q + SLAB * x
            rows = [tile[at:at + SLAB] for tile in tiles]
            out_ref[SIDE * x + q] = jnp.concatenate(rows + tail, axis=0).astype(BF16)


def stack_kernel(*refs):
    out_ref = refs[-1]
    x, _ = place()
    for k in range(SIDE):
        out_ref[wrap(x - k)] = refs[k][...]


def send_halves(rows_ref, own_ref, up_ref, down_ref):
    lead = lax.axis_index("lead")
    for side, ref in ((0, up_ref), (1, down_ref)):
        for h in range(2):
            ref[h] = own_ref[rows_ref[side, h, lead]]


def pick_stack_kernel(rows_ref, *refs):
    own_ref, up_ref, down_ref = refs[4:]
    _, q = place()
    for k in range(SIDE):
        at = pl.multiple_of(wrap(q - k) * SHARE, SHARE)
        for r in range(SIDE):
            own_ref[r, pl.ds(at, SHARE)] = refs[k][r]
    send_halves(rows_ref, own_ref, up_ref, down_ref)


def pick_slab_kernel(rows_ref, got_ref, own_ref, up_ref, down_ref):
    for q in range(SIDE):
        parts = [got_ref[SIDE * x + q, 0:SHARE].astype(F32) for x in range(SIDE)]
        for r in range(SIDE):
            block = jnp.concatenate([p[SLAB * r:SLAB * (r + 1)] for p in parts], axis=0)
            own_ref[r, SHARE * q:SHARE * (q + 1)] = block.astype(BF16)
    send_halves(rows_ref, own_ref, up_ref, down_ref)


def pick_home_kernel(rows_ref, got_ref, own_ref, up_ref, down_ref):
    for r in range(SIDE):
        for q in range(SIDE):
            own_ref[r, SHARE * q:SHARE * (q + 1)] = got_ref[SIDE * r + q]
    send_halves(rows_ref, own_ref, up_ref, down_ref)


def order_kernel(slot_ref, slabs_ref, *refs):
    outs, held_ref = refs[:4], refs[4]
    x, _ = place()
    for t in range(TILES):
        piece = slabs_ref[t // 2].astype(F32)[SLAB * (t % 2):SLAB * (t % 2 + 1)]
        slot = slot_ref[0, t]
        held_ref[lax.bitwise_and(slot - 8 * x, TILES - 1)] = piece.astype(BF16)
    for k in range(SIDE):
        outs[k][...] = held_ref[8 * k:8 * k + 8]


def slab_products(slabs, blocks, product_ref, first):
    for pair in range(len(blocks) // 2):
        wide = jnp.concatenate(blocks[2 * pair:2 * pair + 2], axis=1)
        product = jnp.dot(slabs, wide, preferred_element_type=F32)
        product_ref[first + 2 * pair] = product[:, :NRHS]
        product_ref[first + 2 * pair + 1] = product[:, NRHS:]


def all_slabs(slabs_ref):
    return jnp.concatenate([slabs_ref[m, 0:2 * SLAB] for m in range(GROUP)], axis=0)


def near_kernel(slabs_ref, own_ref, product_ref):
    slab_products(all_slabs(slabs_ref), [own_ref[r] for r in range(SIDE)], product_ref, 0)


def first_kernel(slot_ref, cols_ref, slabs_ref, own_ref, near_ref, low_ref, high_ref,
                 wide_ref, product_ref, total_ref, line_ref):
    x, q = place()
    slab_products(all_slabs(slabs_ref), [low_ref[0], low_ref[1], high_ref[0], high_ref[1]], product_ref, 4)
    product_ref[0:4] = near_ref[...]
    total_ref[...] = jnp.zeros_like(total_ref)
    for t in range(TILES):
        slot = slot_ref[0, t]
        row = lax.shift_right_logical(slot, 3)
        col = cols_ref[row, lax.bitwise_and(slot, 7)]
        total_ref[row] += product_ref[col, SLAB * t:SLAB * (t + 1)]
    firsts = []
    at = pl.multiple_of(q * SHARE, SHARE)
    for r in range(SIDE):
        line_ref[...] = own_ref[r, pl.ds(at, SHARE)].astype(F32)
        high = line_ref[pl.ds(pl.multiple_of(x * SLAB, 8), SLAB), :]
        tail = slabs_ref[SIDE * r + q, 48:PIECE].astype(F32)
        low = jnp.concatenate([tail[0:8, NRHS * k:NRHS * (k + 1)] for k in range(3)], axis=0)
        row = tail[8:9, 0:128] + (tail[8:9, 128:256] + tail[8:9, 256:384])
        firsts.append(GAIN * (high + low - column_of(row, x * SLAB, SLAB) * total_ref[r]))
    first = jnp.concatenate(firsts, axis=0)
    high = first.astype(BF16)
    low = first - high.astype(F32)
    for r in range(SIDE):
        tail = jnp.concatenate([low[SLAB * r:SLAB * (r + 1)], jnp.zeros((8, NRHS), F32)], axis=0).astype(BF16)
        for s in range(SIDE):
            wide_ref[SIDE * r + s, 0:SHARE] = high
            wide_ref[SIDE * r + s, SHARE:128] = tail


def home_product(cols_ref, parts, ext_ref, line_ref):
    x, _ = place()
    total = jnp.zeros((SHARE, NRHS), F32)
    for k in range(8):
        left = jnp.concatenate([part[k] for part in parts], axis=0)
        total += jnp.dot(left, ext_ref[cols_ref[x, k]], preferred_element_type=F32)
    for k in range(SIDE):
        line_ref[pl.ds(pl.multiple_of(wrap(x - k) * SLAB, 8), SLAB), :] = total[SLAB * k:SLAB * (k + 1)]
    return line_ref[0:SHARE]


def fill(ext_ref, own_ref, low_ref, high_ref):
    ext_ref[0:4] = own_ref[...]
    ext_ref[4:6] = low_ref[...]
    ext_ref[6:8] = high_ref[...]


def second_kernel(cols_ref, *refs):
    parts = refs[:4]
    got_ref, own_ref, low_ref, high_ref, start_ref, scale_ref, wide_ref, sum_ref, ext_ref, line_ref = refs[4:]
    fill(ext_ref, own_ref, low_ref, high_ref)
    total = home_product(cols_ref, parts, ext_ref, line_ref)
    row, q = place()
    firsts = []
    for x in range(SIDE):
        line_ref[...] = got_ref[SIDE * x + q].astype(F32)
        firsts.append(line_ref[pl.ds(pl.multiple_of(row * SLAB, 8), SLAB), :] + line_ref[SHARE:120])
    first = jnp.concatenate(firsts, axis=0)
    second = start_ref[...] - first - scale_ref[...] * total
    sum_ref[...] = first + GAIN * second
    second = second.astype(BF16)
    for m in range(GROUP):
        wide_ref[m] = second


def last_kernel(cols_ref, *refs):
    parts = refs[:4]
    own_ref, low_ref, high_ref, sum_ref, scale_ref, out_ref, ext_ref, line_ref = refs[4:]
    fill(ext_ref, own_ref, low_ref, high_ref)
    total = home_product(cols_ref, parts, ext_ref, line_ref)
    out_ref[...] = sum_ref[...] - GAIN * (scale_ref[...] * total)


def arr(shape, dtype):
    return pltpu.VMEM(shape, dtype)


def call(kernel, args, outs, scalars=0, scratch=()):
    vectors = args[scalars:]
    if vectors:
        vectors = [pltpu.with_memory_space_constraint(a, pltpu.VMEM) if near else a for a, near in vectors]
    specs = [SMEM] * scalars + [VMEM] * len(vectors)
    return pl.pallas_call(kernel, in_specs=specs, out_specs=[VMEM] * len(outs),
                          out_shape=outs, scratch_shapes=list(scratch),
                          compiler_params=pltpu.CompilerParams(vmem_limit_bytes=GRANT))(*args[:scalars], *vectors)


def near(*arrays):
    return [(a, True) for a in arrays]


HALVES = [arr((2, TILE, NRHS), BF16), arr((2, TILE, NRHS), BF16)]
OWN = arr((SIDE, TILE, NRHS), BF16)
ROWS = arr((SHARE, NRHS), F32)
EXT = arr((8, TILE, NRHS), BF16)
LINE = arr((128, NRHS), F32)


def body(matrix_tiles, tile_slot, tile_cols, send_rows, residual, diag_inv):
    leads = lax.axis_size("lead")
    rows = send_rows.transpose(1, 2, 0)
    diag = diag_inv.reshape(1, SHARE)

    def halo(up, down):
        return (lax.ppermute(up, "lead", [(i, (i + 1) % leads) for i in range(leads)]),
                lax.ppermute(down, "lead", [(i, (i - 1) % leads) for i in range(leads)]))

    def gather(wide):
        return lax.all_to_all(wide, "grp", 0, 0)

    def along_x(value, k):
        return lax.ppermute(value, "grp", [(m, (m + SIDE * k) % GROUP) for m in range(GROUP)])

    def along_y(value, k):
        return lax.ppermute(value, "grp", [(m, m - m % SIDE + (m + k) % SIDE) for m in range(GROUP)])

    high, start, scale = call(start_kernel, [(residual, False), (diag, False)],
                              [arr((SHARE, NRHS), BF16), ROWS, ROWS])
    shares = [high] + [along_x(high, k) for k in range(1, SIDE)]
    packed, = call(pack_kernel, [(matrix_tiles, False)] + near(start) + [(diag, False)],
                   [arr((GROUP, PIECE, TILE), BF16)])
    slabs = gather(packed)
    column, = call(stack_kernel, near(*shares), [arr((SIDE, SHARE, NRHS), BF16)])
    columns = [column] + [along_y(column, k) for k in range(1, SIDE)]
    own, up, down = call(pick_stack_kernel, [rows] + near(*columns), [OWN] + HALVES, 1)
    lower, upper = halo(up, down)
    product, = call(near_kernel, near(slabs, own), [arr((4, TILES * SLAB, NRHS), F32)])
    wide, = call(first_kernel, [tile_slot, tile_cols] + near(slabs, own, product, lower, upper),
                 [arr((GROUP, 128, NRHS), BF16)], 2,
                 (arr((8, TILES * SLAB, NRHS), F32), arr((SIDE, SLAB, NRHS), F32), arr((SHARE, NRHS), F32)))
    got = gather(wide)
    ordered = call(order_kernel, [tile_slot] + near(slabs), [arr((8, SLAB, TILE), BF16)] * 4, 1,
                   (arr((TILES, SLAB, TILE), BF16),))
    parts = [ordered[0]]
    for k in range(1, SIDE):
        parts.append(along_x(ordered[k], k))
    own, up, down = call(pick_slab_kernel, [rows] + near(got), [OWN] + HALVES, 1)
    lower, upper = halo(up, down)
    wide, partial = call(second_kernel,
                         [tile_cols] + near(*parts, got, own, lower, upper, start, scale),
                         [arr((GROUP, SHARE, NRHS), BF16), ROWS], 1, (EXT, LINE))
    got = gather(wide)
    own, up, down = call(pick_home_kernel, [rows] + near(got), [OWN] + HALVES, 1)
    lower, upper = halo(up, down)
    result, = call(last_kernel, [tile_cols] + near(*parts, own, lower, upper, partial, scale),
                   [jax.ShapeDtypeStruct((SHARE, NRHS), F32)], 1, (EXT, LINE))
    return result


def solution(mesh):
    in_specs = (
        P(("lead", "grp"), None, None),
        P("lead", None),
        P("lead", None),
        P(),
        P(("lead", "grp"), None),
        P(("lead", "grp")),
    )
    out_specs = P(("lead", "grp"), None)
    return jax.shard_map(body, mesh=mesh, in_specs=in_specs, out_specs=out_specs, check_vma=False)
```

time: 95.1 us -> 96.6 us (1.016)
  blocking collectives: 12.9 us -> 29.7 us
  waiting for transfers between devices: 34.7 us -> 26.3 us
  Pallas kernels: 13.7 us -> 8.23 us
  starting transfers between devices: 30.8 us -> 28.7 us
  local copies, waits for them, and re-layouts: 1.37 us -> 2.52 us
    all_to_all x4 -> x1, waiting for transfers between devices: 22 us -> 0.01 us  [gather(): return lax.all_to_all(wide, 'grp', 0, 0)]
    all_to_all x1 -> x2, blocking collectives: 12.9 us -> 29.7 us  [gather(): return lax.all_to_all(wide, 'grp', 0, 0)]
    all_to_all x4 -> x1, starting transfers between devices: 20.7 us -> 6.75 us  [gather(): return lax.all_to_all(wide, 'grp', 0, 0)]
    ppermute x6 -> x15, waiting for transfers between devices: 12.7 us -> 26.3 us  [the longest x6 14.3 us: along_x(): lax.ppermute(value, 'grp', [(m, (m + SIDE * k) % GROUP) for m in range(GR...]
    ppermute x6 -> x15, starting transfers between devices: 10.1 us -> 21.9 us  [the longest x6 7.88 us: along_x(): lax.ppermute(value, 'grp', [(m, (m + SIDE * k) % GROUP) for m in range(GR...]
    pallas_call x9 -> x11, Pallas kernels: 13.7 us -> 8.23 us  [call(): pl.pallas_call(kernel, in_specs=specs, out_specs=[VMEM] * len(outs), out_...]
    unnamed x3 -> x12, local copies, waits for them, and re-layouts: 1.37 us -> 2.52 us
  transfers between devices with their start and end apart: 10 -> 16, of which waited for: 9 -> 11; matrix products, arithmetic and copies ran while one was open for 1% -> 0% of each run, Pallas kernels for 6% -> 2%
where the time goes in v3:
time: 96.6 us; the launch traced here: 95.5 us
  blocking collectives  29.7 us (31%)
  starting transfers between devices  28.7 us (30%)
  waiting for transfers between devices  26.3 us (27%)
  Pallas kernels  8.23 us (9%)
  local copies, waits for them, and re-layouts  2.52 us (3%)
    all_to_all x2, blocking collectives, gather(): return lax.all_to_all(wide, 'grp', 0, 0)  29.7 us
    ppermute x6, waiting for transfers between devices, along_x(): lax.ppermute(value, 'grp', [(m, (m + SIDE * k) % GROUP) for m in range(GR...  14.3 us
    pallas_call x11, Pallas kernels, call(): pl.pallas_call(kernel, in_specs=specs, out_specs=[VMEM] * len(outs), out_...  8.23 us
    ppermute x6, starting transfers between devices, along_x(): lax.ppermute(value, 'grp', [(m, (m + SIDE * k) % GROUP) for m in range(GR...  7.88 us
    all_to_all x1, starting transfers between devices, gather(): return lax.all_to_all(wide, 'grp', 0, 0)  6.75 us
    ppermute x3, waiting for transfers between devices, halo(): lax.ppermute(down, 'lead', [(i, (i - 1) % leads) for i in range(leads)])  6.45 us
    ppermute x3, starting transfers between devices, halo(): lax.ppermute(up, 'lead', [(i, (i + 1) % leads) for i in range(leads)])  6.13 us
    ppermute x3, starting transfers between devices, along_y(): lax.ppermute(value, 'grp', [(m, m - m % SIDE + (m + k) % SIDE) for m in r...  4.68 us
  transfers between devices with their start and end apart: 16, of which 11 were waited for; matrix products, arithmetic and copies ran while one was open for 0% of the time, Pallas kernels for 2%

profile of v3, /device:TPU:97, one launch (start us, length us, event | category | flops | bytes accessed | tf_op | source)
XLA Modules:
  0.0 95.5 jit_solution(11009076576309167214)
XLA Ops:
  0.0 0.8 copy-done.1
  0.8 0.7 copy-done.4
  1.5 0.1 shard_map.64
  1.6 0.0 copy-start
  1.6 1.1 %copy-done = bf16[2,384,384]{2,1,0:T(8,128)(2,1)S(1)} copy-done((bf16[2,384,384]{2,1,0:T(8,128)(2,1)S(1)}, bf16[2,384,384]{2,1,0:T(8,128)(2,1)}, u32[]{:S(2)}) %copy-start) | copy-done | bytes 589848
  2.6 1.0 %shard_map.65 = bf16[16,64,384]{2,1,0:T(8,128)(2,1)} custom-call(bf16[2,384,384]{2,1,0:T(8,128)(2,1)S(1)} %copy-done, f32[96,128]{1,0:T(8,128)S(1)} %get-tuple-element.23.start_ref.refs_8_, f32[1,96]{1,0:T(1,128)S(1)} %bitcast.6), custom_call_target="tpu_custom_call" | custom-call | tf_op jit(solution)/shard_map/pallas_call | solution.py:219
  3.6 6.8 %all-to-all-start = ((bf16[16,64,384]{2,1,0:T(8,128)(2,1)}), bf16[16,64,384]{2,1,0:T(8,128)(2,1)S(1)}, u32[]{:S(2)}, u32[]{:S(2)}) async-start(bf16[16,64,384]{2,1,0:T(8,128)(2,1)} %shard_map.65), calls=%async_computation | async-start | bytes 1572864 | tf_op jit(solution)/shard_map/all_to_all | solution.py:245
  10.4 1.4 %collective-permute-start.3 = (bf16[96,128]{1,0:T(8,128)(2,1)S(1)}, bf16[96,128]{1,0:T(8,128)(2,1)S(1)}, u32[]{:S(2)}, u32[]{:S(2)}) collective-permute-start(bf16[96,128]{1,0:T(8,128)(2,1)S(1)} %get-tuple-element.28.refs_0_), channel_id=1, source_target_pairs={{0,4},{1,5},{2,6},{3,7},{4,8},{5,9},{6,10},{7,11},{8,12},{9,13},{1... | collective-permute-start | bytes 73736 | tf_op jit(solution)/shard_map/ppermute | solution.py:248
  11.7 2.4 %collective-permute-start.4 = (bf16[96,128]{1,0:T(8,128)(2,1)S(1)}, bf16[96,128]{1,0:T(8,128)(2,1)S(1)}, u32[]{:S(2)}, u32[]{:S(2)}) collective-permute-start(bf16[96,128]{1,0:T(8,128)(2,1)S(1)} %get-tuple-element.28.refs_0_), channel_id=1, source_target_pairs={{0,8},{1,9},{2,10},{3,11},{4,12},{5,13},{6,14},{7,15},{8,0},{9,1},... | collective-permute-start | bytes 73736 | tf_op jit(solution)/shard_map/ppermute | solution.py:248
  14.1 1.2 %collective-permute-start.5 = (bf16[96,128]{1,0:T(8,128)(2,1)S(1)}, bf16[96,128]{1,0:T(8,128)(2,1)S(1)}, u32[]{:S(2)}, u32[]{:S(2)}) collective-permute-start(bf16[96,128]{1,0:T(8,128)(2,1)S(1)} %get-tuple-element.28.refs_0_), channel_id=1, source_target_pairs={{0,12},{1,13},{2,14},{3,15},{4,0},{5,1},{6,2},{7,3},{8,4},{9,5},{1... | collective-permute-start | bytes 73736 | tf_op jit(solution)/shard_map/ppermute | solution.py:248
  15.3 4.0 %collective-permute-done.3.refs_1_ = bf16[96,128]{1,0:T(8,128)(2,1)S(1)} collective-permute-done((bf16[96,128]{1,0:T(8,128)(2,1)S(1)}, bf16[96,128]{1,0:T(8,128)(2,1)S(1)}, u32[]{:S(2)}, u32[]{:S(2)}) %collective-permute-start.3) | collective-permute-done | bytes 24608 | tf_op jit(solution)/shard_map/ppermute | solution.py:248
  19.3 3.3 %collective-permute-done.4.refs_2_ = bf16[96,128]{1,0:T(8,128)(2,1)S(1)} collective-permute-done((bf16[96,128]{1,0:T(8,128)(2,1)S(1)}, bf16[96,128]{1,0:T(8,128)(2,1)S(1)}, u32[]{:S(2)}, u32[]{:S(2)}) %collective-permute-start.4) | collective-permute-done | bytes 24608 | tf_op jit(solution)/shard_map/ppermute | solution.py:248
  22.6 0.0 collective-permute-done.5.refs_3_
  22.6 1.4 %collective-permute-start.6 = (bf16[4,96,128]{2,1,0:T(8,128)(2,1)S(1)}, bf16[4,96,128]{2,1,0:T(8,128)(2,1)S(1)}, u32[]{:S(2)}, u32[]{:S(2)}) collective-permute-start(bf16[4,96,128]{2,1,0:T(8,128)(2,1)S(1)} %shard_map.67.refs_0_), channel_id=1, source_target_pairs={{0,1},{1,2},{2,3},{3,0},{4,5},{5,6},{6,7},{7,4},{8,9},{9,10},{10,1... | collective-permute-start | bytes 294920 | tf_op jit(solution)/shard_map/ppermute | solution.py:251
  24.0 2.4 %collective-permute-start.7 = (bf16[4,96,128]{2,1,0:T(8,128)(2,1)S(1)}, bf16[4,96,128]{2,1,0:T(8,128)(2,1)S(1)}, u32[]{:S(2)}, u32[]{:S(2)}) collective-permute-start(bf16[4,96,128]{2,1,0:T(8,128)(2,1)S(1)} %shard_map.67.refs_0_), channel_id=1, source_target_pairs={{0,2},{1,3},{2,0},{3,1},{4,6},{5,7},{6,4},{7,5},{8,10},{9,11},{10,... | collective-permute-start | bytes 294920 | tf_op jit(solution)/shard_map/ppermute | solution.py:251
  26.4 0.9 collective-permute-start.8
  27.3 0.1 collective-permute-done.6.refs_1_
  27.4 2.2 %collective-permute-done.7.refs_2_ = bf16[4,96,128]{2,1,0:T(8,128)(2,1)S(1)} collective-permute-done((bf16[4,96,128]{2,1,0:T(8,128)(2,1)S(1)}, bf16[4,96,128]{2,1,0:T(8,128)(2,1)S(1)}, u32[]{:S(2)}, u32[]{:S(2)}) %collective-permute-start.7) | collective-permute-done | bytes 98336 | tf_op jit(solution)/shard_map/ppermute | solution.py:251
  29.5 0.9 collective-permute-done.8.refs_3_
  30.5 0.6 shard_map.68
  31.1 2.9 %collective-permute-start.10 = (bf16[2,384,128]{2,1,0:T(8,128)(2,1)S(1)}, bf16[2,384,128]{2,1,0:T(8,128)(2,1)S(1)}, u32[]{:S(2)}, u32[]{:S(2)}) collective-permute-start(bf16[2,384,128]{2,1,0:T(8,128)(2,1)S(1)} %get-tuple-element.31), channel_id=1, source_target_pairs={{0,240},{16,0},{32,16},{48,32},{64,48},{80,64},{96,80},{112,96},{1... | collective-permute-start | bytes 589832 | tf_op jit(solution)/shard_map/ppermute | solution.py:242
  34.1 2.8 %collective-permute-start.9 = (bf16[2,384,128]{2,1,0:T(8,128)(2,1)S(1)}, bf16[2,384,128]{2,1,0:T(8,128)(2,1)S(1)}, u32[]{:S(2)}, u32[]{:S(2)}) collective-permute-start(bf16[2,384,128]{2,1,0:T(8,128)(2,1)S(1)} %get-tuple-element.30), channel_id=1, source_target_pairs={{0,16},{16,32},{32,48},{48,64},{64,80},{80,96},{96,112},{112,128},... | collective-permute-start | bytes 589832 | tf_op jit(solution)/shard_map/ppermute | solution.py:241
  36.8 0.0 all-to-all-done.slabs_ref
  36.8 0.6 shard_map.69.near_ref
  37.4 2.8 %collective-permute-done.10.high_ref = bf16[2,384,128]{2,1,0:T(8,128)(2,1)S(1)} collective-permute-done((bf16[2,384,128]{2,1,0:T(8,128)(2,1)S(1)}, bf16[2,384,128]{2,1,0:T(8,128)(2,1)S(1)}, u32[]{:S(2)}, u32[]{:S(2)}) %collective-permute-start.10) | collective-permute-done | bytes 196640 | tf_op jit(solution)/shard_map/ppermute | solution.py:242
  40.1 0.0 collective-permute-done.9.low_ref
  40.2 1.4 %shard_map.70 = bf16[16,128,128]{2,1,0:T(8,128)(2,1)S(1)} custom-call(s32[1,32]{1,0:T(1,128)S(1)} %copy-done.5, s32[4,8]{1,0:T(4,128)S(1)} %copy-done.2, bf16[16,64,384]{2,1,0:T(8,128)(2,1)S(1)} %all-to-all-done.slabs_ref, bf16[4,384,128]{2,1,0:T(8,128)(2,1)S(1)} %get-tuple-element.29.own_ref, f32[4,768,128]{2,1,0:T(8,128)S(1)} %shard_map.69.near_ref, ...), custom_call_target="tpu_custom_call" | custom-call | tf_op jit(solution)/shard_map/pallas_call | solution.py:219
  41.6 15.7 %all_to_all.15.got_ref.refs_4_ = bf16[16,128,128]{2,1,0:T(8,128)(2,1)S(1)} all-to-all(bf16[16,128,128]{2,1,0:T(8,128)(2,1)S(1)} %shard_map.70), channel_id=1, replica_groups=mesh['lead'=16,'grp'=16] {'grp'}, dimensions={0} | all-to-all | bytes 1048576 | tf_op jit(solution)/shard_map/all_to_all | solution.py:245
  57.3 0.7 shard_map.71
  58.0 1.9 %collective-permute-start.11 = (bf16[2,384,128]{2,1,0:T(8,128)(2,1)S(1)}, bf16[2,384,128]{2,1,0:T(8,128)(2,1)S(1)}, u32[]{:S(2)}, u32[]{:S(2)}) collective-permute-start(bf16[2,384,128]{2,1,0:T(8,128)(2,1)S(1)} %get-tuple-element.33), channel_id=1, source_target_pairs={{0,16},{16,32},{32,48},{48,64},{64,80},{80,96},{96,112},{112,128},... | collective-permute-start | bytes 589832 | tf_op jit(solution)/shard_map/ppermute | solution.py:241
  59.9 0.0 collective-permute-start.12
  59.9 0.7 shard_map.66
  60.5 0.1 collective-permute-start
  60.6 2.0 %collective-permute-start.1 = (bf16[8,24,384]{2,1,0:T(8,128)(2,1)S(1)}, bf16[8,24,384]{2,1,0:T(8,128)(2,1)S(1)}, u32[]{:S(2)}, u32[]{:S(2)}) collective-permute-start(bf16[8,24,384]{2,1,0:T(8,128)(2,1)S(1)} %get-tuple-element.26), channel_id=1, source_target_pairs={{0,8},{1,9},{2,10},{3,11},{4,12},{5,13},{6,14},{7,15},{8,0},{9,1},... | collective-permute-start | bytes 442376 | tf_op jit(solution)/shard_map/ppermute | solution.py:248
  62.6 0.9 collective-permute-start.2
  63.5 4.4 %collective-permute-done.refs_1_ = bf16[8,24,384]{2,1,0:T(8,128)(2,1)S(1)} collective-permute-done((bf16[8,24,384]{2,1,0:T(8,128)(2,1)S(1)}, bf16[8,24,384]{2,1,0:T(8,128)(2,1)S(1)}, u32[]{:S(2)}, u32[]{:S(2)}) %collective-permute-start) | collective-permute-done | bytes 147488 | tf_op jit(solution)/shard_map/ppermute | solution.py:248
  67.8 1.4 %collective-permute-done.1.refs_2_ = bf16[8,24,384]{2,1,0:T(8,128)(2,1)S(1)} collective-permute-done((bf16[8,24,384]{2,1,0:T(8,128)(2,1)S(1)}, bf16[8,24,384]{2,1,0:T(8,128)(2,1)S(1)}, u32[]{:S(2)}, u32[]{:S(2)}) %collective-permute-start.1) | collective-permute-done | bytes 147488 | tf_op jit(solution)/shard_map/ppermute | solution.py:248
  69.2 1.2 %collective-permute-done.2.refs_3_ = bf16[8,24,384]{2,1,0:T(8,128)(2,1)S(1)} collective-permute-done((bf16[8,24,384]{2,1,0:T(8,128)(2,1)S(1)}, bf16[8,24,384]{2,1,0:T(8,128)(2,1)S(1)}, u32[]{:S(2)}, u32[]{:S(2)}) %collective-permute-start.2) | collective-permute-done | bytes 147488 | tf_op jit(solution)/shard_map/ppermute | solution.py:248
  70.5 0.0 collective-permute-done.11.refs_6_
  70.5 0.0 collective-permute-done.12.refs_7_
  70.5 1.0 %shard_map.72 = (bf16[16,96,128]{2,1,0:T(8,128)(2,1)S(1)}, f32[96,128]{1,0:T(8,128)S(1)}) custom-call(s32[4,8]{1,0:T(4,128)S(1)} %copy-done.2, bf16[8,24,384]{2,1,0:T(8,128)(2,1)S(1)} %get-tuple-element.24.refs_0_, bf16[8,24,384]{2,1,0:T(8,128)(2,1)S(1)} %collective-permute-done.refs_1_, bf16[8,24,384]{2,1,0:T(8,128)(2,1)S(1)} %collective-permute-done.1.refs_2_, ...), custom_call_target="tpu_custom_call" | custom-call | tf_op jit(solution)/shard_map/pallas_call | solution.py:219
  71.5 14.0 %all_to_all.16.got_ref = bf16[16,96,128]{2,1,0:T(8,128)(2,1)S(1)} all-to-all(bf16[16,96,128]{2,1,0:T(8,128)(2,1)S(1)} %get-tuple-element.36), channel_id=1, replica_groups=mesh['lead'=16,'grp'=16] {'grp'}, dimensions={0} | all-to-all | bytes 786432 | tf_op jit(solution)/shard_map/all_to_all | solution.py:245
  85.5 0.6 shard_map.73
  86.1 1.5 %collective-permute-start.13 = (bf16[2,384,128]{2,1,0:T(8,128)(2,1)S(1)}, bf16[2,384,128]{2,1,0:T(8,128)(2,1)S(1)}, u32[]{:S(2)}, u32[]{:S(2)}) collective-permute-start(bf16[2,384,128]{2,1,0:T(8,128)(2,1)S(1)} %get-tuple-element.38), channel_id=1, source_target_pairs={{0,16},{16,32},{32,48},{48,64},{64,80},{80,96},{96,112},{112,128},... | collective-permute-start | bytes 589832 | tf_op jit(solution)/shard_map/ppermute | solution.py:241
  87.6 0.3 collective-permute-start.14
  87.9 2.3 %collective-permute-done.13.refs_5_ = bf16[2,384,128]{2,1,0:T(8,128)(2,1)S(1)} collective-permute-done((bf16[2,384,128]{2,1,0:T(8,128)(2,1)S(1)}, bf16[2,384,128]{2,1,0:T(8,128)(2,1)S(1)}, u32[]{:S(2)}, u32[]{:S(2)}) %collective-permute-start.13) | collective-permute-done | bytes 196640 | tf_op jit(solution)/shard_map/ppermute | solution.py:241
  90.3 3.7 %collective-permute-done.14.refs_6_ = bf16[2,384,128]{2,1,0:T(8,128)(2,1)S(1)} collective-permute-done((bf16[2,384,128]{2,1,0:T(8,128)(2,1)S(1)}, bf16[2,384,128]{2,1,0:T(8,128)(2,1)S(1)}, u32[]{:S(2)}, u32[]{:S(2)}) %collective-permute-start.14) | collective-permute-done | bytes 196640 | tf_op jit(solution)/shard_map/ppermute | solution.py:242
  93.9 1.6 %shard_map.74 = f32[96,128]{1,0:T(8,128)} custom-call(s32[4,8]{1,0:T(4,128)S(1)} %copy-done.2, bf16[8,24,384]{2,1,0:T(8,128)(2,1)S(1)} %get-tuple-element.24.refs_0_, bf16[8,24,384]{2,1,0:T(8,128)(2,1)S(1)} %collective-permute-done.refs_1_, bf16[8,24,384]{2,1,0:T(8,128)(2,1)S(1)} %collective-permute-done.1.refs_2_, ...), custom_call_target="tpu_custom_call" | custom-call | tf_op jit(solution)/shard_map/pallas_call | solution.py:219
  (9 shorter events, 0.0 us)
Async XLA Ops:
  0.0 0.8 copy-start.1
  0.8 0.7 copy-start.4
  1.6 1.1 %copy-start = (bf16[2,384,384]{2,1,0:T(8,128)(2,1)S(1)}, bf16[2,384,384]{2,1,0:T(8,128)(2,1)}, u32[]{:S(2)}) copy-start(bf16[2,384,384]{2,1,0:T(8,128)(2,1)} %tiles_ref.1) | copy-start | bytes 1769476
  2.6 27.9 %copy-start.3 = (s32[16,2,2]{0,2,1:T(2,128)S(1)}, s32[16,2,2]{0,2,1:T(2,128)}, u32[]{:S(2)}) copy-start(s32[16,2,2]{0,2,1:T(2,128)} %param.9) | copy-start | bytes 772
  3.6 33.2 %all-to-all-start = ((bf16[16,64,384]{2,1,0:T(8,128)(2,1)}), bf16[16,64,384]{2,1,0:T(8,128)(2,1)S(1)}, u32[]{:S(2)}, u32[]{:S(2)}) async-start(bf16[16,64,384]{2,1,0:T(8,128)(2,1)} %shard_map.65), calls=%async_computation | async-start | bytes 1572864 | tf_op jit(solution)/shard_map/all_to_all | solution.py:245
  10.4 9.0 %collective-permute-start.3 = (bf16[96,128]{1,0:T(8,128)(2,1)S(1)}, bf16[96,128]{1,0:T(8,128)(2,1)S(1)}, u32[]{:S(2)}, u32[]{:S(2)}) collective-permute-start(bf16[96,128]{1,0:T(8,128)(2,1)S(1)} %get-tuple-element.28.refs_0_), channel_id=1, source_target_pairs={{0,4},{1,5},{2,6},{3,7},{4,8},{5,9},{6,10},{7,11},{8,12},{9,13},{1... | collective-permute-start | bytes 73736 | tf_op jit(solution)/shard_map/ppermute | solution.py:248
  11.7 10.9 %collective-permute-start.4 = (bf16[96,128]{1,0:T(8,128)(2,1)S(1)}, bf16[96,128]{1,0:T(8,128)(2,1)S(1)}, u32[]{:S(2)}, u32[]{:S(2)}) collective-permute-start(bf16[96,128]{1,0:T(8,128)(2,1)S(1)} %get-tuple-element.28.refs_0_), channel_id=1, source_target_pairs={{0,8},{1,9},{2,10},{3,11},{4,12},{5,13},{6,14},{7,15},{8,0},{9,1},... | collective-permute-start | bytes 73736 | tf_op jit(solution)/shard_map/ppermute | solution.py:248
  14.1 8.5 %collective-permute-start.5 = (bf16[96,128]{1,0:T(8,128)(2,1)S(1)}, bf16[96,128]{1,0:T(8,128)(2,1)S(1)}, u32[]{:S(2)}, u32[]{:S(2)}) collective-permute-start(bf16[96,128]{1,0:T(8,128)(2,1)S(1)} %get-tuple-element.28.refs_0_), channel_id=1, source_target_pairs={{0,12},{1,13},{2,14},{3,15},{4,0},{5,1},{6,2},{7,3},{8,4},{9,5},{1... | collective-permute-start | bytes 73736 | tf_op jit(solution)/shard_map/ppermute | solution.py:248
  22.6 4.8 %collective-permute-start.6 = (bf16[4,96,128]{2,1,0:T(8,128)(2,1)S(1)}, bf16[4,96,128]{2,1,0:T(8,128)(2,1)S(1)}, u32[]{:S(2)}, u32[]{:S(2)}) collective-permute-start(bf16[4,96,128]{2,1,0:T(8,128)(2,1)S(1)} %shard_map.67.refs_0_), channel_id=1, source_target_pairs={{0,1},{1,2},{2,3},{3,0},{4,5},{5,6},{6,7},{7,4},{8,9},{9,10},{10,1... | collective-permute-start | bytes 294920 | tf_op jit(solution)/shard_map/ppermute | solution.py:251
  24.0 5.5 %collective-permute-start.7 = (bf16[4,96,128]{2,1,0:T(8,128)(2,1)S(1)}, bf16[4,96,128]{2,1,0:T(8,128)(2,1)S(1)}, u32[]{:S(2)}, u32[]{:S(2)}) collective-permute-start(bf16[4,96,128]{2,1,0:T(8,128)(2,1)S(1)} %shard_map.67.refs_0_), channel_id=1, source_target_pairs={{0,2},{1,3},{2,0},{3,1},{4,6},{5,7},{6,4},{7,5},{8,10},{9,11},{10,... | collective-permute-start | bytes 294920 | tf_op jit(solution)/shard_map/ppermute | solution.py:251
  26.4 4.1 %collective-permute-start.8 = (bf16[4,96,128]{2,1,0:T(8,128)(2,1)S(1)}, bf16[4,96,128]{2,1,0:T(8,128)(2,1)S(1)}, u32[]{:S(2)}, u32[]{:S(2)}) collective-permute-start(bf16[4,96,128]{2,1,0:T(8,128)(2,1)S(1)} %shard_map.67.refs_0_), channel_id=1, source_target_pairs={{0,3},{1,0},{2,1},{3,2},{4,7},{5,4},{6,5},{7,6},{8,11},{9,8},{10,9... | collective-permute-start | bytes 294920 | tf_op jit(solution)/shard_map/ppermute | solution.py:251
  30.5 9.7 %copy-start.2 = (s32[4,8]{1,0:T(4,128)S(1)}, s32[4,8]{1,0:T(4,128)}, u32[]{:S(2)}) copy-start(s32[4,8]{1,0:T(4,128)} %cols_ref.5) | copy-start | bytes 388
  30.5 9.7 %copy-start.5 = (s32[1,32]{1,0:T(1,128)S(1)}, s32[1,32]{1,0:T(1,128)}, u32[]{:S(2)}) copy-start(s32[1,32]{1,0:T(1,128)} %slot_ref.3) | copy-start | bytes 388
  31.1 9.0 %collective-permute-start.10 = (bf16[2,384,128]{2,1,0:T(8,128)(2,1)S(1)}, bf16[2,384,128]{2,1,0:T(8,128)(2,1)S(1)}, u32[]{:S(2)}, u32[]{:S(2)}) collective-permute-start(bf16[2,384,128]{2,1,0:T(8,128)(2,1)S(1)} %get-tuple-element.31), channel_id=1, source_target_pairs={{0,240},{16,0},{32,16},{48,32},{64,48},{80,64},{96,80},{112,96},{1... | collective-permute-start | bytes 589832 | tf_op jit(solution)/shard_map/ppermute | solution.py:242
  34.1 6.1 %collective-permute-start.9 = (bf16[2,384,128]{2,1,0:T(8,128)(2,1)S(1)}, bf16[2,384,128]{2,1,0:T(8,128)(2,1)S(1)}, u32[]{:S(2)}, u32[]{:S(2)}) collective-permute-start(bf16[2,384,128]{2,1,0:T(8,128)(2,1)S(1)} %get-tuple-element.30), channel_id=1, source_target_pairs={{0,16},{16,32},{32,48},{48,64},{64,80},{80,96},{96,112},{112,128},... | collective-permute-start | bytes 589832 | tf_op jit(solution)/shard_map/ppermute | solution.py:241
  58.0 12.5 %collective-permute-start.11 = (bf16[2,384,128]{2,1,0:T(8,128)(2,1)S(1)}, bf16[2,384,128]{2,1,0:T(8,128)(2,1)S(1)}, u32[]{:S(2)}, u32[]{:S(2)}) collective-permute-start(bf16[2,384,128]{2,1,0:T(8,128)(2,1)S(1)} %get-tuple-element.33), channel_id=1, source_target_pairs={{0,16},{16,32},{32,48},{48,64},{64,80},{80,96},{96,112},{112,128},... | collective-permute-start | bytes 589832 | tf_op jit(solution)/shard_map/ppermute | solution.py:241
  59.9 10.6 %collective-permute-start.12 = (bf16[2,384,128]{2,1,0:T(8,128)(2,1)S(1)}, bf16[2,384,128]{2,1,0:T(8,128)(2,1)S(1)}, u32[]{:S(2)}, u32[]{:S(2)}) collective-permute-start(bf16[2,384,128]{2,1,0:T(8,128)(2,1)S(1)} %get-tuple-element.34), channel_id=1, source_target_pairs={{0,240},{16,0},{32,16},{48,32},{64,48},{80,64},{96,80},{112,96},{1... | collective-permute-start | bytes 589832 | tf_op jit(solution)/shard_map/ppermute | solution.py:242
  60.5 7.3 %collective-permute-start = (bf16[8,24,384]{2,1,0:T(8,128)(2,1)S(1)}, bf16[8,24,384]{2,1,0:T(8,128)(2,1)S(1)}, u32[]{:S(2)}, u32[]{:S(2)}) collective-permute-start(bf16[8,24,384]{2,1,0:T(8,128)(2,1)S(1)} %get-tuple-element.25), channel_id=1, source_target_pairs={{0,4},{1,5},{2,6},{3,7},{4,8},{5,9},{6,10},{7,11},{8,12},{9,13},{1... | collective-permute-start | bytes 442376 | tf_op jit(solution)/shard_map/ppermute | solution.py:248
  60.6 8.6 %collective-permute-start.1 = (bf16[8,24,384]{2,1,0:T(8,128)(2,1)S(1)}, bf16[8,24,384]{2,1,0:T(8,128)(2,1)S(1)}, u32[]{:S(2)}, u32[]{:S(2)}) collective-permute-start(bf16[8,24,384]{2,1,0:T(8,128)(2,1)S(1)} %get-tuple-element.26), channel_id=1, source_target_pairs={{0,8},{1,9},{2,10},{3,11},{4,12},{5,13},{6,14},{7,15},{8,0},{9,1},... | collective-permute-start | bytes 442376 | tf_op jit(solution)/shard_map/ppermute | solution.py:248
  62.6 7.9 %collective-permute-start.2 = (bf16[8,24,384]{2,1,0:T(8,128)(2,1)S(1)}, bf16[8,24,384]{2,1,0:T(8,128)(2,1)S(1)}, u32[]{:S(2)}, u32[]{:S(2)}) collective-permute-start(bf16[8,24,384]{2,1,0:T(8,128)(2,1)S(1)} %get-tuple-element.27), channel_id=1, source_target_pairs={{0,12},{1,13},{2,14},{3,15},{4,0},{5,1},{6,2},{7,3},{8,4},{9,5},{1... | collective-permute-start | bytes 442376 | tf_op jit(solution)/shard_map/ppermute | solution.py:248
  86.1 4.1 %collective-permute-start.13 = (bf16[2,384,128]{2,1,0:T(8,128)(2,1)S(1)}, bf16[2,384,128]{2,1,0:T(8,128)(2,1)S(1)}, u32[]{:S(2)}, u32[]{:S(2)}) collective-permute-start(bf16[2,384,128]{2,1,0:T(8,128)(2,1)S(1)} %get-tuple-element.38), channel_id=1, source_target_pairs={{0,16},{16,32},{32,48},{48,64},{64,80},{80,96},{96,112},{112,128},... | collective-permute-start | bytes 589832 | tf_op jit(solution)/shard_map/ppermute | solution.py:241
  87.6 6.3 %collective-permute-start.14 = (bf16[2,384,128]{2,1,0:T(8,128)(2,1)S(1)}, bf16[2,384,128]{2,1,0:T(8,128)(2,1)S(1)}, u32[]{:S(2)}, u32[]{:S(2)}) collective-permute-start(bf16[2,384,128]{2,1,0:T(8,128)(2,1)S(1)} %get-tuple-element.39), channel_id=1, source_target_pairs={{0,240},{16,0},{32,16},{48,32},{64,48},{80,64},{96,80},{112,96},{1... | collective-permute-start | bytes 589832 | tf_op jit(solution)/shard_map/ppermute | solution.py:242

commit v4 on v3

--- a/solution.py
+++ b/solution.py
@@ -13,7 +13,7 @@
 SHARE = 96
 SLAB = 24
 TILES = 32
-PIECE = 64
+PIECE = 96
 F32 = jnp.float32
 BF16 = jnp.bfloat16
 GRANT = 20 << 20
@@ -42,36 +42,28 @@
     return jnp.concatenate([diag_ref[...], jnp.zeros((1, 128 - SHARE), F32)], axis=1)
 
 
-def start_kernel(residual_ref, diag_ref, high_ref, start_ref, scale_ref):
-    scale = jnp.broadcast_to(column_of(padded(diag_ref), 0, SHARE), (SHARE, NRHS))
+def start_kernel(tiles_ref, residual_ref, diag_ref, out_ref, start_ref, scale_ref):
+    row = padded(diag_ref)
+    scale = jnp.broadcast_to(column_of(row, 0, SHARE), (SHARE, NRHS))
     scaled = residual_ref[...] * scale
     scale_ref[...] = scale
     start_ref[...] = scaled
-    high_ref[...] = scaled.astype(BF16)
-
-
-def pack_kernel(tiles_ref, start_ref, diag_ref, out_ref):
-    scaled = start_ref[...]
-    low = scaled - scaled.astype(BF16).astype(F32)
-    row = padded(diag_ref)
+    high = scaled.astype(BF16).astype(F32)
+    low = scaled - high
+    high = jnp.concatenate([high[32 * k:32 * (k + 1)] for k in range(3)], axis=1).astype(BF16)
     d_high = row.astype(BF16).astype(F32)
     d_mid = (row - d_high).astype(BF16).astype(F32)
     d_rows = jnp.broadcast_to(jnp.concatenate([d_high, d_mid, row - d_high - d_mid], axis=1), (8, TILE))
     tiles = [tiles_ref[j].astype(F32) for j in range(2)]
     for x in range(SIDE):
         mine = low[SLAB * x:SLAB * (x + 1)]
-        tail = [jnp.concatenate([mine[8 * k:8 * k + 8] for k in range(3)], axis=1), d_rows]
+        tail = jnp.concatenate([jnp.concatenate([mine[8 * k:8 * k + 8] for k in range(3)], axis=1), d_rows], axis=0)
+        tail = tail.astype(BF16)
         for q in range(SIDE):
             at = SHARE * q + SLAB * x
-            rows = [tile[at:at + SLAB] for tile in tiles]
-            out_ref[SIDE * x + q] = jnp.concatenate(rows + tail, axis=0).astype(BF16)
-
-
-def stack_kernel(*refs):
-    out_ref = refs[-1]
-    x, _ = place()
-    for k in range(SIDE):
-        out_ref[wrap(x - k)] = refs[k][...]
+            out_ref[SIDE * x + q, 0:48] = jnp.concatenate([tile[at:at + SLAB] for tile in tiles], axis=0).astype(BF16)
+            out_ref[SIDE * x + q, 48:80] = high
+            out_ref[SIDE * x + q, 80:PIECE] = tail
 
 
 def send_halves(rows_ref, own_ref, up_ref, down_ref):
@@ -81,13 +73,11 @@
             ref[h] = own_ref[rows_ref[side, h, lead]]
 
 
-def pick_stack_kernel(rows_ref, *refs):
-    own_ref, up_ref, down_ref = refs[4:]
-    _, q = place()
-    for k in range(SIDE):
-        at = pl.multiple_of(wrap(q - k) * SHARE, SHARE)
-        for r in range(SIDE):
-            own_ref[r, pl.ds(at, SHARE)] = refs[k][r]
+def pick_first_kernel(rows_ref, got_ref, own_ref, up_ref, down_ref):
+    for m in range(GROUP):
+        for k in range(3):
+            at = SHARE * (m % SIDE) + 32 * k
+            own_ref[m // SIDE, at:at + 32] = got_ref[m, 48:80, NRHS * k:NRHS * (k + 1)]
     send_halves(rows_ref, own_ref, up_ref, down_ref)
 
 
@@ -150,7 +140,7 @@
     for r in range(SIDE):
         line_ref[...] = own_ref[r, pl.ds(at, SHARE)].astype(F32)
         high = line_ref[pl.ds(pl.multiple_of(x * SLAB, 8), SLAB), :]
-        tail = slabs_ref[SIDE * r + q, 48:PIECE].astype(F32)
+        tail = slabs_ref[SIDE * r + q, 80:PIECE].astype(F32)
         low = jnp.concatenate([tail[0:8, NRHS * k:NRHS * (k + 1)] for k in range(3)], axis=0)
         row = tail[8:9, 0:128] + (tail[8:9, 128:256] + tail[8:9, 256:384])
         firsts.append(GAIN * (high + low - column_of(row, x * SLAB, SLAB) * total_ref[r]))
@@ -247,18 +237,10 @@
     def along_x(value, k):
         return lax.ppermute(value, "grp", [(m, (m + SIDE * k) % GROUP) for m in range(GROUP)])
 
-    def along_y(value, k):
-        return lax.ppermute(value, "grp", [(m, m - m % SIDE + (m + k) % SIDE) for m in range(GROUP)])
-
-    high, start, scale = call(start_kernel, [(residual, False), (diag, False)],
-                              [arr((SHARE, NRHS), BF16), ROWS, ROWS])
-    shares = [high] + [along_x(high, k) for k in range(1, SIDE)]
-    packed, = call(pack_kernel, [(matrix_tiles, False)] + near(start) + [(diag, False)],
-                   [arr((GROUP, PIECE, TILE), BF16)])
+    packed, start, scale = call(start_kernel, [(matrix_tiles, False), (residual, False), (diag, False)],
+                                [arr((GROUP, PIECE, TILE), BF16), ROWS, ROWS])
     slabs = gather(packed)
-    column, = call(stack_kernel, near(*shares), [arr((SIDE, SHARE, NRHS), BF16)])
-    columns = [column] + [along_y(column, k) for k in range(1, SIDE)]
-    own, up, down = call(pick_stack_kernel, [rows] + near(*columns), [OWN] + HALVES, 1)
+    own, up, down = call(pick_first_kernel, [rows] + near(slabs), [OWN] + HALVES, 1)
     lower, upper = halo(up, down)
     product, = call(near_kernel, near(slabs, own), [arr((4, TILES * SLAB, NRHS), F32)])
     wide, = call(first_kernel, [tile_slot, tile_cols] + near(slabs, own, product, lower, upper),

time: 96.6 us -> 91.6 us (0.948)
  blocking collectives: 29.7 us -> 49.5 us
  starting transfers between devices: 28.7 us -> 14 us
  waiting for transfers between devices: 26.3 us -> 17.8 us
    all_to_all x2 -> x3, blocking collectives: 29.7 us -> 49.5 us  [gather(): return lax.all_to_all(wide, 'grp', 0, 0)]
    ppermute x6 -> x3, waiting for transfers between devices: 14.3 us -> 5.8 us  [along_x(): lax.ppermute(value, 'grp', [(m, (m + SIDE * k) % GROUP) for m in range(GR...]
    all_to_all x1 -> x0, starting transfers between devices: 6.75 us -> none  [gather(): return lax.all_to_all(wide, 'grp', 0, 0)]
    ppermute x6 -> x3, starting transfers between devices: 7.88 us -> 2.93 us  [along_x(): lax.ppermute(value, 'grp', [(m, (m + SIDE * k) % GROUP) for m in range(GR...]
    ppermute x3, starting transfers between devices: 6.13 us -> 11.1 us  [halo(): lax.ppermute(up, 'lead', [(i, (i + 1) % leads) for i in range(leads)])]
    ppermute x3 -> x0, starting transfers between devices: 4.68 us -> none  [along_y(): lax.ppermute(value, 'grp', [(m, m - m % SIDE + (m + k) % SIDE) for m in r...]
    ppermute x3, starting transfers between devices: 3.23 us -> 0.01 us  [halo(): lax.ppermute(down, 'lead', [(i, (i - 1) % leads) for i in range(leads)])]
    ppermute x3 -> x0, waiting for transfers between devices: 3.16 us -> none  [along_y(): lax.ppermute(value, 'grp', [(m, m - m % SIDE + (m + k) % SIDE) for m in r...]
  transfers between devices with their start and end apart: 16 -> 9, of which waited for: 11 -> 6; matrix products, arithmetic and copies ran while one was open for 0% -> 0% of each run, Pallas kernels for 2% -> 1%
where the time goes in v4:
time: 91.6 us; the launch traced here: 91.3 us
  blocking collectives  49.5 us (54%)
  waiting for transfers between devices  17.8 us (19%)
  starting transfers between devices  14 us (15%)
  Pallas kernels  7.33 us (8%)
  local copies, waits for them, and re-layouts  2.53 us (3%)
    all_to_all x3, blocking collectives, gather(): return lax.all_to_all(wide, 'grp', 0, 0)  49.5 us
    ppermute x3, starting transfers between devices, halo(): lax.ppermute(up, 'lead', [(i, (i + 1) % leads) for i in range(leads)])  11.1 us
    ppermute x3, waiting for transfers between devices, halo(): lax.ppermute(down, 'lead', [(i, (i - 1) % leads) for i in range(leads)])  7.38 us
    pallas_call x9, Pallas kernels, call(): pl.pallas_call(kernel, in_specs=specs, out_specs=[VMEM] * len(outs), out_...  7.33 us
    ppermute x3, waiting for transfers between devices, along_x(): lax.ppermute(value, 'grp', [(m, (m + SIDE * k) % GROUP) for m in range(GR...  5.8 us
    ppermute x3, waiting for transfers between devices, halo(): lax.ppermute(up, 'lead', [(i, (i + 1) % leads) for i in range(leads)])  4.65 us
    ppermute x3, starting transfers between devices, along_x(): lax.ppermute(value, 'grp', [(m, (m + SIDE * k) % GROUP) for m in range(GR...  2.93 us
    unnamed x12, local copies, waits for them, and re-layouts  2.53 us
  transfers between devices with their start and end apart: 9, of which 6 were waited for; matrix products, arithmetic and copies ran while one was open for 0% of the time, Pallas kernels for 1%

profile of v4, /device:TPU:97, one launch (start us, length us, event | category | flops | bytes accessed | tf_op | source)
XLA Modules:
  0.0 91.3 jit_solution(5259218738289402844)
XLA Ops:
  0.0 0.0 copy-start
  0.0 1.1 %copy-done = bf16[2,384,384]{2,1,0:T(8,128)(2,1)S(1)} copy-done((bf16[2,384,384]{2,1,0:T(8,128)(2,1)S(1)}, bf16[2,384,384]{2,1,0:T(8,128)(2,1)}, u32[]{:S(2)}) %copy-start) | copy-done | bytes 589848
  1.1 0.0 copy-start.1
  1.1 0.8 copy-done.1
  1.9 0.0 copy-start.5
  1.9 0.7 copy-done.5
  2.5 0.1 shard_map.64
  2.7 0.0 copy-start.2
  2.7 24.0 %all_to_all.15.slabs_ref.got_ref = bf16[16,96,384]{2,1,0:T(8,128)(2,1)S(1)} all-to-all(bf16[16,96,384]{2,1,0:T(8,128)(2,1)S(1)} %get-tuple-element.23), channel_id=1, replica_groups=mesh['lead'=16,'grp'=16] {'grp'}, dimensions={0} | all-to-all | bytes 2359296 | tf_op jit(solution)/shard_map/all_to_all | solution.py:235
  26.6 0.0 copy-done.2
  26.6 0.7 shard_map.66
  27.3 4.8 %collective-permute-start.3 = (bf16[2,384,128]{2,1,0:T(8,128)(2,1)S(1)}, bf16[2,384,128]{2,1,0:T(8,128)(2,1)S(1)}, u32[]{:S(2)}, u32[]{:S(2)}) collective-permute-start(bf16[2,384,128]{2,1,0:T(8,128)(2,1)S(1)} %get-tuple-element.29), channel_id=1, source_target_pairs={{0,16},{16,32},{32,48},{48,64},{64,80},{80,96},{96,112},{112,128},... | collective-permute-start | bytes 589832 | tf_op jit(solution)/shard_map/ppermute | solution.py:231
  32.1 0.0 collective-permute-start.4
  32.1 0.0 copy-start.3
  32.1 0.0 copy-start.4
  32.1 0.6 shard_map.67.near_ref
  32.6 2.0 %collective-permute-done.3.low_ref = bf16[2,384,128]{2,1,0:T(8,128)(2,1)S(1)} collective-permute-done((bf16[2,384,128]{2,1,0:T(8,128)(2,1)S(1)}, bf16[2,384,128]{2,1,0:T(8,128)(2,1)S(1)}, u32[]{:S(2)}, u32[]{:S(2)}) %collective-permute-start.3) | collective-permute-done | bytes 196640 | tf_op jit(solution)/shard_map/ppermute | solution.py:231
  34.7 3.7 %collective-permute-done.4.high_ref = bf16[2,384,128]{2,1,0:T(8,128)(2,1)S(1)} collective-permute-done((bf16[2,384,128]{2,1,0:T(8,128)(2,1)S(1)}, bf16[2,384,128]{2,1,0:T(8,128)(2,1)S(1)}, u32[]{:S(2)}, u32[]{:S(2)}) %collective-permute-start.4) | collective-permute-done | bytes 196640 | tf_op jit(solution)/shard_map/ppermute | solution.py:232
  38.4 0.0 copy-done.3
  38.4 0.0 copy-done.4
  38.4 1.4 %shard_map.68 = bf16[16,128,128]{2,1,0:T(8,128)(2,1)S(1)} custom-call(s32[1,32]{1,0:T(1,128)S(1)} %copy-done.4, s32[4,8]{1,0:T(4,128)S(1)} %copy-done.3, bf16[16,96,384]{2,1,0:T(8,128)(2,1)S(1)} %all_to_all.15.slabs_ref.got_ref, bf16[4,384,128]{2,1,0:T(8,128)(2,1)S(1)} %get-tuple-element.28.own_ref, f32[4,768,128]{2,1,0:T(8,128)S(1)} %shard_map.67.near_ref, ...), custom_call_target="tpu_custom_call" | custom-call | tf_op jit(solution)/shard_map/pallas_call | solution.py:209
  39.8 12.1 %all_to_all.16.got_ref.refs_4_ = bf16[16,128,128]{2,1,0:T(8,128)(2,1)S(1)} all-to-all(bf16[16,128,128]{2,1,0:T(8,128)(2,1)S(1)} %shard_map.68), channel_id=1, replica_groups=mesh['lead'=16,'grp'=16] {'grp'}, dimensions={0} | all-to-all | bytes 1048576 | tf_op jit(solution)/shard_map/all_to_all | solution.py:235
  51.9 0.7 shard_map.69
  52.6 3.1 %collective-permute-start.5 = (bf16[2,384,128]{2,1,0:T(8,128)(2,1)S(1)}, bf16[2,384,128]{2,1,0:T(8,128)(2,1)S(1)}, u32[]{:S(2)}, u32[]{:S(2)}) collective-permute-start(bf16[2,384,128]{2,1,0:T(8,128)(2,1)S(1)} %get-tuple-element.32), channel_id=1, source_target_pairs={{0,16},{16,32},{32,48},{48,64},{64,80},{80,96},{96,112},{112,128},... | collective-permute-start | bytes 589832 | tf_op jit(solution)/shard_map/ppermute | solution.py:231
  55.7 0.0 collective-permute-start.6
  55.7 0.7 shard_map.65
  56.4 0.1 collective-permute-start
  56.5 2.0 %collective-permute-start.1 = (bf16[8,24,384]{2,1,0:T(8,128)(2,1)S(1)}, bf16[8,24,384]{2,1,0:T(8,128)(2,1)S(1)}, u32[]{:S(2)}, u32[]{:S(2)}) collective-permute-start(bf16[8,24,384]{2,1,0:T(8,128)(2,1)S(1)} %get-tuple-element.26), channel_id=1, source_target_pairs={{0,8},{1,9},{2,10},{3,11},{4,12},{5,13},{6,14},{7,15},{8,0},{9,1},... | collective-permute-start | bytes 442376 | tf_op jit(solution)/shard_map/ppermute | solution.py:238
  58.5 0.9 collective-permute-start.2
  59.3 4.9 %collective-permute-done.refs_1_ = bf16[8,24,384]{2,1,0:T(8,128)(2,1)S(1)} collective-permute-done((bf16[8,24,384]{2,1,0:T(8,128)(2,1)S(1)}, bf16[8,24,384]{2,1,0:T(8,128)(2,1)S(1)}, u32[]{:S(2)}, u32[]{:S(2)}) %collective-permute-start) | collective-permute-done | bytes 147488 | tf_op jit(solution)/shard_map/ppermute | solution.py:238
  64.3 0.0 collective-permute-done.1.refs_2_
  64.3 0.9 collective-permute-done.2.refs_3_
  65.1 0.0 collective-permute-done.5.refs_6_
  65.1 0.0 collective-permute-done.6.refs_7_
  65.1 1.0 %shard_map.70 = (bf16[16,96,128]{2,1,0:T(8,128)(2,1)S(1)}, f32[96,128]{1,0:T(8,128)S(1)}) custom-call(s32[4,8]{1,0:T(4,128)S(1)} %copy-done.3, bf16[8,24,384]{2,1,0:T(8,128)(2,1)S(1)} %get-tuple-element.24.refs_0_, bf16[8,24,384]{2,1,0:T(8,128)(2,1)S(1)} %collective-permute-done.refs_1_, bf16[8,24,384]{2,1,0:T(8,128)(2,1)S(1)} %collective-permute-done.1.refs_2_, ...), custom_call_target="tpu_custom_call" | custom-call | tf_op jit(solution)/shard_map/pallas_call | solution.py:209
  66.1 13.4 %all_to_all.17.got_ref = bf16[16,96,128]{2,1,0:T(8,128)(2,1)S(1)} all-to-all(bf16[16,96,128]{2,1,0:T(8,128)(2,1)S(1)} %get-tuple-element.36), channel_id=1, replica_groups=mesh['lead'=16,'grp'=16] {'grp'}, dimensions={0} | all-to-all | bytes 786432 | tf_op jit(solution)/shard_map/all_to_all | solution.py:235
  79.6 0.6 shard_map.71
  80.2 3.2 %collective-permute-start.7 = (bf16[2,384,128]{2,1,0:T(8,128)(2,1)S(1)}, bf16[2,384,128]{2,1,0:T(8,128)(2,1)S(1)}, u32[]{:S(2)}, u32[]{:S(2)}) collective-permute-start(bf16[2,384,128]{2,1,0:T(8,128)(2,1)S(1)} %get-tuple-element.38), channel_id=1, source_target_pairs={{0,16},{16,32},{32,48},{48,64},{64,80},{80,96},{96,112},{112,128},... | collective-permute-start | bytes 589832 | tf_op jit(solution)/shard_map/ppermute | solution.py:231
  83.4 0.0 collective-permute-start.8
  83.4 2.6 %collective-permute-done.7.refs_5_ = bf16[2,384,128]{2,1,0:T(8,128)(2,1)S(1)} collective-permute-done((bf16[2,384,128]{2,1,0:T(8,128)(2,1)S(1)}, bf16[2,384,128]{2,1,0:T(8,128)(2,1)S(1)}, u32[]{:S(2)}, u32[]{:S(2)}) %collective-permute-start.7) | collective-permute-done | bytes 196640 | tf_op jit(solution)/shard_map/ppermute | solution.py:231
  86.0 3.7 %collective-permute-done.8.refs_6_ = bf16[2,384,128]{2,1,0:T(8,128)(2,1)S(1)} collective-permute-done((bf16[2,384,128]{2,1,0:T(8,128)(2,1)S(1)}, bf16[2,384,128]{2,1,0:T(8,128)(2,1)S(1)}, u32[]{:S(2)}, u32[]{:S(2)}) %collective-permute-start.8) | collective-permute-done | bytes 196640 | tf_op jit(solution)/shard_map/ppermute | solution.py:232
  89.7 1.6 %shard_map.72 = f32[96,128]{1,0:T(8,128)} custom-call(s32[4,8]{1,0:T(4,128)S(1)} %copy-done.3, bf16[8,24,384]{2,1,0:T(8,128)(2,1)S(1)} %get-tuple-element.24.refs_0_, bf16[8,24,384]{2,1,0:T(8,128)(2,1)S(1)} %collective-permute-done.refs_1_, bf16[8,24,384]{2,1,0:T(8,128)(2,1)S(1)} %collective-permute-done.1.refs_2_, ...), custom_call_target="tpu_custom_call" | custom-call | tf_op jit(solution)/shard_map/pallas_call | solution.py:209
Async XLA Ops:
  0.0 1.1 %copy-start = (bf16[2,384,384]{2,1,0:T(8,128)(2,1)S(1)}, bf16[2,384,384]{2,1,0:T(8,128)(2,1)}, u32[]{:S(2)}) copy-start(bf16[2,384,384]{2,1,0:T(8,128)(2,1)} %tiles_ref.1) | copy-start | bytes 1769476
  1.1 0.8 copy-start.1
  1.9 0.7 copy-start.5
  2.7 24.0 %copy-start.2 = (s32[16,2,2]{0,2,1:T(2,128)S(1)}, s32[16,2,2]{0,2,1:T(2,128)}, u32[]{:S(2)}) copy-start(s32[16,2,2]{0,2,1:T(2,128)} %param.9) | copy-start | bytes 772
  27.3 7.4 %collective-permute-start.3 = (bf16[2,384,128]{2,1,0:T(8,128)(2,1)S(1)}, bf16[2,384,128]{2,1,0:T(8,128)(2,1)S(1)}, u32[]{:S(2)}, u32[]{:S(2)}) collective-permute-start(bf16[2,384,128]{2,1,0:T(8,128)(2,1)S(1)} %get-tuple-element.29), channel_id=1, source_target_pairs={{0,16},{16,32},{32,48},{48,64},{64,80},{80,96},{96,112},{112,128},... | collective-permute-start | bytes 589832 | tf_op jit(solution)/shard_map/ppermute | solution.py:231
  32.1 6.3 %collective-permute-start.4 = (bf16[2,384,128]{2,1,0:T(8,128)(2,1)S(1)}, bf16[2,384,128]{2,1,0:T(8,128)(2,1)S(1)}, u32[]{:S(2)}, u32[]{:S(2)}) collective-permute-start(bf16[2,384,128]{2,1,0:T(8,128)(2,1)S(1)} %get-tuple-element.30), channel_id=1, source_target_pairs={{0,240},{16,0},{32,16},{48,32},{64,48},{80,64},{96,80},{112,96},{1... | collective-permute-start | bytes 589832 | tf_op jit(solution)/shard_map/ppermute | solution.py:232
  32.1 6.3 %copy-start.3 = (s32[4,8]{1,0:T(4,128)S(1)}, s32[4,8]{1,0:T(4,128)}, u32[]{:S(2)}) copy-start(s32[4,8]{1,0:T(4,128)} %cols_ref.5) | copy-start | bytes 388
  32.1 6.3 %copy-start.4 = (s32[1,32]{1,0:T(1,128)S(1)}, s32[1,32]{1,0:T(1,128)}, u32[]{:S(2)}) copy-start(s32[1,32]{1,0:T(1,128)} %slot_ref.3) | copy-start | bytes 388
  52.6 12.5 %collective-permute-start.5 = (bf16[2,384,128]{2,1,0:T(8,128)(2,1)S(1)}, bf16[2,384,128]{2,1,0:T(8,128)(2,1)S(1)}, u32[]{:S(2)}, u32[]{:S(2)}) collective-permute-start(bf16[2,384,128]{2,1,0:T(8,128)(2,1)S(1)} %get-tuple-element.32), channel_id=1, source_target_pairs={{0,16},{16,32},{32,48},{48,64},{64,80},{80,96},{96,112},{112,128},... | collective-permute-start | bytes 589832 | tf_op jit(solution)/shard_map/ppermute | solution.py:231
  55.7 9.4 %collective-permute-start.6 = (bf16[2,384,128]{2,1,0:T(8,128)(2,1)S(1)}, bf16[2,384,128]{2,1,0:T(8,128)(2,1)S(1)}, u32[]{:S(2)}, u32[]{:S(2)}) collective-permute-start(bf16[2,384,128]{2,1,0:T(8,128)(2,1)S(1)} %get-tuple-element.33), channel_id=1, source_target_pairs={{0,240},{16,0},{32,16},{48,32},{64,48},{80,64},{96,80},{112,96},{1... | collective-permute-start | bytes 589832 | tf_op jit(solution)/shard_map/ppermute | solution.py:232
  56.4 7.9 %collective-permute-start = (bf16[8,24,384]{2,1,0:T(8,128)(2,1)S(1)}, bf16[8,24,384]{2,1,0:T(8,128)(2,1)S(1)}, u32[]{:S(2)}, u32[]{:S(2)}) collective-permute-start(bf16[8,24,384]{2,1,0:T(8,128)(2,1)S(1)} %get-tuple-element.25), channel_id=1, source_target_pairs={{0,4},{1,5},{2,6},{3,7},{4,8},{5,9},{6,10},{7,11},{8,12},{9,13},{1... | collective-permute-start | bytes 442376 | tf_op jit(solution)/shard_map/ppermute | solution.py:238
  56.5 7.8 %collective-permute-start.1 = (bf16[8,24,384]{2,1,0:T(8,128)(2,1)S(1)}, bf16[8,24,384]{2,1,0:T(8,128)(2,1)S(1)}, u32[]{:S(2)}, u32[]{:S(2)}) collective-permute-start(bf16[8,24,384]{2,1,0:T(8,128)(2,1)S(1)} %get-tuple-element.26), channel_id=1, source_target_pairs={{0,8},{1,9},{2,10},{3,11},{4,12},{5,13},{6,14},{7,15},{8,0},{9,1},... | collective-permute-start | bytes 442376 | tf_op jit(solution)/shard_map/ppermute | solution.py:238
  58.5 6.7 %collective-permute-start.2 = (bf16[8,24,384]{2,1,0:T(8,128)(2,1)S(1)}, bf16[8,24,384]{2,1,0:T(8,128)(2,1)S(1)}, u32[]{:S(2)}, u32[]{:S(2)}) collective-permute-start(bf16[8,24,384]{2,1,0:T(8,128)(2,1)S(1)} %get-tuple-element.27), channel_id=1, source_target_pairs={{0,12},{1,13},{2,14},{3,15},{4,0},{5,1},{6,2},{7,3},{8,4},{9,5},{1... | collective-permute-start | bytes 442376 | tf_op jit(solution)/shard_map/ppermute | solution.py:238
  80.2 5.8 %collective-permute-start.7 = (bf16[2,384,128]{2,1,0:T(8,128)(2,1)S(1)}, bf16[2,384,128]{2,1,0:T(8,128)(2,1)S(1)}, u32[]{:S(2)}, u32[]{:S(2)}) collective-permute-start(bf16[2,384,128]{2,1,0:T(8,128)(2,1)S(1)} %get-tuple-element.38), channel_id=1, source_target_pairs={{0,16},{16,32},{32,48},{48,64},{64,80},{80,96},{96,112},{112,128},... | collective-permute-start | bytes 589832 | tf_op jit(solution)/shard_map/ppermute | solution.py:231
  83.4 6.3 %collective-permute-start.8 = (bf16[2,384,128]{2,1,0:T(8,128)(2,1)S(1)}, bf16[2,384,128]{2,1,0:T(8,128)(2,1)S(1)}, u32[]{:S(2)}, u32[]{:S(2)}) collective-permute-start(bf16[2,384,128]{2,1,0:T(8,128)(2,1)S(1)} %get-tuple-element.39), channel_id=1, source_target_pairs={{0,240},{16,0},{32,16},{48,32},{64,48},{80,64},{96,80},{112,96},{1... | collective-permute-start | bytes 589832 | tf_op jit(solution)/shard_map/ppermute | solution.py:232

commit v5 on v4

--- a/solution.py
+++ b/solution.py
@@ -13,7 +13,6 @@
 SHARE = 96
 SLAB = 24
 TILES = 32
-PIECE = 96
 F32 = jnp.float32
 BF16 = jnp.bfloat16
 GRANT = 20 << 20
@@ -42,28 +41,36 @@
     return jnp.concatenate([diag_ref[...], jnp.zeros((1, 128 - SHARE), F32)], axis=1)
 
 
-def start_kernel(tiles_ref, residual_ref, diag_ref, out_ref, start_ref, scale_ref):
+def start_kernel(residual_hbm, diag_hbm, wide_ref, start_ref, scale_ref, residual_ref, diag_ref, sems):
+    copies = [pltpu.make_async_copy(residual_hbm, residual_ref, sems.at[0]),
+              pltpu.make_async_copy(diag_hbm, diag_ref, sems.at[1])]
+    for copy in copies:
+        copy.start()
+    for copy in copies:
+        copy.wait()
     row = padded(diag_ref)
     scale = jnp.broadcast_to(column_of(row, 0, SHARE), (SHARE, NRHS))
     scaled = residual_ref[...] * scale
     scale_ref[...] = scale
     start_ref[...] = scaled
-    high = scaled.astype(BF16).astype(F32)
-    low = scaled - high
-    high = jnp.concatenate([high[32 * k:32 * (k + 1)] for k in range(3)], axis=1).astype(BF16)
+    high = scaled.astype(BF16)
+    low = scaled - high.astype(F32)
     d_high = row.astype(BF16).astype(F32)
     d_mid = (row - d_high).astype(BF16).astype(F32)
-    d_rows = jnp.broadcast_to(jnp.concatenate([d_high, d_mid, row - d_high - d_mid], axis=1), (8, TILE))
+    d_rows = jnp.concatenate([d_high, d_mid] + [row - d_high - d_mid] * 6, axis=0)
+    for x in range(SIDE):
+        tail = jnp.concatenate([low[SLAB * x:SLAB * (x + 1)], d_rows], axis=0).astype(BF16)
+        for q in range(SIDE):
+            wide_ref[SIDE * x + q, 0:SHARE] = high
+            wide_ref[SIDE * x + q, SHARE:128] = tail
+
+
+def pack_kernel(tiles_ref, out_ref):
     tiles = [tiles_ref[j].astype(F32) for j in range(2)]
     for x in range(SIDE):
-        mine = low[SLAB * x:SLAB * (x + 1)]
-        tail = jnp.concatenate([jnp.concatenate([mine[8 * k:8 * k + 8] for k in range(3)], axis=1), d_rows], axis=0)
-        tail = tail.astype(BF16)
         for q in range(SIDE):
             at = SHARE * q + SLAB * x
-            out_ref[SIDE * x + q, 0:48] = jnp.concatenate([tile[at:at + SLAB] for tile in tiles], axis=0).astype(BF16)
-            out_ref[SIDE * x + q, 48:80] = high
-            out_ref[SIDE * x + q, 80:PIECE] = tail
+            out_ref[SIDE * x + q] = jnp.concatenate([tile[at:at + SLAB] for tile in tiles], axis=0).astype(BF16)
 
 
 def send_halves(rows_ref, own_ref, up_ref, down_ref):
@@ -71,14 +78,6 @@
     for side, ref in ((0, up_ref), (1, down_ref)):
         for h in range(2):
             ref[h] = own_ref[rows_ref[side, h, lead]]
-
-
-def pick_first_kernel(rows_ref, got_ref, own_ref, up_ref, down_ref):
-    for m in range(GROUP):
-        for k in range(3):
-            at = SHARE * (m % SIDE) + 32 * k
-            own_ref[m // SIDE, at:at + 32] = got_ref[m, 48:80, NRHS * k:NRHS * (k + 1)]
-    send_halves(rows_ref, own_ref, up_ref, down_ref)
 
 
 def pick_slab_kernel(rows_ref, got_ref, own_ref, up_ref, down_ref):
@@ -93,7 +92,7 @@
 def pick_home_kernel(rows_ref, got_ref, own_ref, up_ref, down_ref):
     for r in range(SIDE):
         for q in range(SIDE):
-            own_ref[r, SHARE * q:SHARE * (q + 1)] = got_ref[SIDE * r + q]
+            own_ref[r, SHARE * q:SHARE * (q + 1)] = got_ref[SIDE * r + q, 0:SHARE]
     send_halves(rows_ref, own_ref, up_ref, down_ref)
 
 
@@ -117,14 +116,14 @@
 
 
 def all_slabs(slabs_ref):
-    return jnp.concatenate([slabs_ref[m, 0:2 * SLAB] for m in range(GROUP)], axis=0)
+    return jnp.concatenate([slabs_ref[m] for m in range(GROUP)], axis=0)
 
 
 def near_kernel(slabs_ref, own_ref, product_ref):
     slab_products(all_slabs(slabs_ref), [own_ref[r] for r in range(SIDE)], product_ref, 0)
 
 
-def first_kernel(slot_ref, cols_ref, slabs_ref, own_ref, near_ref, low_ref, high_ref,
+def first_kernel(slot_ref, cols_ref, slabs_ref, got_ref, near_ref, low_ref, high_ref,
                  wide_ref, product_ref, total_ref, line_ref):
     x, q = place()
     slab_products(all_slabs(slabs_ref), [low_ref[0], low_ref[1], high_ref[0], high_ref[1]], product_ref, 4)
@@ -136,22 +135,20 @@
         col = cols_ref[row, lax.bitwise_and(slot, 7)]
         total_ref[row] += product_ref[col, SLAB * t:SLAB * (t + 1)]
     firsts = []
-    at = pl.multiple_of(q * SHARE, SHARE)
     for r in range(SIDE):
-        line_ref[...] = own_ref[r, pl.ds(at, SHARE)].astype(F32)
+        whole = got_ref[SIDE * r + q].astype(F32)
+        line_ref[...] = whole
         high = line_ref[pl.ds(pl.multiple_of(x * SLAB, 8), SLAB), :]
-        tail = slabs_ref[SIDE * r + q, 80:PIECE].astype(F32)
-        low = jnp.concatenate([tail[0:8, NRHS * k:NRHS * (k + 1)] for k in range(3)], axis=0)
-        row = tail[8:9, 0:128] + (tail[8:9, 128:256] + tail[8:9, 256:384])
-        firsts.append(GAIN * (high + low - column_of(row, x * SLAB, SLAB) * total_ref[r]))
+        row = whole[120:121] + (whole[121:122] + whole[122:123])
+        firsts.append(GAIN * (high + whole[SHARE:120] - column_of(row, x * SLAB, SLAB) * total_ref[r]))
     first = jnp.concatenate(firsts, axis=0)
     high = first.astype(BF16)
     low = first - high.astype(F32)
     for r in range(SIDE):
-        tail = jnp.concatenate([low[SLAB * r:SLAB * (r + 1)], jnp.zeros((8, NRHS), F32)], axis=0).astype(BF16)
+        tail = low[SLAB * r:SLAB * (r + 1)].astype(BF16)
         for s in range(SIDE):
             wide_ref[SIDE * r + s, 0:SHARE] = high
-            wide_ref[SIDE * r + s, SHARE:128] = tail
+            wide_ref[SIDE * r + s, SHARE:120] = tail
 
 
 def home_product(cols_ref, parts, ext_ref, line_ref):
@@ -179,7 +176,7 @@
     row, q = place()
     firsts = []
     for x in range(SIDE):
-        line_ref[...] = got_ref[SIDE * x + q].astype(F32)
+        line_ref[0:120] = got_ref[SIDE * x + q].astype(F32)
         firsts.append(line_ref[pl.ds(pl.multiple_of(row * SLAB, 8), SLAB), :] + line_ref[SHARE:120])
     first = jnp.concatenate(firsts, axis=0)
     second = start_ref[...] - first - scale_ref[...] * total
@@ -201,18 +198,18 @@
     return pltpu.VMEM(shape, dtype)
 
 
-def call(kernel, args, outs, scalars=0, scratch=()):
+def call(kernel, args, outs, scalars=0, scratch=(), far=0):
     vectors = args[scalars:]
-    if vectors:
-        vectors = [pltpu.with_memory_space_constraint(a, pltpu.VMEM) if near else a for a, near in vectors]
-    specs = [SMEM] * scalars + [VMEM] * len(vectors)
+    space = pltpu.HBM if far else pltpu.VMEM
+    vectors = [pltpu.with_memory_space_constraint(a, space) for a in vectors]
+    specs = [SMEM] * scalars + [pl.BlockSpec(memory_space=space)] * len(vectors)
     return pl.pallas_call(kernel, in_specs=specs, out_specs=[VMEM] * len(outs),
                           out_shape=outs, scratch_shapes=list(scratch),
                           compiler_params=pltpu.CompilerParams(vmem_limit_bytes=GRANT))(*args[:scalars], *vectors)
 
 
 def near(*arrays):
-    return [(a, True) for a in arrays]
+    return list(arrays)
 
 
 HALVES = [arr((2, TILE, NRHS), BF16), arr((2, TILE, NRHS), BF16)]
@@ -237,15 +234,17 @@
     def along_x(value, k):
         return lax.ppermute(value, "grp", [(m, (m + SIDE * k) % GROUP) for m in range(GROUP)])
 
-    packed, start, scale = call(start_kernel, [(matrix_tiles, False), (residual, False), (diag, False)],
-                                [arr((GROUP, PIECE, TILE), BF16), ROWS, ROWS])
+    wide, start, scale = call(start_kernel, [residual, diag], [arr((GROUP, 128, NRHS), BF16), ROWS, ROWS],
+                              scratch=(ROWS, arr((1, SHARE), F32), pltpu.SemaphoreType.DMA((2,))), far=1)
+    got = gather(wide)
+    packed, = call(pack_kernel, near(matrix_tiles), [arr((GROUP, 2 * SLAB, TILE), BF16)])
     slabs = gather(packed)
-    own, up, down = call(pick_first_kernel, [rows] + near(slabs), [OWN] + HALVES, 1)
+    own, up, down = call(pick_home_kernel, [rows] + near(got), [OWN] + HALVES, 1)
     lower, upper = halo(up, down)
     product, = call(near_kernel, near(slabs, own), [arr((4, TILES * SLAB, NRHS), F32)])
-    wide, = call(first_kernel, [tile_slot, tile_cols] + near(slabs, own, product, lower, upper),
-                 [arr((GROUP, 128, NRHS), BF16)], 2,
-                 (arr((8, TILES * SLAB, NRHS), F32), arr((SIDE, SLAB, NRHS), F32), arr((SHARE, NRHS), F32)))
+    wide, = call(first_kernel, [tile_slot, tile_cols] + near(slabs, got, product, lower, upper),
+                 [arr((GROUP, 120, NRHS), BF16)], 2,
+                 (arr((8, TILES * SLAB, NRHS), F32), arr((SIDE, SLAB, NRHS), F32), LINE))
     got = gather(wide)
     ordered = call(order_kernel, [tile_slot] + near(slabs), [arr((8, SLAB, TILE), BF16)] * 4, 1,
                    (arr((TILES, SLAB, TILE), BF16),))

time: 91.6 us -> 91.8 us (level)
  blocking collectives: 49.5 us -> 30.3 us
  waiting for transfers between devices: 17.8 us -> 28 us
  starting transfers between devices: 14 us -> 21.3 us
  Pallas kernels: 7.33 us -> 9.76 us
  local copies, waits for them, and re-layouts: 2.53 us -> 1.08 us
    all_to_all x3 -> x2, blocking collectives: 49.5 us -> 30.3 us  [gather(): return lax.all_to_all(wide, 'grp', 0, 0)]
    all_to_all x0 -> x2, waiting for transfers between devices: none -> 12.6 us  [gather(): return lax.all_to_all(wide, 'grp', 0, 0)]
    all_to_all x0 -> x2, starting transfers between devices: none -> 10.3 us  [gather(): return lax.all_to_all(wide, 'grp', 0, 0)]
    ppermute x3, starting transfers between devices: 11.1 us -> 7.77 us  [halo(): lax.ppermute(up, 'lead', [(i, (i + 1) % leads) for i in range(leads)])]
    pallas_call x9 -> x10, Pallas kernels: 7.33 us -> 9.76 us  [call(): pl.pallas_call(kernel, in_specs=specs, out_specs=[VMEM] * len(outs), out_...]
    ppermute x3, waiting for transfers between devices: 4.65 us -> 2.34 us  [halo(): lax.ppermute(up, 'lead', [(i, (i + 1) % leads) for i in range(leads)])]
    ppermute x3, waiting for transfers between devices: 7.38 us -> 5.54 us  [halo(): lax.ppermute(down, 'lead', [(i, (i - 1) % leads) for i in range(leads)])]
    ppermute x3, waiting for transfers between devices: 5.8 us -> 7.51 us  [along_x(): lax.ppermute(value, 'grp', [(m, (m + SIDE * k) % GROUP) for m in range(GR...]
  transfers between devices with their start and end apart: 9 -> 11, of which waited for: 6 -> 7; matrix products, arithmetic and copies ran while one was open for 0% -> 0% of each run, Pallas kernels for 1% -> 3%
where the time goes in v5:
time: 91.8 us; the launch traced here: 90.6 us
  blocking collectives  30.3 us (33%)
  waiting for transfers between devices  28 us (31%)
  starting transfers between devices  21.3 us (23%)
  Pallas kernels  9.76 us (11%)
  local copies, waits for them, and re-layouts  1.08 us (1%)
    all_to_all x2, blocking collectives, gather(): return lax.all_to_all(wide, 'grp', 0, 0)  30.3 us
    all_to_all x2, waiting for transfers between devices, gather(): return lax.all_to_all(wide, 'grp', 0, 0)  12.6 us
    all_to_all x2, starting transfers between devices, gather(): return lax.all_to_all(wide, 'grp', 0, 0)  10.3 us
    pallas_call x10, Pallas kernels, call(): pl.pallas_call(kernel, in_specs=specs, out_specs=[VMEM] * len(outs), out_...  9.76 us
    ppermute x3, starting transfers between devices, halo(): lax.ppermute(up, 'lead', [(i, (i + 1) % leads) for i in range(leads)])  7.77 us
    ppermute x3, waiting for transfers between devices, along_x(): lax.ppermute(value, 'grp', [(m, (m + SIDE * k) % GROUP) for m in range(GR...  7.51 us
    ppermute x3, waiting for transfers between devices, halo(): lax.ppermute(down, 'lead', [(i, (i - 1) % leads) for i in range(leads)])  5.54 us
    ppermute x3, starting transfers between devices, along_x(): lax.ppermute(value, 'grp', [(m, (m + SIDE * k) % GROUP) for m in range(GR...  2.93 us
  transfers between devices with their start and end apart: 11, of which 7 were waited for; matrix products, arithmetic and copies ran while one was open for 0% of the time, Pallas kernels for 3%

profile of v5, /device:TPU:97, one launch (start us, length us, event | category | flops | bytes accessed | tf_op | source)
XLA Modules:
  0.0 90.6 jit_solution(18161039353718361115)
XLA Ops:
  0.0 1.8 %shard_map.66 = (bf16[16,128,128]{2,1,0:T(8,128)(2,1)}, f32[96,128]{1,0:T(8,128)S(1)}, f32[96,128]{1,0:T(8,128)S(1)}) custom-call(f32[96,128]{1,0:T(8,128)} %residual_hbm.1, f32[1,96]{1,0:T(1,128)} %bitcast.5), custom_call_target="tpu_custom_call" | custom-call | tf_op jit(solution)/shard_map/pallas_call | solution.py:206
  1.8 0.0 copy-start.2
  1.8 6.8 %all-to-all-start.1 = ((bf16[16,128,128]{2,1,0:T(8,128)(2,1)}), bf16[16,128,128]{2,1,0:T(8,128)(2,1)S(1)}, u32[]{:S(2)}, u32[]{:S(2)}) async-start(bf16[16,128,128]{2,1,0:T(8,128)(2,1)} %get-tuple-element.27), calls=%async_computation.1 | async-start | bytes 1048576 | tf_op jit(solution)/shard_map/all_to_all | solution.py:232
  8.6 0.0 copy-start
  8.6 1.1 %copy-done = bf16[2,384,384]{2,1,0:T(8,128)(2,1)S(1)} copy-done((bf16[2,384,384]{2,1,0:T(8,128)(2,1)S(1)}, bf16[2,384,384]{2,1,0:T(8,128)(2,1)}, u32[]{:S(2)}) %copy-start) | copy-done | bytes 589848
  9.6 0.9 shard_map.64
  10.5 8.4 %all-to-all-done.1.got_ref = bf16[16,128,128]{2,1,0:T(8,128)(2,1)S(1)} async-done(((bf16[16,128,128]{2,1,0:T(8,128)(2,1)}), bf16[16,128,128]{2,1,0:T(8,128)(2,1)S(1)}, u32[]{:S(2)}, u32[]{:S(2)}) %all-to-all-start.1) | async-done | bytes 524320 | tf_op jit(solution)/shard_map/all_to_all | solution.py:232
  18.9 3.6 %all-to-all-start = ((bf16[16,48,384]{2,1,0:T(8,128)(2,1)}), bf16[16,48,384]{2,1,0:T(8,128)(2,1)S(1)}, u32[]{:S(2)}, u32[]{:S(2)}) async-start(bf16[16,48,384]{2,1,0:T(8,128)(2,1)} %shard_map.64), calls=%async_computation | async-start | bytes 1179648 | tf_op jit(solution)/shard_map/all_to_all | solution.py:232
  22.5 0.0 copy-start.1
  22.5 0.0 copy-start.3
  22.5 0.0 copy-done.2
  22.5 0.6 shard_map.67
  23.2 4.8 %collective-permute-start.3 = (bf16[2,384,128]{2,1,0:T(8,128)(2,1)S(1)}, bf16[2,384,128]{2,1,0:T(8,128)(2,1)S(1)}, u32[]{:S(2)}, u32[]{:S(2)}) collective-permute-start(bf16[2,384,128]{2,1,0:T(8,128)(2,1)S(1)} %get-tuple-element.29), channel_id=1, source_target_pairs={{0,16},{16,32},{32,48},{48,64},{64,80},{80,96},{96,112},{112,128},... | collective-permute-start | bytes 589832 | tf_op jit(solution)/shard_map/ppermute | solution.py:228
  28.0 0.0 collective-permute-start.4
  28.0 4.2 %all-to-all-done.slabs_ref = bf16[16,48,384]{2,1,0:T(8,128)(2,1)S(1)} async-done(((bf16[16,48,384]{2,1,0:T(8,128)(2,1)}), bf16[16,48,384]{2,1,0:T(8,128)(2,1)S(1)}, u32[]{:S(2)}, u32[]{:S(2)}) %all-to-all-start) | async-done | bytes 589856 | tf_op jit(solution)/shard_map/all_to_all | solution.py:232
  32.2 0.6 shard_map.68.near_ref
  32.7 0.0 collective-permute-done.3.low_ref
  32.7 1.9 %collective-permute-done.4.high_ref = bf16[2,384,128]{2,1,0:T(8,128)(2,1)S(1)} collective-permute-done((bf16[2,384,128]{2,1,0:T(8,128)(2,1)S(1)}, bf16[2,384,128]{2,1,0:T(8,128)(2,1)S(1)}, u32[]{:S(2)}, u32[]{:S(2)}) %collective-permute-start.4) | collective-permute-done | bytes 196640 | tf_op jit(solution)/shard_map/ppermute | solution.py:229
  34.6 0.0 copy-done.1
  34.6 0.0 copy-done.3
  34.6 1.4 %shard_map.69 = bf16[16,120,128]{2,1,0:T(8,128)(2,1)S(1)} custom-call(s32[1,32]{1,0:T(1,128)S(1)} %copy-done.3, s32[4,8]{1,0:T(4,128)S(1)} %copy-done.1, bf16[16,48,384]{2,1,0:T(8,128)(2,1)S(1)} %all-to-all-done.slabs_ref, bf16[16,128,128]{2,1,0:T(8,128)(2,1)S(1)} %all-to-all-done.1.got_ref, f32[4,768,128]{2,1,0:T(8,128)S(1)} %shard_map.68.near_ref, ...), custom_call_target="tpu_custom_call" | custom-call | tf_op jit(solution)/shard_map/pallas_call | solution.py:206
  36.0 16.8 %all_to_all.20.got_ref.refs_4_ = bf16[16,120,128]{2,1,0:T(8,128)(2,1)S(1)} all-to-all(bf16[16,120,128]{2,1,0:T(8,128)(2,1)S(1)} %shard_map.69), channel_id=1, replica_groups=mesh['lead'=16,'grp'=16] {'grp'}, dimensions={0} | all-to-all | bytes 983040 | tf_op jit(solution)/shard_map/all_to_all | solution.py:232
  52.8 0.7 shard_map.70
  53.4 1.4 %collective-permute-start.5 = (bf16[2,384,128]{2,1,0:T(8,128)(2,1)S(1)}, bf16[2,384,128]{2,1,0:T(8,128)(2,1)S(1)}, u32[]{:S(2)}, u32[]{:S(2)}) collective-permute-start(bf16[2,384,128]{2,1,0:T(8,128)(2,1)S(1)} %get-tuple-element.32), channel_id=1, source_target_pairs={{0,16},{16,32},{32,48},{48,64},{64,80},{80,96},{96,112},{112,128},... | collective-permute-start | bytes 589832 | tf_op jit(solution)/shard_map/ppermute | solution.py:228
  54.9 0.0 collective-permute-start.6
  54.9 0.7 shard_map.65
  55.6 0.1 collective-permute-start
  55.6 2.0 %collective-permute-start.1 = (bf16[8,24,384]{2,1,0:T(8,128)(2,1)S(1)}, bf16[8,24,384]{2,1,0:T(8,128)(2,1)S(1)}, u32[]{:S(2)}, u32[]{:S(2)}) collective-permute-start(bf16[8,24,384]{2,1,0:T(8,128)(2,1)S(1)} %get-tuple-element.25), channel_id=1, source_target_pairs={{0,8},{1,9},{2,10},{3,11},{4,12},{5,13},{6,14},{7,15},{8,0},{9,1},... | collective-permute-start | bytes 442376 | tf_op jit(solution)/shard_map/ppermute | solution.py:235
  57.7 0.8 collective-permute-start.2
  58.5 7.2 %collective-permute-done.refs_1_ = bf16[8,24,384]{2,1,0:T(8,128)(2,1)S(1)} collective-permute-done((bf16[8,24,384]{2,1,0:T(8,128)(2,1)S(1)}, bf16[8,24,384]{2,1,0:T(8,128)(2,1)S(1)}, u32[]{:S(2)}, u32[]{:S(2)}) %collective-permute-start) | collective-permute-done | bytes 147488 | tf_op jit(solution)/shard_map/ppermute | solution.py:235
  65.7 0.0 collective-permute-done.1.refs_2_
  65.7 0.3 collective-permute-done.2.refs_3_
  66.0 0.0 collective-permute-done.5.refs_6_
  66.0 0.0 collective-permute-done.6.refs_7_
  66.0 1.0 %shard_map.71 = (bf16[16,96,128]{2,1,0:T(8,128)(2,1)S(1)}, f32[96,128]{1,0:T(8,128)S(1)}) custom-call(s32[4,8]{1,0:T(4,128)S(1)} %copy-done.1, bf16[8,24,384]{2,1,0:T(8,128)(2,1)S(1)} %get-tuple-element.23.refs_0_, bf16[8,24,384]{2,1,0:T(8,128)(2,1)S(1)} %collective-permute-done.refs_1_, bf16[8,24,384]{2,1,0:T(8,128)(2,1)S(1)} %collective-permute-done.1.refs_2_, ...), custom_call_target="tpu_custom_call" | custom-call | tf_op jit(solution)/shard_map/pallas_call | solution.py:206
  67.0 13.5 %all_to_all.21.got_ref = bf16[16,96,128]{2,1,0:T(8,128)(2,1)S(1)} all-to-all(bf16[16,96,128]{2,1,0:T(8,128)(2,1)S(1)} %get-tuple-element.36), channel_id=1, replica_groups=mesh['lead'=16,'grp'=16] {'grp'}, dimensions={0} | all-to-all | bytes 786432 | tf_op jit(solution)/shard_map/all_to_all | solution.py:232
  80.5 0.6 shard_map.72
  81.2 1.5 %collective-permute-start.7 = (bf16[2,384,128]{2,1,0:T(8,128)(2,1)S(1)}, bf16[2,384,128]{2,1,0:T(8,128)(2,1)S(1)}, u32[]{:S(2)}, u32[]{:S(2)}) collective-permute-start(bf16[2,384,128]{2,1,0:T(8,128)(2,1)S(1)} %get-tuple-element.38), channel_id=1, source_target_pairs={{0,16},{16,32},{32,48},{48,64},{64,80},{80,96},{96,112},{112,128},... | collective-permute-start | bytes 589832 | tf_op jit(solution)/shard_map/ppermute | solution.py:228
  82.7 0.3 collective-permute-start.8
  83.0 2.3 %collective-permute-done.7.refs_5_ = bf16[2,384,128]{2,1,0:T(8,128)(2,1)S(1)} collective-permute-done((bf16[2,384,128]{2,1,0:T(8,128)(2,1)S(1)}, bf16[2,384,128]{2,1,0:T(8,128)(2,1)S(1)}, u32[]{:S(2)}, u32[]{:S(2)}) %collective-permute-start.7) | collective-permute-done | bytes 196640 | tf_op jit(solution)/shard_map/ppermute | solution.py:228
  85.3 3.7 %collective-permute-done.8.refs_6_ = bf16[2,384,128]{2,1,0:T(8,128)(2,1)S(1)} collective-permute-done((bf16[2,384,128]{2,1,0:T(8,128)(2,1)S(1)}, bf16[2,384,128]{2,1,0:T(8,128)(2,1)S(1)}, u32[]{:S(2)}, u32[]{:S(2)}) %collective-permute-start.8) | collective-permute-done | bytes 196640 | tf_op jit(solution)/shard_map/ppermute | solution.py:229
  89.0 1.6 %shard_map.73 = f32[96,128]{1,0:T(8,128)} custom-call(s32[4,8]{1,0:T(4,128)S(1)} %copy-done.1, bf16[8,24,384]{2,1,0:T(8,128)(2,1)S(1)} %get-tuple-element.23.refs_0_, bf16[8,24,384]{2,1,0:T(8,128)(2,1)S(1)} %collective-permute-done.refs_1_, bf16[8,24,384]{2,1,0:T(8,128)(2,1)S(1)} %collective-permute-done.1.refs_2_, ...), custom_call_target="tpu_custom_call" | custom-call | tf_op jit(solution)/shard_map/pallas_call | solution.py:206
Async XLA Ops:
  1.8 20.8 %copy-start.2 = (s32[16,2,2]{0,2,1:T(2,128)S(1)}, s32[16,2,2]{0,2,1:T(2,128)}, u32[]{:S(2)}) copy-start(s32[16,2,2]{0,2,1:T(2,128)} %param.9) | copy-start | bytes 772
  1.8 17.1 %all-to-all-start.1 = ((bf16[16,128,128]{2,1,0:T(8,128)(2,1)}), bf16[16,128,128]{2,1,0:T(8,128)(2,1)S(1)}, u32[]{:S(2)}, u32[]{:S(2)}) async-start(bf16[16,128,128]{2,1,0:T(8,128)(2,1)} %get-tuple-element.27), calls=%async_computation.1 | async-start | bytes 1048576 | tf_op jit(solution)/shard_map/all_to_all | solution.py:232
  8.6 1.1 %copy-start = (bf16[2,384,384]{2,1,0:T(8,128)(2,1)S(1)}, bf16[2,384,384]{2,1,0:T(8,128)(2,1)}, u32[]{:S(2)}) copy-start(bf16[2,384,384]{2,1,0:T(8,128)(2,1)} %tiles_ref.1) | copy-start | bytes 1769476
  18.9 13.2 %all-to-all-start = ((bf16[16,48,384]{2,1,0:T(8,128)(2,1)}), bf16[16,48,384]{2,1,0:T(8,128)(2,1)S(1)}, u32[]{:S(2)}, u32[]{:S(2)}) async-start(bf16[16,48,384]{2,1,0:T(8,128)(2,1)} %shard_map.64), calls=%async_computation | async-start | bytes 1179648 | tf_op jit(solution)/shard_map/all_to_all | solution.py:232
  22.5 12.1 %copy-start.1 = (s32[4,8]{1,0:T(4,128)S(1)}, s32[4,8]{1,0:T(4,128)}, u32[]{:S(2)}) copy-start(s32[4,8]{1,0:T(4,128)} %cols_ref.5) | copy-start | bytes 388
  22.5 12.1 %copy-start.3 = (s32[1,32]{1,0:T(1,128)S(1)}, s32[1,32]{1,0:T(1,128)}, u32[]{:S(2)}) copy-start(s32[1,32]{1,0:T(1,128)} %slot_ref.3) | copy-start | bytes 388
  23.2 9.6 %collective-permute-start.3 = (bf16[2,384,128]{2,1,0:T(8,128)(2,1)S(1)}, bf16[2,384,128]{2,1,0:T(8,128)(2,1)S(1)}, u32[]{:S(2)}, u32[]{:S(2)}) collective-permute-start(bf16[2,384,128]{2,1,0:T(8,128)(2,1)S(1)} %get-tuple-element.29), channel_id=1, source_target_pairs={{0,16},{16,32},{32,48},{48,64},{64,80},{80,96},{96,112},{112,128},... | collective-permute-start | bytes 589832 | tf_op jit(solution)/shard_map/ppermute | solution.py:228
  28.0 6.6 %collective-permute-start.4 = (bf16[2,384,128]{2,1,0:T(8,128)(2,1)S(1)}, bf16[2,384,128]{2,1,0:T(8,128)(2,1)S(1)}, u32[]{:S(2)}, u32[]{:S(2)}) collective-permute-start(bf16[2,384,128]{2,1,0:T(8,128)(2,1)S(1)} %get-tuple-element.30), channel_id=1, source_target_pairs={{0,240},{16,0},{32,16},{48,32},{64,48},{80,64},{96,80},{112,96},{1... | collective-permute-start | bytes 589832 | tf_op jit(solution)/shard_map/ppermute | solution.py:229
  53.4 12.6 %collective-permute-start.5 = (bf16[2,384,128]{2,1,0:T(8,128)(2,1)S(1)}, bf16[2,384,128]{2,1,0:T(8,128)(2,1)S(1)}, u32[]{:S(2)}, u32[]{:S(2)}) collective-permute-start(bf16[2,384,128]{2,1,0:T(8,128)(2,1)S(1)} %get-tuple-element.32), channel_id=1, source_target_pairs={{0,16},{16,32},{32,48},{48,64},{64,80},{80,96},{96,112},{112,128},... | collective-permute-start | bytes 589832 | tf_op jit(solution)/shard_map/ppermute | solution.py:228
  54.9 11.1 %collective-permute-start.6 = (bf16[2,384,128]{2,1,0:T(8,128)(2,1)S(1)}, bf16[2,384,128]{2,1,0:T(8,128)(2,1)S(1)}, u32[]{:S(2)}, u32[]{:S(2)}) collective-permute-start(bf16[2,384,128]{2,1,0:T(8,128)(2,1)S(1)} %get-tuple-element.33), channel_id=1, source_target_pairs={{0,240},{16,0},{32,16},{48,32},{64,48},{80,64},{96,80},{112,96},{1... | collective-permute-start | bytes 589832 | tf_op jit(solution)/shard_map/ppermute | solution.py:229
  55.6 10.1 %collective-permute-start = (bf16[8,24,384]{2,1,0:T(8,128)(2,1)S(1)}, bf16[8,24,384]{2,1,0:T(8,128)(2,1)S(1)}, u32[]{:S(2)}, u32[]{:S(2)}) collective-permute-start(bf16[8,24,384]{2,1,0:T(8,128)(2,1)S(1)} %get-tuple-element.24), channel_id=1, source_target_pairs={{0,4},{1,5},{2,6},{3,7},{4,8},{5,9},{6,10},{7,11},{8,12},{9,13},{1... | collective-permute-start | bytes 442376 | tf_op jit(solution)/shard_map/ppermute | solution.py:235
  55.6 10.0 %collective-permute-start.1 = (bf16[8,24,384]{2,1,0:T(8,128)(2,1)S(1)}, bf16[8,24,384]{2,1,0:T(8,128)(2,1)S(1)}, u32[]{:S(2)}, u32[]{:S(2)}) collective-permute-start(bf16[8,24,384]{2,1,0:T(8,128)(2,1)S(1)} %get-tuple-element.25), channel_id=1, source_target_pairs={{0,8},{1,9},{2,10},{3,11},{4,12},{5,13},{6,14},{7,15},{8,0},{9,1},... | collective-permute-start | bytes 442376 | tf_op jit(solution)/shard_map/ppermute | solution.py:235
  57.7 8.3 %collective-permute-start.2 = (bf16[8,24,384]{2,1,0:T(8,128)(2,1)S(1)}, bf16[8,24,384]{2,1,0:T(8,128)(2,1)S(1)}, u32[]{:S(2)}, u32[]{:S(2)}) collective-permute-start(bf16[8,24,384]{2,1,0:T(8,128)(2,1)S(1)} %get-tuple-element.26), channel_id=1, source_target_pairs={{0,12},{1,13},{2,14},{3,15},{4,0},{5,1},{6,2},{7,3},{8,4},{9,5},{1... | collective-permute-start | bytes 442376 | tf_op jit(solution)/shard_map/ppermute | solution.py:235
  81.2 4.1 %collective-permute-start.7 = (bf16[2,384,128]{2,1,0:T(8,128)(2,1)S(1)}, bf16[2,384,128]{2,1,0:T(8,128)(2,1)S(1)}, u32[]{:S(2)}, u32[]{:S(2)}) collective-permute-start(bf16[2,384,128]{2,1,0:T(8,128)(2,1)S(1)} %get-tuple-element.38), channel_id=1, source_target_pairs={{0,16},{16,32},{32,48},{48,64},{64,80},{80,96},{96,112},{112,128},... | collective-permute-start | bytes 589832 | tf_op jit(solution)/shard_map/ppermute | solution.py:228
  82.7 6.3 %collective-permute-start.8 = (bf16[2,384,128]{2,1,0:T(8,128)(2,1)S(1)}, bf16[2,384,128]{2,1,0:T(8,128)(2,1)S(1)}, u32[]{:S(2)}, u32[]{:S(2)}) collective-permute-start(bf16[2,384,128]{2,1,0:T(8,128)(2,1)S(1)} %get-tuple-element.39), channel_id=1, source_target_pairs={{0,240},{16,0},{32,16},{48,32},{64,48},{80,64},{96,80},{112,96},{1... | collective-permute-start | bytes 589832 | tf_op jit(solution)/shard_map/ppermute | solution.py:229

commit v6 on v5

--- a/solution.py
+++ b/solution.py
@@ -41,12 +41,17 @@
     return jnp.concatenate([diag_ref[...], jnp.zeros((1, 128 - SHARE), F32)], axis=1)
 
 
-def start_kernel(residual_hbm, diag_hbm, wide_ref, start_ref, scale_ref, residual_ref, diag_ref, sems):
+def start_kernel(tiles_hbm, residual_hbm, diag_hbm, part0, part1, part2, part3, wide_ref, start_ref, scale_ref,
+                 residual_ref, diag_ref, sems):
+    _, q = place()
     copies = [pltpu.make_async_copy(residual_hbm, residual_ref, sems.at[0]),
               pltpu.make_async_copy(diag_hbm, diag_ref, sems.at[1])]
+    for k, part in enumerate((part0, part1, part2, part3)):
+        at = pl.multiple_of(wrap(q + k) * SHARE, SHARE)
+        copies.append(pltpu.make_async_copy(tiles_hbm.at[:, pl.ds(at, SHARE)], part, sems.at[2 + k]))
     for copy in copies:
         copy.start()
-    for copy in copies:
+    for copy in copies[:2]:
         copy.wait()
     row = padded(diag_ref)
     scale = jnp.broadcast_to(column_of(row, 0, SHARE), (SHARE, NRHS))
@@ -60,17 +65,23 @@
     d_rows = jnp.concatenate([d_high, d_mid] + [row - d_high - d_mid] * 6, axis=0)
     for x in range(SIDE):
         tail = jnp.concatenate([low[SLAB * x:SLAB * (x + 1)], d_rows], axis=0).astype(BF16)
-        for q in range(SIDE):
-            wide_ref[SIDE * x + q, 0:SHARE] = high
-            wide_ref[SIDE * x + q, SHARE:128] = tail
-
-
-def pack_kernel(tiles_ref, out_ref):
-    tiles = [tiles_ref[j].astype(F32) for j in range(2)]
-    for x in range(SIDE):
-        for q in range(SIDE):
-            at = SHARE * q + SLAB * x
-            out_ref[SIDE * x + q] = jnp.concatenate([tile[at:at + SLAB] for tile in tiles], axis=0).astype(BF16)
+        for y in range(SIDE):
+            wide_ref[SIDE * x + y, 0:SHARE] = high
+            wide_ref[SIDE * x + y, SHARE:128] = tail
+    for copy in copies[2:]:
+        copy.wait()
+
+
+def split_kernel(*refs):
+    parts, outs, held_ref = refs[:4], refs[4:8], refs[8]
+    x, q = place()
+    for k in range(SIDE):
+        tiles = [parts[k][j].astype(F32) for j in range(2)]
+        for s in range(SIDE):
+            pair = jnp.concatenate([tile[SLAB * s:SLAB * (s + 1)] for tile in tiles], axis=0)
+            held_ref[wrap(s - x), wrap(q - k)] = pair.astype(BF16)
+    for k in range(SIDE):
+        outs[k][...] = held_ref[k]
 
 
 def send_halves(rows_ref, own_ref, up_ref, down_ref):
@@ -96,13 +107,19 @@
     send_halves(rows_ref, own_ref, up_ref, down_ref)
 
 
-def order_kernel(slot_ref, slabs_ref, *refs):
-    outs, held_ref = refs[:4], refs[4]
+def slot_of(slot_ref, x, k, i):
+    return slot_ref[0, 8 * wrap(x - k) + i]
+
+
+def order_kernel(slot_ref, *refs):
+    parts, outs, held_ref = refs[:4], refs[4:8], refs[8]
     x, _ = place()
-    for t in range(TILES):
-        piece = slabs_ref[t // 2].astype(F32)[SLAB * (t % 2):SLAB * (t % 2 + 1)]
-        slot = slot_ref[0, t]
-        held_ref[lax.bitwise_and(slot - 8 * x, TILES - 1)] = piece.astype(BF16)
+    for k in range(SIDE):
+        for y in range(SIDE):
+            pair = parts[k][y].astype(F32)
+            for j in range(2):
+                to = lax.bitwise_and(slot_of(slot_ref, x, k, 2 * y + j) - 8 * x, TILES - 1)
+                held_ref[to] = pair[SLAB * j:SLAB * (j + 1)].astype(BF16)
     for k in range(SIDE):
         outs[k][...] = held_ref[8 * k:8 * k + 8]
 
@@ -115,22 +132,23 @@
         product_ref[first + 2 * pair + 1] = product[:, NRHS:]
 
 
-def all_slabs(slabs_ref):
-    return jnp.concatenate([slabs_ref[m] for m in range(GROUP)], axis=0)
-
-
-def near_kernel(slabs_ref, own_ref, product_ref):
-    slab_products(all_slabs(slabs_ref), [own_ref[r] for r in range(SIDE)], product_ref, 0)
-
-
-def first_kernel(slot_ref, cols_ref, slabs_ref, got_ref, near_ref, low_ref, high_ref,
-                 wide_ref, product_ref, total_ref, line_ref):
+def all_slabs(parts):
+    return jnp.concatenate([part[y] for part in parts for y in range(SIDE)], axis=0)
+
+
+def near_kernel(*refs):
+    own_ref, product_ref = refs[4:]
+    slab_products(all_slabs(refs[:4]), [own_ref[r] for r in range(SIDE)], product_ref, 0)
+
+
+def first_kernel(slot_ref, cols_ref, *refs):
+    got_ref, near_ref, low_ref, high_ref, wide_ref, product_ref, total_ref, line_ref = refs[4:]
     x, q = place()
-    slab_products(all_slabs(slabs_ref), [low_ref[0], low_ref[1], high_ref[0], high_ref[1]], product_ref, 4)
+    slab_products(all_slabs(refs[:4]), [low_ref[0], low_ref[1], high_ref[0], high_ref[1]], product_ref, 4)
     product_ref[0:4] = near_ref[...]
     total_ref[...] = jnp.zeros_like(total_ref)
     for t in range(TILES):
-        slot = slot_ref[0, t]
+        slot = slot_of(slot_ref, x, t // 8, t % 8)
         row = lax.shift_right_logical(slot, 3)
         col = cols_ref[row, lax.bitwise_and(slot, 7)]
         total_ref[row] += product_ref[col, SLAB * t:SLAB * (t + 1)]
@@ -229,24 +247,33 @@
                 lax.ppermute(down, "lead", [(i, (i - 1) % leads) for i in range(leads)]))
 
     def gather(wide):
-        return lax.all_to_all(wide, "grp", 0, 0)
+        return lax.all_to_all(pltpu.with_memory_space_constraint(wide, pltpu.VMEM), "grp", 0, 0)
 
     def along_x(value, k):
         return lax.ppermute(value, "grp", [(m, (m + SIDE * k) % GROUP) for m in range(GROUP)])
 
-    wide, start, scale = call(start_kernel, [residual, diag], [arr((GROUP, 128, NRHS), BF16), ROWS, ROWS],
-                              scratch=(ROWS, arr((1, SHARE), F32), pltpu.SemaphoreType.DMA((2,))), far=1)
+    def along_y(value, k):
+        return lax.ppermute(value, "grp", [(m, m - m % SIDE + (m + k) % SIDE) for m in range(GROUP)])
+
+    *quarters, wide, start, scale = call(
+        start_kernel, [matrix_tiles, residual, diag],
+        [arr((2, SHARE, TILE), BF16)] * 4 + [arr((GROUP, 128, NRHS), BF16), ROWS, ROWS],
+        scratch=(ROWS, arr((1, SHARE), F32), pltpu.SemaphoreType.DMA((6,))), far=1)
+    for k in range(1, SIDE):
+        quarters[k] = along_y(quarters[k], k)
     got = gather(wide)
-    packed, = call(pack_kernel, near(matrix_tiles), [arr((GROUP, 2 * SLAB, TILE), BF16)])
-    slabs = gather(packed)
+    slabs = list(call(split_kernel, near(*quarters), [arr((SIDE, 2 * SLAB, TILE), BF16)] * 4, 0,
+                 (arr((SIDE, SIDE, 2 * SLAB, TILE), BF16),)))
+    for k in range(1, SIDE):
+        slabs[k] = along_x(slabs[k], k)
     own, up, down = call(pick_home_kernel, [rows] + near(got), [OWN] + HALVES, 1)
     lower, upper = halo(up, down)
-    product, = call(near_kernel, near(slabs, own), [arr((4, TILES * SLAB, NRHS), F32)])
-    wide, = call(first_kernel, [tile_slot, tile_cols] + near(slabs, got, product, lower, upper),
+    product, = call(near_kernel, near(*slabs, own), [arr((4, TILES * SLAB, NRHS), F32)])
+    wide, = call(first_kernel, [tile_slot, tile_cols] + near(*slabs, got, product, lower, upper),
                  [arr((GROUP, 120, NRHS), BF16)], 2,
                  (arr((8, TILES * SLAB, NRHS), F32), arr((SIDE, SLAB, NRHS), F32), LINE))
     got = gather(wide)
-    ordered = call(order_kernel, [tile_slot] + near(slabs), [arr((8, SLAB, TILE), BF16)] * 4, 1,
+    ordered = call(order_kernel, [tile_slot] + near(*slabs), [arr((8, SLAB, TILE), BF16)] * 4, 1,
                    (arr((TILES, SLAB, TILE), BF16),))
     parts = [ordered[0]]
     for k in range(1, SIDE):

time: 91.8 us -> 94.8 us (1.033)
  starting transfers between devices: 21.3 us -> 29.9 us
  waiting for transfers between devices: 28 us -> 24.4 us
  local copies, waits for them, and re-layouts: 1.08 us -> 0.02 us
    all_to_all x2 -> x1, waiting for transfers between devices: 12.6 us -> 5.5 us  [gather(): lax.all_to_all(pltpu.with_memory_space_constraint(wide, pltpu.VMEM), 'grp...]
    ppermute x3 -> x6, waiting for transfers between devices: 7.51 us -> 12.7 us  [along_x(): lax.ppermute(value, 'grp', [(m, (m + SIDE * k) % GROUP) for m in range(GR...]
    ppermute x0 -> x3, starting transfers between devices: none -> 4.94 us  [along_y(): lax.ppermute(value, 'grp', [(m, m - m % SIDE + (m + k) % SIDE) for m in r...]
    ppermute x3 -> x6, starting transfers between devices: 2.93 us -> 7.09 us  [along_x(): lax.ppermute(value, 'grp', [(m, (m + SIDE * k) % GROUP) for m in range(GR...]
    all_to_all x2 -> x1, starting transfers between devices: 10.3 us -> 6.77 us  [gather(): lax.all_to_all(pltpu.with_memory_space_constraint(wide, pltpu.VMEM), 'grp...]
    ppermute x3, starting transfers between devices: 0.29 us -> 2.15 us  [halo(): lax.ppermute(down, 'lead', [(i, (i - 1) % leads) for i in range(leads)])]
    ppermute x3, waiting for transfers between devices: 5.54 us -> 3.7 us  [halo(): lax.ppermute(down, 'lead', [(i, (i - 1) % leads) for i in range(leads)])]
    ppermute x3, starting transfers between devices: 7.77 us -> 8.97 us  [halo(): lax.ppermute(up, 'lead', [(i, (i + 1) % leads) for i in range(leads)])]
  transfers between devices with their start and end apart: 11 -> 16, of which waited for: 7 -> 8; matrix products, arithmetic and copies ran while one was open for 0% -> 0% of each run, Pallas kernels for 3% -> 2%
where the time goes in v6:
time: 94.8 us; the launch traced here: 94.1 us
  blocking collectives  30.4 us (32%)
  starting transfers between devices  29.9 us (32%)
  waiting for transfers between devices  24.4 us (26%)
  Pallas kernels  9.3 us (10%)
    all_to_all x2, blocking collectives, gather(): lax.all_to_all(pltpu.with_memory_space_constraint(wide, pltpu.VMEM), 'grp...  30.4 us
    ppermute x6, waiting for transfers between devices, along_x(): lax.ppermute(value, 'grp', [(m, (m + SIDE * k) % GROUP) for m in range(GR...  12.7 us
    pallas_call x10, Pallas kernels, call(): pl.pallas_call(kernel, in_specs=specs, out_specs=[VMEM] * len(outs), out_...  9.3 us
    ppermute x3, starting transfers between devices, halo(): lax.ppermute(up, 'lead', [(i, (i + 1) % leads) for i in range(leads)])  8.97 us
    ppermute x6, starting transfers between devices, along_x(): lax.ppermute(value, 'grp', [(m, (m + SIDE * k) % GROUP) for m in range(GR...  7.09 us
    all_to_all x1, starting transfers between devices, gather(): lax.all_to_all(pltpu.with_memory_space_constraint(wide, pltpu.VMEM), 'grp...  6.77 us
    all_to_all x1, waiting for transfers between devices, gather(): lax.all_to_all(pltpu.with_memory_space_constraint(wide, pltpu.VMEM), 'grp...  5.5 us
    ppermute x3, starting transfers between devices, along_y(): lax.ppermute(value, 'grp', [(m, m - m % SIDE + (m + k) % SIDE) for m in r...  4.94 us
  transfers between devices with their start and end apart: 16, of which 8 were waited for; matrix products, arithmetic and copies ran while one was open for 0% of the time, Pallas kernels for 2%

profile of v6, /device:TPU:97, one launch (start us, length us, event | category | flops | bytes accessed | tf_op | source)
XLA Modules:
  0.0 94.1 jit_solution(3328210788824236297)
XLA Ops:
  0.0 2.0 %shard_map.64 = (bf16[2,96,384]{2,1,0:T(8,128)(2,1)S(1)}, bf16[2,96,384]{2,1,0:T(8,128)(2,1)S(1)}, bf16[2,96,384]{2,1,0:T(8,128)(2,1)S(1)}, bf16[2,96,384]{2,1,0...) custom-call(bf16[2,384,384]{2,1,0:T(8,128)(2,1)} %tiles_hbm.1, ...), custom_call_target="tpu_custom_call" | custom-call | tf_op jit(solution)/shard_map/pallas_call | solution.py:224
  2.0 6.8 %all-to-all-start = ((bf16[16,128,128]{2,1,0:T(8,128)(2,1)}), bf16[16,128,128]{2,1,0:T(8,128)(2,1)S(1)}, u32[]{:S(2)}, u32[]{:S(2)}) async-start(bf16[16,128,128]{2,1,0:T(8,128)(2,1)} %get-tuple-element.43), calls=%async_computation | async-start | bytes 1048576 | tf_op jit(solution)/shard_map/all_to_all | solution.py:250
  8.8 1.4 %collective-permute-start = (bf16[2,96,384]{2,1,0:T(8,128)(2,1)S(1)}, bf16[2,96,384]{2,1,0:T(8,128)(2,1)S(1)}, u32[]{:S(2)}, u32[]{:S(2)}) collective-permute-start(bf16[2,96,384]{2,1,0:T(8,128)(2,1)S(1)} %get-tuple-element.32), channel_id=1, source_target_pairs={{0,1},{1,2},{2,3},{3,0},{4,5},{5,6},{6,7},{7,4},{8,9},{9,10},{10,1... | collective-permute-start | bytes 442376 | tf_op jit(solution)/shard_map/ppermute | solution.py:256
  10.2 2.4 %collective-permute-start.1 = (bf16[2,96,384]{2,1,0:T(8,128)(2,1)S(1)}, bf16[2,96,384]{2,1,0:T(8,128)(2,1)S(1)}, u32[]{:S(2)}, u32[]{:S(2)}) collective-permute-start(bf16[2,96,384]{2,1,0:T(8,128)(2,1)S(1)} %get-tuple-element.33), channel_id=1, source_target_pairs={{0,2},{1,3},{2,0},{3,1},{4,6},{5,7},{6,4},{7,5},{8,10},{9,11},{10,... | collective-permute-start | bytes 442376 | tf_op jit(solution)/shard_map/ppermute | solution.py:256
  12.6 1.2 %collective-permute-start.2 = (bf16[2,96,384]{2,1,0:T(8,128)(2,1)S(1)}, bf16[2,96,384]{2,1,0:T(8,128)(2,1)S(1)}, u32[]{:S(2)}, u32[]{:S(2)}) collective-permute-start(bf16[2,96,384]{2,1,0:T(8,128)(2,1)S(1)} %get-tuple-element.34), channel_id=1, source_target_pairs={{0,3},{1,0},{2,1},{3,2},{4,7},{5,4},{6,5},{7,6},{8,11},{9,8},{10,9... | collective-permute-start | bytes 442376 | tf_op jit(solution)/shard_map/ppermute | solution.py:256
  13.8 5.5 %all-to-all-done.got_ref.refs_4_ = bf16[16,128,128]{2,1,0:T(8,128)(2,1)S(1)} async-done(((bf16[16,128,128]{2,1,0:T(8,128)(2,1)}), bf16[16,128,128]{2,1,0:T(8,128)(2,1)S(1)}, u32[]{:S(2)}, u32[]{:S(2)}) %all-to-all-start) | async-done | bytes 524320 | tf_op jit(solution)/shard_map/all_to_all | solution.py:250
  19.3 0.0 copy-done.1
  19.3 0.6 shard_map.67
  19.9 2.0 %collective-permute-start.10 = (bf16[2,384,128]{2,1,0:T(8,128)(2,1)S(1)}, bf16[2,384,128]{2,1,0:T(8,128)(2,1)S(1)}, u32[]{:S(2)}, u32[]{:S(2)}) collective-permute-start(bf16[2,384,128]{2,1,0:T(8,128)(2,1)S(1)} %get-tuple-element.46), channel_id=1, source_target_pairs={{0,240},{16,0},{32,16},{48,32},{64,48},{80,64},{96,80},{112,96},{1... | collective-permute-start | bytes 589832 | tf_op jit(solution)/shard_map/ppermute | solution.py:247
  21.9 2.8 %collective-permute-start.9 = (bf16[2,384,128]{2,1,0:T(8,128)(2,1)S(1)}, bf16[2,384,128]{2,1,0:T(8,128)(2,1)S(1)}, u32[]{:S(2)}, u32[]{:S(2)}) collective-permute-start(bf16[2,384,128]{2,1,0:T(8,128)(2,1)S(1)} %get-tuple-element.45), channel_id=1, source_target_pairs={{0,16},{16,32},{32,48},{48,64},{64,80},{80,96},{96,112},{112,128},... | collective-permute-start | bytes 589832 | tf_op jit(solution)/shard_map/ppermute | solution.py:246
  24.7 0.0 collective-permute-done.refs_1_
  24.7 0.0 collective-permute-done.1.refs_2_
  24.7 0.0 collective-permute-done.2.refs_3_
  24.7 0.0 copy-start
  24.7 0.0 copy-start.2
  24.7 0.1 shard_map.65
  24.8 0.6 collective-permute-start.3
  25.4 2.7 %collective-permute-start.4 = (bf16[4,48,384]{2,1,0:T(8,128)(2,1)S(1)}, bf16[4,48,384]{2,1,0:T(8,128)(2,1)S(1)}, u32[]{:S(2)}, u32[]{:S(2)}) collective-permute-start(bf16[4,48,384]{2,1,0:T(8,128)(2,1)S(1)} %get-tuple-element.37), channel_id=1, source_target_pairs={{0,8},{1,9},{2,10},{3,11},{4,12},{5,13},{6,14},{7,15},{8,0},{9,1},... | collective-permute-start | bytes 442376 | tf_op jit(solution)/shard_map/ppermute | solution.py:253
  28.1 0.9 collective-permute-start.5
  29.0 1.8 %collective-permute-done.3.refs_1_ = bf16[4,48,384]{2,1,0:T(8,128)(2,1)S(1)} collective-permute-done((bf16[4,48,384]{2,1,0:T(8,128)(2,1)S(1)}, bf16[4,48,384]{2,1,0:T(8,128)(2,1)S(1)}, u32[]{:S(2)}, u32[]{:S(2)}) %collective-permute-start.3) | collective-permute-done | bytes 147488 | tf_op jit(solution)/shard_map/ppermute | solution.py:253
  30.8 3.1 %collective-permute-done.4.refs_2_ = bf16[4,48,384]{2,1,0:T(8,128)(2,1)S(1)} collective-permute-done((bf16[4,48,384]{2,1,0:T(8,128)(2,1)S(1)}, bf16[4,48,384]{2,1,0:T(8,128)(2,1)S(1)}, u32[]{:S(2)}, u32[]{:S(2)}) %collective-permute-start.4) | collective-permute-done | bytes 147488 | tf_op jit(solution)/shard_map/ppermute | solution.py:253
  33.8 0.4 collective-permute-done.5.refs_3_
  34.2 0.6 shard_map.68.refs_5_
  34.8 0.0 collective-permute-done.10.refs_7_
  34.8 0.0 collective-permute-done.9.refs_6_
  34.8 0.0 copy-done
  34.8 1.4 %shard_map.69 = bf16[16,120,128]{2,1,0:T(8,128)(2,1)S(1)} custom-call(s32[1,32]{1,0:T(1,128)S(1)} %copy-done.2, s32[4,8]{1,0:T(4,128)S(1)} %copy-done, bf16[4,48,384]{2,1,0:T(8,128)(2,1)S(1)} %get-tuple-element.35.refs_0_, bf16[4,48,384]{2,1,0:T(8,128)(2,1)S(1)} %collective-permute-done.3.refs_1_, bf16[4,48,384]{2,1,0:T(8,128)(2,1)S(1)} %collective-permute-done.4.refs_2_, ...), custom_call_target="tpu_custom_call" | custom-call | tf_op jit(solution)/shard_map/pallas_call | solution.py:224
  36.2 16.8 %all_to_all.15.got_ref.refs_4_ = bf16[16,120,128]{2,1,0:T(8,128)(2,1)S(1)} all-to-all(bf16[16,120,128]{2,1,0:T(8,128)(2,1)S(1)} %shard_map.69), channel_id=1, replica_groups=mesh['lead'=16,'grp'=16] {'grp'}, dimensions={0} | all-to-all | bytes 983040 | tf_op jit(solution)/shard_map/all_to_all | solution.py:250
  53.0 0.7 shard_map.70
  53.7 4.8 %collective-permute-start.11 = (bf16[2,384,128]{2,1,0:T(8,128)(2,1)S(1)}, bf16[2,384,128]{2,1,0:T(8,128)(2,1)S(1)}, u32[]{:S(2)}, u32[]{:S(2)}) collective-permute-start(bf16[2,384,128]{2,1,0:T(8,128)(2,1)S(1)} %get-tuple-element.48), channel_id=1, source_target_pairs={{0,16},{16,32},{32,48},{48,64},{64,80},{80,96},{96,112},{112,128},... | collective-permute-start | bytes 589832 | tf_op jit(solution)/shard_map/ppermute | solution.py:246
  58.4 0.0 collective-permute-start.12
  58.5 0.7 shard_map.66
  59.1 0.1 collective-permute-start.6
  59.2 2.0 %collective-permute-start.7 = (bf16[8,24,384]{2,1,0:T(8,128)(2,1)S(1)}, bf16[8,24,384]{2,1,0:T(8,128)(2,1)S(1)}, u32[]{:S(2)}, u32[]{:S(2)}) collective-permute-start(bf16[8,24,384]{2,1,0:T(8,128)(2,1)S(1)} %get-tuple-element.41), channel_id=1, source_target_pairs={{0,8},{1,9},{2,10},{3,11},{4,12},{5,13},{6,14},{7,15},{8,0},{9,1},... | collective-permute-start | bytes 442376 | tf_op jit(solution)/shard_map/ppermute | solution.py:253
  61.2 0.8 collective-permute-start.8
  62.1 6.5 %collective-permute-done.6.refs_1_ = bf16[8,24,384]{2,1,0:T(8,128)(2,1)S(1)} collective-permute-done((bf16[8,24,384]{2,1,0:T(8,128)(2,1)S(1)}, bf16[8,24,384]{2,1,0:T(8,128)(2,1)S(1)}, u32[]{:S(2)}, u32[]{:S(2)}) %collective-permute-start.6) | collective-permute-done | bytes 147488 | tf_op jit(solution)/shard_map/ppermute | solution.py:253
  68.6 0.0 collective-permute-done.7.refs_2_
  68.6 0.9 collective-permute-done.8.refs_3_
  69.5 0.0 collective-permute-done.11.refs_6_
  69.5 0.0 collective-permute-done.12.refs_7_
  69.5 1.0 %shard_map.71 = (bf16[16,96,128]{2,1,0:T(8,128)(2,1)S(1)}, f32[96,128]{1,0:T(8,128)S(1)}) custom-call(s32[4,8]{1,0:T(4,128)S(1)} %copy-done, bf16[8,24,384]{2,1,0:T(8,128)(2,1)S(1)} %get-tuple-element.39.refs_0_, bf16[8,24,384]{2,1,0:T(8,128)(2,1)S(1)} %collective-permute-done.6.refs_1_, bf16[8,24,384]{2,1,0:T(8,128)(2,1)S(1)} %collective-permute-done.7.refs_2_, ...), custom_call_target="tpu_custom_call" | custom-call | tf_op jit(solution)/shard_map/pallas_call | solution.py:224
  70.5 13.6 %all_to_all.16.got_ref = bf16[16,96,128]{2,1,0:T(8,128)(2,1)S(1)} all-to-all(bf16[16,96,128]{2,1,0:T(8,128)(2,1)S(1)} %get-tuple-element.52), channel_id=1, replica_groups=mesh['lead'=16,'grp'=16] {'grp'}, dimensions={0} | all-to-all | bytes 786432 | tf_op jit(solution)/shard_map/all_to_all | solution.py:250
  84.2 0.6 shard_map.72
  84.8 1.5 %collective-permute-start.13 = (bf16[2,384,128]{2,1,0:T(8,128)(2,1)S(1)}, bf16[2,384,128]{2,1,0:T(8,128)(2,1)S(1)}, u32[]{:S(2)}, u32[]{:S(2)}) collective-permute-start(bf16[2,384,128]{2,1,0:T(8,128)(2,1)S(1)} %get-tuple-element.54), channel_id=1, source_target_pairs={{0,16},{16,32},{32,48},{48,64},{64,80},{80,96},{96,112},{112,128},... | collective-permute-start | bytes 589832 | tf_op jit(solution)/shard_map/ppermute | solution.py:246
  86.2 0.1 collective-permute-start.14
  86.4 2.5 %collective-permute-done.13.refs_5_ = bf16[2,384,128]{2,1,0:T(8,128)(2,1)S(1)} collective-permute-done((bf16[2,384,128]{2,1,0:T(8,128)(2,1)S(1)}, bf16[2,384,128]{2,1,0:T(8,128)(2,1)S(1)}, u32[]{:S(2)}, u32[]{:S(2)}) %collective-permute-start.13) | collective-permute-done | bytes 196640 | tf_op jit(solution)/shard_map/ppermute | solution.py:246
  88.9 3.7 %collective-permute-done.14.refs_6_ = bf16[2,384,128]{2,1,0:T(8,128)(2,1)S(1)} collective-permute-done((bf16[2,384,128]{2,1,0:T(8,128)(2,1)S(1)}, bf16[2,384,128]{2,1,0:T(8,128)(2,1)S(1)}, u32[]{:S(2)}, u32[]{:S(2)}) %collective-permute-start.14) | collective-permute-done | bytes 196640 | tf_op jit(solution)/shard_map/ppermute | solution.py:247
  92.5 1.6 %shard_map.73 = f32[96,128]{1,0:T(8,128)} custom-call(s32[4,8]{1,0:T(4,128)S(1)} %copy-done, bf16[8,24,384]{2,1,0:T(8,128)(2,1)S(1)} %get-tuple-element.39.refs_0_, bf16[8,24,384]{2,1,0:T(8,128)(2,1)S(1)} %collective-permute-done.6.refs_1_, bf16[8,24,384]{2,1,0:T(8,128)(2,1)S(1)} %collective-permute-done.7.refs_2_, ...), custom_call_target="tpu_custom_call" | custom-call | tf_op jit(solution)/shard_map/pallas_call | solution.py:224
  (2 shorter events, 0.0 us)
Async XLA Ops:
  0.0 19.3 %copy-start.1 = (s32[16,2,2]{0,2,1:T(2,128)S(1)}, s32[16,2,2]{0,2,1:T(2,128)}, u32[]{:S(2)}) copy-start(s32[16,2,2]{0,2,1:T(2,128)} %param.9) | copy-start | bytes 772
  2.0 17.2 %all-to-all-start = ((bf16[16,128,128]{2,1,0:T(8,128)(2,1)}), bf16[16,128,128]{2,1,0:T(8,128)(2,1)S(1)}, u32[]{:S(2)}, u32[]{:S(2)}) async-start(bf16[16,128,128]{2,1,0:T(8,128)(2,1)} %get-tuple-element.43), calls=%async_computation | async-start | bytes 1048576 | tf_op jit(solution)/shard_map/all_to_all | solution.py:250
  8.8 15.9 %collective-permute-start = (bf16[2,96,384]{2,1,0:T(8,128)(2,1)S(1)}, bf16[2,96,384]{2,1,0:T(8,128)(2,1)S(1)}, u32[]{:S(2)}, u32[]{:S(2)}) collective-permute-start(bf16[2,96,384]{2,1,0:T(8,128)(2,1)S(1)} %get-tuple-element.32), channel_id=1, source_target_pairs={{0,1},{1,2},{2,3},{3,0},{4,5},{5,6},{6,7},{7,4},{8,9},{9,10},{10,1... | collective-permute-start | bytes 442376 | tf_op jit(solution)/shard_map/ppermute | solution.py:256
  10.2 14.5 %collective-permute-start.1 = (bf16[2,96,384]{2,1,0:T(8,128)(2,1)S(1)}, bf16[2,96,384]{2,1,0:T(8,128)(2,1)S(1)}, u32[]{:S(2)}, u32[]{:S(2)}) collective-permute-start(bf16[2,96,384]{2,1,0:T(8,128)(2,1)S(1)} %get-tuple-element.33), channel_id=1, source_target_pairs={{0,2},{1,3},{2,0},{3,1},{4,6},{5,7},{6,4},{7,5},{8,10},{9,11},{10,... | collective-permute-start | bytes 442376 | tf_op jit(solution)/shard_map/ppermute | solution.py:256
  12.6 12.1 %collective-permute-start.2 = (bf16[2,96,384]{2,1,0:T(8,128)(2,1)S(1)}, bf16[2,96,384]{2,1,0:T(8,128)(2,1)S(1)}, u32[]{:S(2)}, u32[]{:S(2)}) collective-permute-start(bf16[2,96,384]{2,1,0:T(8,128)(2,1)S(1)} %get-tuple-element.34), channel_id=1, source_target_pairs={{0,3},{1,0},{2,1},{3,2},{4,7},{5,4},{6,5},{7,6},{8,11},{9,8},{10,9... | collective-permute-start | bytes 442376 | tf_op jit(solution)/shard_map/ppermute | solution.py:256
  19.9 14.9 %collective-permute-start.10 = (bf16[2,384,128]{2,1,0:T(8,128)(2,1)S(1)}, bf16[2,384,128]{2,1,0:T(8,128)(2,1)S(1)}, u32[]{:S(2)}, u32[]{:S(2)}) collective-permute-start(bf16[2,384,128]{2,1,0:T(8,128)(2,1)S(1)} %get-tuple-element.46), channel_id=1, source_target_pairs={{0,240},{16,0},{32,16},{48,32},{64,48},{80,64},{96,80},{112,96},{1... | collective-permute-start | bytes 589832 | tf_op jit(solution)/shard_map/ppermute | solution.py:247
  21.9 12.9 %collective-permute-start.9 = (bf16[2,384,128]{2,1,0:T(8,128)(2,1)S(1)}, bf16[2,384,128]{2,1,0:T(8,128)(2,1)S(1)}, u32[]{:S(2)}, u32[]{:S(2)}) collective-permute-start(bf16[2,384,128]{2,1,0:T(8,128)(2,1)S(1)} %get-tuple-element.45), channel_id=1, source_target_pairs={{0,16},{16,32},{32,48},{48,64},{64,80},{80,96},{96,112},{112,128},... | collective-permute-start | bytes 589832 | tf_op jit(solution)/shard_map/ppermute | solution.py:246
  24.7 10.1 %copy-start = (s32[4,8]{1,0:T(4,128)S(1)}, s32[4,8]{1,0:T(4,128)}, u32[]{:S(2)}) copy-start(s32[4,8]{1,0:T(4,128)} %cols_ref.5) | copy-start | bytes 388
  24.7 10.1 %copy-start.2 = (s32[1,32]{1,0:T(1,128)S(1)}, s32[1,32]{1,0:T(1,128)}, u32[]{:S(2)}) copy-start(s32[1,32]{1,0:T(1,128)} %slot_ref.3) | copy-start | bytes 388
  24.8 5.9 %collective-permute-start.3 = (bf16[4,48,384]{2,1,0:T(8,128)(2,1)S(1)}, bf16[4,48,384]{2,1,0:T(8,128)(2,1)S(1)}, u32[]{:S(2)}, u32[]{:S(2)}) collective-permute-start(bf16[4,48,384]{2,1,0:T(8,128)(2,1)S(1)} %get-tuple-element.36), channel_id=1, source_target_pairs={{0,4},{1,5},{2,6},{3,7},{4,8},{5,9},{6,10},{7,11},{8,12},{9,13},{1... | collective-permute-start | bytes 442376 | tf_op jit(solution)/shard_map/ppermute | solution.py:253
  25.4 8.4 %collective-permute-start.4 = (bf16[4,48,384]{2,1,0:T(8,128)(2,1)S(1)}, bf16[4,48,384]{2,1,0:T(8,128)(2,1)S(1)}, u32[]{:S(2)}, u32[]{:S(2)}) collective-permute-start(bf16[4,48,384]{2,1,0:T(8,128)(2,1)S(1)} %get-tuple-element.37), channel_id=1, source_target_pairs={{0,8},{1,9},{2,10},{3,11},{4,12},{5,13},{6,14},{7,15},{8,0},{9,1},... | collective-permute-start | bytes 442376 | tf_op jit(solution)/shard_map/ppermute | solution.py:253
  28.1 6.1 %collective-permute-start.5 = (bf16[4,48,384]{2,1,0:T(8,128)(2,1)S(1)}, bf16[4,48,384]{2,1,0:T(8,128)(2,1)S(1)}, u32[]{:S(2)}, u32[]{:S(2)}) collective-permute-start(bf16[4,48,384]{2,1,0:T(8,128)(2,1)S(1)} %get-tuple-element.38), channel_id=1, source_target_pairs={{0,12},{1,13},{2,14},{3,15},{4,0},{5,1},{6,2},{7,3},{8,4},{9,5},{1... | collective-permute-start | bytes 442376 | tf_op jit(solution)/shard_map/ppermute | solution.py:253
  53.7 15.8 %collective-permute-start.11 = (bf16[2,384,128]{2,1,0:T(8,128)(2,1)S(1)}, bf16[2,384,128]{2,1,0:T(8,128)(2,1)S(1)}, u32[]{:S(2)}, u32[]{:S(2)}) collective-permute-start(bf16[2,384,128]{2,1,0:T(8,128)(2,1)S(1)} %get-tuple-element.48), channel_id=1, source_target_pairs={{0,16},{16,32},{32,48},{48,64},{64,80},{80,96},{96,112},{112,128},... | collective-permute-start | bytes 589832 | tf_op jit(solution)/shard_map/ppermute | solution.py:246
  58.4 11.1 %collective-permute-start.12 = (bf16[2,384,128]{2,1,0:T(8,128)(2,1)S(1)}, bf16[2,384,128]{2,1,0:T(8,128)(2,1)S(1)}, u32[]{:S(2)}, u32[]{:S(2)}) collective-permute-start(bf16[2,384,128]{2,1,0:T(8,128)(2,1)S(1)} %get-tuple-element.49), channel_id=1, source_target_pairs={{0,240},{16,0},{32,16},{48,32},{64,48},{80,64},{96,80},{112,96},{1... | collective-permute-start | bytes 589832 | tf_op jit(solution)/shard_map/ppermute | solution.py:247
  59.1 9.5 %collective-permute-start.6 = (bf16[8,24,384]{2,1,0:T(8,128)(2,1)S(1)}, bf16[8,24,384]{2,1,0:T(8,128)(2,1)S(1)}, u32[]{:S(2)}, u32[]{:S(2)}) collective-permute-start(bf16[8,24,384]{2,1,0:T(8,128)(2,1)S(1)} %get-tuple-element.40), channel_id=1, source_target_pairs={{0,4},{1,5},{2,6},{3,7},{4,8},{5,9},{6,10},{7,11},{8,12},{9,13},{1... | collective-permute-start | bytes 442376 | tf_op jit(solution)/shard_map/ppermute | solution.py:253
  59.2 9.4 %collective-permute-start.7 = (bf16[8,24,384]{2,1,0:T(8,128)(2,1)S(1)}, bf16[8,24,384]{2,1,0:T(8,128)(2,1)S(1)}, u32[]{:S(2)}, u32[]{:S(2)}) collective-permute-start(bf16[8,24,384]{2,1,0:T(8,128)(2,1)S(1)} %get-tuple-element.41), channel_id=1, source_target_pairs={{0,8},{1,9},{2,10},{3,11},{4,12},{5,13},{6,14},{7,15},{8,0},{9,1},... | collective-permute-start | bytes 442376 | tf_op jit(solution)/shard_map/ppermute | solution.py:253
  61.2 8.3 %collective-permute-start.8 = (bf16[8,24,384]{2,1,0:T(8,128)(2,1)S(1)}, bf16[8,24,384]{2,1,0:T(8,128)(2,1)S(1)}, u32[]{:S(2)}, u32[]{:S(2)}) collective-permute-start(bf16[8,24,384]{2,1,0:T(8,128)(2,1)S(1)} %get-tuple-element.42), channel_id=1, source_target_pairs={{0,12},{1,13},{2,14},{3,15},{4,0},{5,1},{6,2},{7,3},{8,4},{9,5},{1... | collective-permute-start | bytes 442376 | tf_op jit(solution)/shard_map/ppermute | solution.py:253
  84.8 4.1 %collective-permute-start.13 = (bf16[2,384,128]{2,1,0:T(8,128)(2,1)S(1)}, bf16[2,384,128]{2,1,0:T(8,128)(2,1)S(1)}, u32[]{:S(2)}, u32[]{:S(2)}) collective-permute-start(bf16[2,384,128]{2,1,0:T(8,128)(2,1)S(1)} %get-tuple-element.54), channel_id=1, source_target_pairs={{0,16},{16,32},{32,48},{48,64},{64,80},{80,96},{96,112},{112,128},... | collective-permute-start | bytes 589832 | tf_op jit(solution)/shard_map/ppermute | solution.py:246
  86.2 6.3 %collective-permute-start.14 = (bf16[2,384,128]{2,1,0:T(8,128)(2,1)S(1)}, bf16[2,384,128]{2,1,0:T(8,128)(2,1)S(1)}, u32[]{:S(2)}, u32[]{:S(2)}) collective-permute-start(bf16[2,384,128]{2,1,0:T(8,128)(2,1)S(1)} %get-tuple-element.55), channel_id=1, source_target_pairs={{0,240},{16,0},{32,16},{48,32},{64,48},{80,64},{96,80},{112,96},{1... | collective-permute-start | bytes 589832 | tf_op jit(solution)/shard_map/ppermute | solution.py:247

commit v7 on v6

v7 whole, which is shorter than its diff:
```python
import jax
import jax.numpy as jnp
from jax import lax
from jax.experimental import pallas as pl
from jax.experimental.pallas import tpu as pltpu
from jax.sharding import PartitionSpec as P


TILE = 384
NRHS = 128
SIDE = 4
GROUP = 16
SHARE = 96
SLAB = 24
TILES = 32
PIECE = 216
F32 = jnp.float32
BF16 = jnp.bfloat16
GRANT = 20 << 20
GAIN = 8.0 / 7.0

VMEM = pl.BlockSpec(memory_space=pltpu.VMEM)
SMEM = pl.BlockSpec(memory_space=pltpu.SMEM)


def place():
    member = lax.axis_index("grp")
    return lax.shift_right_logical(member, 2), lax.bitwise_and(member, 3)


def wrap(index):
    return lax.bitwise_and(index, 3)


def column_of(row, first, count):
    line = lax.broadcasted_iota(jnp.int32, (count, 128), 0) + first
    lane = lax.broadcasted_iota(jnp.int32, (count, 128), 1)
    return jnp.sum(jnp.where(line == lane, jnp.broadcast_to(row, (count, 128)), 0.0), axis=1, keepdims=True)


def padded(diag_ref):
    return jnp.concatenate([diag_ref[...], jnp.zeros((1, 128 - SHARE), F32)], axis=1)


def start_kernel(tiles_hbm, residual_hbm, diag_hbm, part0, part1, part2, part3, wide_ref, start_ref, scale_ref,
                 line_ref, residual_ref, diag_ref, sems):
    _, q = place()
    copies = [pltpu.make_async_copy(residual_hbm, residual_ref, sems.at[0]),
              pltpu.make_async_copy(diag_hbm, diag_ref, sems.at[1])]
    for k, part in enumerate((part0, part1, part2, part3)):
        at = pl.multiple_of(wrap(q + k) * SHARE, SHARE)
        copies.append(pltpu.make_async_copy(tiles_hbm.at[:, pl.ds(at, SHARE)], part, sems.at[2 + k]))
    for copy in copies:
        copy.start()
    for copy in copies[:2]:
        copy.wait()
    row = padded(diag_ref)
    d_high = row.astype(BF16).astype(F32)
    d_mid = (row - d_high).astype(BF16).astype(F32)
    line_ref[...] = jnp.broadcast_to(jnp.concatenate([d_high, d_mid, row - d_high - d_mid], axis=1), (8, TILE))
    scale = jnp.broadcast_to(column_of(row, 0, SHARE), (SHARE, NRHS))
    scaled = residual_ref[...] * scale
    scale_ref[...] = scale
    start_ref[...] = scaled
    spread(scaled, wide_ref)
    for copy in copies[2:]:
        copy.wait()


def spread(value, wide_ref):
    value = value.astype(BF16)
    for m in range(GROUP):
        wide_ref[m] = value


def thirds(rows):
    return jnp.concatenate([rows[8 * k:8 * k + 8] for k in range(3)], axis=1)


def unthirds(rows):
    return jnp.concatenate([rows[:, NRHS * k:NRHS * (k + 1)] for k in range(3)], axis=0)


def split_kernel(*refs):
    parts, (start_ref, line_ref), outs, held_ref = refs[:4], refs[4:6], refs[6:10], refs[10]
    x, q = place()
    high = start_ref[...].astype(BF16).astype(F32)
    low = start_ref[...] - high
    for s in range(SIDE):
        at = slice(SLAB * s, SLAB * (s + 1))
        tail = jnp.concatenate([thirds(high[at]), thirds(low[at]), line_ref[...]], axis=0)
        held_ref[wrap(s - x), 192:PIECE] = tail.astype(BF16)
    for k in range(SIDE):
        tiles = [parts[k][j].astype(F32) for j in range(2)]
        to = pl.multiple_of(48 * wrap(q - k), 48)
        for s in range(SIDE):
            pair = jnp.concatenate([tile[SLAB * s:SLAB * (s + 1)] for tile in tiles], axis=0)
            held_ref[wrap(s - x), pl.ds(to, 48)] = pair.astype(BF16)
    for k in range(SIDE):
        outs[k][...] = held_ref[k]


def send_halves(rows_ref, own_ref, up_ref, down_ref):
    lead = lax.axis_index("lead")
    for side, ref in ((0, up_ref), (1, down_ref)):
        for h in range(2):
            ref[h] = own_ref[rows_ref[side, h, lead]]


def pick_slab_kernel(rows_ref, got_ref, own_ref, up_ref, down_ref):
    for q in range(SIDE):
        parts = [got_ref[SIDE * x + q].astype(F32) for x in range(SIDE)]
        for r in range(SIDE):
            block = jnp.concatenate([p[SLAB * r:SLAB * (r + 1)] for p in parts], axis=0)
            own_ref[r, SHARE * q:SHARE * (q + 1)] = block.astype(BF16)
    send_halves(rows_ref, own_ref, up_ref, down_ref)


def pick_home_kernel(rows_ref, got_ref, own_ref, up_ref, down_ref):
    for r in range(SIDE):
        for q in range(SIDE):
            own_ref[r, SHARE * q:SHARE * (q + 1)] = got_ref[SIDE * r + q]
    send_halves(rows_ref, own_ref, up_ref, down_ref)


def slot_of(slot_ref, x, k, i):
    return slot_ref[0, 8 * wrap(x - k) + i]


def order_kernel(slot_ref, *refs):
    parts, outs, held_ref = refs[:4], refs[4:8], refs[8]
    x, _ = place()
    for k in range(SIDE):
        for y in range(SIDE):
            pair = parts[k][48 * y:48 * (y + 1)].astype(F32)
            for j in range(2):
                to = lax.bitwise_and(slot_of(slot_ref, x, k, 2 * y + j) - 8 * x, TILES - 1)
                held_ref[to] = pair[SLAB * j:SLAB * (j + 1)].astype(BF16)
    for k in range(SIDE):
        outs[k][...] = held_ref[8 * k:8 * k + 8]


def slab_products(slabs, blocks, product_ref, first):
    for pair in range(len(blocks) // 2):
        wide = jnp.concatenate(blocks[2 * pair:2 * pair + 2], axis=1)
        product = jnp.dot(slabs, wide, preferred_element_type=F32)
        product_ref[first + 2 * pair] = product[:, :NRHS]
        product_ref[first + 2 * pair + 1] = product[:, NRHS:]


def all_slabs(parts):
    return jnp.concatenate([part[0:192] for part in parts], axis=0)


def near_kernel(*refs):
    own_ref, product_ref = refs[4:]
    slab_products(all_slabs(refs[:4]), [own_ref[r] for r in range(SIDE)], product_ref, 0)


def slab_total(slot_ref, cols_ref, parts, near_ref, low_ref, high_ref, product_ref, total_ref):
    x, _ = place()
    slab_products(all_slabs(parts), [low_ref[0], low_ref[1], high_ref[0], high_ref[1]], product_ref, 4)
    product_ref[0:4] = near_ref[...]
    total_ref[...] = jnp.zeros_like(total_ref)
    for t in range(TILES):
        slot = slot_of(slot_ref, x, t // 8, t % 8)
        row = lax.shift_right_logical(slot, 3)
        col = cols_ref[row, lax.bitwise_and(slot, 7)]
        total_ref[row] += product_ref[col, SLAB * t:SLAB * (t + 1)]


def first_kernel(slot_ref, cols_ref, *refs):
    parts, halo, (wide_ref, first_ref, start_ref, scale_ref), work = refs[:4], refs[4:7], refs[7:11], refs[11:]
    slab_total(slot_ref, cols_ref, parts, *halo, *work)
    total_ref = work[1]
    x, _ = place()
    for k in range(SIDE):
        tail = parts[k][192:PIECE].astype(F32)
        row = tail[16:17, 0:128] + (tail[16:17, 128:256] + tail[16:17, 256:384])
        start = unthirds(tail[0:8]) + unthirds(tail[8:16])
        scale = jnp.broadcast_to(column_of(row, x * SLAB, SLAB), (SLAB, NRHS))
        r = wrap(x - k)
        start_ref[r] = start
        scale_ref[r] = scale
        first_ref[r] = GAIN * (start - scale * total_ref[r])
    spread(jnp.concatenate([first_ref[r] for r in range(SIDE)], axis=0), wide_ref)


def second_kernel(slot_ref, cols_ref, *refs):
    parts, halo, (first_ref, start_ref, scale_ref) = refs[:4], refs[4:7], refs[7:10]
    wide_ref, outs, work = refs[10], refs[11:15], refs[15:]
    slab_total(slot_ref, cols_ref, parts, *halo, *work)
    x, _ = place()
    seconds = []
    total_ref = work[1]
    for r in range(SIDE):
        second = start_ref[r] - first_ref[r] - scale_ref[r] * total_ref[r]
        seconds.append(second)
        total_ref[r] = first_ref[r] + GAIN * second
    spread(jnp.concatenate(seconds, axis=0), wide_ref)
    for k in range(SIDE):
        outs[k][...] = total_ref[wrap(x + k)]


def last_kernel(cols_ref, *refs):
    parts, sums, (own_ref, low_ref, high_ref, scale_ref, out_ref, ext_ref) = refs[:4], refs[4:8], refs[8:]
    x, _ = place()
    ext_ref[0:4] = own_ref[...]
    ext_ref[4:6] = low_ref[...]
    ext_ref[6:8] = high_ref[...]
    total = jnp.zeros((SHARE, NRHS), F32)
    for k in range(8):
        left = jnp.concatenate([part[k] for part in parts], axis=0)
        total += jnp.dot(left, ext_ref[cols_ref[x, k]], preferred_element_type=F32)
    for k in range(SIDE):
        at = pl.ds(pl.multiple_of(wrap(x - k) * SLAB, 8), SLAB)
        out_ref[at, :] = sums[k][...] - GAIN * (scale_ref[at, :] * total[SLAB * k:SLAB * (k + 1)])


def arr(shape, dtype):
    return pltpu.VMEM(shape, dtype)


def call(kernel, args, outs, scalars=0, scratch=(), far=0):
    vectors = args[scalars:]
    space = pltpu.HBM if far else pltpu.VMEM
    vectors = [pltpu.with_memory_space_constraint(a, space) for a in vectors]
    specs = [SMEM] * scalars + [pl.BlockSpec(memory_space=space)] * len(vectors)
    return pl.pallas_call(kernel, in_specs=specs, out_specs=[VMEM] * len(outs),
                          out_shape=outs, scratch_shapes=list(scratch),
                          compiler_params=pltpu.CompilerParams(vmem_limit_bytes=GRANT))(*args[:scalars], *vectors)


def near(*arrays):
    return list(arrays)


HALVES = [arr((2, TILE, NRHS), BF16), arr((2, TILE, NRHS), BF16)]
OWN = arr((SIDE, TILE, NRHS), BF16)
ROWS = arr((SHARE, NRHS), F32)
EXT = arr((8, TILE, NRHS), BF16)
SLABS = arr((SIDE, SLAB, NRHS), F32)
WIDE = arr((GROUP, SHARE, NRHS), BF16)
NEAR = arr((4, TILES * SLAB, NRHS), F32)
WORK = (arr((8, TILES * SLAB, NRHS), F32), SLABS)


def body(matrix_tiles, tile_slot, tile_cols, send_rows, residual, diag_inv):
    leads = lax.axis_size("lead")
    rows = send_rows.transpose(1, 2, 0)
    diag = diag_inv.reshape(1, SHARE)

    def halo(up, down):
        lower = lax.ppermute(up, "lead", [(i, (i + 1) % leads) for i in range(leads)])
        upper = lax.ppermute(down, "lead", [(i, (i - 1) % leads) for i in range(leads)])
        return lower, upper

    def gather(wide):
        return lax.all_to_all(wide, "grp", 0, 0)

    def choose(kernel, got):
        return call(kernel, [rows] + near(got), [OWN] + HALVES, 1)

    def along_x(values):
        pairs = [[(m, (m + SIDE * k) % GROUP) for m in range(GROUP)] for k in range(SIDE)]
        return exchange(values, pairs)

    def along_y(values):
        pairs = [[(m, m - m % SIDE + (m + k) % SIDE) for m in range(GROUP)] for k in range(SIDE)]
        return exchange(values, pairs)

    def exchange(values, pairs):
        out = [values[0]]
        for k in range(1, SIDE):
            out.append(lax.ppermute(values[k], "grp", pairs[k]))
        return out

    *quarters, wide, start, scale, line = call(
        start_kernel, [matrix_tiles, residual, diag],
        [arr((2, SHARE, TILE), BF16)] * 4 + [WIDE, ROWS, ROWS, arr((8, TILE), F32)],
        scratch=(ROWS, arr((1, SHARE), F32), pltpu.SemaphoreType.DMA((6,))), far=1)
    quarters = along_y(quarters)
    got = gather(wide)
    slabs = call(split_kernel, near(*quarters, start, line), [arr((PIECE, TILE), BF16)] * 4, 0,
                 (arr((SIDE, PIECE, TILE), BF16),))
    slabs = along_x(slabs)
    own, up, down = choose(pick_home_kernel, got)
    halos = halo(up, down)
    ordered = call(order_kernel, [tile_slot] + near(*slabs), [arr((8, SLAB, TILE), BF16)] * 4, 1,
                   (arr((TILES, SLAB, TILE), BF16),))
    product, = call(near_kernel, near(*slabs, own), [NEAR])
    wide, *state = call(first_kernel, [tile_slot, tile_cols] + near(*slabs, product, *halos),
                        [WIDE] + [SLABS] * 3, 2, WORK)
    own, up, down = choose(pick_slab_kernel, gather(wide))
    halos = halo(up, down)
    parts = along_x(ordered)
    product, = call(near_kernel, near(*slabs, own), [NEAR])
    wide, *sums = call(second_kernel, [tile_slot, tile_cols] + near(*slabs, product, *halos, *state),
                       [WIDE] + [arr((SLAB, NRHS), F32)] * 4, 2, WORK)
    own, up, down = choose(pick_slab_kernel, gather(wide))
    halos = halo(up, down)
    sums = along_x(sums)
    result, = call(last_kernel, [tile_cols] + near(*parts, *sums, own, *halos, scale),
                   [jax.ShapeDtypeStruct((SHARE, NRHS), F32)], 1, (EXT,))
    return result


def solution(mesh):
    in_specs = (
        P(("lead", "grp"), None, None),
        P("lead", None),
        P("lead", None),
        P(),
        P(("lead", "grp"), None),
        P(("lead", "grp")),
    )
    out_specs = P(("lead", "grp"), None)
    return jax.shard_map(body, mesh=mesh, in_specs=in_specs, out_specs=out_specs, check_vma=False)
```

time: 94.8 us -> 96 us (1.013)
  the two profiles are of different devices: /device:TPU:97 before, /device:TPU:2 now
where the time goes in v7:
time: 96 us; the launch traced here: 95.7 us
  starting transfers between devices  39 us (41%)
  blocking collectives  27.9 us (29%)
  waiting for transfers between devices  17.8 us (19%)
  Pallas kernels  10.3 us (11%)
    all_to_all x2, blocking collectives, gather(): return lax.all_to_all(wide, 'grp', 0, 0)  27.9 us
    ppermute x12, starting transfers between devices, exchange(): out.append(lax.ppermute(values[k], 'grp', pairs[k]))  20.7 us
    ppermute x12, waiting for transfers between devices, exchange(): out.append(lax.ppermute(values[k], 'grp', pairs[k]))  12.6 us
    ppermute x3, starting transfers between devices, halo(): lax.ppermute(down, 'lead', [(i, (i - 1) % leads) for i in range(leads)])  10.7 us
    pallas_call x11, Pallas kernels, call(): pl.pallas_call(kernel, in_specs=specs, out_specs=[VMEM] * len(outs), out_...  10.3 us
    all_to_all x1, starting transfers between devices, gather(): return lax.all_to_all(wide, 'grp', 0, 0)  7.49 us
    ppermute x3, waiting for transfers between devices, halo(): lax.ppermute(up, 'lead', [(i, (i + 1) % leads) for i in range(leads)])  2.76 us
    all_to_all x1, waiting for transfers between devices, gather(): return lax.all_to_all(wide, 'grp', 0, 0)  2.38 us
  transfers between devices with their start and end apart: 19, of which 10 were waited for; matrix products, arithmetic and copies ran while one was open for 0% of the time, Pallas kernels for 3%

profile of v7, /device:TPU:2, one launch (start us, length us, event | category | flops | bytes accessed | tf_op | source)
XLA Modules:
  0.0 95.7 jit_solution(2095893847131759966)
XLA Ops:
  0.0 2.0 %shard_map.64 = (bf16[2,96,384]{2,1,0:T(8,128)(2,1)S(1)}, bf16[2,96,384]{2,1,0:T(8,128)(2,1)S(1)}, bf16[2,96,384]{2,1,0:T(8,128)(2,1)S(1)}, bf16[2,96,384]{2,1,0...) custom-call(bf16[2,384,384]{2,1,0:T(8,128)(2,1)} %tiles_hbm.1, ...), custom_call_target="tpu_custom_call" | custom-call | tf_op jit(solution)/shard_map/pallas_call | solution.py:229
  2.0 7.5 %all-to-all-start = ((bf16[16,96,128]{2,1,0:T(8,128)(2,1)}), bf16[16,96,128]{2,1,0:T(8,128)(2,1)S(1)}, u32[]{:S(2)}, u32[]{:S(2)}) async-start(bf16[16,96,128]{2,1,0:T(8,128)(2,1)} %get-tuple-element.53), calls=%async_computation | async-start | bytes 786432 | tf_op jit(solution)/shard_map/all_to_all | solution.py:259
  9.5 1.5 %collective-permute-start = (bf16[2,96,384]{2,1,0:T(8,128)(2,1)S(1)}, bf16[2,96,384]{2,1,0:T(8,128)(2,1)S(1)}, u32[]{:S(2)}, u32[]{:S(2)}) collective-permute-start(bf16[2,96,384]{2,1,0:T(8,128)(2,1)S(1)} %get-tuple-element.40), channel_id=1, source_target_pairs={{0,1},{1,2},{2,3},{3,0},{4,5},{5,6},{6,7},{7,4},{8,9},{9,10},{10,1... | collective-permute-start | bytes 442376 | tf_op jit(solution)/shard_map/ppermute | solution.py:275
  10.9 2.7 %collective-permute-start.1 = (bf16[2,96,384]{2,1,0:T(8,128)(2,1)S(1)}, bf16[2,96,384]{2,1,0:T(8,128)(2,1)S(1)}, u32[]{:S(2)}, u32[]{:S(2)}) collective-permute-start(bf16[2,96,384]{2,1,0:T(8,128)(2,1)S(1)} %get-tuple-element.41), channel_id=1, source_target_pairs={{0,2},{1,3},{2,0},{3,1},{4,6},{5,7},{6,4},{7,5},{8,10},{9,11},{10,... | collective-permute-start | bytes 442376 | tf_op jit(solution)/shard_map/ppermute | solution.py:275
  13.6 1.5 %collective-permute-start.2 = (bf16[2,96,384]{2,1,0:T(8,128)(2,1)S(1)}, bf16[2,96,384]{2,1,0:T(8,128)(2,1)S(1)}, u32[]{:S(2)}, u32[]{:S(2)}) collective-permute-start(bf16[2,96,384]{2,1,0:T(8,128)(2,1)S(1)} %get-tuple-element.42), channel_id=1, source_target_pairs={{0,3},{1,0},{2,1},{3,2},{4,7},{5,4},{6,5},{7,6},{8,11},{9,8},{10,9... | collective-permute-start | bytes 442376 | tf_op jit(solution)/shard_map/ppermute | solution.py:275
  15.1 2.4 %all-to-all-done.got_ref = bf16[16,96,128]{2,1,0:T(8,128)(2,1)S(1)} async-done(((bf16[16,96,128]{2,1,0:T(8,128)(2,1)}), bf16[16,96,128]{2,1,0:T(8,128)(2,1)S(1)}, u32[]{:S(2)}, u32[]{:S(2)}) %all-to-all-start) | async-done | bytes 393248 | tf_op jit(solution)/shard_map/all_to_all | solution.py:259
  17.5 0.7 copy-done
  18.1 0.6 shard_map.67
  18.8 3.7 %collective-permute-start.10 = (bf16[2,384,128]{2,1,0:T(8,128)(2,1)S(1)}, bf16[2,384,128]{2,1,0:T(8,128)(2,1)S(1)}, u32[]{:S(2)}, u32[]{:S(2)}) collective-permute-start(bf16[2,384,128]{2,1,0:T(8,128)(2,1)S(1)} %get-tuple-element.56), channel_id=1, source_target_pairs={{0,240},{16,0},{32,16},{48,32},{64,48},{80,64},{96,80},{112,96},{1... | collective-permute-start | bytes 589832 | tf_op jit(solution)/shard_map/ppermute | solution.py:255
  22.5 0.0 collective-permute-done.refs_1_
  22.5 0.9 collective-permute-done.1.refs_2_
  23.5 0.0 collective-permute-done.2.refs_3_
  23.5 0.1 shard_map.65
  23.6 1.4 %collective-permute-start.3 = (bf16[216,384]{1,0:T(8,128)(2,1)S(1)}, bf16[216,384]{1,0:T(8,128)(2,1)S(1)}, u32[]{:S(2)}, u32[]{:S(2)}) collective-permute-start(bf16[216,384]{1,0:T(8,128)(2,1)S(1)} %get-tuple-element.46), channel_id=1, source_target_pairs={{0,4},{1,5},{2,6},{3,7},{4,8},{5,9},{6,10},{7,11},{8,12},{9,13},{1... | collective-permute-start | bytes 497672 | tf_op jit(solution)/shard_map/ppermute | solution.py:275
  25.0 1.5 %collective-permute-start.4 = (bf16[216,384]{1,0:T(8,128)(2,1)S(1)}, bf16[216,384]{1,0:T(8,128)(2,1)S(1)}, u32[]{:S(2)}, u32[]{:S(2)}) collective-permute-start(bf16[216,384]{1,0:T(8,128)(2,1)S(1)} %get-tuple-element.47), channel_id=1, source_target_pairs={{0,8},{1,9},{2,10},{3,11},{4,12},{5,13},{6,14},{7,15},{8,0},{9,1},... | collective-permute-start | bytes 497672 | tf_op jit(solution)/shard_map/ppermute | solution.py:275
  26.5 1.7 %collective-permute-start.5 = (bf16[216,384]{1,0:T(8,128)(2,1)S(1)}, bf16[216,384]{1,0:T(8,128)(2,1)S(1)}, u32[]{:S(2)}, u32[]{:S(2)}) collective-permute-start(bf16[216,384]{1,0:T(8,128)(2,1)S(1)} %get-tuple-element.48), channel_id=1, source_target_pairs={{0,12},{1,13},{2,14},{3,15},{4,0},{5,1},{6,2},{7,3},{8,4},{9,5},{1... | collective-permute-start | bytes 497672 | tf_op jit(solution)/shard_map/ppermute | solution.py:275
  28.2 2.0 %collective-permute-done.3.refs_1_ = bf16[216,384]{1,0:T(8,128)(2,1)S(1)} collective-permute-done((bf16[216,384]{1,0:T(8,128)(2,1)S(1)}, bf16[216,384]{1,0:T(8,128)(2,1)S(1)}, u32[]{:S(2)}, u32[]{:S(2)}) %collective-permute-start.3) | collective-permute-done | bytes 165920 | tf_op jit(solution)/shard_map/ppermute | solution.py:275
  30.2 3.3 %collective-permute-done.4.refs_2_ = bf16[216,384]{1,0:T(8,128)(2,1)S(1)} collective-permute-done((bf16[216,384]{1,0:T(8,128)(2,1)S(1)}, bf16[216,384]{1,0:T(8,128)(2,1)S(1)}, u32[]{:S(2)}, u32[]{:S(2)}) %collective-permute-start.4) | collective-permute-done | bytes 165920 | tf_op jit(solution)/shard_map/ppermute | solution.py:275
  33.5 1.1 %collective-permute-done.5.refs_3_ = bf16[216,384]{1,0:T(8,128)(2,1)S(1)} collective-permute-done((bf16[216,384]{1,0:T(8,128)(2,1)S(1)}, bf16[216,384]{1,0:T(8,128)(2,1)S(1)}, u32[]{:S(2)}, u32[]{:S(2)}) %collective-permute-start.5) | collective-permute-done | bytes 165920 | tf_op jit(solution)/shard_map/ppermute | solution.py:275
  34.6 0.6 shard_map.68.refs_4_
  35.2 0.0 collective-permute-done.9.refs_5_
  35.2 1.4 %shard_map.69 = (bf16[16,96,128]{2,1,0:T(8,128)(2,1)S(1)}, f32[4,24,128]{2,1,0:T(8,128)S(1)}, f32[4,24,128]{2,1,0:T(8,128)S(1)}, f32[4,24,128]{2,1,0:T(8,128)S(1)}) custom-call(s32[1,32]{1,0:T(1,128)S(1)} %copy-done.2, s32[4,8]{1,0:T(4,128)S(1)} %copy-done.1, bf16[216,384]{1,0:T(8,128)(2,1)S(1)} %get-tuple-element.45.refs_0_, ...), custom_call_target="tpu_custom_call" | custom-call | tf_op jit(solution)/shard_map/pallas_call | solution.py:229
  36.6 14.3 %all_to_all.15.got_ref = bf16[16,96,128]{2,1,0:T(8,128)(2,1)S(1)} all-to-all(bf16[16,96,128]{2,1,0:T(8,128)(2,1)S(1)} %get-tuple-element.57), channel_id=1, replica_groups=mesh['lead'=16,'grp'=16] {'grp'}, dimensions={0} | all-to-all | bytes 786432 | tf_op jit(solution)/shard_map/all_to_all | solution.py:259
  50.9 0.7 shard_map.70
  51.6 0.0 collective-permute-start.11
  51.6 4.0 %collective-permute-start.12 = (bf16[2,384,128]{2,1,0:T(8,128)(2,1)S(1)}, bf16[2,384,128]{2,1,0:T(8,128)(2,1)S(1)}, u32[]{:S(2)}, u32[]{:S(2)}) collective-permute-start(bf16[2,384,128]{2,1,0:T(8,128)(2,1)S(1)} %get-tuple-element.60), channel_id=1, source_target_pairs={{0,240},{16,0},{32,16},{48,32},{64,48},{80,64},{96,80},{112,96},{1... | collective-permute-start | bytes 589832 | tf_op jit(solution)/shard_map/ppermute | solution.py:255
  55.7 0.6 shard_map.71.refs_4_
  56.2 2.8 %collective-permute-done.11.refs_5_ = bf16[2,384,128]{2,1,0:T(8,128)(2,1)S(1)} collective-permute-done((bf16[2,384,128]{2,1,0:T(8,128)(2,1)S(1)}, bf16[2,384,128]{2,1,0:T(8,128)(2,1)S(1)}, u32[]{:S(2)}, u32[]{:S(2)}) %collective-permute-start.11) | collective-permute-done | bytes 196640 | tf_op jit(solution)/shard_map/ppermute | solution.py:254
  59.0 0.0 collective-permute-done.12.refs_6_
  59.0 1.4 %shard_map.72 = (bf16[16,96,128]{2,1,0:T(8,128)(2,1)S(1)}, f32[24,128]{1,0:T(8,128)S(1)}, f32[24,128]{1,0:T(8,128)S(1)}, f32[24,128]{1,0:T(8,128)S(1)}, f32[24,128]{1,0:T(8,128)S(1)}) custom-call(s32[1,32]{1,0:T(1,128)S(1)} %copy-done.2, s32[4,8]{1,0:T(4,128)S(1)} %copy-done.1, bf16[216,384]{1,0:T(8,128)(2,1)S(1)} %get-tuple-element.45.refs_0_, ...), custom_call_target="tpu_custom_call" | custom-call | tf_op jit(solution)/shard_map/pallas_call | solution.py:229
  60.4 13.6 %all_to_all.16.got_ref = bf16[16,96,128]{2,1,0:T(8,128)(2,1)S(1)} all-to-all(bf16[16,96,128]{2,1,0:T(8,128)(2,1)S(1)} %get-tuple-element.68), channel_id=1, replica_groups=mesh['lead'=16,'grp'=16] {'grp'}, dimensions={0} | all-to-all | bytes 786432 | tf_op jit(solution)/shard_map/all_to_all | solution.py:259
  74.0 0.7 shard_map.73
  74.7 0.0 collective-permute-start.16
  74.7 2.9 %collective-permute-start.17 = (bf16[2,384,128]{2,1,0:T(8,128)(2,1)S(1)}, bf16[2,384,128]{2,1,0:T(8,128)(2,1)S(1)}, u32[]{:S(2)}, u32[]{:S(2)}) collective-permute-start(bf16[2,384,128]{2,1,0:T(8,128)(2,1)S(1)} %get-tuple-element.71), channel_id=1, source_target_pairs={{0,240},{16,0},{32,16},{48,32},{64,48},{80,64},{96,80},{112,96},{1... | collective-permute-start | bytes 589832 | tf_op jit(solution)/shard_map/ppermute | solution.py:255
  77.7 0.7 shard_map.66
  78.3 1.3 %collective-permute-start.6 = (bf16[8,24,384]{2,1,0:T(8,128)(2,1)S(1)}, bf16[8,24,384]{2,1,0:T(8,128)(2,1)S(1)}, u32[]{:S(2)}, u32[]{:S(2)}) collective-permute-start(bf16[8,24,384]{2,1,0:T(8,128)(2,1)S(1)} %get-tuple-element.50), channel_id=1, source_target_pairs={{0,4},{1,5},{2,6},{3,7},{4,8},{5,9},{6,10},{7,11},{8,12},{9,13},{1... | collective-permute-start | bytes 442376 | tf_op jit(solution)/shard_map/ppermute | solution.py:275
  79.7 2.8 %collective-permute-start.7 = (bf16[8,24,384]{2,1,0:T(8,128)(2,1)S(1)}, bf16[8,24,384]{2,1,0:T(8,128)(2,1)S(1)}, u32[]{:S(2)}, u32[]{:S(2)}) collective-permute-start(bf16[8,24,384]{2,1,0:T(8,128)(2,1)S(1)} %get-tuple-element.51), channel_id=1, source_target_pairs={{0,8},{1,9},{2,10},{3,11},{4,12},{5,13},{6,14},{7,15},{8,0},{9,1},... | collective-permute-start | bytes 442376 | tf_op jit(solution)/shard_map/ppermute | solution.py:275
  82.5 0.7 collective-permute-start.8
  83.2 1.0 %collective-permute-done.6.refs_1_ = bf16[8,24,384]{2,1,0:T(8,128)(2,1)S(1)} collective-permute-done((bf16[8,24,384]{2,1,0:T(8,128)(2,1)S(1)}, bf16[8,24,384]{2,1,0:T(8,128)(2,1)S(1)}, u32[]{:S(2)}, u32[]{:S(2)}) %collective-permute-start.6) | collective-permute-done | bytes 147488 | tf_op jit(solution)/shard_map/ppermute | solution.py:275
  84.2 1.6 %collective-permute-start.13 = (f32[24,128]{1,0:T(8,128)S(1)}, f32[24,128]{1,0:T(8,128)S(1)}, u32[]{:S(2)}, u32[]{:S(2)}) collective-permute-start(f32[24,128]{1,0:T(8,128)S(1)} %get-tuple-element.65), channel_id=1, source_target_pairs={{0,4},{1,5},{2,6},{3,7},{4,8},{5,9},{6,10},{7,11},{8,12},{9,13},{1... | collective-permute-start | bytes 36872 | tf_op jit(solution)/shard_map/ppermute | solution.py:275
  85.8 0.6 collective-permute-done.7.refs_2_
  86.3 4.1 %collective-permute-start.14 = (f32[24,128]{1,0:T(8,128)S(1)}, f32[24,128]{1,0:T(8,128)S(1)}, u32[]{:S(2)}, u32[]{:S(2)}) collective-permute-start(f32[24,128]{1,0:T(8,128)S(1)} %get-tuple-element.66), channel_id=1, source_target_pairs={{0,8},{1,9},{2,10},{3,11},{4,12},{5,13},{6,14},{7,15},{8,0},{9,1},... | collective-permute-start | bytes 36872 | tf_op jit(solution)/shard_map/ppermute | solution.py:275
  90.4 0.0 collective-permute-done.8.refs_3_
  90.4 0.0 collective-permute-start.15
  90.4 0.0 collective-permute-done.13.refs_5_
  90.4 1.7 %collective-permute-done.14.refs_6_ = f32[24,128]{1,0:T(8,128)S(1)} collective-permute-done((f32[24,128]{1,0:T(8,128)S(1)}, f32[24,128]{1,0:T(8,128)S(1)}, u32[]{:S(2)}, u32[]{:S(2)}) %collective-permute-start.14) | collective-permute-done | bytes 12320 | tf_op jit(solution)/shard_map/ppermute | solution.py:275
  92.1 2.0 %collective-permute-done.15.refs_7_ = f32[24,128]{1,0:T(8,128)S(1)} collective-permute-done((f32[24,128]{1,0:T(8,128)S(1)}, f32[24,128]{1,0:T(8,128)S(1)}, u32[]{:S(2)}, u32[]{:S(2)}) %collective-permute-start.15) | collective-permute-done | bytes 12320 | tf_op jit(solution)/shard_map/ppermute | solution.py:275
  94.1 1.6 %shard_map.74 = f32[96,128]{1,0:T(8,128)} custom-call(s32[4,8]{1,0:T(4,128)S(1)} %copy-done.1, bf16[8,24,384]{2,1,0:T(8,128)(2,1)S(1)} %get-tuple-element.49.refs_0_, bf16[8,24,384]{2,1,0:T(8,128)(2,1)S(1)} %collective-permute-done.6.refs_1_, bf16[8,24,384]{2,1,0:T(8,128)(2,1)S(1)} %collective-permute-done.7.refs_2_, ...), custom_call_target="tpu_custom_call" | custom-call | tf_op jit(solution)/shard_map/pallas_call | solution.py:229
  (9 shorter events, 0.0 us)
Async XLA Ops:
  2.0 15.5 %all-to-all-start = ((bf16[16,96,128]{2,1,0:T(8,128)(2,1)}), bf16[16,96,128]{2,1,0:T(8,128)(2,1)S(1)}, u32[]{:S(2)}, u32[]{:S(2)}) async-start(bf16[16,96,128]{2,1,0:T(8,128)(2,1)} %get-tuple-element.53), calls=%async_computation | async-start | bytes 786432 | tf_op jit(solution)/shard_map/all_to_all | solution.py:259
  9.5 13.0 %collective-permute-start = (bf16[2,96,384]{2,1,0:T(8,128)(2,1)S(1)}, bf16[2,96,384]{2,1,0:T(8,128)(2,1)S(1)}, u32[]{:S(2)}, u32[]{:S(2)}) collective-permute-start(bf16[2,96,384]{2,1,0:T(8,128)(2,1)S(1)} %get-tuple-element.40), channel_id=1, source_target_pairs={{0,1},{1,2},{2,3},{3,0},{4,5},{5,6},{6,7},{7,4},{8,9},{9,10},{10,1... | collective-permute-start | bytes 442376 | tf_op jit(solution)/shard_map/ppermute | solution.py:275
  10.9 12.5 %collective-permute-start.1 = (bf16[2,96,384]{2,1,0:T(8,128)(2,1)S(1)}, bf16[2,96,384]{2,1,0:T(8,128)(2,1)S(1)}, u32[]{:S(2)}, u32[]{:S(2)}) collective-permute-start(bf16[2,96,384]{2,1,0:T(8,128)(2,1)S(1)} %get-tuple-element.41), channel_id=1, source_target_pairs={{0,2},{1,3},{2,0},{3,1},{4,6},{5,7},{6,4},{7,5},{8,10},{9,11},{10,... | collective-permute-start | bytes 442376 | tf_op jit(solution)/shard_map/ppermute | solution.py:275
  13.6 9.9 %collective-permute-start.2 = (bf16[2,96,384]{2,1,0:T(8,128)(2,1)S(1)}, bf16[2,96,384]{2,1,0:T(8,128)(2,1)S(1)}, u32[]{:S(2)}, u32[]{:S(2)}) collective-permute-start(bf16[2,96,384]{2,1,0:T(8,128)(2,1)S(1)} %get-tuple-element.42), channel_id=1, source_target_pairs={{0,3},{1,0},{2,1},{3,2},{4,7},{5,4},{6,5},{7,6},{8,11},{9,8},{10,9... | collective-permute-start | bytes 442376 | tf_op jit(solution)/shard_map/ppermute | solution.py:275
  17.5 0.7 copy-start
  18.8 16.4 %collective-permute-start.10 = (bf16[2,384,128]{2,1,0:T(8,128)(2,1)S(1)}, bf16[2,384,128]{2,1,0:T(8,128)(2,1)S(1)}, u32[]{:S(2)}, u32[]{:S(2)}) collective-permute-start(bf16[2,384,128]{2,1,0:T(8,128)(2,1)S(1)} %get-tuple-element.56), channel_id=1, source_target_pairs={{0,240},{16,0},{32,16},{48,32},{64,48},{80,64},{96,80},{112,96},{1... | collective-permute-start | bytes 589832 | tf_op jit(solution)/shard_map/ppermute | solution.py:255
  22.5 12.7 %collective-permute-start.9 = (bf16[2,384,128]{2,1,0:T(8,128)(2,1)S(1)}, bf16[2,384,128]{2,1,0:T(8,128)(2,1)S(1)}, u32[]{:S(2)}, u32[]{:S(2)}) collective-permute-start(bf16[2,384,128]{2,1,0:T(8,128)(2,1)S(1)} %get-tuple-element.55), channel_id=1, source_target_pairs={{0,16},{16,32},{32,48},{48,64},{64,80},{80,96},{96,112},{112,128},... | collective-permute-start | bytes 589832 | tf_op jit(solution)/shard_map/ppermute | solution.py:254
  23.5 11.7 %copy-start.1 = (s32[4,8]{1,0:T(4,128)S(1)}, s32[4,8]{1,0:T(4,128)}, u32[]{:S(2)}) copy-start(s32[4,8]{1,0:T(4,128)} %cols_ref.5) | copy-start | bytes 388
  23.5 11.7 %copy-start.2 = (s32[1,32]{1,0:T(1,128)S(1)}, s32[1,32]{1,0:T(1,128)}, u32[]{:S(2)}) copy-start(s32[1,32]{1,0:T(1,128)} %slot_ref.5) | copy-start | bytes 388
  23.6 6.6 %collective-permute-start.3 = (bf16[216,384]{1,0:T(8,128)(2,1)S(1)}, bf16[216,384]{1,0:T(8,128)(2,1)S(1)}, u32[]{:S(2)}, u32[]{:S(2)}) collective-permute-start(bf16[216,384]{1,0:T(8,128)(2,1)S(1)} %get-tuple-element.46), channel_id=1, source_target_pairs={{0,4},{1,5},{2,6},{3,7},{4,8},{5,9},{6,10},{7,11},{8,12},{9,13},{1... | collective-permute-start | bytes 497672 | tf_op jit(solution)/shard_map/ppermute | solution.py:275
  25.0 8.5 %collective-permute-start.4 = (bf16[216,384]{1,0:T(8,128)(2,1)S(1)}, bf16[216,384]{1,0:T(8,128)(2,1)S(1)}, u32[]{:S(2)}, u32[]{:S(2)}) collective-permute-start(bf16[216,384]{1,0:T(8,128)(2,1)S(1)} %get-tuple-element.47), channel_id=1, source_target_pairs={{0,8},{1,9},{2,10},{3,11},{4,12},{5,13},{6,14},{7,15},{8,0},{9,1},... | collective-permute-start | bytes 497672 | tf_op jit(solution)/shard_map/ppermute | solution.py:275
  26.5 8.1 %collective-permute-start.5 = (bf16[216,384]{1,0:T(8,128)(2,1)S(1)}, bf16[216,384]{1,0:T(8,128)(2,1)S(1)}, u32[]{:S(2)}, u32[]{:S(2)}) collective-permute-start(bf16[216,384]{1,0:T(8,128)(2,1)S(1)} %get-tuple-element.48), channel_id=1, source_target_pairs={{0,12},{1,13},{2,14},{3,15},{4,0},{5,1},{6,2},{7,3},{8,4},{9,5},{1... | collective-permute-start | bytes 497672 | tf_op jit(solution)/shard_map/ppermute | solution.py:275
  51.6 7.4 %collective-permute-start.11 = (bf16[2,384,128]{2,1,0:T(8,128)(2,1)S(1)}, bf16[2,384,128]{2,1,0:T(8,128)(2,1)S(1)}, u32[]{:S(2)}, u32[]{:S(2)}) collective-permute-start(bf16[2,384,128]{2,1,0:T(8,128)(2,1)S(1)} %get-tuple-element.59), channel_id=1, source_target_pairs={{0,16},{16,32},{32,48},{48,64},{64,80},{80,96},{96,112},{112,128},... | collective-permute-start | bytes 589832 | tf_op jit(solution)/shard_map/ppermute | solution.py:254
  51.6 7.4 %collective-permute-start.12 = (bf16[2,384,128]{2,1,0:T(8,128)(2,1)S(1)}, bf16[2,384,128]{2,1,0:T(8,128)(2,1)S(1)}, u32[]{:S(2)}, u32[]{:S(2)}) collective-permute-start(bf16[2,384,128]{2,1,0:T(8,128)(2,1)S(1)} %get-tuple-element.60), channel_id=1, source_target_pairs={{0,240},{16,0},{32,16},{48,32},{64,48},{80,64},{96,80},{112,96},{1... | collective-permute-start | bytes 589832 | tf_op jit(solution)/shard_map/ppermute | solution.py:255
  74.7 19.4 %collective-permute-start.16 = (bf16[2,384,128]{2,1,0:T(8,128)(2,1)S(1)}, bf16[2,384,128]{2,1,0:T(8,128)(2,1)S(1)}, u32[]{:S(2)}, u32[]{:S(2)}) collective-permute-start(bf16[2,384,128]{2,1,0:T(8,128)(2,1)S(1)} %get-tuple-element.70), channel_id=1, source_target_pairs={{0,16},{16,32},{32,48},{48,64},{64,80},{80,96},{96,112},{112,128},... | collective-permute-start | bytes 589832 | tf_op jit(solution)/shard_map/ppermute | solution.py:254
  74.7 19.4 %collective-permute-start.17 = (bf16[2,384,128]{2,1,0:T(8,128)(2,1)S(1)}, bf16[2,384,128]{2,1,0:T(8,128)(2,1)S(1)}, u32[]{:S(2)}, u32[]{:S(2)}) collective-permute-start(bf16[2,384,128]{2,1,0:T(8,128)(2,1)S(1)} %get-tuple-element.71), channel_id=1, source_target_pairs={{0,240},{16,0},{32,16},{48,32},{64,48},{80,64},{96,80},{112,96},{1... | collective-permute-start | bytes 589832 | tf_op jit(solution)/shard_map/ppermute | solution.py:255
  78.3 5.9 %collective-permute-start.6 = (bf16[8,24,384]{2,1,0:T(8,128)(2,1)S(1)}, bf16[8,24,384]{2,1,0:T(8,128)(2,1)S(1)}, u32[]{:S(2)}, u32[]{:S(2)}) collective-permute-start(bf16[8,24,384]{2,1,0:T(8,128)(2,1)S(1)} %get-tuple-element.50), channel_id=1, source_target_pairs={{0,4},{1,5},{2,6},{3,7},{4,8},{5,9},{6,10},{7,11},{8,12},{9,13},{1... | collective-permute-start | bytes 442376 | tf_op jit(solution)/shard_map/ppermute | solution.py:275
  79.7 6.7 %collective-permute-start.7 = (bf16[8,24,384]{2,1,0:T(8,128)(2,1)S(1)}, bf16[8,24,384]{2,1,0:T(8,128)(2,1)S(1)}, u32[]{:S(2)}, u32[]{:S(2)}) collective-permute-start(bf16[8,24,384]{2,1,0:T(8,128)(2,1)S(1)} %get-tuple-element.51), channel_id=1, source_target_pairs={{0,8},{1,9},{2,10},{3,11},{4,12},{5,13},{6,14},{7,15},{8,0},{9,1},... | collective-permute-start | bytes 442376 | tf_op jit(solution)/shard_map/ppermute | solution.py:275
  82.5 7.9 %collective-permute-start.8 = (bf16[8,24,384]{2,1,0:T(8,128)(2,1)S(1)}, bf16[8,24,384]{2,1,0:T(8,128)(2,1)S(1)}, u32[]{:S(2)}, u32[]{:S(2)}) collective-permute-start(bf16[8,24,384]{2,1,0:T(8,128)(2,1)S(1)} %get-tuple-element.52), channel_id=1, source_target_pairs={{0,12},{1,13},{2,14},{3,15},{4,0},{5,1},{6,2},{7,3},{8,4},{9,5},{1... | collective-permute-start | bytes 442376 | tf_op jit(solution)/shard_map/ppermute | solution.py:275
  84.2 6.2 %collective-permute-start.13 = (f32[24,128]{1,0:T(8,128)S(1)}, f32[24,128]{1,0:T(8,128)S(1)}, u32[]{:S(2)}, u32[]{:S(2)}) collective-permute-start(f32[24,128]{1,0:T(8,128)S(1)} %get-tuple-element.65), channel_id=1, source_target_pairs={{0,4},{1,5},{2,6},{3,7},{4,8},{5,9},{6,10},{7,11},{8,12},{9,13},{1... | collective-permute-start | bytes 36872 | tf_op jit(solution)/shard_map/ppermute | solution.py:275
  86.3 5.7 %collective-permute-start.14 = (f32[24,128]{1,0:T(8,128)S(1)}, f32[24,128]{1,0:T(8,128)S(1)}, u32[]{:S(2)}, u32[]{:S(2)}) collective-permute-start(f32[24,128]{1,0:T(8,128)S(1)} %get-tuple-element.66), channel_id=1, source_target_pairs={{0,8},{1,9},{2,10},{3,11},{4,12},{5,13},{6,14},{7,15},{8,0},{9,1},... | collective-permute-start | bytes 36872 | tf_op jit(solution)/shard_map/ppermute | solution.py:275
  90.4 3.7 %collective-permute-start.15 = (f32[24,128]{1,0:T(8,128)S(1)}, f32[24,128]{1,0:T(8,128)S(1)}, u32[]{:S(2)}, u32[]{:S(2)}) collective-permute-start(f32[24,128]{1,0:T(8,128)S(1)} %get-tuple-element.67), channel_id=1, source_target_pairs={{0,12},{1,13},{2,14},{3,15},{4,0},{5,1},{6,2},{7,3},{8,4},{9,5},{1... | collective-permute-start | bytes 36872 | tf_op jit(solution)/shard_map/ppermute | solution.py:275

commit v8 on v7

--- a/solution.py
+++ b/solution.py
@@ -100,11 +100,22 @@
         outs[k][...] = held_ref[k]
 
 
+def table_kernel(slot_ref, cols_ref, rows_ref, slot_out, cols_out, rows_out):
+    for t in range(TILES):
+        slot_out[0, t] = slot_ref[0, t]
+    for r in range(SIDE):
+        for k in range(8):
+            cols_out[r, k] = cols_ref[r, k]
+    lead = lax.axis_index("lead")
+    for side in range(2):
+        for h in range(2):
+            rows_out[side, h] = rows_ref[side, h, lead]
+
+
 def send_halves(rows_ref, own_ref, up_ref, down_ref):
-    lead = lax.axis_index("lead")
     for side, ref in ((0, up_ref), (1, down_ref)):
         for h in range(2):
-            ref[h] = own_ref[rows_ref[side, h, lead]]
+            ref[h] = own_ref[rows_ref[side, h]]
 
 
 def pick_slab_kernel(rows_ref, got_ref, own_ref, up_ref, down_ref):
@@ -226,9 +237,10 @@
     space = pltpu.HBM if far else pltpu.VMEM
     vectors = [pltpu.with_memory_space_constraint(a, space) for a in vectors]
     specs = [SMEM] * scalars + [pl.BlockSpec(memory_space=space)] * len(vectors)
+    tables = [pltpu.with_memory_space_constraint(a, pltpu.SMEM) for a in args[:scalars]]
     return pl.pallas_call(kernel, in_specs=specs, out_specs=[VMEM] * len(outs),
                           out_shape=outs, scratch_shapes=list(scratch),
-                          compiler_params=pltpu.CompilerParams(vmem_limit_bytes=GRANT))(*args[:scalars], *vectors)
+                          compiler_params=pltpu.CompilerParams(vmem_limit_bytes=GRANT))(*tables, *vectors)
 
 
 def near(*arrays):
@@ -279,6 +291,10 @@
         start_kernel, [matrix_tiles, residual, diag],
         [arr((2, SHARE, TILE), BF16)] * 4 + [WIDE, ROWS, ROWS, arr((8, TILE), F32)],
         scratch=(ROWS, arr((1, SHARE), F32), pltpu.SemaphoreType.DMA((6,))), far=1)
+    tables = [pltpu.SMEM((1, TILES), jnp.int32), pltpu.SMEM((SIDE, 8), jnp.int32), pltpu.SMEM((2, 2), jnp.int32)]
+    tile_slot, tile_cols, rows = pl.pallas_call(
+        table_kernel, name="tables", in_specs=[SMEM] * 3, out_specs=[SMEM] * 3, out_shape=tables)(
+        tile_slot, tile_cols, rows)
     quarters = along_y(quarters)
     got = gather(wide)
     slabs = call(split_kernel, near(*quarters, start, line), [arr((PIECE, TILE), BF16)] * 4, 0,

time: 96 us -> 92.5 us (0.964)
  Pallas kernels: 10.3 us -> 7.09 us
    pallas_call x11, Pallas kernels: 10.3 us -> 6.29 us  [call(): pl.pallas_call(kernel, in_specs=specs, out_specs=[VMEM] * len(outs), out_...]
    ppermute x12, waiting for transfers between devices: 12.6 us -> 13.9 us  [exchange(): out.append(lax.ppermute(values[k], 'grp', pairs[k]))]
  transfers between devices with their start and end apart: 19 -> 19, of which waited for: 10 -> 10; matrix products, arithmetic and copies ran while one was open for 0% -> 0% of each run, Pallas kernels for 3% -> 2%
where the time goes in v8:
time: 92.5 us; the launch traced here: 92.2 us
  starting transfers between devices  38.9 us (42%)
  blocking collectives  28 us (30%)
  waiting for transfers between devices  18.2 us (20%)
  Pallas kernels  7.09 us (8%)
    all_to_all x2, blocking collectives, gather(): return lax.all_to_all(wide, 'grp', 0, 0)  28 us
    ppermute x12, starting transfers between devices, exchange(): out.append(lax.ppermute(values[k], 'grp', pairs[k]))  20.7 us
    ppermute x12, waiting for transfers between devices, exchange(): out.append(lax.ppermute(values[k], 'grp', pairs[k]))  13.9 us
    ppermute x3, starting transfers between devices, halo(): lax.ppermute(down, 'lead', [(i, (i - 1) % leads) for i in range(leads)])  10.6 us
    all_to_all x1, starting transfers between devices, gather(): return lax.all_to_all(wide, 'grp', 0, 0)  7.49 us
    pallas_call x11, Pallas kernels, call(): pl.pallas_call(kernel, in_specs=specs, out_specs=[VMEM] * len(outs), out_...  6.29 us
    ppermute x3, waiting for transfers between devices, halo(): lax.ppermute(up, 'lead', [(i, (i + 1) % leads) for i in range(leads)])  2.76 us
  transfers between devices with their start and end apart: 19, of which 10 were waited for; matrix products, arithmetic and copies ran while one was open for 0% of the time, Pallas kernels for 2%

profile of v8, /device:TPU:2, one launch (start us, length us, event | category | flops | bytes accessed | tf_op | source)
XLA Modules:
  0.0 92.2 jit_solution(16492981188492025682)
XLA Ops:
  0.0 2.0 %shard_map.64 = (bf16[2,96,384]{2,1,0:T(8,128)(2,1)S(1)}, bf16[2,96,384]{2,1,0:T(8,128)(2,1)S(1)}, bf16[2,96,384]{2,1,0:T(8,128)(2,1)S(1)}, bf16[2,96,384]{2,1,0...) custom-call(bf16[2,384,384]{2,1,0:T(8,128)(2,1)} %tiles_hbm.1, ...), custom_call_target="tpu_custom_call" | custom-call | tf_op jit(solution)/shard_map/pallas_call | solution.py:241
  2.0 7.5 %all-to-all-start = ((bf16[16,96,128]{2,1,0:T(8,128)(2,1)}), bf16[16,96,128]{2,1,0:T(8,128)(2,1)S(1)}, u32[]{:S(2)}, u32[]{:S(2)}) async-start(bf16[16,96,128]{2,1,0:T(8,128)(2,1)} %get-tuple-element.59), calls=%async_computation | async-start | bytes 786432 | tf_op jit(solution)/shard_map/all_to_all | solution.py:271
  9.5 1.5 %collective-permute-start = (bf16[2,96,384]{2,1,0:T(8,128)(2,1)S(1)}, bf16[2,96,384]{2,1,0:T(8,128)(2,1)S(1)}, u32[]{:S(2)}, u32[]{:S(2)}) collective-permute-start(bf16[2,96,384]{2,1,0:T(8,128)(2,1)S(1)} %get-tuple-element.45), channel_id=1, source_target_pairs={{0,1},{1,2},{2,3},{3,0},{4,5},{5,6},{6,7},{7,4},{8,9},{9,10},{10,1... | collective-permute-start | bytes 442376 | tf_op jit(solution)/shard_map/ppermute | solution.py:287
  10.9 2.7 %collective-permute-start.1 = (bf16[2,96,384]{2,1,0:T(8,128)(2,1)S(1)}, bf16[2,96,384]{2,1,0:T(8,128)(2,1)S(1)}, u32[]{:S(2)}, u32[]{:S(2)}) collective-permute-start(bf16[2,96,384]{2,1,0:T(8,128)(2,1)S(1)} %get-tuple-element.46), channel_id=1, source_target_pairs={{0,2},{1,3},{2,0},{3,1},{4,6},{5,7},{6,4},{7,5},{8,10},{9,11},{10,... | collective-permute-start | bytes 442376 | tf_op jit(solution)/shard_map/ppermute | solution.py:287
  13.6 1.5 %collective-permute-start.2 = (bf16[2,96,384]{2,1,0:T(8,128)(2,1)S(1)}, bf16[2,96,384]{2,1,0:T(8,128)(2,1)S(1)}, u32[]{:S(2)}, u32[]{:S(2)}) collective-permute-start(bf16[2,96,384]{2,1,0:T(8,128)(2,1)S(1)} %get-tuple-element.47), channel_id=1, source_target_pairs={{0,3},{1,0},{2,1},{3,2},{4,7},{5,4},{6,5},{7,6},{8,11},{9,8},{10,9... | collective-permute-start | bytes 442376 | tf_op jit(solution)/shard_map/ppermute | solution.py:287
  15.1 0.8 tables.1
  15.9 1.6 %all-to-all-done.got_ref = bf16[16,96,128]{2,1,0:T(8,128)(2,1)S(1)} async-done(((bf16[16,96,128]{2,1,0:T(8,128)(2,1)}), bf16[16,96,128]{2,1,0:T(8,128)(2,1)S(1)}, u32[]{:S(2)}, u32[]{:S(2)}) %all-to-all-start) | async-done | bytes 393248 | tf_op jit(solution)/shard_map/all_to_all | solution.py:271
  17.5 0.1 shard_map.67
  17.5 3.7 %collective-permute-start.10 = (bf16[2,384,128]{2,1,0:T(8,128)(2,1)S(1)}, bf16[2,384,128]{2,1,0:T(8,128)(2,1)S(1)}, u32[]{:S(2)}, u32[]{:S(2)}) collective-permute-start(bf16[2,384,128]{2,1,0:T(8,128)(2,1)S(1)} %get-tuple-element.62), channel_id=1, source_target_pairs={{0,240},{16,0},{32,16},{48,32},{64,48},{80,64},{96,80},{112,96},{1... | collective-permute-start | bytes 589832 | tf_op jit(solution)/shard_map/ppermute | solution.py:267
  21.3 0.0 collective-permute-start.9
  21.3 0.0 collective-permute-done.refs_1_
  21.3 2.2 %collective-permute-done.1.refs_2_ = bf16[2,96,384]{2,1,0:T(8,128)(2,1)S(1)} collective-permute-done((bf16[2,96,384]{2,1,0:T(8,128)(2,1)S(1)}, bf16[2,96,384]{2,1,0:T(8,128)(2,1)S(1)}, u32[]{:S(2)}, u32[]{:S(2)}) %collective-permute-start.1) | collective-permute-done | bytes 147488 | tf_op jit(solution)/shard_map/ppermute | solution.py:287
  23.5 0.0 collective-permute-done.2.refs_3_
  23.5 0.1 shard_map.65
  23.6 1.4 %collective-permute-start.3 = (bf16[216,384]{1,0:T(8,128)(2,1)S(1)}, bf16[216,384]{1,0:T(8,128)(2,1)S(1)}, u32[]{:S(2)}, u32[]{:S(2)}) collective-permute-start(bf16[216,384]{1,0:T(8,128)(2,1)S(1)} %get-tuple-element.51), channel_id=1, source_target_pairs={{0,4},{1,5},{2,6},{3,7},{4,8},{5,9},{6,10},{7,11},{8,12},{9,13},{1... | collective-permute-start | bytes 497672 | tf_op jit(solution)/shard_map/ppermute | solution.py:287
  25.0 1.3 %collective-permute-start.4 = (bf16[216,384]{1,0:T(8,128)(2,1)S(1)}, bf16[216,384]{1,0:T(8,128)(2,1)S(1)}, u32[]{:S(2)}, u32[]{:S(2)}) collective-permute-start(bf16[216,384]{1,0:T(8,128)(2,1)S(1)} %get-tuple-element.52), channel_id=1, source_target_pairs={{0,8},{1,9},{2,10},{3,11},{4,12},{5,13},{6,14},{7,15},{8,0},{9,1},... | collective-permute-start | bytes 497672 | tf_op jit(solution)/shard_map/ppermute | solution.py:287
  26.3 1.9 %collective-permute-start.5 = (bf16[216,384]{1,0:T(8,128)(2,1)S(1)}, bf16[216,384]{1,0:T(8,128)(2,1)S(1)}, u32[]{:S(2)}, u32[]{:S(2)}) collective-permute-start(bf16[216,384]{1,0:T(8,128)(2,1)S(1)} %get-tuple-element.53), channel_id=1, source_target_pairs={{0,12},{1,13},{2,14},{3,15},{4,0},{5,1},{6,2},{7,3},{8,4},{9,5},{1... | collective-permute-start | bytes 497672 | tf_op jit(solution)/shard_map/ppermute | solution.py:287
  28.2 2.0 %collective-permute-done.3.refs_1_ = bf16[216,384]{1,0:T(8,128)(2,1)S(1)} collective-permute-done((bf16[216,384]{1,0:T(8,128)(2,1)S(1)}, bf16[216,384]{1,0:T(8,128)(2,1)S(1)}, u32[]{:S(2)}, u32[]{:S(2)}) %collective-permute-start.3) | collective-permute-done | bytes 165920 | tf_op jit(solution)/shard_map/ppermute | solution.py:287
  30.2 3.3 %collective-permute-done.4.refs_2_ = bf16[216,384]{1,0:T(8,128)(2,1)S(1)} collective-permute-done((bf16[216,384]{1,0:T(8,128)(2,1)S(1)}, bf16[216,384]{1,0:T(8,128)(2,1)S(1)}, u32[]{:S(2)}, u32[]{:S(2)}) %collective-permute-start.4) | collective-permute-done | bytes 165920 | tf_op jit(solution)/shard_map/ppermute | solution.py:287
  33.5 1.1 %collective-permute-done.5.refs_3_ = bf16[216,384]{1,0:T(8,128)(2,1)S(1)} collective-permute-done((bf16[216,384]{1,0:T(8,128)(2,1)S(1)}, bf16[216,384]{1,0:T(8,128)(2,1)S(1)}, u32[]{:S(2)}, u32[]{:S(2)}) %collective-permute-start.5) | collective-permute-done | bytes 165920 | tf_op jit(solution)/shard_map/ppermute | solution.py:287
  34.6 0.6 shard_map.68.refs_4_
  35.2 0.0 collective-permute-done.9.refs_5_
  35.2 0.8 shard_map.69
  36.0 14.4 %all_to_all.15.got_ref = bf16[16,96,128]{2,1,0:T(8,128)(2,1)S(1)} all-to-all(bf16[16,96,128]{2,1,0:T(8,128)(2,1)S(1)} %get-tuple-element.63), channel_id=1, replica_groups=mesh['lead'=16,'grp'=16] {'grp'}, dimensions={0} | all-to-all | bytes 786432 | tf_op jit(solution)/shard_map/all_to_all | solution.py:271
  50.4 0.1 shard_map.70
  50.5 0.0 collective-permute-start.11
  50.5 4.0 %collective-permute-start.12 = (bf16[2,384,128]{2,1,0:T(8,128)(2,1)S(1)}, bf16[2,384,128]{2,1,0:T(8,128)(2,1)S(1)}, u32[]{:S(2)}, u32[]{:S(2)}) collective-permute-start(bf16[2,384,128]{2,1,0:T(8,128)(2,1)S(1)} %get-tuple-element.66), channel_id=1, source_target_pairs={{0,240},{16,0},{32,16},{48,32},{64,48},{80,64},{96,80},{112,96},{1... | collective-permute-start | bytes 589832 | tf_op jit(solution)/shard_map/ppermute | solution.py:267
  54.5 0.6 shard_map.71.refs_4_
  55.0 2.8 %collective-permute-done.11.refs_5_ = bf16[2,384,128]{2,1,0:T(8,128)(2,1)S(1)} collective-permute-done((bf16[2,384,128]{2,1,0:T(8,128)(2,1)S(1)}, bf16[2,384,128]{2,1,0:T(8,128)(2,1)S(1)}, u32[]{:S(2)}, u32[]{:S(2)}) %collective-permute-start.11) | collective-permute-done | bytes 196640 | tf_op jit(solution)/shard_map/ppermute | solution.py:266
  57.8 0.0 collective-permute-done.12.refs_6_
  57.8 0.8 shard_map.72
  58.7 13.6 %all_to_all.16.got_ref = bf16[16,96,128]{2,1,0:T(8,128)(2,1)S(1)} all-to-all(bf16[16,96,128]{2,1,0:T(8,128)(2,1)S(1)} %get-tuple-element.74), channel_id=1, replica_groups=mesh['lead'=16,'grp'=16] {'grp'}, dimensions={0} | all-to-all | bytes 786432 | tf_op jit(solution)/shard_map/all_to_all | solution.py:271
  72.3 0.1 shard_map.73
  72.4 0.0 collective-permute-start.16
  72.4 2.9 %collective-permute-start.17 = (bf16[2,384,128]{2,1,0:T(8,128)(2,1)S(1)}, bf16[2,384,128]{2,1,0:T(8,128)(2,1)S(1)}, u32[]{:S(2)}, u32[]{:S(2)}) collective-permute-start(bf16[2,384,128]{2,1,0:T(8,128)(2,1)S(1)} %get-tuple-element.77), channel_id=1, source_target_pairs={{0,240},{16,0},{32,16},{48,32},{64,48},{80,64},{96,80},{112,96},{1... | collective-permute-start | bytes 589832 | tf_op jit(solution)/shard_map/ppermute | solution.py:267
  75.3 0.1 shard_map.66
  75.5 1.3 %collective-permute-start.6 = (bf16[8,24,384]{2,1,0:T(8,128)(2,1)S(1)}, bf16[8,24,384]{2,1,0:T(8,128)(2,1)S(1)}, u32[]{:S(2)}, u32[]{:S(2)}) collective-permute-start(bf16[8,24,384]{2,1,0:T(8,128)(2,1)S(1)} %get-tuple-element.55), channel_id=1, source_target_pairs={{0,4},{1,5},{2,6},{3,7},{4,8},{5,9},{6,10},{7,11},{8,12},{9,13},{1... | collective-permute-start | bytes 442376 | tf_op jit(solution)/shard_map/ppermute | solution.py:287
  76.8 2.8 %collective-permute-start.7 = (bf16[8,24,384]{2,1,0:T(8,128)(2,1)S(1)}, bf16[8,24,384]{2,1,0:T(8,128)(2,1)S(1)}, u32[]{:S(2)}, u32[]{:S(2)}) collective-permute-start(bf16[8,24,384]{2,1,0:T(8,128)(2,1)S(1)} %get-tuple-element.56), channel_id=1, source_target_pairs={{0,8},{1,9},{2,10},{3,11},{4,12},{5,13},{6,14},{7,15},{8,0},{9,1},... | collective-permute-start | bytes 442376 | tf_op jit(solution)/shard_map/ppermute | solution.py:287
  79.6 0.7 collective-permute-start.8
  80.3 1.0 %collective-permute-done.6.refs_1_ = bf16[8,24,384]{2,1,0:T(8,128)(2,1)S(1)} collective-permute-done((bf16[8,24,384]{2,1,0:T(8,128)(2,1)S(1)}, bf16[8,24,384]{2,1,0:T(8,128)(2,1)S(1)}, u32[]{:S(2)}, u32[]{:S(2)}) %collective-permute-start.6) | collective-permute-done | bytes 147488 | tf_op jit(solution)/shard_map/ppermute | solution.py:287
  81.3 1.6 %collective-permute-start.13 = (f32[24,128]{1,0:T(8,128)S(1)}, f32[24,128]{1,0:T(8,128)S(1)}, u32[]{:S(2)}, u32[]{:S(2)}) collective-permute-start(f32[24,128]{1,0:T(8,128)S(1)} %get-tuple-element.71), channel_id=1, source_target_pairs={{0,4},{1,5},{2,6},{3,7},{4,8},{5,9},{6,10},{7,11},{8,12},{9,13},{1... | collective-permute-start | bytes 36872 | tf_op jit(solution)/shard_map/ppermute | solution.py:287
  82.9 0.6 collective-permute-done.7.refs_2_
  83.5 4.1 %collective-permute-start.14 = (f32[24,128]{1,0:T(8,128)S(1)}, f32[24,128]{1,0:T(8,128)S(1)}, u32[]{:S(2)}, u32[]{:S(2)}) collective-permute-start(f32[24,128]{1,0:T(8,128)S(1)} %get-tuple-element.72), channel_id=1, source_target_pairs={{0,8},{1,9},{2,10},{3,11},{4,12},{5,13},{6,14},{7,15},{8,0},{9,1},... | collective-permute-start | bytes 36872 | tf_op jit(solution)/shard_map/ppermute | solution.py:287
  87.5 1.7 %collective-permute-done.14.refs_6_ = f32[24,128]{1,0:T(8,128)S(1)} collective-permute-done((f32[24,128]{1,0:T(8,128)S(1)}, f32[24,128]{1,0:T(8,128)S(1)}, u32[]{:S(2)}, u32[]{:S(2)}) %collective-permute-start.14) | collective-permute-done | bytes 12320 | tf_op jit(solution)/shard_map/ppermute | solution.py:287
  89.2 2.0 %collective-permute-done.15.refs_7_ = f32[24,128]{1,0:T(8,128)S(1)} collective-permute-done((f32[24,128]{1,0:T(8,128)S(1)}, f32[24,128]{1,0:T(8,128)S(1)}, u32[]{:S(2)}, u32[]{:S(2)}) %collective-permute-start.15) | collective-permute-done | bytes 12320 | tf_op jit(solution)/shard_map/ppermute | solution.py:287
  91.2 0.0 collective-permute-done.16.refs_9_
  91.2 0.0 collective-permute-done.17.refs_10_
  91.2 1.0 %shard_map.74 = f32[96,128]{1,0:T(8,128)} custom-call(s32[4,8]{1,0:T(4,128)S(4)} %get-tuple-element.42.cols_ref, bf16[8,24,384]{2,1,0:T(8,128)(2,1)S(1)} %get-tuple-element.54.refs_0_, bf16[8,24,384]{2,1,0:T(8,128)(2,1)S(1)} %collective-permute-done.6.refs_1_, bf16[8,24,384]{2,1,0:T(8,128)(2,1)S(1)} %collective-permute-done.7.refs_2_, ...), custom_call_target="tpu_custom_call" | custom-call | tf_op jit(solution)/shard_map/pallas_call | solution.py:241
  (4 shorter events, 0.0 us)
Async XLA Ops:
  2.0 15.5 %all-to-all-start = ((bf16[16,96,128]{2,1,0:T(8,128)(2,1)}), bf16[16,96,128]{2,1,0:T(8,128)(2,1)S(1)}, u32[]{:S(2)}, u32[]{:S(2)}) async-start(bf16[16,96,128]{2,1,0:T(8,128)(2,1)} %get-tuple-element.59), calls=%async_computation | async-start | bytes 786432 | tf_op jit(solution)/shard_map/all_to_all | solution.py:271
  9.5 11.8 %collective-permute-start = (bf16[2,96,384]{2,1,0:T(8,128)(2,1)S(1)}, bf16[2,96,384]{2,1,0:T(8,128)(2,1)S(1)}, u32[]{:S(2)}, u32[]{:S(2)}) collective-permute-start(bf16[2,96,384]{2,1,0:T(8,128)(2,1)S(1)} %get-tuple-element.45), channel_id=1, source_target_pairs={{0,1},{1,2},{2,3},{3,0},{4,5},{5,6},{6,7},{7,4},{8,9},{9,10},{10,1... | collective-permute-start | bytes 442376 | tf_op jit(solution)/shard_map/ppermute | solution.py:287
  10.9 12.5 %collective-permute-start.1 = (bf16[2,96,384]{2,1,0:T(8,128)(2,1)S(1)}, bf16[2,96,384]{2,1,0:T(8,128)(2,1)S(1)}, u32[]{:S(2)}, u32[]{:S(2)}) collective-permute-start(bf16[2,96,384]{2,1,0:T(8,128)(2,1)S(1)} %get-tuple-element.46), channel_id=1, source_target_pairs={{0,2},{1,3},{2,0},{3,1},{4,6},{5,7},{6,4},{7,5},{8,10},{9,11},{10,... | collective-permute-start | bytes 442376 | tf_op jit(solution)/shard_map/ppermute | solution.py:287
  13.6 9.9 %collective-permute-start.2 = (bf16[2,96,384]{2,1,0:T(8,128)(2,1)S(1)}, bf16[2,96,384]{2,1,0:T(8,128)(2,1)S(1)}, u32[]{:S(2)}, u32[]{:S(2)}) collective-permute-start(bf16[2,96,384]{2,1,0:T(8,128)(2,1)S(1)} %get-tuple-element.47), channel_id=1, source_target_pairs={{0,3},{1,0},{2,1},{3,2},{4,7},{5,4},{6,5},{7,6},{8,11},{9,8},{10,9... | collective-permute-start | bytes 442376 | tf_op jit(solution)/shard_map/ppermute | solution.py:287
  17.5 17.7 %collective-permute-start.10 = (bf16[2,384,128]{2,1,0:T(8,128)(2,1)S(1)}, bf16[2,384,128]{2,1,0:T(8,128)(2,1)S(1)}, u32[]{:S(2)}, u32[]{:S(2)}) collective-permute-start(bf16[2,384,128]{2,1,0:T(8,128)(2,1)S(1)} %get-tuple-element.62), channel_id=1, source_target_pairs={{0,240},{16,0},{32,16},{48,32},{64,48},{80,64},{96,80},{112,96},{1... | collective-permute-start | bytes 589832 | tf_op jit(solution)/shard_map/ppermute | solution.py:267
  21.3 13.9 %collective-permute-start.9 = (bf16[2,384,128]{2,1,0:T(8,128)(2,1)S(1)}, bf16[2,384,128]{2,1,0:T(8,128)(2,1)S(1)}, u32[]{:S(2)}, u32[]{:S(2)}) collective-permute-start(bf16[2,384,128]{2,1,0:T(8,128)(2,1)S(1)} %get-tuple-element.61), channel_id=1, source_target_pairs={{0,16},{16,32},{32,48},{48,64},{64,80},{80,96},{96,112},{112,128},... | collective-permute-start | bytes 589832 | tf_op jit(solution)/shard_map/ppermute | solution.py:266
  23.6 6.6 %collective-permute-start.3 = (bf16[216,384]{1,0:T(8,128)(2,1)S(1)}, bf16[216,384]{1,0:T(8,128)(2,1)S(1)}, u32[]{:S(2)}, u32[]{:S(2)}) collective-permute-start(bf16[216,384]{1,0:T(8,128)(2,1)S(1)} %get-tuple-element.51), channel_id=1, source_target_pairs={{0,4},{1,5},{2,6},{3,7},{4,8},{5,9},{6,10},{7,11},{8,12},{9,13},{1... | collective-permute-start | bytes 497672 | tf_op jit(solution)/shard_map/ppermute | solution.py:287
  25.0 8.5 %collective-permute-start.4 = (bf16[216,384]{1,0:T(8,128)(2,1)S(1)}, bf16[216,384]{1,0:T(8,128)(2,1)S(1)}, u32[]{:S(2)}, u32[]{:S(2)}) collective-permute-start(bf16[216,384]{1,0:T(8,128)(2,1)S(1)} %get-tuple-element.52), channel_id=1, source_target_pairs={{0,8},{1,9},{2,10},{3,11},{4,12},{5,13},{6,14},{7,15},{8,0},{9,1},... | collective-permute-start | bytes 497672 | tf_op jit(solution)/shard_map/ppermute | solution.py:287
  26.3 8.3 %collective-permute-start.5 = (bf16[216,384]{1,0:T(8,128)(2,1)S(1)}, bf16[216,384]{1,0:T(8,128)(2,1)S(1)}, u32[]{:S(2)}, u32[]{:S(2)}) collective-permute-start(bf16[216,384]{1,0:T(8,128)(2,1)S(1)} %get-tuple-element.53), channel_id=1, source_target_pairs={{0,12},{1,13},{2,14},{3,15},{4,0},{5,1},{6,2},{7,3},{8,4},{9,5},{1... | collective-permute-start | bytes 497672 | tf_op jit(solution)/shard_map/ppermute | solution.py:287
  50.5 7.3 %collective-permute-start.11 = (bf16[2,384,128]{2,1,0:T(8,128)(2,1)S(1)}, bf16[2,384,128]{2,1,0:T(8,128)(2,1)S(1)}, u32[]{:S(2)}, u32[]{:S(2)}) collective-permute-start(bf16[2,384,128]{2,1,0:T(8,128)(2,1)S(1)} %get-tuple-element.65), channel_id=1, source_target_pairs={{0,16},{16,32},{32,48},{48,64},{64,80},{80,96},{96,112},{112,128},... | collective-permute-start | bytes 589832 | tf_op jit(solution)/shard_map/ppermute | solution.py:266
  50.5 7.3 %collective-permute-start.12 = (bf16[2,384,128]{2,1,0:T(8,128)(2,1)S(1)}, bf16[2,384,128]{2,1,0:T(8,128)(2,1)S(1)}, u32[]{:S(2)}, u32[]{:S(2)}) collective-permute-start(bf16[2,384,128]{2,1,0:T(8,128)(2,1)S(1)} %get-tuple-element.66), channel_id=1, source_target_pairs={{0,240},{16,0},{32,16},{48,32},{64,48},{80,64},{96,80},{112,96},{1... | collective-permute-start | bytes 589832 | tf_op jit(solution)/shard_map/ppermute | solution.py:267
  72.4 18.9 %collective-permute-start.16 = (bf16[2,384,128]{2,1,0:T(8,128)(2,1)S(1)}, bf16[2,384,128]{2,1,0:T(8,128)(2,1)S(1)}, u32[]{:S(2)}, u32[]{:S(2)}) collective-permute-start(bf16[2,384,128]{2,1,0:T(8,128)(2,1)S(1)} %get-tuple-element.76), channel_id=1, source_target_pairs={{0,16},{16,32},{32,48},{48,64},{64,80},{80,96},{96,112},{112,128},... | collective-permute-start | bytes 589832 | tf_op jit(solution)/shard_map/ppermute | solution.py:266
  72.4 18.8 %collective-permute-start.17 = (bf16[2,384,128]{2,1,0:T(8,128)(2,1)S(1)}, bf16[2,384,128]{2,1,0:T(8,128)(2,1)S(1)}, u32[]{:S(2)}, u32[]{:S(2)}) collective-permute-start(bf16[2,384,128]{2,1,0:T(8,128)(2,1)S(1)} %get-tuple-element.77), channel_id=1, source_target_pairs={{0,240},{16,0},{32,16},{48,32},{64,48},{80,64},{96,80},{112,96},{1... | collective-permute-start | bytes 589832 | tf_op jit(solution)/shard_map/ppermute | solution.py:267
  75.5 5.9 %collective-permute-start.6 = (bf16[8,24,384]{2,1,0:T(8,128)(2,1)S(1)}, bf16[8,24,384]{2,1,0:T(8,128)(2,1)S(1)}, u32[]{:S(2)}, u32[]{:S(2)}) collective-permute-start(bf16[8,24,384]{2,1,0:T(8,128)(2,1)S(1)} %get-tuple-element.55), channel_id=1, source_target_pairs={{0,4},{1,5},{2,6},{3,7},{4,8},{5,9},{6,10},{7,11},{8,12},{9,13},{1... | collective-permute-start | bytes 442376 | tf_op jit(solution)/shard_map/ppermute | solution.py:287
  76.8 6.7 %collective-permute-start.7 = (bf16[8,24,384]{2,1,0:T(8,128)(2,1)S(1)}, bf16[8,24,384]{2,1,0:T(8,128)(2,1)S(1)}, u32[]{:S(2)}, u32[]{:S(2)}) collective-permute-start(bf16[8,24,384]{2,1,0:T(8,128)(2,1)S(1)} %get-tuple-element.56), channel_id=1, source_target_pairs={{0,8},{1,9},{2,10},{3,11},{4,12},{5,13},{6,14},{7,15},{8,0},{9,1},... | collective-permute-start | bytes 442376 | tf_op jit(solution)/shard_map/ppermute | solution.py:287
  79.6 7.9 %collective-permute-start.8 = (bf16[8,24,384]{2,1,0:T(8,128)(2,1)S(1)}, bf16[8,24,384]{2,1,0:T(8,128)(2,1)S(1)}, u32[]{:S(2)}, u32[]{:S(2)}) collective-permute-start(bf16[8,24,384]{2,1,0:T(8,128)(2,1)S(1)} %get-tuple-element.57), channel_id=1, source_target_pairs={{0,12},{1,13},{2,14},{3,15},{4,0},{5,1},{6,2},{7,3},{8,4},{9,5},{1... | collective-permute-start | bytes 442376 | tf_op jit(solution)/shard_map/ppermute | solution.py:287
  81.3 6.2 %collective-permute-start.13 = (f32[24,128]{1,0:T(8,128)S(1)}, f32[24,128]{1,0:T(8,128)S(1)}, u32[]{:S(2)}, u32[]{:S(2)}) collective-permute-start(f32[24,128]{1,0:T(8,128)S(1)} %get-tuple-element.71), channel_id=1, source_target_pairs={{0,4},{1,5},{2,6},{3,7},{4,8},{5,9},{6,10},{7,11},{8,12},{9,13},{1... | collective-permute-start | bytes 36872 | tf_op jit(solution)/shard_map/ppermute | solution.py:287
  83.5 5.7 %collective-permute-start.14 = (f32[24,128]{1,0:T(8,128)S(1)}, f32[24,128]{1,0:T(8,128)S(1)}, u32[]{:S(2)}, u32[]{:S(2)}) collective-permute-start(f32[24,128]{1,0:T(8,128)S(1)} %get-tuple-element.72), channel_id=1, source_target_pairs={{0,8},{1,9},{2,10},{3,11},{4,12},{5,13},{6,14},{7,15},{8,0},{9,1},... | collective-permute-start | bytes 36872 | tf_op jit(solution)/shard_map/ppermute | solution.py:287
  87.5 3.7 %collective-permute-start.15 = (f32[24,128]{1,0:T(8,128)S(1)}, f32[24,128]{1,0:T(8,128)S(1)}, u32[]{:S(2)}, u32[]{:S(2)}) collective-permute-start(f32[24,128]{1,0:T(8,128)S(1)} %get-tuple-element.73), channel_id=1, source_target_pairs={{0,12},{1,13},{2,14},{3,15},{4,0},{5,1},{6,2},{7,3},{8,4},{9,5},{1... | collective-permute-start | bytes 36872 | tf_op jit(solution)/shard_map/ppermute | solution.py:287

commit v9 on v8

--- a/solution.py
+++ b/solution.py
@@ -120,7 +120,7 @@
 
 def pick_slab_kernel(rows_ref, got_ref, own_ref, up_ref, down_ref):
     for q in range(SIDE):
-        parts = [got_ref[SIDE * x + q].astype(F32) for x in range(SIDE)]
+        parts = [got_ref[SIDE * x + q, 0:SHARE].astype(F32) for x in range(SIDE)]
         for r in range(SIDE):
             block = jnp.concatenate([p[SLAB * r:SLAB * (r + 1)] for p in parts], axis=0)
             own_ref[r, SHARE * q:SHARE * (q + 1)] = block.astype(BF16)
@@ -199,23 +199,27 @@
 
 def second_kernel(slot_ref, cols_ref, *refs):
     parts, halo, (first_ref, start_ref, scale_ref) = refs[:4], refs[4:7], refs[7:10]
-    wide_ref, outs, work = refs[10], refs[11:15], refs[15:]
+    wide_ref, work = refs[10], refs[11:]
     slab_total(slot_ref, cols_ref, parts, *halo, *work)
-    x, _ = place()
-    seconds = []
     total_ref = work[1]
+    seconds, rests = [], []
     for r in range(SIDE):
-        second = start_ref[r] - first_ref[r] - scale_ref[r] * total_ref[r]
+        first = first_ref[r]
+        second = start_ref[r] - first - scale_ref[r] * total_ref[r]
         seconds.append(second)
-        total_ref[r] = first_ref[r] + GAIN * second
-    spread(jnp.concatenate(seconds, axis=0), wide_ref)
-    for k in range(SIDE):
-        outs[k][...] = total_ref[wrap(x + k)]
+        rest = first - first.astype(BF16).astype(F32) + GAIN * (second - second.astype(BF16).astype(F32))
+        rests.append(rest.astype(BF16))
+    high = jnp.concatenate(seconds, axis=0).astype(BF16)
+    for r in range(SIDE):
+        for s in range(SIDE):
+            wide_ref[SIDE * r + s, 0:SHARE] = high
+            wide_ref[SIDE * r + s, SHARE:120] = rests[r]
 
 
 def last_kernel(cols_ref, *refs):
-    parts, sums, (own_ref, low_ref, high_ref, scale_ref, out_ref, ext_ref) = refs[:4], refs[4:8], refs[8:]
-    x, _ = place()
+    parts, halo, (got_ref, first_ref, scale_ref, out_ref, ext_ref, line_ref) = refs[:4], refs[4:7], refs[7:]
+    own_ref, low_ref, high_ref = halo
+    x, q = place()
     ext_ref[0:4] = own_ref[...]
     ext_ref[4:6] = low_ref[...]
     ext_ref[6:8] = high_ref[...]
@@ -224,8 +228,11 @@
         left = jnp.concatenate([part[k] for part in parts], axis=0)
         total += jnp.dot(left, ext_ref[cols_ref[x, k]], preferred_element_type=F32)
     for k in range(SIDE):
-        at = pl.ds(pl.multiple_of(wrap(x - k) * SLAB, 8), SLAB)
-        out_ref[at, :] = sums[k][...] - GAIN * (scale_ref[at, :] * total[SLAB * k:SLAB * (k + 1)])
+        line_ref[pl.ds(pl.multiple_of(wrap(x - k) * SLAB, 8), SLAB), :] = total[SLAB * k:SLAB * (k + 1)]
+    mine = pl.ds(pl.multiple_of(q * SHARE, SHARE), SHARE)
+    rest = jnp.concatenate([got_ref[SIDE * s + q, SHARE:120].astype(F32) for s in range(SIDE)], axis=0)
+    second = own_ref[x, mine].astype(F32) - scale_ref[...] * line_ref[...]
+    out_ref[...] = first_ref[x, mine].astype(F32) + rest + GAIN * second
 
 
 def arr(shape, dtype):
@@ -307,17 +314,17 @@
     product, = call(near_kernel, near(*slabs, own), [NEAR])
     wide, *state = call(first_kernel, [tile_slot, tile_cols] + near(*slabs, product, *halos),
                         [WIDE] + [SLABS] * 3, 2, WORK)
-    own, up, down = choose(pick_slab_kernel, gather(wide))
+    first, up, down = choose(pick_slab_kernel, gather(wide))
     halos = halo(up, down)
     parts = along_x(ordered)
-    product, = call(near_kernel, near(*slabs, own), [NEAR])
-    wide, *sums = call(second_kernel, [tile_slot, tile_cols] + near(*slabs, product, *halos, *state),
-                       [WIDE] + [arr((SLAB, NRHS), F32)] * 4, 2, WORK)
-    own, up, down = choose(pick_slab_kernel, gather(wide))
+    product, = call(near_kernel, near(*slabs, first), [NEAR])
+    wide, = call(second_kernel, [tile_slot, tile_cols] + near(*slabs, product, *halos, *state),
+                 [arr((GROUP, 120, NRHS), BF16)], 2, WORK)
+    got = gather(wide)
+    own, up, down = choose(pick_slab_kernel, got)
     halos = halo(up, down)
-    sums = along_x(sums)
-    result, = call(last_kernel, [tile_cols] + near(*parts, *sums, own, *halos, scale),
-                   [jax.ShapeDtypeStruct((SHARE, NRHS), F32)], 1, (EXT,))
+    result, = call(last_kernel, [tile_cols] + near(*parts, own, *halos, got, first, scale),
+                   [jax.ShapeDtypeStruct((SHARE, NRHS), F32)], 1, (EXT, ROWS))
     return result
 
 

time: 92.5 us -> 88.3 us (0.955)
  the two profiles are of different devices: /device:TPU:2 before, /device:TPU:97 now
where the time goes in v9:
time: 88.3 us; the launch traced here: 87.6 us
  starting transfers between devices  32.3 us (37%)
  blocking collectives  27.7 us (31%)
  waiting for transfers between devices  20.5 us (23%)
  Pallas kernels  7.08 us (8%)
    all_to_all x2, blocking collectives, gather(): return lax.all_to_all(wide, 'grp', 0, 0)  27.7 us
    ppermute x9, starting transfers between devices, exchange(): out.append(lax.ppermute(values[k], 'grp', pairs[k]))  12.8 us
    ppermute x9, waiting for transfers between devices, exchange(): out.append(lax.ppermute(values[k], 'grp', pairs[k]))  12.2 us
    ppermute x3, starting transfers between devices, halo(): lax.ppermute(up, 'lead', [(i, (i + 1) % leads) for i in range(leads)])  10.2 us
    all_to_all x1, starting transfers between devices, gather(): return lax.all_to_all(wide, 'grp', 0, 0)  6.77 us
    pallas_call x11, Pallas kernels, call(): pl.pallas_call(kernel, in_specs=specs, out_specs=[VMEM] * len(outs), out_...  6.28 us
    ppermute x3, waiting for transfers between devices, halo(): lax.ppermute(down, 'lead', [(i, (i - 1) % leads) for i in range(leads)])  3.7 us
    all_to_all x1, waiting for transfers between devices, gather(): return lax.all_to_all(wide, 'grp', 0, 0)  2.53 us
  transfers between devices with their start and end apart: 16, of which 9 were waited for; matrix products, arithmetic and copies ran while one was open for 0% of the time, Pallas kernels for 3%

profile of v9, /device:TPU:97, one launch (start us, length us, event | category | flops | bytes accessed | tf_op | source)
XLA Modules:
  0.0 87.6 jit_solution(6974324221666606986)
XLA Ops:
  0.0 2.0 %shard_map.64 = (bf16[2,96,384]{2,1,0:T(8,128)(2,1)S(1)}, bf16[2,96,384]{2,1,0:T(8,128)(2,1)S(1)}, bf16[2,96,384]{2,1,0:T(8,128)(2,1)S(1)}, bf16[2,96,384]{2,1,0...) custom-call(bf16[2,384,384]{2,1,0:T(8,128)(2,1)} %tiles_hbm.1, ...), custom_call_target="tpu_custom_call" | custom-call | tf_op jit(solution)/shard_map/pallas_call | solution.py:248
  2.0 6.8 %all-to-all-start = ((bf16[16,96,128]{2,1,0:T(8,128)(2,1)}), bf16[16,96,128]{2,1,0:T(8,128)(2,1)S(1)}, u32[]{:S(2)}, u32[]{:S(2)}) async-start(bf16[16,96,128]{2,1,0:T(8,128)(2,1)} %get-tuple-element.54), calls=%async_computation | async-start | bytes 786432 | tf_op jit(solution)/shard_map/all_to_all | solution.py:278
  8.8 1.4 %collective-permute-start = (bf16[2,96,384]{2,1,0:T(8,128)(2,1)S(1)}, bf16[2,96,384]{2,1,0:T(8,128)(2,1)S(1)}, u32[]{:S(2)}, u32[]{:S(2)}) collective-permute-start(bf16[2,96,384]{2,1,0:T(8,128)(2,1)S(1)} %get-tuple-element.40), channel_id=1, source_target_pairs={{0,1},{1,2},{2,3},{3,0},{4,5},{5,6},{6,7},{7,4},{8,9},{9,10},{10,1... | collective-permute-start | bytes 442376 | tf_op jit(solution)/shard_map/ppermute | solution.py:294
  10.1 2.4 %collective-permute-start.1 = (bf16[2,96,384]{2,1,0:T(8,128)(2,1)S(1)}, bf16[2,96,384]{2,1,0:T(8,128)(2,1)S(1)}, u32[]{:S(2)}, u32[]{:S(2)}) collective-permute-start(bf16[2,96,384]{2,1,0:T(8,128)(2,1)S(1)} %get-tuple-element.41), channel_id=1, source_target_pairs={{0,2},{1,3},{2,0},{3,1},{4,6},{5,7},{6,4},{7,5},{8,10},{9,11},{10,... | collective-permute-start | bytes 442376 | tf_op jit(solution)/shard_map/ppermute | solution.py:294
  12.5 1.2 %collective-permute-start.2 = (bf16[2,96,384]{2,1,0:T(8,128)(2,1)S(1)}, bf16[2,96,384]{2,1,0:T(8,128)(2,1)S(1)}, u32[]{:S(2)}, u32[]{:S(2)}) collective-permute-start(bf16[2,96,384]{2,1,0:T(8,128)(2,1)S(1)} %get-tuple-element.42), channel_id=1, source_target_pairs={{0,3},{1,0},{2,1},{3,2},{4,7},{5,4},{6,5},{7,6},{8,11},{9,8},{10,9... | collective-permute-start | bytes 442376 | tf_op jit(solution)/shard_map/ppermute | solution.py:294
  13.7 0.8 tables.1
  14.5 2.5 %all-to-all-done.got_ref = bf16[16,96,128]{2,1,0:T(8,128)(2,1)S(1)} async-done(((bf16[16,96,128]{2,1,0:T(8,128)(2,1)}), bf16[16,96,128]{2,1,0:T(8,128)(2,1)S(1)}, u32[]{:S(2)}, u32[]{:S(2)}) %all-to-all-start) | async-done | bytes 393248 | tf_op jit(solution)/shard_map/all_to_all | solution.py:278
  17.0 0.1 shard_map.67
  17.1 2.5 %collective-permute-start.10 = (bf16[2,384,128]{2,1,0:T(8,128)(2,1)S(1)}, bf16[2,384,128]{2,1,0:T(8,128)(2,1)S(1)}, u32[]{:S(2)}, u32[]{:S(2)}) collective-permute-start(bf16[2,384,128]{2,1,0:T(8,128)(2,1)S(1)} %get-tuple-element.57), channel_id=1, source_target_pairs={{0,240},{16,0},{32,16},{48,32},{64,48},{80,64},{96,80},{112,96},{1... | collective-permute-start | bytes 589832 | tf_op jit(solution)/shard_map/ppermute | solution.py:274
  19.6 2.8 %collective-permute-start.9 = (bf16[2,384,128]{2,1,0:T(8,128)(2,1)S(1)}, bf16[2,384,128]{2,1,0:T(8,128)(2,1)S(1)}, u32[]{:S(2)}, u32[]{:S(2)}) collective-permute-start(bf16[2,384,128]{2,1,0:T(8,128)(2,1)S(1)} %get-tuple-element.56), channel_id=1, source_target_pairs={{0,16},{16,32},{32,48},{48,64},{64,80},{80,96},{96,112},{112,128},... | collective-permute-start | bytes 589832 | tf_op jit(solution)/shard_map/ppermute | solution.py:273
  22.4 0.0 collective-permute-done.refs_1_
  22.4 0.1 collective-permute-done.1.refs_2_
  22.5 0.2 collective-permute-done.2.refs_3_
  22.7 0.1 shard_map.65
  22.9 1.4 %collective-permute-start.3 = (bf16[216,384]{1,0:T(8,128)(2,1)S(1)}, bf16[216,384]{1,0:T(8,128)(2,1)S(1)}, u32[]{:S(2)}, u32[]{:S(2)}) collective-permute-start(bf16[216,384]{1,0:T(8,128)(2,1)S(1)} %get-tuple-element.46), channel_id=1, source_target_pairs={{0,4},{1,5},{2,6},{3,7},{4,8},{5,9},{6,10},{7,11},{8,12},{9,13},{1... | collective-permute-start | bytes 497672 | tf_op jit(solution)/shard_map/ppermute | solution.py:294
  24.3 2.5 %collective-permute-start.4 = (bf16[216,384]{1,0:T(8,128)(2,1)S(1)}, bf16[216,384]{1,0:T(8,128)(2,1)S(1)}, u32[]{:S(2)}, u32[]{:S(2)}) collective-permute-start(bf16[216,384]{1,0:T(8,128)(2,1)S(1)} %get-tuple-element.47), channel_id=1, source_target_pairs={{0,8},{1,9},{2,10},{3,11},{4,12},{5,13},{6,14},{7,15},{8,0},{9,1},... | collective-permute-start | bytes 497672 | tf_op jit(solution)/shard_map/ppermute | solution.py:294
  26.8 1.0 %collective-permute-start.5 = (bf16[216,384]{1,0:T(8,128)(2,1)S(1)}, bf16[216,384]{1,0:T(8,128)(2,1)S(1)}, u32[]{:S(2)}, u32[]{:S(2)}) collective-permute-start(bf16[216,384]{1,0:T(8,128)(2,1)S(1)} %get-tuple-element.48), channel_id=1, source_target_pairs={{0,12},{1,13},{2,14},{3,15},{4,0},{5,1},{6,2},{7,3},{8,4},{9,5},{1... | collective-permute-start | bytes 497672 | tf_op jit(solution)/shard_map/ppermute | solution.py:294
  27.8 0.6 collective-permute-done.3.refs_1_
  28.3 5.3 %collective-permute-done.4.refs_2_ = bf16[216,384]{1,0:T(8,128)(2,1)S(1)} collective-permute-done((bf16[216,384]{1,0:T(8,128)(2,1)S(1)}, bf16[216,384]{1,0:T(8,128)(2,1)S(1)}, u32[]{:S(2)}, u32[]{:S(2)}) %collective-permute-start.4) | collective-permute-done | bytes 165920 | tf_op jit(solution)/shard_map/ppermute | solution.py:294
  33.6 0.0 collective-permute-done.5.refs_3_
  33.6 0.6 shard_map.68.refs_4_
  34.2 0.0 collective-permute-done.10.refs_6_
  34.2 0.0 collective-permute-done.9.refs_5_
  34.2 0.8 shard_map.69
  35.1 15.7 %all_to_all.15.got_ref = bf16[16,96,128]{2,1,0:T(8,128)(2,1)S(1)} all-to-all(bf16[16,96,128]{2,1,0:T(8,128)(2,1)S(1)} %get-tuple-element.58), channel_id=1, replica_groups=mesh['lead'=16,'grp'=16] {'grp'}, dimensions={0} | all-to-all | bytes 786432 | tf_op jit(solution)/shard_map/all_to_all | solution.py:278
  50.7 0.1 shard_map.70
  50.8 4.5 %collective-permute-start.11 = (bf16[2,384,128]{2,1,0:T(8,128)(2,1)S(1)}, bf16[2,384,128]{2,1,0:T(8,128)(2,1)S(1)}, u32[]{:S(2)}, u32[]{:S(2)}) collective-permute-start(bf16[2,384,128]{2,1,0:T(8,128)(2,1)S(1)} %get-tuple-element.60), channel_id=1, source_target_pairs={{0,16},{16,32},{32,48},{48,64},{64,80},{80,96},{96,112},{112,128},... | collective-permute-start | bytes 589832 | tf_op jit(solution)/shard_map/ppermute | solution.py:273
  55.4 0.0 collective-permute-start.12
  55.4 0.6 shard_map.71.refs_4_
  55.9 2.0 %collective-permute-done.11.refs_5_ = bf16[2,384,128]{2,1,0:T(8,128)(2,1)S(1)} collective-permute-done((bf16[2,384,128]{2,1,0:T(8,128)(2,1)S(1)}, bf16[2,384,128]{2,1,0:T(8,128)(2,1)S(1)}, u32[]{:S(2)}, u32[]{:S(2)}) %collective-permute-start.11) | collective-permute-done | bytes 196640 | tf_op jit(solution)/shard_map/ppermute | solution.py:273
  58.0 3.7 %collective-permute-done.12.refs_6_ = bf16[2,384,128]{2,1,0:T(8,128)(2,1)S(1)} collective-permute-done((bf16[2,384,128]{2,1,0:T(8,128)(2,1)S(1)}, bf16[2,384,128]{2,1,0:T(8,128)(2,1)S(1)}, u32[]{:S(2)}, u32[]{:S(2)}) %collective-permute-start.12) | collective-permute-done | bytes 196640 | tf_op jit(solution)/shard_map/ppermute | solution.py:274
  61.7 0.8 shard_map.72
  62.5 12.0 %all_to_all.16.got_ref.refs_7_ = bf16[16,120,128]{2,1,0:T(8,128)(2,1)S(1)} all-to-all(bf16[16,120,128]{2,1,0:T(8,128)(2,1)S(1)} %shard_map.72), channel_id=1, replica_groups=mesh['lead'=16,'grp'=16] {'grp'}, dimensions={0} | all-to-all | bytes 983040 | tf_op jit(solution)/shard_map/all_to_all | solution.py:278
  74.5 0.1 shard_map.73
  74.6 2.9 %collective-permute-start.13 = (bf16[2,384,128]{2,1,0:T(8,128)(2,1)S(1)}, bf16[2,384,128]{2,1,0:T(8,128)(2,1)S(1)}, u32[]{:S(2)}, u32[]{:S(2)}) collective-permute-start(bf16[2,384,128]{2,1,0:T(8,128)(2,1)S(1)} %get-tuple-element.66), channel_id=1, source_target_pairs={{0,16},{16,32},{32,48},{48,64},{64,80},{80,96},{96,112},{112,128},... | collective-permute-start | bytes 589832 | tf_op jit(solution)/shard_map/ppermute | solution.py:273
  77.6 0.0 collective-permute-start.14
  77.6 0.1 shard_map.66
  77.7 0.1 collective-permute-start.6
  77.8 2.0 %collective-permute-start.7 = (bf16[8,24,384]{2,1,0:T(8,128)(2,1)S(1)}, bf16[8,24,384]{2,1,0:T(8,128)(2,1)S(1)}, u32[]{:S(2)}, u32[]{:S(2)}) collective-permute-start(bf16[8,24,384]{2,1,0:T(8,128)(2,1)S(1)} %get-tuple-element.51), channel_id=1, source_target_pairs={{0,8},{1,9},{2,10},{3,11},{4,12},{5,13},{6,14},{7,15},{8,0},{9,1},... | collective-permute-start | bytes 442376 | tf_op jit(solution)/shard_map/ppermute | solution.py:294
  79.8 0.8 collective-permute-start.8
  80.6 5.2 %collective-permute-done.6.refs_1_ = bf16[8,24,384]{2,1,0:T(8,128)(2,1)S(1)} collective-permute-done((bf16[8,24,384]{2,1,0:T(8,128)(2,1)S(1)}, bf16[8,24,384]{2,1,0:T(8,128)(2,1)S(1)}, u32[]{:S(2)}, u32[]{:S(2)}) %collective-permute-start.6) | collective-permute-done | bytes 147488 | tf_op jit(solution)/shard_map/ppermute | solution.py:294
  85.8 0.0 collective-permute-done.7.refs_2_
  85.8 0.9 collective-permute-done.8.refs_3_
  86.6 0.0 collective-permute-done.13.refs_5_
  86.6 0.0 collective-permute-done.14.refs_6_
  86.6 1.0 %shard_map.74 = f32[96,128]{1,0:T(8,128)} custom-call(s32[4,8]{1,0:T(4,128)S(4)} %get-tuple-element.37.cols_ref, bf16[8,24,384]{2,1,0:T(8,128)(2,1)S(1)} %get-tuple-element.49.refs_0_, bf16[8,24,384]{2,1,0:T(8,128)(2,1)S(1)} %collective-permute-done.6.refs_1_, bf16[8,24,384]{2,1,0:T(8,128)(2,1)S(1)} %collective-permute-done.7.refs_2_, ...), custom_call_target="tpu_custom_call" | custom-call | tf_op jit(solution)/shard_map/pallas_call | solution.py:248
Async XLA Ops:
  2.0 15.1 %all-to-all-start = ((bf16[16,96,128]{2,1,0:T(8,128)(2,1)}), bf16[16,96,128]{2,1,0:T(8,128)(2,1)S(1)}, u32[]{:S(2)}, u32[]{:S(2)}) async-start(bf16[16,96,128]{2,1,0:T(8,128)(2,1)} %get-tuple-element.54), calls=%async_computation | async-start | bytes 786432 | tf_op jit(solution)/shard_map/all_to_all | solution.py:278
  8.8 13.6 %collective-permute-start = (bf16[2,96,384]{2,1,0:T(8,128)(2,1)S(1)}, bf16[2,96,384]{2,1,0:T(8,128)(2,1)S(1)}, u32[]{:S(2)}, u32[]{:S(2)}) collective-permute-start(bf16[2,96,384]{2,1,0:T(8,128)(2,1)S(1)} %get-tuple-element.40), channel_id=1, source_target_pairs={{0,1},{1,2},{2,3},{3,0},{4,5},{5,6},{6,7},{7,4},{8,9},{9,10},{10,1... | collective-permute-start | bytes 442376 | tf_op jit(solution)/shard_map/ppermute | solution.py:294
  10.1 12.4 %collective-permute-start.1 = (bf16[2,96,384]{2,1,0:T(8,128)(2,1)S(1)}, bf16[2,96,384]{2,1,0:T(8,128)(2,1)S(1)}, u32[]{:S(2)}, u32[]{:S(2)}) collective-permute-start(bf16[2,96,384]{2,1,0:T(8,128)(2,1)S(1)} %get-tuple-element.41), channel_id=1, source_target_pairs={{0,2},{1,3},{2,0},{3,1},{4,6},{5,7},{6,4},{7,5},{8,10},{9,11},{10,... | collective-permute-start | bytes 442376 | tf_op jit(solution)/shard_map/ppermute | solution.py:294
  12.5 10.2 %collective-permute-start.2 = (bf16[2,96,384]{2,1,0:T(8,128)(2,1)S(1)}, bf16[2,96,384]{2,1,0:T(8,128)(2,1)S(1)}, u32[]{:S(2)}, u32[]{:S(2)}) collective-permute-start(bf16[2,96,384]{2,1,0:T(8,128)(2,1)S(1)} %get-tuple-element.42), channel_id=1, source_target_pairs={{0,3},{1,0},{2,1},{3,2},{4,7},{5,4},{6,5},{7,6},{8,11},{9,8},{10,9... | collective-permute-start | bytes 442376 | tf_op jit(solution)/shard_map/ppermute | solution.py:294
  17.1 17.1 %collective-permute-start.10 = (bf16[2,384,128]{2,1,0:T(8,128)(2,1)S(1)}, bf16[2,384,128]{2,1,0:T(8,128)(2,1)S(1)}, u32[]{:S(2)}, u32[]{:S(2)}) collective-permute-start(bf16[2,384,128]{2,1,0:T(8,128)(2,1)S(1)} %get-tuple-element.57), channel_id=1, source_target_pairs={{0,240},{16,0},{32,16},{48,32},{64,48},{80,64},{96,80},{112,96},{1... | collective-permute-start | bytes 589832 | tf_op jit(solution)/shard_map/ppermute | solution.py:274
  19.6 14.6 %collective-permute-start.9 = (bf16[2,384,128]{2,1,0:T(8,128)(2,1)S(1)}, bf16[2,384,128]{2,1,0:T(8,128)(2,1)S(1)}, u32[]{:S(2)}, u32[]{:S(2)}) collective-permute-start(bf16[2,384,128]{2,1,0:T(8,128)(2,1)S(1)} %get-tuple-element.56), channel_id=1, source_target_pairs={{0,16},{16,32},{32,48},{48,64},{64,80},{80,96},{96,112},{112,128},... | collective-permute-start | bytes 589832 | tf_op jit(solution)/shard_map/ppermute | solution.py:273
  22.9 5.5 %collective-permute-start.3 = (bf16[216,384]{1,0:T(8,128)(2,1)S(1)}, bf16[216,384]{1,0:T(8,128)(2,1)S(1)}, u32[]{:S(2)}, u32[]{:S(2)}) collective-permute-start(bf16[216,384]{1,0:T(8,128)(2,1)S(1)} %get-tuple-element.46), channel_id=1, source_target_pairs={{0,4},{1,5},{2,6},{3,7},{4,8},{5,9},{6,10},{7,11},{8,12},{9,13},{1... | collective-permute-start | bytes 497672 | tf_op jit(solution)/shard_map/ppermute | solution.py:294
  24.3 9.3 %collective-permute-start.4 = (bf16[216,384]{1,0:T(8,128)(2,1)S(1)}, bf16[216,384]{1,0:T(8,128)(2,1)S(1)}, u32[]{:S(2)}, u32[]{:S(2)}) collective-permute-start(bf16[216,384]{1,0:T(8,128)(2,1)S(1)} %get-tuple-element.47), channel_id=1, source_target_pairs={{0,8},{1,9},{2,10},{3,11},{4,12},{5,13},{6,14},{7,15},{8,0},{9,1},... | collective-permute-start | bytes 497672 | tf_op jit(solution)/shard_map/ppermute | solution.py:294
  26.8 6.9 %collective-permute-start.5 = (bf16[216,384]{1,0:T(8,128)(2,1)S(1)}, bf16[216,384]{1,0:T(8,128)(2,1)S(1)}, u32[]{:S(2)}, u32[]{:S(2)}) collective-permute-start(bf16[216,384]{1,0:T(8,128)(2,1)S(1)} %get-tuple-element.48), channel_id=1, source_target_pairs={{0,12},{1,13},{2,14},{3,15},{4,0},{5,1},{6,2},{7,3},{8,4},{9,5},{1... | collective-permute-start | bytes 497672 | tf_op jit(solution)/shard_map/ppermute | solution.py:294
  50.8 7.1 %collective-permute-start.11 = (bf16[2,384,128]{2,1,0:T(8,128)(2,1)S(1)}, bf16[2,384,128]{2,1,0:T(8,128)(2,1)S(1)}, u32[]{:S(2)}, u32[]{:S(2)}) collective-permute-start(bf16[2,384,128]{2,1,0:T(8,128)(2,1)S(1)} %get-tuple-element.60), channel_id=1, source_target_pairs={{0,16},{16,32},{32,48},{48,64},{64,80},{80,96},{96,112},{112,128},... | collective-permute-start | bytes 589832 | tf_op jit(solution)/shard_map/ppermute | solution.py:273
  55.4 6.3 %collective-permute-start.12 = (bf16[2,384,128]{2,1,0:T(8,128)(2,1)S(1)}, bf16[2,384,128]{2,1,0:T(8,128)(2,1)S(1)}, u32[]{:S(2)}, u32[]{:S(2)}) collective-permute-start(bf16[2,384,128]{2,1,0:T(8,128)(2,1)S(1)} %get-tuple-element.61), channel_id=1, source_target_pairs={{0,240},{16,0},{32,16},{48,32},{64,48},{80,64},{96,80},{112,96},{1... | collective-permute-start | bytes 589832 | tf_op jit(solution)/shard_map/ppermute | solution.py:274
  74.6 12.0 %collective-permute-start.13 = (bf16[2,384,128]{2,1,0:T(8,128)(2,1)S(1)}, bf16[2,384,128]{2,1,0:T(8,128)(2,1)S(1)}, u32[]{:S(2)}, u32[]{:S(2)}) collective-permute-start(bf16[2,384,128]{2,1,0:T(8,128)(2,1)S(1)} %get-tuple-element.66), channel_id=1, source_target_pairs={{0,16},{16,32},{32,48},{48,64},{64,80},{80,96},{96,112},{112,128},... | collective-permute-start | bytes 589832 | tf_op jit(solution)/shard_map/ppermute | solution.py:273
  77.6 9.1 %collective-permute-start.14 = (bf16[2,384,128]{2,1,0:T(8,128)(2,1)S(1)}, bf16[2,384,128]{2,1,0:T(8,128)(2,1)S(1)}, u32[]{:S(2)}, u32[]{:S(2)}) collective-permute-start(bf16[2,384,128]{2,1,0:T(8,128)(2,1)S(1)} %get-tuple-element.67), channel_id=1, source_target_pairs={{0,240},{16,0},{32,16},{48,32},{64,48},{80,64},{96,80},{112,96},{1... | collective-permute-start | bytes 589832 | tf_op jit(solution)/shard_map/ppermute | solution.py:274
  77.7 8.1 %collective-permute-start.6 = (bf16[8,24,384]{2,1,0:T(8,128)(2,1)S(1)}, bf16[8,24,384]{2,1,0:T(8,128)(2,1)S(1)}, u32[]{:S(2)}, u32[]{:S(2)}) collective-permute-start(bf16[8,24,384]{2,1,0:T(8,128)(2,1)S(1)} %get-tuple-element.50), channel_id=1, source_target_pairs={{0,4},{1,5},{2,6},{3,7},{4,8},{5,9},{6,10},{7,11},{8,12},{9,13},{1... | collective-permute-start | bytes 442376 | tf_op jit(solution)/shard_map/ppermute | solution.py:294
  77.8 8.0 %collective-permute-start.7 = (bf16[8,24,384]{2,1,0:T(8,128)(2,1)S(1)}, bf16[8,24,384]{2,1,0:T(8,128)(2,1)S(1)}, u32[]{:S(2)}, u32[]{:S(2)}) collective-permute-start(bf16[8,24,384]{2,1,0:T(8,128)(2,1)S(1)} %get-tuple-element.51), channel_id=1, source_target_pairs={{0,8},{1,9},{2,10},{3,11},{4,12},{5,13},{6,14},{7,15},{8,0},{9,1},... | collective-permute-start | bytes 442376 | tf_op jit(solution)/shard_map/ppermute | solution.py:294
  79.8 6.8 %collective-permute-start.8 = (bf16[8,24,384]{2,1,0:T(8,128)(2,1)S(1)}, bf16[8,24,384]{2,1,0:T(8,128)(2,1)S(1)}, u32[]{:S(2)}, u32[]{:S(2)}) collective-permute-start(bf16[8,24,384]{2,1,0:T(8,128)(2,1)S(1)} %get-tuple-element.52), channel_id=1, source_target_pairs={{0,12},{1,13},{2,14},{3,15},{4,0},{5,1},{6,2},{7,3},{8,4},{9,5},{1... | collective-permute-start | bytes 442376 | tf_op jit(solution)/shard_map/ppermute | solution.py:294

commit v10 on v9

--- a/solution.py
+++ b/solution.py
@@ -43,7 +43,7 @@
 
 
 def start_kernel(tiles_hbm, residual_hbm, diag_hbm, part0, part1, part2, part3, wide_ref, start_ref, scale_ref,
-                 line_ref, residual_ref, diag_ref, sems):
+                 line_ref, residual_ref, diag_ref, high_ref, sems):
     _, q = place()
     copies = [pltpu.make_async_copy(residual_hbm, residual_ref, sems.at[0]),
               pltpu.make_async_copy(diag_hbm, diag_ref, sems.at[1])]
@@ -62,8 +62,11 @@
     scaled = residual_ref[...] * scale
     scale_ref[...] = scale
     start_ref[...] = scaled
-    spread(scaled, wide_ref)
-    for copy in copies[2:]:
+    high_ref[...] = scaled.astype(BF16)
+    pieces = [pltpu.make_async_copy(high_ref, wide_ref.at[m], sems.at[6 + m]) for m in range(GROUP)]
+    for piece in pieces:
+        piece.start()
+    for copy in copies[2:] + pieces:
         copy.wait()
 
 
@@ -163,21 +166,35 @@
     return jnp.concatenate([part[0:192] for part in parts], axis=0)
 
 
-def near_kernel(*refs):
-    own_ref, product_ref = refs[4:]
-    slab_products(all_slabs(refs[:4]), [own_ref[r] for r in range(SIDE)], product_ref, 0)
-
-
-def slab_total(slot_ref, cols_ref, parts, near_ref, low_ref, high_ref, product_ref, total_ref):
+def add_up(slot_ref, cols_ref, block_of, product_ref, total_ref):
     x, _ = place()
-    slab_products(all_slabs(parts), [low_ref[0], low_ref[1], high_ref[0], high_ref[1]], product_ref, 4)
-    product_ref[0:4] = near_ref[...]
-    total_ref[...] = jnp.zeros_like(total_ref)
+    product_ref[0] = jnp.zeros((TILES * SLAB, NRHS), F32)
     for t in range(TILES):
         slot = slot_of(slot_ref, x, t // 8, t % 8)
         row = lax.shift_right_logical(slot, 3)
-        col = cols_ref[row, lax.bitwise_and(slot, 7)]
-        total_ref[row] += product_ref[col, SLAB * t:SLAB * (t + 1)]
+        block = block_of(cols_ref[row, lax.bitwise_and(slot, 7)])
+        total_ref[row] += product_ref[block, SLAB * t:SLAB * (t + 1)]
+
+
+def own_block(col):
+    return jnp.where(col < 4, col + 1, 0)
+
+
+def halo_block(col):
+    return jnp.maximum(col - 3, 0)
+
+
+def near_kernel(slot_ref, cols_ref, *refs):
+    own_ref, total_ref, product_ref = refs[4:]
+    slab_products(all_slabs(refs[:4]), [own_ref[r] for r in range(SIDE)], product_ref, 1)
+    total_ref[...] = jnp.zeros_like(total_ref)
+    add_up(slot_ref, cols_ref, own_block, product_ref, total_ref)
+
+
+def slab_total(slot_ref, cols_ref, parts, near_ref, low_ref, high_ref, product_ref, total_ref):
+    slab_products(all_slabs(parts), [low_ref[0], low_ref[1], high_ref[0], high_ref[1]], product_ref, 1)
+    total_ref[...] = near_ref[...]
+    add_up(slot_ref, cols_ref, halo_block, product_ref, total_ref)
 
 
 def first_kernel(slot_ref, cols_ref, *refs):
@@ -216,36 +233,49 @@
             wide_ref[SIDE * r + s, SHARE:120] = rests[r]
 
 
-def last_kernel(cols_ref, *refs):
-    parts, halo, (got_ref, first_ref, scale_ref, out_ref, ext_ref, line_ref) = refs[:4], refs[4:7], refs[7:]
-    own_ref, low_ref, high_ref = halo
-    x, q = place()
-    ext_ref[0:4] = own_ref[...]
-    ext_ref[4:6] = low_ref[...]
-    ext_ref[6:8] = high_ref[...]
+def home_total(cols_ref, block_of, parts, ext_ref, line_ref):
+    x, _ = place()
+    ext_ref[0] = jnp.zeros((TILE, NRHS), BF16)
     total = jnp.zeros((SHARE, NRHS), F32)
     for k in range(8):
         left = jnp.concatenate([part[k] for part in parts], axis=0)
-        total += jnp.dot(left, ext_ref[cols_ref[x, k]], preferred_element_type=F32)
+        total += jnp.dot(left, ext_ref[block_of(cols_ref[x, k])], preferred_element_type=F32)
     for k in range(SIDE):
         line_ref[pl.ds(pl.multiple_of(wrap(x - k) * SLAB, 8), SLAB), :] = total[SLAB * k:SLAB * (k + 1)]
+    return line_ref[...]
+
+
+def third_kernel(cols_ref, *refs):
+    parts, (own_ref, got_ref, first_ref, scale_ref, sum_ref, ext_ref, line_ref) = refs[:4], refs[4:]
+    x, q = place()
+    ext_ref[1:5] = own_ref[...]
+    total = home_total(cols_ref, own_block, parts, ext_ref, line_ref)
     mine = pl.ds(pl.multiple_of(q * SHARE, SHARE), SHARE)
     rest = jnp.concatenate([got_ref[SIDE * s + q, SHARE:120].astype(F32) for s in range(SIDE)], axis=0)
-    second = own_ref[x, mine].astype(F32) - scale_ref[...] * line_ref[...]
-    out_ref[...] = first_ref[x, mine].astype(F32) + rest + GAIN * second
+    second = own_ref[x, mine].astype(F32) - scale_ref[...] * total
+    sum_ref[...] = first_ref[x, mine].astype(F32) + rest + GAIN * second
+
+
+def last_kernel(cols_ref, *refs):
+    parts, (low_ref, high_ref, sum_ref, scale_ref, out_ref, ext_ref, line_ref) = refs[:4], refs[4:]
+    ext_ref[1:3] = low_ref[...]
+    ext_ref[3:5] = high_ref[...]
+    total = home_total(cols_ref, halo_block, parts, ext_ref, line_ref)
+    out_ref[...] = sum_ref[...] - GAIN * (scale_ref[...] * total)
 
 
 def arr(shape, dtype):
     return pltpu.VMEM(shape, dtype)
 
 
-def call(kernel, args, outs, scalars=0, scratch=(), far=0):
+def call(kernel, args, outs, scalars=0, scratch=(), far=0, away=()):
     vectors = args[scalars:]
     space = pltpu.HBM if far else pltpu.VMEM
     vectors = [pltpu.with_memory_space_constraint(a, space) for a in vectors]
     specs = [SMEM] * scalars + [pl.BlockSpec(memory_space=space)] * len(vectors)
     tables = [pltpu.with_memory_space_constraint(a, pltpu.SMEM) for a in args[:scalars]]
-    return pl.pallas_call(kernel, in_specs=specs, out_specs=[VMEM] * len(outs),
+    return pl.pallas_call(kernel, in_specs=specs,
+                          out_specs=[pl.BlockSpec(memory_space=pltpu.HBM) if n in away else VMEM for n in range(len(outs))],
                           out_shape=outs, scratch_shapes=list(scratch),
                           compiler_params=pltpu.CompilerParams(vmem_limit_bytes=GRANT))(*tables, *vectors)
 
@@ -257,11 +287,10 @@
 HALVES = [arr((2, TILE, NRHS), BF16), arr((2, TILE, NRHS), BF16)]
 OWN = arr((SIDE, TILE, NRHS), BF16)
 ROWS = arr((SHARE, NRHS), F32)
-EXT = arr((8, TILE, NRHS), BF16)
+EXT = arr((5, TILE, NRHS), BF16)
 SLABS = arr((SIDE, SLAB, NRHS), F32)
 WIDE = arr((GROUP, SHARE, NRHS), BF16)
-NEAR = arr((4, TILES * SLAB, NRHS), F32)
-WORK = (arr((8, TILES * SLAB, NRHS), F32), SLABS)
+WORK = (arr((5, TILES * SLAB, NRHS), F32), SLABS)
 
 
 def body(matrix_tiles, tile_slot, tile_cols, send_rows, residual, diag_inv):
@@ -296,8 +325,9 @@
 
     *quarters, wide, start, scale, line = call(
         start_kernel, [matrix_tiles, residual, diag],
-        [arr((2, SHARE, TILE), BF16)] * 4 + [WIDE, ROWS, ROWS, arr((8, TILE), F32)],
-        scratch=(ROWS, arr((1, SHARE), F32), pltpu.SemaphoreType.DMA((6,))), far=1)
+        [arr((2, SHARE, TILE), BF16)] * 4 + [pltpu.HBM((GROUP, SHARE, NRHS), BF16), ROWS, ROWS, arr((8, TILE), F32)],
+        scratch=(ROWS, arr((1, SHARE), F32), arr((SHARE, NRHS), BF16), pltpu.SemaphoreType.DMA((6 + GROUP,))), far=1,
+        away=(4,))
     tables = [pltpu.SMEM((1, TILES), jnp.int32), pltpu.SMEM((SIDE, 8), jnp.int32), pltpu.SMEM((2, 2), jnp.int32)]
     tile_slot, tile_cols, rows = pl.pallas_call(
         table_kernel, name="tables", in_specs=[SMEM] * 3, out_specs=[SMEM] * 3, out_shape=tables)(
@@ -311,19 +341,20 @@
     halos = halo(up, down)
     ordered = call(order_kernel, [tile_slot] + near(*slabs), [arr((8, SLAB, TILE), BF16)] * 4, 1,
                    (arr((TILES, SLAB, TILE), BF16),))
-    product, = call(near_kernel, near(*slabs, own), [NEAR])
+    product, = call(near_kernel, [tile_slot, tile_cols] + near(*slabs, own), [SLABS], 2, WORK[:1])
     wide, *state = call(first_kernel, [tile_slot, tile_cols] + near(*slabs, product, *halos),
                         [WIDE] + [SLABS] * 3, 2, WORK)
     first, up, down = choose(pick_slab_kernel, gather(wide))
     halos = halo(up, down)
     parts = along_x(ordered)
-    product, = call(near_kernel, near(*slabs, first), [NEAR])
+    product, = call(near_kernel, [tile_slot, tile_cols] + near(*slabs, first), [SLABS], 2, WORK[:1])
     wide, = call(second_kernel, [tile_slot, tile_cols] + near(*slabs, product, *halos, *state),
                  [arr((GROUP, 120, NRHS), BF16)], 2, WORK)
     got = gather(wide)
     own, up, down = choose(pick_slab_kernel, got)
     halos = halo(up, down)
-    result, = call(last_kernel, [tile_cols] + near(*parts, own, *halos, got, first, scale),
+    partial, = call(third_kernel, [tile_cols] + near(*parts, own, got, first, scale), [ROWS], 1, (EXT, ROWS))
+    result, = call(last_kernel, [tile_cols] + near(*parts, *halos, partial, scale),
                    [jax.ShapeDtypeStruct((SHARE, NRHS), F32)], 1, (EXT, ROWS))
     return result
 

time: 88.3 us -> 88.6 us (level)
    ppermute x3, starting transfers between devices: 2.52 us -> 0.01 us  [halo(): lax.ppermute(down, 'lead', [(i, (i - 1) % leads) for i in range(leads)])]
    ppermute x3, starting transfers between devices: 10.2 us -> 12.7 us  [halo(): lax.ppermute(up, 'lead', [(i, (i + 1) % leads) for i in range(leads)])]
    pallas_call x11 -> x12, Pallas kernels: 6.28 us -> 6.74 us  [call(): pl.pallas_call(kernel, in_specs=specs, out_specs=[pl.BlockSpec(memory_spa...]
where the time goes in v10:
time: 88.6 us; the launch traced here: 87.9 us
  starting transfers between devices  32.2 us (36%)
  blocking collectives  27.7 us (31%)
  waiting for transfers between devices  20.4 us (23%)
  Pallas kernels  7.54 us (9%)
    all_to_all x2, blocking collectives, gather(): return lax.all_to_all(wide, 'grp', 0, 0)  27.7 us
    ppermute x9, starting transfers between devices, exchange(): out.append(lax.ppermute(values[k], 'grp', pairs[k]))  12.8 us
    ppermute x3, starting transfers between devices, halo(): lax.ppermute(up, 'lead', [(i, (i + 1) % leads) for i in range(leads)])  12.7 us
    ppermute x9, waiting for transfers between devices, exchange(): out.append(lax.ppermute(values[k], 'grp', pairs[k]))  12.3 us
    all_to_all x1, starting transfers between devices, gather(): return lax.all_to_all(wide, 'grp', 0, 0)  6.77 us
    pallas_call x12, Pallas kernels, call(): pl.pallas_call(kernel, in_specs=specs, out_specs=[pl.BlockSpec(memory_spa...  6.74 us
    ppermute x3, waiting for transfers between devices, halo(): lax.ppermute(down, 'lead', [(i, (i - 1) % leads) for i in range(leads)])  3.7 us
    all_to_all x1, waiting for transfers between devices, gather(): return lax.all_to_all(wide, 'grp', 0, 0)  2.53 us
  transfers between devices with their start and end apart: 16, of which 9 were waited for; matrix products, arithmetic and copies ran while one was open for 0% of the time, Pallas kernels for 3%

profile of v10, /device:TPU:97, one launch (start us, length us, event | category | flops | bytes accessed | tf_op | source)
XLA Modules:
  0.0 87.9 jit_solution(14946154642206818155)
XLA Ops:
  0.0 1.8 %shard_map.64 = (bf16[2,96,384]{2,1,0:T(8,128)(2,1)S(1)}, bf16[2,96,384]{2,1,0:T(8,128)(2,1)S(1)}, bf16[2,96,384]{2,1,0:T(8,128)(2,1)S(1)}, bf16[2,96,384]{2,1,0...) custom-call(bf16[2,384,384]{2,1,0:T(8,128)(2,1)} %tiles_hbm.1, ...), custom_call_target="tpu_custom_call" | custom-call | tf_op jit(solution)/shard_map/pallas_call | solution.py:277
  1.8 6.8 %all-to-all-start = ((bf16[16,96,128]{2,1,0:T(8,128)(2,1)}), bf16[16,96,128]{2,1,0:T(8,128)(2,1)S(1)}, u32[]{:S(2)}, u32[]{:S(2)}) async-start(bf16[16,96,128]{2,1,0:T(8,128)(2,1)} %get-tuple-element.54), calls=%async_computation | async-start | bytes 786432 | tf_op jit(solution)/shard_map/all_to_all | solution.py:307
  8.6 1.4 %collective-permute-start = (bf16[2,96,384]{2,1,0:T(8,128)(2,1)S(1)}, bf16[2,96,384]{2,1,0:T(8,128)(2,1)S(1)}, u32[]{:S(2)}, u32[]{:S(2)}) collective-permute-start(bf16[2,96,384]{2,1,0:T(8,128)(2,1)S(1)} %get-tuple-element.40), channel_id=1, source_target_pairs={{0,1},{1,2},{2,3},{3,0},{4,5},{5,6},{6,7},{7,4},{8,9},{9,10},{10,1... | collective-permute-start | bytes 442376 | tf_op jit(solution)/shard_map/ppermute | solution.py:323
  10.0 2.4 %collective-permute-start.1 = (bf16[2,96,384]{2,1,0:T(8,128)(2,1)S(1)}, bf16[2,96,384]{2,1,0:T(8,128)(2,1)S(1)}, u32[]{:S(2)}, u32[]{:S(2)}) collective-permute-start(bf16[2,96,384]{2,1,0:T(8,128)(2,1)S(1)} %get-tuple-element.41), channel_id=1, source_target_pairs={{0,2},{1,3},{2,0},{3,1},{4,6},{5,7},{6,4},{7,5},{8,10},{9,11},{10,... | collective-permute-start | bytes 442376 | tf_op jit(solution)/shard_map/ppermute | solution.py:323
  12.4 1.2 %collective-permute-start.2 = (bf16[2,96,384]{2,1,0:T(8,128)(2,1)S(1)}, bf16[2,96,384]{2,1,0:T(8,128)(2,1)S(1)}, u32[]{:S(2)}, u32[]{:S(2)}) collective-permute-start(bf16[2,96,384]{2,1,0:T(8,128)(2,1)S(1)} %get-tuple-element.42), channel_id=1, source_target_pairs={{0,3},{1,0},{2,1},{3,2},{4,7},{5,4},{6,5},{7,6},{8,11},{9,8},{10,9... | collective-permute-start | bytes 442376 | tf_op jit(solution)/shard_map/ppermute | solution.py:323
  13.6 0.8 tables.1
  14.4 2.5 %all-to-all-done.got_ref = bf16[16,96,128]{2,1,0:T(8,128)(2,1)S(1)} async-done(((bf16[16,96,128]{2,1,0:T(8,128)(2,1)}), bf16[16,96,128]{2,1,0:T(8,128)(2,1)S(1)}, u32[]{:S(2)}, u32[]{:S(2)}) %all-to-all-start) | async-done | bytes 393248 | tf_op jit(solution)/shard_map/all_to_all | solution.py:307
  16.9 0.1 shard_map.67
  17.0 5.2 %collective-permute-start.9 = (bf16[2,384,128]{2,1,0:T(8,128)(2,1)S(1)}, bf16[2,384,128]{2,1,0:T(8,128)(2,1)S(1)}, u32[]{:S(2)}, u32[]{:S(2)}) collective-permute-start(bf16[2,384,128]{2,1,0:T(8,128)(2,1)S(1)} %get-tuple-element.56), channel_id=1, source_target_pairs={{0,16},{16,32},{32,48},{48,64},{64,80},{80,96},{96,112},{112,128},... | collective-permute-start | bytes 589832 | tf_op jit(solution)/shard_map/ppermute | solution.py:302
  22.2 0.0 collective-permute-start.10
  22.2 0.0 collective-permute-done.refs_1_
  22.2 0.2 collective-permute-done.1.refs_2_
  22.4 0.2 collective-permute-done.2.refs_3_
  22.6 0.1 shard_map.65
  22.7 1.4 %collective-permute-start.3 = (bf16[216,384]{1,0:T(8,128)(2,1)S(1)}, bf16[216,384]{1,0:T(8,128)(2,1)S(1)}, u32[]{:S(2)}, u32[]{:S(2)}) collective-permute-start(bf16[216,384]{1,0:T(8,128)(2,1)S(1)} %get-tuple-element.46), channel_id=1, source_target_pairs={{0,4},{1,5},{2,6},{3,7},{4,8},{5,9},{6,10},{7,11},{8,12},{9,13},{1... | collective-permute-start | bytes 497672 | tf_op jit(solution)/shard_map/ppermute | solution.py:323
  24.2 2.5 %collective-permute-start.4 = (bf16[216,384]{1,0:T(8,128)(2,1)S(1)}, bf16[216,384]{1,0:T(8,128)(2,1)S(1)}, u32[]{:S(2)}, u32[]{:S(2)}) collective-permute-start(bf16[216,384]{1,0:T(8,128)(2,1)S(1)} %get-tuple-element.47), channel_id=1, source_target_pairs={{0,8},{1,9},{2,10},{3,11},{4,12},{5,13},{6,14},{7,15},{8,0},{9,1},... | collective-permute-start | bytes 497672 | tf_op jit(solution)/shard_map/ppermute | solution.py:323
  26.6 1.0 %collective-permute-start.5 = (bf16[216,384]{1,0:T(8,128)(2,1)S(1)}, bf16[216,384]{1,0:T(8,128)(2,1)S(1)}, u32[]{:S(2)}, u32[]{:S(2)}) collective-permute-start(bf16[216,384]{1,0:T(8,128)(2,1)S(1)} %get-tuple-element.48), channel_id=1, source_target_pairs={{0,12},{1,13},{2,14},{3,15},{4,0},{5,1},{6,2},{7,3},{8,4},{9,5},{1... | collective-permute-start | bytes 497672 | tf_op jit(solution)/shard_map/ppermute | solution.py:323
  27.7 0.6 collective-permute-done.3.refs_1_
  28.2 5.3 %collective-permute-done.4.refs_2_ = bf16[216,384]{1,0:T(8,128)(2,1)S(1)} collective-permute-done((bf16[216,384]{1,0:T(8,128)(2,1)S(1)}, bf16[216,384]{1,0:T(8,128)(2,1)S(1)}, u32[]{:S(2)}, u32[]{:S(2)}) %collective-permute-start.4) | collective-permute-done | bytes 165920 | tf_op jit(solution)/shard_map/ppermute | solution.py:323
  33.5 0.0 collective-permute-done.5.refs_3_
  33.5 0.7 shard_map.68.refs_4_
  34.2 0.0 collective-permute-done.9.refs_5_
  34.3 0.0 collective-permute-done.10.refs_6_
  34.3 0.8 shard_map.69
  35.1 15.7 %all_to_all.15.got_ref = bf16[16,96,128]{2,1,0:T(8,128)(2,1)S(1)} all-to-all(bf16[16,96,128]{2,1,0:T(8,128)(2,1)S(1)} %get-tuple-element.58), channel_id=1, replica_groups=mesh['lead'=16,'grp'=16] {'grp'}, dimensions={0} | all-to-all | bytes 786432 | tf_op jit(solution)/shard_map/all_to_all | solution.py:307
  50.7 0.1 shard_map.70
  50.8 4.5 %collective-permute-start.11 = (bf16[2,384,128]{2,1,0:T(8,128)(2,1)S(1)}, bf16[2,384,128]{2,1,0:T(8,128)(2,1)S(1)}, u32[]{:S(2)}, u32[]{:S(2)}) collective-permute-start(bf16[2,384,128]{2,1,0:T(8,128)(2,1)S(1)} %get-tuple-element.60), channel_id=1, source_target_pairs={{0,16},{16,32},{32,48},{48,64},{64,80},{80,96},{96,112},{112,128},... | collective-permute-start | bytes 589832 | tf_op jit(solution)/shard_map/ppermute | solution.py:302
  55.4 0.0 collective-permute-start.12
  55.4 0.7 shard_map.71.refs_4_
  56.1 1.9 %collective-permute-done.11.refs_5_ = bf16[2,384,128]{2,1,0:T(8,128)(2,1)S(1)} collective-permute-done((bf16[2,384,128]{2,1,0:T(8,128)(2,1)S(1)}, bf16[2,384,128]{2,1,0:T(8,128)(2,1)S(1)}, u32[]{:S(2)}, u32[]{:S(2)}) %collective-permute-start.11) | collective-permute-done | bytes 196640 | tf_op jit(solution)/shard_map/ppermute | solution.py:302
  58.0 3.7 %collective-permute-done.12.refs_6_ = bf16[2,384,128]{2,1,0:T(8,128)(2,1)S(1)} collective-permute-done((bf16[2,384,128]{2,1,0:T(8,128)(2,1)S(1)}, bf16[2,384,128]{2,1,0:T(8,128)(2,1)S(1)}, u32[]{:S(2)}, u32[]{:S(2)}) %collective-permute-start.12) | collective-permute-done | bytes 196640 | tf_op jit(solution)/shard_map/ppermute | solution.py:303
  61.7 0.8 shard_map.72
  62.4 12.0 %all_to_all.16.got_ref.refs_5_ = bf16[16,120,128]{2,1,0:T(8,128)(2,1)S(1)} all-to-all(bf16[16,120,128]{2,1,0:T(8,128)(2,1)S(1)} %shard_map.72), channel_id=1, replica_groups=mesh['lead'=16,'grp'=16] {'grp'}, dimensions={0} | all-to-all | bytes 983040 | tf_op jit(solution)/shard_map/all_to_all | solution.py:307
  74.4 0.1 shard_map.73
  74.5 2.9 %collective-permute-start.13 = (bf16[2,384,128]{2,1,0:T(8,128)(2,1)S(1)}, bf16[2,384,128]{2,1,0:T(8,128)(2,1)S(1)}, u32[]{:S(2)}, u32[]{:S(2)}) collective-permute-start(bf16[2,384,128]{2,1,0:T(8,128)(2,1)S(1)} %get-tuple-element.65), channel_id=1, source_target_pairs={{0,16},{16,32},{32,48},{48,64},{64,80},{80,96},{96,112},{112,128},... | collective-permute-start | bytes 589832 | tf_op jit(solution)/shard_map/ppermute | solution.py:302
  77.5 0.0 collective-permute-start.14
  77.5 0.1 shard_map.66
  77.6 0.1 collective-permute-start.6
  77.7 2.0 %collective-permute-start.7 = (bf16[8,24,384]{2,1,0:T(8,128)(2,1)S(1)}, bf16[8,24,384]{2,1,0:T(8,128)(2,1)S(1)}, u32[]{:S(2)}, u32[]{:S(2)}) collective-permute-start(bf16[8,24,384]{2,1,0:T(8,128)(2,1)S(1)} %get-tuple-element.51), channel_id=1, source_target_pairs={{0,8},{1,9},{2,10},{3,11},{4,12},{5,13},{6,14},{7,15},{8,0},{9,1},... | collective-permute-start | bytes 442376 | tf_op jit(solution)/shard_map/ppermute | solution.py:323
  79.7 0.8 collective-permute-start.8
  80.5 5.2 %collective-permute-done.6.refs_1_ = bf16[8,24,384]{2,1,0:T(8,128)(2,1)S(1)} collective-permute-done((bf16[8,24,384]{2,1,0:T(8,128)(2,1)S(1)}, bf16[8,24,384]{2,1,0:T(8,128)(2,1)S(1)}, u32[]{:S(2)}, u32[]{:S(2)}) %collective-permute-start.6) | collective-permute-done | bytes 147488 | tf_op jit(solution)/shard_map/ppermute | solution.py:323
  85.7 0.0 collective-permute-done.7.refs_2_
  85.7 0.9 collective-permute-done.8.refs_3_
  86.5 0.4 shard_map.74.refs_6_
  86.9 0.0 collective-permute-done.13.refs_4_
  86.9 0.0 collective-permute-done.14.refs_5_
  86.9 1.0 %shard_map.75 = f32[96,128]{1,0:T(8,128)} custom-call(s32[4,8]{1,0:T(4,128)S(4)} %get-tuple-element.37.cols_ref, bf16[8,24,384]{2,1,0:T(8,128)(2,1)S(1)} %get-tuple-element.49.refs_0_, bf16[8,24,384]{2,1,0:T(8,128)(2,1)S(1)} %collective-permute-done.6.refs_1_, bf16[8,24,384]{2,1,0:T(8,128)(2,1)S(1)} %collective-permute-done.7.refs_2_, ...), custom_call_target="tpu_custom_call" | custom-call | tf_op jit(solution)/shard_map/pallas_call | solution.py:277
Async XLA Ops:
  1.8 15.1 %all-to-all-start = ((bf16[16,96,128]{2,1,0:T(8,128)(2,1)}), bf16[16,96,128]{2,1,0:T(8,128)(2,1)S(1)}, u32[]{:S(2)}, u32[]{:S(2)}) async-start(bf16[16,96,128]{2,1,0:T(8,128)(2,1)} %get-tuple-element.54), calls=%async_computation | async-start | bytes 786432 | tf_op jit(solution)/shard_map/all_to_all | solution.py:307
  8.6 13.6 %collective-permute-start = (bf16[2,96,384]{2,1,0:T(8,128)(2,1)S(1)}, bf16[2,96,384]{2,1,0:T(8,128)(2,1)S(1)}, u32[]{:S(2)}, u32[]{:S(2)}) collective-permute-start(bf16[2,96,384]{2,1,0:T(8,128)(2,1)S(1)} %get-tuple-element.40), channel_id=1, source_target_pairs={{0,1},{1,2},{2,3},{3,0},{4,5},{5,6},{6,7},{7,4},{8,9},{9,10},{10,1... | collective-permute-start | bytes 442376 | tf_op jit(solution)/shard_map/ppermute | solution.py:323
  10.0 12.4 %collective-permute-start.1 = (bf16[2,96,384]{2,1,0:T(8,128)(2,1)S(1)}, bf16[2,96,384]{2,1,0:T(8,128)(2,1)S(1)}, u32[]{:S(2)}, u32[]{:S(2)}) collective-permute-start(bf16[2,96,384]{2,1,0:T(8,128)(2,1)S(1)} %get-tuple-element.41), channel_id=1, source_target_pairs={{0,2},{1,3},{2,0},{3,1},{4,6},{5,7},{6,4},{7,5},{8,10},{9,11},{10,... | collective-permute-start | bytes 442376 | tf_op jit(solution)/shard_map/ppermute | solution.py:323
  12.4 10.2 %collective-permute-start.2 = (bf16[2,96,384]{2,1,0:T(8,128)(2,1)S(1)}, bf16[2,96,384]{2,1,0:T(8,128)(2,1)S(1)}, u32[]{:S(2)}, u32[]{:S(2)}) collective-permute-start(bf16[2,96,384]{2,1,0:T(8,128)(2,1)S(1)} %get-tuple-element.42), channel_id=1, source_target_pairs={{0,3},{1,0},{2,1},{3,2},{4,7},{5,4},{6,5},{7,6},{8,11},{9,8},{10,9... | collective-permute-start | bytes 442376 | tf_op jit(solution)/shard_map/ppermute | solution.py:323
  17.0 17.3 %collective-permute-start.9 = (bf16[2,384,128]{2,1,0:T(8,128)(2,1)S(1)}, bf16[2,384,128]{2,1,0:T(8,128)(2,1)S(1)}, u32[]{:S(2)}, u32[]{:S(2)}) collective-permute-start(bf16[2,384,128]{2,1,0:T(8,128)(2,1)S(1)} %get-tuple-element.56), channel_id=1, source_target_pairs={{0,16},{16,32},{32,48},{48,64},{64,80},{80,96},{96,112},{112,128},... | collective-permute-start | bytes 589832 | tf_op jit(solution)/shard_map/ppermute | solution.py:302
  22.2 12.1 %collective-permute-start.10 = (bf16[2,384,128]{2,1,0:T(8,128)(2,1)S(1)}, bf16[2,384,128]{2,1,0:T(8,128)(2,1)S(1)}, u32[]{:S(2)}, u32[]{:S(2)}) collective-permute-start(bf16[2,384,128]{2,1,0:T(8,128)(2,1)S(1)} %get-tuple-element.57), channel_id=1, source_target_pairs={{0,240},{16,0},{32,16},{48,32},{64,48},{80,64},{96,80},{112,96},{1... | collective-permute-start | bytes 589832 | tf_op jit(solution)/shard_map/ppermute | solution.py:303
  22.7 5.5 %collective-permute-start.3 = (bf16[216,384]{1,0:T(8,128)(2,1)S(1)}, bf16[216,384]{1,0:T(8,128)(2,1)S(1)}, u32[]{:S(2)}, u32[]{:S(2)}) collective-permute-start(bf16[216,384]{1,0:T(8,128)(2,1)S(1)} %get-tuple-element.46), channel_id=1, source_target_pairs={{0,4},{1,5},{2,6},{3,7},{4,8},{5,9},{6,10},{7,11},{8,12},{9,13},{1... | collective-permute-start | bytes 497672 | tf_op jit(solution)/shard_map/ppermute | solution.py:323
  24.2 9.3 %collective-permute-start.4 = (bf16[216,384]{1,0:T(8,128)(2,1)S(1)}, bf16[216,384]{1,0:T(8,128)(2,1)S(1)}, u32[]{:S(2)}, u32[]{:S(2)}) collective-permute-start(bf16[216,384]{1,0:T(8,128)(2,1)S(1)} %get-tuple-element.47), channel_id=1, source_target_pairs={{0,8},{1,9},{2,10},{3,11},{4,12},{5,13},{6,14},{7,15},{8,0},{9,1},... | collective-permute-start | bytes 497672 | tf_op jit(solution)/shard_map/ppermute | solution.py:323
  26.6 6.9 %collective-permute-start.5 = (bf16[216,384]{1,0:T(8,128)(2,1)S(1)}, bf16[216,384]{1,0:T(8,128)(2,1)S(1)}, u32[]{:S(2)}, u32[]{:S(2)}) collective-permute-start(bf16[216,384]{1,0:T(8,128)(2,1)S(1)} %get-tuple-element.48), channel_id=1, source_target_pairs={{0,12},{1,13},{2,14},{3,15},{4,0},{5,1},{6,2},{7,3},{8,4},{9,5},{1... | collective-permute-start | bytes 497672 | tf_op jit(solution)/shard_map/ppermute | solution.py:323
  50.8 7.1 %collective-permute-start.11 = (bf16[2,384,128]{2,1,0:T(8,128)(2,1)S(1)}, bf16[2,384,128]{2,1,0:T(8,128)(2,1)S(1)}, u32[]{:S(2)}, u32[]{:S(2)}) collective-permute-start(bf16[2,384,128]{2,1,0:T(8,128)(2,1)S(1)} %get-tuple-element.60), channel_id=1, source_target_pairs={{0,16},{16,32},{32,48},{48,64},{64,80},{80,96},{96,112},{112,128},... | collective-permute-start | bytes 589832 | tf_op jit(solution)/shard_map/ppermute | solution.py:302
  55.4 6.3 %collective-permute-start.12 = (bf16[2,384,128]{2,1,0:T(8,128)(2,1)S(1)}, bf16[2,384,128]{2,1,0:T(8,128)(2,1)S(1)}, u32[]{:S(2)}, u32[]{:S(2)}) collective-permute-start(bf16[2,384,128]{2,1,0:T(8,128)(2,1)S(1)} %get-tuple-element.61), channel_id=1, source_target_pairs={{0,240},{16,0},{32,16},{48,32},{64,48},{80,64},{96,80},{112,96},{1... | collective-permute-start | bytes 589832 | tf_op jit(solution)/shard_map/ppermute | solution.py:303
  74.5 12.4 %collective-permute-start.13 = (bf16[2,384,128]{2,1,0:T(8,128)(2,1)S(1)}, bf16[2,384,128]{2,1,0:T(8,128)(2,1)S(1)}, u32[]{:S(2)}, u32[]{:S(2)}) collective-permute-start(bf16[2,384,128]{2,1,0:T(8,128)(2,1)S(1)} %get-tuple-element.65), channel_id=1, source_target_pairs={{0,16},{16,32},{32,48},{48,64},{64,80},{80,96},{96,112},{112,128},... | collective-permute-start | bytes 589832 | tf_op jit(solution)/shard_map/ppermute | solution.py:302
  77.5 9.4 %collective-permute-start.14 = (bf16[2,384,128]{2,1,0:T(8,128)(2,1)S(1)}, bf16[2,384,128]{2,1,0:T(8,128)(2,1)S(1)}, u32[]{:S(2)}, u32[]{:S(2)}) collective-permute-start(bf16[2,384,128]{2,1,0:T(8,128)(2,1)S(1)} %get-tuple-element.66), channel_id=1, source_target_pairs={{0,240},{16,0},{32,16},{48,32},{64,48},{80,64},{96,80},{112,96},{1... | collective-permute-start | bytes 589832 | tf_op jit(solution)/shard_map/ppermute | solution.py:303
  77.6 8.1 %collective-permute-start.6 = (bf16[8,24,384]{2,1,0:T(8,128)(2,1)S(1)}, bf16[8,24,384]{2,1,0:T(8,128)(2,1)S(1)}, u32[]{:S(2)}, u32[]{:S(2)}) collective-permute-start(bf16[8,24,384]{2,1,0:T(8,128)(2,1)S(1)} %get-tuple-element.50), channel_id=1, source_target_pairs={{0,4},{1,5},{2,6},{3,7},{4,8},{5,9},{6,10},{7,11},{8,12},{9,13},{1... | collective-permute-start | bytes 442376 | tf_op jit(solution)/shard_map/ppermute | solution.py:323
  77.7 8.0 %collective-permute-start.7 = (bf16[8,24,384]{2,1,0:T(8,128)(2,1)S(1)}, bf16[8,24,384]{2,1,0:T(8,128)(2,1)S(1)}, u32[]{:S(2)}, u32[]{:S(2)}) collective-permute-start(bf16[8,24,384]{2,1,0:T(8,128)(2,1)S(1)} %get-tuple-element.51), channel_id=1, source_target_pairs={{0,8},{1,9},{2,10},{3,11},{4,12},{5,13},{6,14},{7,15},{8,0},{9,1},... | collective-permute-start | bytes 442376 | tf_op jit(solution)/shard_map/ppermute | solution.py:323
  79.7 6.8 %collective-permute-start.8 = (bf16[8,24,384]{2,1,0:T(8,128)(2,1)S(1)}, bf16[8,24,384]{2,1,0:T(8,128)(2,1)S(1)}, u32[]{:S(2)}, u32[]{:S(2)}) collective-permute-start(bf16[8,24,384]{2,1,0:T(8,128)(2,1)S(1)} %get-tuple-element.52), channel_id=1, source_target_pairs={{0,12},{1,13},{2,14},{3,15},{4,0},{5,1},{6,2},{7,3},{8,4},{9,5},{1... | collective-permute-start | bytes 442376 | tf_op jit(solution)/shard_map/ppermute | solution.py:323

commit v11 on v9

--- a/solution.py
+++ b/solution.py
@@ -42,7 +42,7 @@
     return jnp.concatenate([diag_ref[...], jnp.zeros((1, 128 - SHARE), F32)], axis=1)
 
 
-def start_kernel(tiles_hbm, residual_hbm, diag_hbm, part0, part1, part2, part3, wide_ref, start_ref, scale_ref,
+def start_kernel(tiles_hbm, residual_hbm, diag_hbm, part0, part1, part2, part3, high_ref, start_ref, scale_ref,
                  line_ref, residual_ref, diag_ref, sems):
     _, q = place()
     copies = [pltpu.make_async_copy(residual_hbm, residual_ref, sems.at[0]),
@@ -62,7 +62,7 @@
     scaled = residual_ref[...] * scale
     scale_ref[...] = scale
     start_ref[...] = scaled
-    spread(scaled, wide_ref)
+    high_ref[...] = scaled.astype(BF16)
     for copy in copies[2:]:
         copy.wait()
 
@@ -127,10 +127,20 @@
     send_halves(rows_ref, own_ref, up_ref, down_ref)
 
 
-def pick_home_kernel(rows_ref, got_ref, own_ref, up_ref, down_ref):
-    for r in range(SIDE):
-        for q in range(SIDE):
-            own_ref[r, SHARE * q:SHARE * (q + 1)] = got_ref[SIDE * r + q]
+def stack_kernel(*refs):
+    out_ref = refs[-1]
+    x, _ = place()
+    for k in range(SIDE):
+        out_ref[wrap(x - k)] = refs[k][...]
+
+
+def pick_stack_kernel(rows_ref, *refs):
+    own_ref, up_ref, down_ref = refs[4:]
+    _, q = place()
+    for k in range(SIDE):
+        at = pl.multiple_of(wrap(q - k) * SHARE, SHARE)
+        for r in range(SIDE):
+            own_ref[r, pl.ds(at, SHARE)] = refs[k][r]
     send_halves(rows_ref, own_ref, up_ref, down_ref)
 
 
@@ -277,8 +287,8 @@
     def gather(wide):
         return lax.all_to_all(wide, "grp", 0, 0)
 
-    def choose(kernel, got):
-        return call(kernel, [rows] + near(got), [OWN] + HALVES, 1)
+    def choose(kernel, *got):
+        return call(kernel, [rows] + near(*got), [OWN] + HALVES, 1)
 
     def along_x(values):
         pairs = [[(m, (m + SIDE * k) % GROUP) for m in range(GROUP)] for k in range(SIDE)]
@@ -294,20 +304,22 @@
             out.append(lax.ppermute(values[k], "grp", pairs[k]))
         return out
 
-    *quarters, wide, start, scale, line = call(
+    *quarters, high, start, scale, line = call(
         start_kernel, [matrix_tiles, residual, diag],
-        [arr((2, SHARE, TILE), BF16)] * 4 + [WIDE, ROWS, ROWS, arr((8, TILE), F32)],
+        [arr((2, SHARE, TILE), BF16)] * 4 + [arr((SHARE, NRHS), BF16), ROWS, ROWS, arr((8, TILE), F32)],
         scratch=(ROWS, arr((1, SHARE), F32), pltpu.SemaphoreType.DMA((6,))), far=1)
     tables = [pltpu.SMEM((1, TILES), jnp.int32), pltpu.SMEM((SIDE, 8), jnp.int32), pltpu.SMEM((2, 2), jnp.int32)]
     tile_slot, tile_cols, rows = pl.pallas_call(
         table_kernel, name="tables", in_specs=[SMEM] * 3, out_specs=[SMEM] * 3, out_shape=tables)(
         tile_slot, tile_cols, rows)
+    shares = along_x([high] * SIDE)
     quarters = along_y(quarters)
-    got = gather(wide)
+    column, = call(stack_kernel, near(*shares), [arr((SIDE, SHARE, NRHS), BF16)])
+    columns = along_y([column] * SIDE)
     slabs = call(split_kernel, near(*quarters, start, line), [arr((PIECE, TILE), BF16)] * 4, 0,
                  (arr((SIDE, PIECE, TILE), BF16),))
     slabs = along_x(slabs)
-    own, up, down = choose(pick_home_kernel, got)
+    own, up, down = choose(pick_stack_kernel, *columns)
     halos = halo(up, down)
     ordered = call(order_kernel, [tile_slot] + near(*slabs), [arr((8, SLAB, TILE), BF16)] * 4, 1,
                    (arr((TILES, SLAB, TILE), BF16),))

time: 88.3 us -> 92.6 us (1.049)
  waiting for transfers between devices: 20.5 us -> 29.3 us
  starting transfers between devices: 32.3 us -> 27.7 us
  blocking collectives: 27.7 us -> 28.8 us
    ppermute x9 -> x15, waiting for transfers between devices: 12.2 us -> 23.6 us  [exchange(): out.append(lax.ppermute(values[k], 'grp', pairs[k]))]
    all_to_all x1 -> x0, starting transfers between devices: 6.77 us -> none  [gather(): return lax.all_to_all(wide, 'grp', 0, 0)]
    ppermute x9 -> x15, starting transfers between devices: 12.8 us -> 18 us  [exchange(): out.append(lax.ppermute(values[k], 'grp', pairs[k]))]
    all_to_all x1 -> x0, waiting for transfers between devices: 2.53 us -> none  [gather(): return lax.all_to_all(wide, 'grp', 0, 0)]
    ppermute x3, starting transfers between devices: 2.52 us -> 0.01 us  [halo(): lax.ppermute(down, 'lead', [(i, (i - 1) % leads) for i in range(leads)])]
    all_to_all x2, blocking collectives: 27.7 us -> 28.8 us  [gather(): return lax.all_to_all(wide, 'grp', 0, 0)]
    pallas_call x11 -> x12, Pallas kernels: 6.28 us -> 5.56 us  [call(): pl.pallas_call(kernel, in_specs=specs, out_specs=[VMEM] * len(outs), out_...]
  transfers between devices with their start and end apart: 16 -> 21, of which waited for: 9 -> 10; matrix products, arithmetic and copies ran while one was open for 0% -> 0% of each run, Pallas kernels for 3% -> 2%
where the time goes in v11:
time: 92.6 us; the launch traced here: 92.3 us
  waiting for transfers between devices  29.3 us (32%)
  blocking collectives  28.8 us (31%)
  starting transfers between devices  27.7 us (30%)
  Pallas kernels  6.36 us (7%)
    all_to_all x2, blocking collectives, gather(): return lax.all_to_all(wide, 'grp', 0, 0)  28.8 us
    ppermute x15, waiting for transfers between devices, exchange(): out.append(lax.ppermute(values[k], 'grp', pairs[k]))  23.6 us
    ppermute x15, starting transfers between devices, exchange(): out.append(lax.ppermute(values[k], 'grp', pairs[k]))  18 us
    ppermute x3, starting transfers between devices, halo(): lax.ppermute(up, 'lead', [(i, (i + 1) % leads) for i in range(leads)])  9.66 us
    pallas_call x12, Pallas kernels, call(): pl.pallas_call(kernel, in_specs=specs, out_specs=[VMEM] * len(outs), out_...  5.56 us
    ppermute x3, waiting for transfers between devices, halo(): lax.ppermute(down, 'lead', [(i, (i - 1) % leads) for i in range(leads)])  3.7 us
    ppermute x3, waiting for transfers between devices, halo(): lax.ppermute(up, 'lead', [(i, (i + 1) % leads) for i in range(leads)])  2.04 us
  transfers between devices with their start and end apart: 21, of which 10 were waited for; matrix products, arithmetic and copies ran while one was open for 0% of the time, Pallas kernels for 2%

profile of v11, /device:TPU:97, one launch (start us, length us, event | category | flops | bytes accessed | tf_op | source)
XLA Modules:
  0.0 92.3 jit_solution(3464063470418784227)
XLA Ops:
  0.0 1.2 %shard_map.64 = (bf16[2,96,384]{2,1,0:T(8,128)(2,1)S(1)}, bf16[2,96,384]{2,1,0:T(8,128)(2,1)S(1)}, bf16[2,96,384]{2,1,0:T(8,128)(2,1)S(1)}, bf16[2,96,384]{2,1,0...) custom-call(bf16[2,384,384]{2,1,0:T(8,128)(2,1)} %tiles_hbm.1, ...), custom_call_target="tpu_custom_call" | custom-call | tf_op jit(solution)/shard_map/pallas_call | solution.py:258
  1.2 2.8 %collective-permute-start.10 = (bf16[96,128]{1,0:T(8,128)(2,1)S(1)}, bf16[96,128]{1,0:T(8,128)(2,1)S(1)}, u32[]{:S(2)}, u32[]{:S(2)}) collective-permute-start(bf16[96,128]{1,0:T(8,128)(2,1)S(1)} %get-tuple-element.54.refs_0_), channel_id=1, source_target_pairs={{0,8},{1,9},{2,10},{3,11},{4,12},{5,13},{6,14},{7,15},{8,0},{9,1},... | collective-permute-start | bytes 73736 | tf_op jit(solution)/shard_map/ppermute | solution.py:304
  4.1 0.9 collective-permute-start.11
  4.9 0.6 collective-permute-start.9
  5.5 0.0 collective-permute-done.10.refs_2_
  5.5 1.5 %collective-permute-done.11.refs_3_ = bf16[96,128]{1,0:T(8,128)(2,1)S(1)} collective-permute-done((bf16[96,128]{1,0:T(8,128)(2,1)S(1)}, bf16[96,128]{1,0:T(8,128)(2,1)S(1)}, u32[]{:S(2)}, u32[]{:S(2)}) %collective-permute-start.11) | collective-permute-done | bytes 24608 | tf_op jit(solution)/shard_map/ppermute | solution.py:304
  7.0 1.8 %collective-permute-done.9.refs_1_ = bf16[96,128]{1,0:T(8,128)(2,1)S(1)} collective-permute-done((bf16[96,128]{1,0:T(8,128)(2,1)S(1)}, bf16[96,128]{1,0:T(8,128)(2,1)S(1)}, u32[]{:S(2)}, u32[]{:S(2)}) %collective-permute-start.9) | collective-permute-done | bytes 24608 | tf_op jit(solution)/shard_map/ppermute | solution.py:304
  8.8 1.4 %collective-permute-start.12 = (bf16[4,96,128]{2,1,0:T(8,128)(2,1)S(1)}, bf16[4,96,128]{2,1,0:T(8,128)(2,1)S(1)}, u32[]{:S(2)}, u32[]{:S(2)}) collective-permute-start(bf16[4,96,128]{2,1,0:T(8,128)(2,1)S(1)} %shard_map.67.refs_0_), channel_id=1, source_target_pairs={{0,1},{1,2},{2,3},{3,0},{4,5},{5,6},{6,7},{7,4},{8,9},{9,10},{10,1... | collective-permute-start | bytes 294920 | tf_op jit(solution)/shard_map/ppermute | solution.py:304
  10.2 1.3 %collective-permute-start = (bf16[2,96,384]{2,1,0:T(8,128)(2,1)S(1)}, bf16[2,96,384]{2,1,0:T(8,128)(2,1)S(1)}, u32[]{:S(2)}, u32[]{:S(2)}) collective-permute-start(bf16[2,96,384]{2,1,0:T(8,128)(2,1)S(1)} %get-tuple-element.40), channel_id=1, source_target_pairs={{0,1},{1,2},{2,3},{3,0},{4,5},{5,6},{6,7},{7,4},{8,9},{9,10},{10,1... | collective-permute-start | bytes 442376 | tf_op jit(solution)/shard_map/ppermute | solution.py:304
  11.5 1.4 %collective-permute-start.1 = (bf16[2,96,384]{2,1,0:T(8,128)(2,1)S(1)}, bf16[2,96,384]{2,1,0:T(8,128)(2,1)S(1)}, u32[]{:S(2)}, u32[]{:S(2)}) collective-permute-start(bf16[2,96,384]{2,1,0:T(8,128)(2,1)S(1)} %get-tuple-element.41), channel_id=1, source_target_pairs={{0,2},{1,3},{2,0},{3,1},{4,6},{5,7},{6,4},{7,5},{8,10},{9,11},{10,... | collective-permute-start | bytes 442376 | tf_op jit(solution)/shard_map/ppermute | solution.py:304
  12.9 2.0 %collective-permute-start.2 = (bf16[2,96,384]{2,1,0:T(8,128)(2,1)S(1)}, bf16[2,96,384]{2,1,0:T(8,128)(2,1)S(1)}, u32[]{:S(2)}, u32[]{:S(2)}) collective-permute-start(bf16[2,96,384]{2,1,0:T(8,128)(2,1)S(1)} %get-tuple-element.42), channel_id=1, source_target_pairs={{0,3},{1,0},{2,1},{3,2},{4,7},{5,4},{6,5},{7,6},{8,11},{9,8},{10,9... | collective-permute-start | bytes 442376 | tf_op jit(solution)/shard_map/ppermute | solution.py:304
  14.9 0.3 collective-permute-start.13
  15.2 0.0 collective-permute-done.12.refs_1_
  15.2 1.5 %collective-permute-start.14 = (bf16[4,96,128]{2,1,0:T(8,128)(2,1)S(1)}, bf16[4,96,128]{2,1,0:T(8,128)(2,1)S(1)}, u32[]{:S(2)}, u32[]{:S(2)}) collective-permute-start(bf16[4,96,128]{2,1,0:T(8,128)(2,1)S(1)} %shard_map.67.refs_0_), channel_id=1, source_target_pairs={{0,3},{1,0},{2,1},{3,2},{4,7},{5,4},{6,5},{7,6},{8,11},{9,8},{10,9... | collective-permute-start | bytes 294920 | tf_op jit(solution)/shard_map/ppermute | solution.py:304
  16.8 0.8 tables.1
  17.6 3.9 %collective-permute-done.13.refs_2_ = bf16[4,96,128]{2,1,0:T(8,128)(2,1)S(1)} collective-permute-done((bf16[4,96,128]{2,1,0:T(8,128)(2,1)S(1)}, bf16[4,96,128]{2,1,0:T(8,128)(2,1)S(1)}, u32[]{:S(2)}, u32[]{:S(2)}) %collective-permute-start.13) | collective-permute-done | bytes 98336 | tf_op jit(solution)/shard_map/ppermute | solution.py:304
  21.4 0.4 collective-permute-done.14.refs_3_
  21.9 0.1 shard_map.68
  21.9 6.6 %collective-permute-start.15 = (bf16[2,384,128]{2,1,0:T(8,128)(2,1)S(1)}, bf16[2,384,128]{2,1,0:T(8,128)(2,1)S(1)}, u32[]{:S(2)}, u32[]{:S(2)}) collective-permute-start(bf16[2,384,128]{2,1,0:T(8,128)(2,1)S(1)} %get-tuple-element.56), channel_id=1, source_target_pairs={{0,16},{16,32},{32,48},{48,64},{64,80},{80,96},{96,112},{112,128},... | collective-permute-start | bytes 589832 | tf_op jit(solution)/shard_map/ppermute | solution.py:283
  28.5 0.0 collective-permute-done.2.refs_3_
  28.5 0.1 shard_map.65
  28.7 0.1 collective-permute-start.3
  28.8 1.2 %collective-permute-start.4 = (bf16[216,384]{1,0:T(8,128)(2,1)S(1)}, bf16[216,384]{1,0:T(8,128)(2,1)S(1)}, u32[]{:S(2)}, u32[]{:S(2)}) collective-permute-start(bf16[216,384]{1,0:T(8,128)(2,1)S(1)} %get-tuple-element.47), channel_id=1, source_target_pairs={{0,8},{1,9},{2,10},{3,11},{4,12},{5,13},{6,14},{7,15},{8,0},{9,1},... | collective-permute-start | bytes 497672 | tf_op jit(solution)/shard_map/ppermute | solution.py:304
  30.0 1.5 %collective-permute-start.5 = (bf16[216,384]{1,0:T(8,128)(2,1)S(1)}, bf16[216,384]{1,0:T(8,128)(2,1)S(1)}, u32[]{:S(2)}, u32[]{:S(2)}) collective-permute-start(bf16[216,384]{1,0:T(8,128)(2,1)S(1)} %get-tuple-element.48), channel_id=1, source_target_pairs={{0,12},{1,13},{2,14},{3,15},{4,0},{5,1},{6,2},{7,3},{8,4},{9,5},{1... | collective-permute-start | bytes 497672 | tf_op jit(solution)/shard_map/ppermute | solution.py:304
  31.4 7.5 %collective-permute-done.3.refs_1_ = bf16[216,384]{1,0:T(8,128)(2,1)S(1)} collective-permute-done((bf16[216,384]{1,0:T(8,128)(2,1)S(1)}, bf16[216,384]{1,0:T(8,128)(2,1)S(1)}, u32[]{:S(2)}, u32[]{:S(2)}) %collective-permute-start.3) | collective-permute-done | bytes 165920 | tf_op jit(solution)/shard_map/ppermute | solution.py:304
  39.0 0.0 collective-permute-done.4.refs_2_
  39.0 0.9 %collective-permute-done.5.refs_3_ = bf16[216,384]{1,0:T(8,128)(2,1)S(1)} collective-permute-done((bf16[216,384]{1,0:T(8,128)(2,1)S(1)}, bf16[216,384]{1,0:T(8,128)(2,1)S(1)}, u32[]{:S(2)}, u32[]{:S(2)}) %collective-permute-start.5) | collective-permute-done | bytes 165920 | tf_op jit(solution)/shard_map/ppermute | solution.py:304
  39.9 0.6 shard_map.69.refs_4_
  40.5 0.0 collective-permute-done.16.refs_6_
  40.5 0.8 shard_map.70
  41.3 14.9 %all_to_all.10.got_ref = bf16[16,96,128]{2,1,0:T(8,128)(2,1)S(1)} all-to-all(bf16[16,96,128]{2,1,0:T(8,128)(2,1)S(1)} %get-tuple-element.58), channel_id=1, replica_groups=mesh['lead'=16,'grp'=16] {'grp'}, dimensions={0} | all-to-all | bytes 786432 | tf_op jit(solution)/shard_map/all_to_all | solution.py:288
  56.2 0.1 shard_map.71
  56.3 1.7 %collective-permute-start.17 = (bf16[2,384,128]{2,1,0:T(8,128)(2,1)S(1)}, bf16[2,384,128]{2,1,0:T(8,128)(2,1)S(1)}, u32[]{:S(2)}, u32[]{:S(2)}) collective-permute-start(bf16[2,384,128]{2,1,0:T(8,128)(2,1)S(1)} %get-tuple-element.60), channel_id=1, source_target_pairs={{0,16},{16,32},{32,48},{48,64},{64,80},{80,96},{96,112},{112,128},... | collective-permute-start | bytes 589832 | tf_op jit(solution)/shard_map/ppermute | solution.py:283
  58.0 0.6 shard_map.72.refs_4_
  58.6 2.0 %collective-permute-done.17.refs_5_ = bf16[2,384,128]{2,1,0:T(8,128)(2,1)S(1)} collective-permute-done((bf16[2,384,128]{2,1,0:T(8,128)(2,1)S(1)}, bf16[2,384,128]{2,1,0:T(8,128)(2,1)S(1)}, u32[]{:S(2)}, u32[]{:S(2)}) %collective-permute-start.17) | collective-permute-done | bytes 196640 | tf_op jit(solution)/shard_map/ppermute | solution.py:283
  60.6 3.7 %collective-permute-done.18.refs_6_ = bf16[2,384,128]{2,1,0:T(8,128)(2,1)S(1)} collective-permute-done((bf16[2,384,128]{2,1,0:T(8,128)(2,1)S(1)}, bf16[2,384,128]{2,1,0:T(8,128)(2,1)S(1)}, u32[]{:S(2)}, u32[]{:S(2)}) %collective-permute-start.18) | collective-permute-done | bytes 196640 | tf_op jit(solution)/shard_map/ppermute | solution.py:284
  64.3 0.8 shard_map.73
  65.2 14.0 %all_to_all.11.got_ref.refs_7_ = bf16[16,120,128]{2,1,0:T(8,128)(2,1)S(1)} all-to-all(bf16[16,120,128]{2,1,0:T(8,128)(2,1)S(1)} %shard_map.73), channel_id=1, replica_groups=mesh['lead'=16,'grp'=16] {'grp'}, dimensions={0} | all-to-all | bytes 983040 | tf_op jit(solution)/shard_map/all_to_all | solution.py:288
  79.2 0.1 shard_map.74
  79.3 1.3 %collective-permute-start.19 = (bf16[2,384,128]{2,1,0:T(8,128)(2,1)S(1)}, bf16[2,384,128]{2,1,0:T(8,128)(2,1)S(1)}, u32[]{:S(2)}, u32[]{:S(2)}) collective-permute-start(bf16[2,384,128]{2,1,0:T(8,128)(2,1)S(1)} %get-tuple-element.66), channel_id=1, source_target_pairs={{0,16},{16,32},{32,48},{48,64},{64,80},{80,96},{96,112},{112,128},... | collective-permute-start | bytes 589832 | tf_op jit(solution)/shard_map/ppermute | solution.py:283
  80.6 0.1 shard_map.66
  80.7 0.1 collective-permute-start.6
  80.8 1.9 %collective-permute-start.7 = (bf16[8,24,384]{2,1,0:T(8,128)(2,1)S(1)}, bf16[8,24,384]{2,1,0:T(8,128)(2,1)S(1)}, u32[]{:S(2)}, u32[]{:S(2)}) collective-permute-start(bf16[8,24,384]{2,1,0:T(8,128)(2,1)S(1)} %get-tuple-element.51), channel_id=1, source_target_pairs={{0,8},{1,9},{2,10},{3,11},{4,12},{5,13},{6,14},{7,15},{8,0},{9,1},... | collective-permute-start | bytes 442376 | tf_op jit(solution)/shard_map/ppermute | solution.py:304
  82.7 1.0 %collective-permute-start.8 = (bf16[8,24,384]{2,1,0:T(8,128)(2,1)S(1)}, bf16[8,24,384]{2,1,0:T(8,128)(2,1)S(1)}, u32[]{:S(2)}, u32[]{:S(2)}) collective-permute-start(bf16[8,24,384]{2,1,0:T(8,128)(2,1)S(1)} %get-tuple-element.52), channel_id=1, source_target_pairs={{0,12},{1,13},{2,14},{3,15},{4,0},{5,1},{6,2},{7,3},{8,4},{9,5},{1... | collective-permute-start | bytes 442376 | tf_op jit(solution)/shard_map/ppermute | solution.py:304
  83.8 7.2 %collective-permute-done.6.refs_1_ = bf16[8,24,384]{2,1,0:T(8,128)(2,1)S(1)} collective-permute-done((bf16[8,24,384]{2,1,0:T(8,128)(2,1)S(1)}, bf16[8,24,384]{2,1,0:T(8,128)(2,1)S(1)}, u32[]{:S(2)}, u32[]{:S(2)}) %collective-permute-start.6) | collective-permute-done | bytes 147488 | tf_op jit(solution)/shard_map/ppermute | solution.py:304
  91.0 0.0 collective-permute-done.7.refs_2_
  91.0 0.3 collective-permute-done.8.refs_3_
  91.3 1.0 %shard_map.75 = f32[96,128]{1,0:T(8,128)} custom-call(s32[4,8]{1,0:T(4,128)S(4)} %get-tuple-element.37.cols_ref, bf16[8,24,384]{2,1,0:T(8,128)(2,1)S(1)} %get-tuple-element.49.refs_0_, bf16[8,24,384]{2,1,0:T(8,128)(2,1)S(1)} %collective-permute-done.6.refs_1_, bf16[8,24,384]{2,1,0:T(8,128)(2,1)S(1)} %collective-permute-done.7.refs_2_, ...), custom_call_target="tpu_custom_call" | custom-call | tf_op jit(solution)/shard_map/pallas_call | solution.py:258
  (9 shorter events, 0.0 us)
Async XLA Ops:
  1.2 4.3 %collective-permute-start.10 = (bf16[96,128]{1,0:T(8,128)(2,1)S(1)}, bf16[96,128]{1,0:T(8,128)(2,1)S(1)}, u32[]{:S(2)}, u32[]{:S(2)}) collective-permute-start(bf16[96,128]{1,0:T(8,128)(2,1)S(1)} %get-tuple-element.54.refs_0_), channel_id=1, source_target_pairs={{0,8},{1,9},{2,10},{3,11},{4,12},{5,13},{6,14},{7,15},{8,0},{9,1},... | collective-permute-start | bytes 73736 | tf_op jit(solution)/shard_map/ppermute | solution.py:304
  4.1 2.9 %collective-permute-start.11 = (bf16[96,128]{1,0:T(8,128)(2,1)S(1)}, bf16[96,128]{1,0:T(8,128)(2,1)S(1)}, u32[]{:S(2)}, u32[]{:S(2)}) collective-permute-start(bf16[96,128]{1,0:T(8,128)(2,1)S(1)} %get-tuple-element.54.refs_0_), channel_id=1, source_target_pairs={{0,12},{1,13},{2,14},{3,15},{4,0},{5,1},{6,2},{7,3},{8,4},{9,5},{1... | collective-permute-start | bytes 73736 | tf_op jit(solution)/shard_map/ppermute | solution.py:304
  4.9 3.9 %collective-permute-start.9 = (bf16[96,128]{1,0:T(8,128)(2,1)S(1)}, bf16[96,128]{1,0:T(8,128)(2,1)S(1)}, u32[]{:S(2)}, u32[]{:S(2)}) collective-permute-start(bf16[96,128]{1,0:T(8,128)(2,1)S(1)} %get-tuple-element.54.refs_0_), channel_id=1, source_target_pairs={{0,4},{1,5},{2,6},{3,7},{4,8},{5,9},{6,10},{7,11},{8,12},{9,13},{1... | collective-permute-start | bytes 73736 | tf_op jit(solution)/shard_map/ppermute | solution.py:304
  8.8 6.4 %collective-permute-start.12 = (bf16[4,96,128]{2,1,0:T(8,128)(2,1)S(1)}, bf16[4,96,128]{2,1,0:T(8,128)(2,1)S(1)}, u32[]{:S(2)}, u32[]{:S(2)}) collective-permute-start(bf16[4,96,128]{2,1,0:T(8,128)(2,1)S(1)} %shard_map.67.refs_0_), channel_id=1, source_target_pairs={{0,1},{1,2},{2,3},{3,0},{4,5},{5,6},{6,7},{7,4},{8,9},{9,10},{10,1... | collective-permute-start | bytes 294920 | tf_op jit(solution)/shard_map/ppermute | solution.py:304
  10.2 18.3 %collective-permute-start = (bf16[2,96,384]{2,1,0:T(8,128)(2,1)S(1)}, bf16[2,96,384]{2,1,0:T(8,128)(2,1)S(1)}, u32[]{:S(2)}, u32[]{:S(2)}) collective-permute-start(bf16[2,96,384]{2,1,0:T(8,128)(2,1)S(1)} %get-tuple-element.40), channel_id=1, source_target_pairs={{0,1},{1,2},{2,3},{3,0},{4,5},{5,6},{6,7},{7,4},{8,9},{9,10},{10,1... | collective-permute-start | bytes 442376 | tf_op jit(solution)/shard_map/ppermute | solution.py:304
  11.5 17.0 %collective-permute-start.1 = (bf16[2,96,384]{2,1,0:T(8,128)(2,1)S(1)}, bf16[2,96,384]{2,1,0:T(8,128)(2,1)S(1)}, u32[]{:S(2)}, u32[]{:S(2)}) collective-permute-start(bf16[2,96,384]{2,1,0:T(8,128)(2,1)S(1)} %get-tuple-element.41), channel_id=1, source_target_pairs={{0,2},{1,3},{2,0},{3,1},{4,6},{5,7},{6,4},{7,5},{8,10},{9,11},{10,... | collective-permute-start | bytes 442376 | tf_op jit(solution)/shard_map/ppermute | solution.py:304
  12.9 15.6 %collective-permute-start.2 = (bf16[2,96,384]{2,1,0:T(8,128)(2,1)S(1)}, bf16[2,96,384]{2,1,0:T(8,128)(2,1)S(1)}, u32[]{:S(2)}, u32[]{:S(2)}) collective-permute-start(bf16[2,96,384]{2,1,0:T(8,128)(2,1)S(1)} %get-tuple-element.42), channel_id=1, source_target_pairs={{0,3},{1,0},{2,1},{3,2},{4,7},{5,4},{6,5},{7,6},{8,11},{9,8},{10,9... | collective-permute-start | bytes 442376 | tf_op jit(solution)/shard_map/ppermute | solution.py:304
  14.9 6.6 %collective-permute-start.13 = (bf16[4,96,128]{2,1,0:T(8,128)(2,1)S(1)}, bf16[4,96,128]{2,1,0:T(8,128)(2,1)S(1)}, u32[]{:S(2)}, u32[]{:S(2)}) collective-permute-start(bf16[4,96,128]{2,1,0:T(8,128)(2,1)S(1)} %shard_map.67.refs_0_), channel_id=1, source_target_pairs={{0,2},{1,3},{2,0},{3,1},{4,6},{5,7},{6,4},{7,5},{8,10},{9,11},{10,... | collective-permute-start | bytes 294920 | tf_op jit(solution)/shard_map/ppermute | solution.py:304
  15.2 6.6 %collective-permute-start.14 = (bf16[4,96,128]{2,1,0:T(8,128)(2,1)S(1)}, bf16[4,96,128]{2,1,0:T(8,128)(2,1)S(1)}, u32[]{:S(2)}, u32[]{:S(2)}) collective-permute-start(bf16[4,96,128]{2,1,0:T(8,128)(2,1)S(1)} %shard_map.67.refs_0_), channel_id=1, source_target_pairs={{0,3},{1,0},{2,1},{3,2},{4,7},{5,4},{6,5},{7,6},{8,11},{9,8},{10,9... | collective-permute-start | bytes 294920 | tf_op jit(solution)/shard_map/ppermute | solution.py:304
  21.9 18.5 %collective-permute-start.15 = (bf16[2,384,128]{2,1,0:T(8,128)(2,1)S(1)}, bf16[2,384,128]{2,1,0:T(8,128)(2,1)S(1)}, u32[]{:S(2)}, u32[]{:S(2)}) collective-permute-start(bf16[2,384,128]{2,1,0:T(8,128)(2,1)S(1)} %get-tuple-element.56), channel_id=1, source_target_pairs={{0,16},{16,32},{32,48},{48,64},{64,80},{80,96},{96,112},{112,128},... | collective-permute-start | bytes 589832 | tf_op jit(solution)/shard_map/ppermute | solution.py:283
  28.5 11.9 %collective-permute-start.16 = (bf16[2,384,128]{2,1,0:T(8,128)(2,1)S(1)}, bf16[2,384,128]{2,1,0:T(8,128)(2,1)S(1)}, u32[]{:S(2)}, u32[]{:S(2)}) collective-permute-start(bf16[2,384,128]{2,1,0:T(8,128)(2,1)S(1)} %get-tuple-element.57), channel_id=1, source_target_pairs={{0,240},{16,0},{32,16},{48,32},{64,48},{80,64},{96,80},{112,96},{1... | collective-permute-start | bytes 589832 | tf_op jit(solution)/shard_map/ppermute | solution.py:284
  28.7 10.3 %collective-permute-start.3 = (bf16[216,384]{1,0:T(8,128)(2,1)S(1)}, bf16[216,384]{1,0:T(8,128)(2,1)S(1)}, u32[]{:S(2)}, u32[]{:S(2)}) collective-permute-start(bf16[216,384]{1,0:T(8,128)(2,1)S(1)} %get-tuple-element.46), channel_id=1, source_target_pairs={{0,4},{1,5},{2,6},{3,7},{4,8},{5,9},{6,10},{7,11},{8,12},{9,13},{1... | collective-permute-start | bytes 497672 | tf_op jit(solution)/shard_map/ppermute | solution.py:304
  28.8 10.2 %collective-permute-start.4 = (bf16[216,384]{1,0:T(8,128)(2,1)S(1)}, bf16[216,384]{1,0:T(8,128)(2,1)S(1)}, u32[]{:S(2)}, u32[]{:S(2)}) collective-permute-start(bf16[216,384]{1,0:T(8,128)(2,1)S(1)} %get-tuple-element.47), channel_id=1, source_target_pairs={{0,8},{1,9},{2,10},{3,11},{4,12},{5,13},{6,14},{7,15},{8,0},{9,1},... | collective-permute-start | bytes 497672 | tf_op jit(solution)/shard_map/ppermute | solution.py:304
  30.0 9.9 %collective-permute-start.5 = (bf16[216,384]{1,0:T(8,128)(2,1)S(1)}, bf16[216,384]{1,0:T(8,128)(2,1)S(1)}, u32[]{:S(2)}, u32[]{:S(2)}) collective-permute-start(bf16[216,384]{1,0:T(8,128)(2,1)S(1)} %get-tuple-element.48), channel_id=1, source_target_pairs={{0,12},{1,13},{2,14},{3,15},{4,0},{5,1},{6,2},{7,3},{8,4},{9,5},{1... | collective-permute-start | bytes 497672 | tf_op jit(solution)/shard_map/ppermute | solution.py:304
  56.3 4.3 %collective-permute-start.17 = (bf16[2,384,128]{2,1,0:T(8,128)(2,1)S(1)}, bf16[2,384,128]{2,1,0:T(8,128)(2,1)S(1)}, u32[]{:S(2)}, u32[]{:S(2)}) collective-permute-start(bf16[2,384,128]{2,1,0:T(8,128)(2,1)S(1)} %get-tuple-element.60), channel_id=1, source_target_pairs={{0,16},{16,32},{32,48},{48,64},{64,80},{80,96},{96,112},{112,128},... | collective-permute-start | bytes 589832 | tf_op jit(solution)/shard_map/ppermute | solution.py:283
  58.0 6.3 %collective-permute-start.18 = (bf16[2,384,128]{2,1,0:T(8,128)(2,1)S(1)}, bf16[2,384,128]{2,1,0:T(8,128)(2,1)S(1)}, u32[]{:S(2)}, u32[]{:S(2)}) collective-permute-start(bf16[2,384,128]{2,1,0:T(8,128)(2,1)S(1)} %get-tuple-element.61), channel_id=1, source_target_pairs={{0,240},{16,0},{32,16},{48,32},{64,48},{80,64},{96,80},{112,96},{1... | collective-permute-start | bytes 589832 | tf_op jit(solution)/shard_map/ppermute | solution.py:284
  79.3 12.1 %collective-permute-start.19 = (bf16[2,384,128]{2,1,0:T(8,128)(2,1)S(1)}, bf16[2,384,128]{2,1,0:T(8,128)(2,1)S(1)}, u32[]{:S(2)}, u32[]{:S(2)}) collective-permute-start(bf16[2,384,128]{2,1,0:T(8,128)(2,1)S(1)} %get-tuple-element.66), channel_id=1, source_target_pairs={{0,16},{16,32},{32,48},{48,64},{64,80},{80,96},{96,112},{112,128},... | collective-permute-start | bytes 589832 | tf_op jit(solution)/shard_map/ppermute | solution.py:283
  80.6 10.7 %collective-permute-start.20 = (bf16[2,384,128]{2,1,0:T(8,128)(2,1)S(1)}, bf16[2,384,128]{2,1,0:T(8,128)(2,1)S(1)}, u32[]{:S(2)}, u32[]{:S(2)}) collective-permute-start(bf16[2,384,128]{2,1,0:T(8,128)(2,1)S(1)} %get-tuple-element.67), channel_id=1, source_target_pairs={{0,240},{16,0},{32,16},{48,32},{64,48},{80,64},{96,80},{112,96},{1... | collective-permute-start | bytes 589832 | tf_op jit(solution)/shard_map/ppermute | solution.py:284
  80.7 10.3 %collective-permute-start.6 = (bf16[8,24,384]{2,1,0:T(8,128)(2,1)S(1)}, bf16[8,24,384]{2,1,0:T(8,128)(2,1)S(1)}, u32[]{:S(2)}, u32[]{:S(2)}) collective-permute-start(bf16[8,24,384]{2,1,0:T(8,128)(2,1)S(1)} %get-tuple-element.50), channel_id=1, source_target_pairs={{0,4},{1,5},{2,6},{3,7},{4,8},{5,9},{6,10},{7,11},{8,12},{9,13},{1... | collective-permute-start | bytes 442376 | tf_op jit(solution)/shard_map/ppermute | solution.py:304
  80.8 10.2 %collective-permute-start.7 = (bf16[8,24,384]{2,1,0:T(8,128)(2,1)S(1)}, bf16[8,24,384]{2,1,0:T(8,128)(2,1)S(1)}, u32[]{:S(2)}, u32[]{:S(2)}) collective-permute-start(bf16[8,24,384]{2,1,0:T(8,128)(2,1)S(1)} %get-tuple-element.51), channel_id=1, source_target_pairs={{0,8},{1,9},{2,10},{3,11},{4,12},{5,13},{6,14},{7,15},{8,0},{9,1},... | collective-permute-start | bytes 442376 | tf_op jit(solution)/shard_map/ppermute | solution.py:304
  82.7 8.6 %collective-permute-start.8 = (bf16[8,24,384]{2,1,0:T(8,128)(2,1)S(1)}, bf16[8,24,384]{2,1,0:T(8,128)(2,1)S(1)}, u32[]{:S(2)}, u32[]{:S(2)}) collective-permute-start(bf16[8,24,384]{2,1,0:T(8,128)(2,1)S(1)} %get-tuple-element.52), channel_id=1, source_target_pairs={{0,12},{1,13},{2,14},{3,15},{4,0},{5,1},{6,2},{7,3},{8,4},{9,5},{1... | collective-permute-start | bytes 442376 | tf_op jit(solution)/shard_map/ppermute | solution.py:304

commit v12 on v9

--- a/solution.py
+++ b/solution.py
@@ -43,7 +43,7 @@
 
 
 def start_kernel(tiles_hbm, residual_hbm, diag_hbm, part0, part1, part2, part3, wide_ref, start_ref, scale_ref,
-                 line_ref, residual_ref, diag_ref, sems):
+                 line_ref, residual_ref, diag_ref, high_ref, sems):
     _, q = place()
     copies = [pltpu.make_async_copy(residual_hbm, residual_ref, sems.at[0]),
               pltpu.make_async_copy(diag_hbm, diag_ref, sems.at[1])]
@@ -62,8 +62,11 @@
     scaled = residual_ref[...] * scale
     scale_ref[...] = scale
     start_ref[...] = scaled
-    spread(scaled, wide_ref)
-    for copy in copies[2:]:
+    high_ref[...] = scaled.astype(BF16)
+    pieces = [pltpu.make_async_copy(high_ref, wide_ref.at[m], sems.at[6 + m]) for m in range(GROUP)]
+    for piece in pieces:
+        piece.start()
+    for copy in copies[2:] + pieces:
         copy.wait()
 
 
@@ -163,25 +166,37 @@
     return jnp.concatenate([part[0:192] for part in parts], axis=0)
 
 
-def near_kernel(*refs):
-    own_ref, product_ref = refs[4:]
-    slab_products(all_slabs(refs[:4]), [own_ref[r] for r in range(SIDE)], product_ref, 0)
-
-
-def slab_total(slot_ref, cols_ref, parts, near_ref, low_ref, high_ref, product_ref, total_ref):
+def add_up(slot_ref, cols_ref, base, blocks, parts, product_ref, total_ref):
     x, _ = place()
-    slab_products(all_slabs(parts), [low_ref[0], low_ref[1], high_ref[0], high_ref[1]], product_ref, 4)
-    product_ref[0:4] = near_ref[...]
-    total_ref[...] = jnp.zeros_like(total_ref)
+    product_ref[0] = jnp.zeros((TILES * SLAB, NRHS), F32)
+    slab_products(all_slabs(parts), blocks, product_ref, 1)
     for t in range(TILES):
         slot = slot_of(slot_ref, x, t // 8, t % 8)
         row = lax.shift_right_logical(slot, 3)
-        col = cols_ref[row, lax.bitwise_and(slot, 7)]
-        total_ref[row] += product_ref[col, SLAB * t:SLAB * (t + 1)]
+        block = cols_ref[row, lax.bitwise_and(slot, 7)] - base + 1
+        block = jnp.where(block > len(blocks), 0, jnp.maximum(block, 0))
+        total_ref[row] += product_ref[block, SLAB * t:SLAB * (t + 1)]
+
+
+def near_kernel(slot_ref, cols_ref, *refs):
+    own_ref, total_ref, product_ref = refs[4:]
+    total_ref[...] = jnp.zeros_like(total_ref)
+    add_up(slot_ref, cols_ref, 0, [own_ref[r] for r in range(SIDE)], refs[:4], product_ref, total_ref)
+
+
+def half_kernel(slot_ref, cols_ref, *refs):
+    near_ref, high_ref, total_ref, product_ref = refs[4:]
+    total_ref[...] = near_ref[...]
+    add_up(slot_ref, cols_ref, 6, [high_ref[0], high_ref[1]], refs[:4], product_ref, total_ref)
+
+
+def slab_total(slot_ref, cols_ref, parts, near_ref, low_ref, product_ref, total_ref):
+    total_ref[...] = near_ref[...]
+    add_up(slot_ref, cols_ref, 4, [low_ref[0], low_ref[1]], parts, product_ref, total_ref)
 
 
 def first_kernel(slot_ref, cols_ref, *refs):
-    parts, halo, (wide_ref, first_ref, start_ref, scale_ref), work = refs[:4], refs[4:7], refs[7:11], refs[11:]
+    parts, halo, (wide_ref, first_ref, start_ref, scale_ref), work = refs[:4], refs[4:6], refs[6:10], refs[10:]
     slab_total(slot_ref, cols_ref, parts, *halo, *work)
     total_ref = work[1]
     x, _ = place()
@@ -198,8 +213,8 @@
 
 
 def second_kernel(slot_ref, cols_ref, *refs):
-    parts, halo, (first_ref, start_ref, scale_ref) = refs[:4], refs[4:7], refs[7:10]
-    wide_ref, work = refs[10], refs[11:]
+    parts, halo, (first_ref, start_ref, scale_ref) = refs[:4], refs[4:6], refs[6:9]
+    wide_ref, work = refs[9], refs[10:]
     slab_total(slot_ref, cols_ref, parts, *halo, *work)
     total_ref = work[1]
     seconds, rests = [], []
@@ -239,13 +254,14 @@
     return pltpu.VMEM(shape, dtype)
 
 
-def call(kernel, args, outs, scalars=0, scratch=(), far=0):
+def call(kernel, args, outs, scalars=0, scratch=(), far=0, away=()):
     vectors = args[scalars:]
     space = pltpu.HBM if far else pltpu.VMEM
     vectors = [pltpu.with_memory_space_constraint(a, space) for a in vectors]
     specs = [SMEM] * scalars + [pl.BlockSpec(memory_space=space)] * len(vectors)
     tables = [pltpu.with_memory_space_constraint(a, pltpu.SMEM) for a in args[:scalars]]
-    return pl.pallas_call(kernel, in_specs=specs, out_specs=[VMEM] * len(outs),
+    return pl.pallas_call(kernel, in_specs=specs,
+                          out_specs=[pl.BlockSpec(memory_space=pltpu.HBM) if n in away else VMEM for n in range(len(outs))],
                           out_shape=outs, scratch_shapes=list(scratch),
                           compiler_params=pltpu.CompilerParams(vmem_limit_bytes=GRANT))(*tables, *vectors)
 
@@ -260,8 +276,7 @@
 EXT = arr((8, TILE, NRHS), BF16)
 SLABS = arr((SIDE, SLAB, NRHS), F32)
 WIDE = arr((GROUP, SHARE, NRHS), BF16)
-NEAR = arr((4, TILES * SLAB, NRHS), F32)
-WORK = (arr((8, TILES * SLAB, NRHS), F32), SLABS)
+WORK = (arr((5, TILES * SLAB, NRHS), F32), SLABS)
 
 
 def body(matrix_tiles, tile_slot, tile_cols, send_rows, residual, diag_inv):
@@ -296,8 +311,9 @@
 
     *quarters, wide, start, scale, line = call(
         start_kernel, [matrix_tiles, residual, diag],
-        [arr((2, SHARE, TILE), BF16)] * 4 + [WIDE, ROWS, ROWS, arr((8, TILE), F32)],
-        scratch=(ROWS, arr((1, SHARE), F32), pltpu.SemaphoreType.DMA((6,))), far=1)
+        [arr((2, SHARE, TILE), BF16)] * 4 + [pltpu.HBM((GROUP, SHARE, NRHS), BF16), ROWS, ROWS, arr((8, TILE), F32)],
+        scratch=(ROWS, arr((1, SHARE), F32), arr((SHARE, NRHS), BF16), pltpu.SemaphoreType.DMA((6 + GROUP,))), far=1,
+        away=(4,))
     tables = [pltpu.SMEM((1, TILES), jnp.int32), pltpu.SMEM((SIDE, 8), jnp.int32), pltpu.SMEM((2, 2), jnp.int32)]
     tile_slot, tile_cols, rows = pl.pallas_call(
         table_kernel, name="tables", in_specs=[SMEM] * 3, out_specs=[SMEM] * 3, out_shape=tables)(
@@ -311,14 +327,16 @@
     halos = halo(up, down)
     ordered = call(order_kernel, [tile_slot] + near(*slabs), [arr((8, SLAB, TILE), BF16)] * 4, 1,
                    (arr((TILES, SLAB, TILE), BF16),))
-    product, = call(near_kernel, near(*slabs, own), [NEAR])
-    wide, *state = call(first_kernel, [tile_slot, tile_cols] + near(*slabs, product, *halos),
+    total, = call(near_kernel, [tile_slot, tile_cols] + near(*slabs, own), [SLABS], 2, WORK[:1])
+    total, = call(half_kernel, [tile_slot, tile_cols] + near(*slabs, total, halos[1]), [SLABS], 2, WORK[:1])
+    wide, *state = call(first_kernel, [tile_slot, tile_cols] + near(*slabs, total, halos[0]),
                         [WIDE] + [SLABS] * 3, 2, WORK)
     first, up, down = choose(pick_slab_kernel, gather(wide))
     halos = halo(up, down)
     parts = along_x(ordered)
-    product, = call(near_kernel, near(*slabs, first), [NEAR])
-    wide, = call(second_kernel, [tile_slot, tile_cols] + near(*slabs, product, *halos, *state),
+    total, = call(near_kernel, [tile_slot, tile_cols] + near(*slabs, first), [SLABS], 2, WORK[:1])
+    total, = call(half_kernel, [tile_slot, tile_cols] + near(*slabs, total, halos[1]), [SLABS], 2, WORK[:1])
+    wide, = call(second_kernel, [tile_slot, tile_cols] + near(*slabs, total, halos[0], *state),
                  [arr((GROUP, 120, NRHS), BF16)], 2, WORK)
     got = gather(wide)
     own, up, down = choose(pick_slab_kernel, got)

time: 88.3 us -> 90.2 us (1.022)
  the two profiles are of different devices: /device:TPU:97 before, /device:TPU:6 now
where the time goes in v12:
time: 90.2 us; the launch traced here: 89.9 us
  starting transfers between devices  30.5 us (34%)
  blocking collectives  28.1 us (31%)
  waiting for transfers between devices  23.4 us (26%)
  Pallas kernels  7.82 us (9%)
    all_to_all x2, blocking collectives, gather(): return lax.all_to_all(wide, 'grp', 0, 0)  28.1 us
    ppermute x9, waiting for transfers between devices, exchange(): out.append(lax.ppermute(values[k], 'grp', pairs[k]))  16.8 us
    ppermute x9, starting transfers between devices, exchange(): out.append(lax.ppermute(values[k], 'grp', pairs[k]))  11.9 us
    ppermute x3, starting transfers between devices, halo(): lax.ppermute(down, 'lead', [(i, (i - 1) % leads) for i in range(leads)])  11.2 us
    all_to_all x1, starting transfers between devices, gather(): return lax.all_to_all(wide, 'grp', 0, 0)  7.44 us
    pallas_call x13, Pallas kernels, call(): pl.pallas_call(kernel, in_specs=specs, out_specs=[pl.BlockSpec(memory_spa...  7.02 us
    ppermute x3, waiting for transfers between devices, halo(): lax.ppermute(up, 'lead', [(i, (i + 1) % leads) for i in range(leads)])  2.59 us
    ppermute x3, waiting for transfers between devices, halo(): lax.ppermute(down, 'lead', [(i, (i - 1) % leads) for i in range(leads)])  2.45 us
  transfers between devices with their start and end apart: 16, of which 10 were waited for; matrix products, arithmetic and copies ran while one was open for 0% of the time, Pallas kernels for 4%

profile of v12, /device:TPU:6, one launch (start us, length us, event | category | flops | bytes accessed | tf_op | source)
XLA Modules:
  0.0 89.9 jit_solution(3710344070514368754)
XLA Ops:
  0.0 1.8 %shard_map.64 = (bf16[2,96,384]{2,1,0:T(8,128)(2,1)S(1)}, bf16[2,96,384]{2,1,0:T(8,128)(2,1)S(1)}, bf16[2,96,384]{2,1,0:T(8,128)(2,1)S(1)}, bf16[2,96,384]{2,1,0...) custom-call(bf16[2,384,384]{2,1,0:T(8,128)(2,1)} %tiles_hbm.1, ...), custom_call_target="tpu_custom_call" | custom-call | tf_op jit(solution)/shard_map/pallas_call | solution.py:263
  1.8 7.4 %all-to-all-start = ((bf16[16,96,128]{2,1,0:T(8,128)(2,1)}), bf16[16,96,128]{2,1,0:T(8,128)(2,1)S(1)}, u32[]{:S(2)}, u32[]{:S(2)}) async-start(bf16[16,96,128]{2,1,0:T(8,128)(2,1)} %get-tuple-element.54), calls=%async_computation | async-start | bytes 786432 | tf_op jit(solution)/shard_map/all_to_all | solution.py:293
  9.3 1.5 %collective-permute-start = (bf16[2,96,384]{2,1,0:T(8,128)(2,1)S(1)}, bf16[2,96,384]{2,1,0:T(8,128)(2,1)S(1)}, u32[]{:S(2)}, u32[]{:S(2)}) collective-permute-start(bf16[2,96,384]{2,1,0:T(8,128)(2,1)S(1)} %get-tuple-element.40), channel_id=1, source_target_pairs={{0,1},{1,2},{2,3},{3,0},{4,5},{5,6},{6,7},{7,4},{8,9},{9,10},{10,1... | collective-permute-start | bytes 442376 | tf_op jit(solution)/shard_map/ppermute | solution.py:309
  10.7 2.7 %collective-permute-start.1 = (bf16[2,96,384]{2,1,0:T(8,128)(2,1)S(1)}, bf16[2,96,384]{2,1,0:T(8,128)(2,1)S(1)}, u32[]{:S(2)}, u32[]{:S(2)}) collective-permute-start(bf16[2,96,384]{2,1,0:T(8,128)(2,1)S(1)} %get-tuple-element.41), channel_id=1, source_target_pairs={{0,2},{1,3},{2,0},{3,1},{4,6},{5,7},{6,4},{7,5},{8,10},{9,11},{10,... | collective-permute-start | bytes 442376 | tf_op jit(solution)/shard_map/ppermute | solution.py:309
  13.4 1.5 %collective-permute-start.2 = (bf16[2,96,384]{2,1,0:T(8,128)(2,1)S(1)}, bf16[2,96,384]{2,1,0:T(8,128)(2,1)S(1)}, u32[]{:S(2)}, u32[]{:S(2)}) collective-permute-start(bf16[2,96,384]{2,1,0:T(8,128)(2,1)S(1)} %get-tuple-element.42), channel_id=1, source_target_pairs={{0,3},{1,0},{2,1},{3,2},{4,7},{5,4},{6,5},{7,6},{8,11},{9,8},{10,9... | collective-permute-start | bytes 442376 | tf_op jit(solution)/shard_map/ppermute | solution.py:309
  14.9 0.8 tables.1
  15.7 1.6 %all-to-all-done.got_ref = bf16[16,96,128]{2,1,0:T(8,128)(2,1)S(1)} async-done(((bf16[16,96,128]{2,1,0:T(8,128)(2,1)}), bf16[16,96,128]{2,1,0:T(8,128)(2,1)S(1)}, u32[]{:S(2)}, u32[]{:S(2)}) %all-to-all-start) | async-done | bytes 393248 | tf_op jit(solution)/shard_map/all_to_all | solution.py:293
  17.3 0.1 shard_map.67
  17.3 4.1 %collective-permute-start.9 = (bf16[2,384,128]{2,1,0:T(8,128)(2,1)S(1)}, bf16[2,384,128]{2,1,0:T(8,128)(2,1)S(1)}, u32[]{:S(2)}, u32[]{:S(2)}) collective-permute-start(bf16[2,384,128]{2,1,0:T(8,128)(2,1)S(1)} %get-tuple-element.56), channel_id=1, source_target_pairs={{0,240},{16,0},{32,16},{48,32},{64,48},{80,64},{96,80},{112,96},{1... | collective-permute-start | bytes 589832 | tf_op jit(solution)/shard_map/ppermute | solution.py:289
  21.4 0.0 collective-permute-start.10
  21.4 0.0 collective-permute-done.refs_1_
  21.4 1.7 %collective-permute-done.1.refs_2_ = bf16[2,96,384]{2,1,0:T(8,128)(2,1)S(1)} collective-permute-done((bf16[2,96,384]{2,1,0:T(8,128)(2,1)S(1)}, bf16[2,96,384]{2,1,0:T(8,128)(2,1)S(1)}, u32[]{:S(2)}, u32[]{:S(2)}) %collective-permute-start.1) | collective-permute-done | bytes 147488 | tf_op jit(solution)/shard_map/ppermute | solution.py:309
  23.1 0.0 collective-permute-done.2.refs_3_
  23.1 0.1 shard_map.65
  23.2 0.8 collective-permute-start.3
  24.0 2.2 %collective-permute-start.4 = (bf16[216,384]{1,0:T(8,128)(2,1)S(1)}, bf16[216,384]{1,0:T(8,128)(2,1)S(1)}, u32[]{:S(2)}, u32[]{:S(2)}) collective-permute-start(bf16[216,384]{1,0:T(8,128)(2,1)S(1)} %get-tuple-element.47), channel_id=1, source_target_pairs={{0,8},{1,9},{2,10},{3,11},{4,12},{5,13},{6,14},{7,15},{8,0},{9,1},... | collective-permute-start | bytes 497672 | tf_op jit(solution)/shard_map/ppermute | solution.py:309
  26.2 0.1 collective-permute-start.5
  26.4 4.1 %collective-permute-done.3.refs_1_ = bf16[216,384]{1,0:T(8,128)(2,1)S(1)} collective-permute-done((bf16[216,384]{1,0:T(8,128)(2,1)S(1)}, bf16[216,384]{1,0:T(8,128)(2,1)S(1)}, u32[]{:S(2)}, u32[]{:S(2)}) %collective-permute-start.3) | collective-permute-done | bytes 165920 | tf_op jit(solution)/shard_map/ppermute | solution.py:309
  30.4 2.2 %collective-permute-done.4.refs_2_ = bf16[216,384]{1,0:T(8,128)(2,1)S(1)} collective-permute-done((bf16[216,384]{1,0:T(8,128)(2,1)S(1)}, bf16[216,384]{1,0:T(8,128)(2,1)S(1)}, u32[]{:S(2)}, u32[]{:S(2)}) %collective-permute-start.4) | collective-permute-done | bytes 165920 | tf_op jit(solution)/shard_map/ppermute | solution.py:309
  32.6 1.5 %collective-permute-done.5.refs_3_ = bf16[216,384]{1,0:T(8,128)(2,1)S(1)} collective-permute-done((bf16[216,384]{1,0:T(8,128)(2,1)S(1)}, bf16[216,384]{1,0:T(8,128)(2,1)S(1)}, u32[]{:S(2)}, u32[]{:S(2)}) %collective-permute-start.5) | collective-permute-done | bytes 165920 | tf_op jit(solution)/shard_map/ppermute | solution.py:309
  34.1 0.7 shard_map.68.refs_4_
  34.9 0.0 collective-permute-done.9.refs_5_
  34.9 0.5 shard_map.69.refs_4_
  35.4 0.0 collective-permute-done.10.refs_5_
  35.4 0.6 shard_map.70
  36.0 14.7 %all_to_all.15.got_ref = bf16[16,96,128]{2,1,0:T(8,128)(2,1)S(1)} all-to-all(bf16[16,96,128]{2,1,0:T(8,128)(2,1)S(1)} %get-tuple-element.58), channel_id=1, replica_groups=mesh['lead'=16,'grp'=16] {'grp'}, dimensions={0} | all-to-all | bytes 786432 | tf_op jit(solution)/shard_map/all_to_all | solution.py:293
  50.7 0.1 shard_map.71
  50.8 4.2 %collective-permute-start.11 = (bf16[2,384,128]{2,1,0:T(8,128)(2,1)S(1)}, bf16[2,384,128]{2,1,0:T(8,128)(2,1)S(1)}, u32[]{:S(2)}, u32[]{:S(2)}) collective-permute-start(bf16[2,384,128]{2,1,0:T(8,128)(2,1)S(1)} %get-tuple-element.60), channel_id=1, source_target_pairs={{0,240},{16,0},{32,16},{48,32},{64,48},{80,64},{96,80},{112,96},{1... | collective-permute-start | bytes 589832 | tf_op jit(solution)/shard_map/ppermute | solution.py:289
  55.0 0.0 collective-permute-start.12
  55.0 0.7 shard_map.72.refs_4_
  55.7 2.4 %collective-permute-done.11.refs_5_ = bf16[2,384,128]{2,1,0:T(8,128)(2,1)S(1)} collective-permute-done((bf16[2,384,128]{2,1,0:T(8,128)(2,1)S(1)}, bf16[2,384,128]{2,1,0:T(8,128)(2,1)S(1)}, u32[]{:S(2)}, u32[]{:S(2)}) %collective-permute-start.11) | collective-permute-done | bytes 196640 | tf_op jit(solution)/shard_map/ppermute | solution.py:289
  58.2 0.5 shard_map.73.refs_4_
  58.7 2.6 %collective-permute-done.12.refs_5_ = bf16[2,384,128]{2,1,0:T(8,128)(2,1)S(1)} collective-permute-done((bf16[2,384,128]{2,1,0:T(8,128)(2,1)S(1)}, bf16[2,384,128]{2,1,0:T(8,128)(2,1)S(1)}, u32[]{:S(2)}, u32[]{:S(2)}) %collective-permute-start.12) | collective-permute-done | bytes 196640 | tf_op jit(solution)/shard_map/ppermute | solution.py:288
  61.3 0.6 shard_map.74
  61.8 13.4 %all_to_all.16.got_ref.refs_7_ = bf16[16,120,128]{2,1,0:T(8,128)(2,1)S(1)} all-to-all(bf16[16,120,128]{2,1,0:T(8,128)(2,1)S(1)} %shard_map.74), channel_id=1, replica_groups=mesh['lead'=16,'grp'=16] {'grp'}, dimensions={0} | all-to-all | bytes 983040 | tf_op jit(solution)/shard_map/all_to_all | solution.py:293
  75.3 0.1 shard_map.75
  75.4 0.0 collective-permute-start.13
  75.4 2.9 %collective-permute-start.14 = (bf16[2,384,128]{2,1,0:T(8,128)(2,1)S(1)}, bf16[2,384,128]{2,1,0:T(8,128)(2,1)S(1)}, u32[]{:S(2)}, u32[]{:S(2)}) collective-permute-start(bf16[2,384,128]{2,1,0:T(8,128)(2,1)S(1)} %get-tuple-element.67), channel_id=1, source_target_pairs={{0,240},{16,0},{32,16},{48,32},{64,48},{80,64},{96,80},{112,96},{1... | collective-permute-start | bytes 589832 | tf_op jit(solution)/shard_map/ppermute | solution.py:289
  78.3 0.1 shard_map.66
  78.5 2.2 %collective-permute-start.6 = (bf16[8,24,384]{2,1,0:T(8,128)(2,1)S(1)}, bf16[8,24,384]{2,1,0:T(8,128)(2,1)S(1)}, u32[]{:S(2)}, u32[]{:S(2)}) collective-permute-start(bf16[8,24,384]{2,1,0:T(8,128)(2,1)S(1)} %get-tuple-element.50), channel_id=1, source_target_pairs={{0,4},{1,5},{2,6},{3,7},{4,8},{5,9},{6,10},{7,11},{8,12},{9,13},{1... | collective-permute-start | bytes 442376 | tf_op jit(solution)/shard_map/ppermute | solution.py:309
  80.7 0.5 collective-permute-start.7
  81.1 0.5 collective-permute-start.8
  81.6 3.3 %collective-permute-done.6.refs_1_ = bf16[8,24,384]{2,1,0:T(8,128)(2,1)S(1)} collective-permute-done((bf16[8,24,384]{2,1,0:T(8,128)(2,1)S(1)}, bf16[8,24,384]{2,1,0:T(8,128)(2,1)S(1)}, u32[]{:S(2)}, u32[]{:S(2)}) %collective-permute-start.6) | collective-permute-done | bytes 147488 | tf_op jit(solution)/shard_map/ppermute | solution.py:309
  84.9 2.5 %collective-permute-done.7.refs_2_ = bf16[8,24,384]{2,1,0:T(8,128)(2,1)S(1)} collective-permute-done((bf16[8,24,384]{2,1,0:T(8,128)(2,1)S(1)}, bf16[8,24,384]{2,1,0:T(8,128)(2,1)S(1)}, u32[]{:S(2)}, u32[]{:S(2)}) %collective-permute-start.7) | collective-permute-done | bytes 147488 | tf_op jit(solution)/shard_map/ppermute | solution.py:309
  87.4 1.5 %collective-permute-done.8.refs_3_ = bf16[8,24,384]{2,1,0:T(8,128)(2,1)S(1)} collective-permute-done((bf16[8,24,384]{2,1,0:T(8,128)(2,1)S(1)}, bf16[8,24,384]{2,1,0:T(8,128)(2,1)S(1)}, u32[]{:S(2)}, u32[]{:S(2)}) %collective-permute-start.8) | collective-permute-done | bytes 147488 | tf_op jit(solution)/shard_map/ppermute | solution.py:309
  88.9 0.0 collective-permute-done.13.refs_5_
  88.9 0.0 collective-permute-done.14.refs_6_
  88.9 1.0 %shard_map.76 = f32[96,128]{1,0:T(8,128)} custom-call(s32[4,8]{1,0:T(4,128)S(4)} %get-tuple-element.37.cols_ref, bf16[8,24,384]{2,1,0:T(8,128)(2,1)S(1)} %get-tuple-element.49.refs_0_, bf16[8,24,384]{2,1,0:T(8,128)(2,1)S(1)} %collective-permute-done.6.refs_1_, bf16[8,24,384]{2,1,0:T(8,128)(2,1)S(1)} %collective-permute-done.7.refs_2_, ...), custom_call_target="tpu_custom_call" | custom-call | tf_op jit(solution)/shard_map/pallas_call | solution.py:263
Async XLA Ops:
  1.8 15.4 %all-to-all-start = ((bf16[16,96,128]{2,1,0:T(8,128)(2,1)}), bf16[16,96,128]{2,1,0:T(8,128)(2,1)S(1)}, u32[]{:S(2)}, u32[]{:S(2)}) async-start(bf16[16,96,128]{2,1,0:T(8,128)(2,1)} %get-tuple-element.54), calls=%async_computation | async-start | bytes 786432 | tf_op jit(solution)/shard_map/all_to_all | solution.py:293
  9.3 12.1 %collective-permute-start = (bf16[2,96,384]{2,1,0:T(8,128)(2,1)S(1)}, bf16[2,96,384]{2,1,0:T(8,128)(2,1)S(1)}, u32[]{:S(2)}, u32[]{:S(2)}) collective-permute-start(bf16[2,96,384]{2,1,0:T(8,128)(2,1)S(1)} %get-tuple-element.40), channel_id=1, source_target_pairs={{0,1},{1,2},{2,3},{3,0},{4,5},{5,6},{6,7},{7,4},{8,9},{9,10},{10,1... | collective-permute-start | bytes 442376 | tf_op jit(solution)/shard_map/ppermute | solution.py:309
  10.7 12.4 %collective-permute-start.1 = (bf16[2,96,384]{2,1,0:T(8,128)(2,1)S(1)}, bf16[2,96,384]{2,1,0:T(8,128)(2,1)S(1)}, u32[]{:S(2)}, u32[]{:S(2)}) collective-permute-start(bf16[2,96,384]{2,1,0:T(8,128)(2,1)S(1)} %get-tuple-element.41), channel_id=1, source_target_pairs={{0,2},{1,3},{2,0},{3,1},{4,6},{5,7},{6,4},{7,5},{8,10},{9,11},{10,... | collective-permute-start | bytes 442376 | tf_op jit(solution)/shard_map/ppermute | solution.py:309
  13.4 9.7 %collective-permute-start.2 = (bf16[2,96,384]{2,1,0:T(8,128)(2,1)S(1)}, bf16[2,96,384]{2,1,0:T(8,128)(2,1)S(1)}, u32[]{:S(2)}, u32[]{:S(2)}) collective-permute-start(bf16[2,96,384]{2,1,0:T(8,128)(2,1)S(1)} %get-tuple-element.42), channel_id=1, source_target_pairs={{0,3},{1,0},{2,1},{3,2},{4,7},{5,4},{6,5},{7,6},{8,11},{9,8},{10,9... | collective-permute-start | bytes 442376 | tf_op jit(solution)/shard_map/ppermute | solution.py:309
  17.3 17.6 %collective-permute-start.9 = (bf16[2,384,128]{2,1,0:T(8,128)(2,1)S(1)}, bf16[2,384,128]{2,1,0:T(8,128)(2,1)S(1)}, u32[]{:S(2)}, u32[]{:S(2)}) collective-permute-start(bf16[2,384,128]{2,1,0:T(8,128)(2,1)S(1)} %get-tuple-element.56), channel_id=1, source_target_pairs={{0,240},{16,0},{32,16},{48,32},{64,48},{80,64},{96,80},{112,96},{1... | collective-permute-start | bytes 589832 | tf_op jit(solution)/shard_map/ppermute | solution.py:289
  21.4 14.0 %collective-permute-start.10 = (bf16[2,384,128]{2,1,0:T(8,128)(2,1)S(1)}, bf16[2,384,128]{2,1,0:T(8,128)(2,1)S(1)}, u32[]{:S(2)}, u32[]{:S(2)}) collective-permute-start(bf16[2,384,128]{2,1,0:T(8,128)(2,1)S(1)} %get-tuple-element.57), channel_id=1, source_target_pairs={{0,16},{16,32},{32,48},{48,64},{64,80},{80,96},{96,112},{112,128},... | collective-permute-start | bytes 589832 | tf_op jit(solution)/shard_map/ppermute | solution.py:288
  23.2 7.2 %collective-permute-start.3 = (bf16[216,384]{1,0:T(8,128)(2,1)S(1)}, bf16[216,384]{1,0:T(8,128)(2,1)S(1)}, u32[]{:S(2)}, u32[]{:S(2)}) collective-permute-start(bf16[216,384]{1,0:T(8,128)(2,1)S(1)} %get-tuple-element.46), channel_id=1, source_target_pairs={{0,4},{1,5},{2,6},{3,7},{4,8},{5,9},{6,10},{7,11},{8,12},{9,13},{1... | collective-permute-start | bytes 497672 | tf_op jit(solution)/shard_map/ppermute | solution.py:309
  24.0 8.6 %collective-permute-start.4 = (bf16[216,384]{1,0:T(8,128)(2,1)S(1)}, bf16[216,384]{1,0:T(8,128)(2,1)S(1)}, u32[]{:S(2)}, u32[]{:S(2)}) collective-permute-start(bf16[216,384]{1,0:T(8,128)(2,1)S(1)} %get-tuple-element.47), channel_id=1, source_target_pairs={{0,8},{1,9},{2,10},{3,11},{4,12},{5,13},{6,14},{7,15},{8,0},{9,1},... | collective-permute-start | bytes 497672 | tf_op jit(solution)/shard_map/ppermute | solution.py:309
  26.2 7.9 %collective-permute-start.5 = (bf16[216,384]{1,0:T(8,128)(2,1)S(1)}, bf16[216,384]{1,0:T(8,128)(2,1)S(1)}, u32[]{:S(2)}, u32[]{:S(2)}) collective-permute-start(bf16[216,384]{1,0:T(8,128)(2,1)S(1)} %get-tuple-element.48), channel_id=1, source_target_pairs={{0,12},{1,13},{2,14},{3,15},{4,0},{5,1},{6,2},{7,3},{8,4},{9,5},{1... | collective-permute-start | bytes 497672 | tf_op jit(solution)/shard_map/ppermute | solution.py:309
  50.8 7.4 %collective-permute-start.11 = (bf16[2,384,128]{2,1,0:T(8,128)(2,1)S(1)}, bf16[2,384,128]{2,1,0:T(8,128)(2,1)S(1)}, u32[]{:S(2)}, u32[]{:S(2)}) collective-permute-start(bf16[2,384,128]{2,1,0:T(8,128)(2,1)S(1)} %get-tuple-element.60), channel_id=1, source_target_pairs={{0,240},{16,0},{32,16},{48,32},{64,48},{80,64},{96,80},{112,96},{1... | collective-permute-start | bytes 589832 | tf_op jit(solution)/shard_map/ppermute | solution.py:289
  55.0 6.3 %collective-permute-start.12 = (bf16[2,384,128]{2,1,0:T(8,128)(2,1)S(1)}, bf16[2,384,128]{2,1,0:T(8,128)(2,1)S(1)}, u32[]{:S(2)}, u32[]{:S(2)}) collective-permute-start(bf16[2,384,128]{2,1,0:T(8,128)(2,1)S(1)} %get-tuple-element.61), channel_id=1, source_target_pairs={{0,16},{16,32},{32,48},{48,64},{64,80},{80,96},{96,112},{112,128},... | collective-permute-start | bytes 589832 | tf_op jit(solution)/shard_map/ppermute | solution.py:288
  75.4 13.5 %collective-permute-start.13 = (bf16[2,384,128]{2,1,0:T(8,128)(2,1)S(1)}, bf16[2,384,128]{2,1,0:T(8,128)(2,1)S(1)}, u32[]{:S(2)}, u32[]{:S(2)}) collective-permute-start(bf16[2,384,128]{2,1,0:T(8,128)(2,1)S(1)} %get-tuple-element.66), channel_id=1, source_target_pairs={{0,16},{16,32},{32,48},{48,64},{64,80},{80,96},{96,112},{112,128},... | collective-permute-start | bytes 589832 | tf_op jit(solution)/shard_map/ppermute | solution.py:288
  75.4 13.5 %collective-permute-start.14 = (bf16[2,384,128]{2,1,0:T(8,128)(2,1)S(1)}, bf16[2,384,128]{2,1,0:T(8,128)(2,1)S(1)}, u32[]{:S(2)}, u32[]{:S(2)}) collective-permute-start(bf16[2,384,128]{2,1,0:T(8,128)(2,1)S(1)} %get-tuple-element.67), channel_id=1, source_target_pairs={{0,240},{16,0},{32,16},{48,32},{64,48},{80,64},{96,80},{112,96},{1... | collective-permute-start | bytes 589832 | tf_op jit(solution)/shard_map/ppermute | solution.py:289
  78.5 6.5 %collective-permute-start.6 = (bf16[8,24,384]{2,1,0:T(8,128)(2,1)S(1)}, bf16[8,24,384]{2,1,0:T(8,128)(2,1)S(1)}, u32[]{:S(2)}, u32[]{:S(2)}) collective-permute-start(bf16[8,24,384]{2,1,0:T(8,128)(2,1)S(1)} %get-tuple-element.50), channel_id=1, source_target_pairs={{0,4},{1,5},{2,6},{3,7},{4,8},{5,9},{6,10},{7,11},{8,12},{9,13},{1... | collective-permute-start | bytes 442376 | tf_op jit(solution)/shard_map/ppermute | solution.py:309
  80.7 6.7 %collective-permute-start.7 = (bf16[8,24,384]{2,1,0:T(8,128)(2,1)S(1)}, bf16[8,24,384]{2,1,0:T(8,128)(2,1)S(1)}, u32[]{:S(2)}, u32[]{:S(2)}) collective-permute-start(bf16[8,24,384]{2,1,0:T(8,128)(2,1)S(1)} %get-tuple-element.51), channel_id=1, source_target_pairs={{0,8},{1,9},{2,10},{3,11},{4,12},{5,13},{6,14},{7,15},{8,0},{9,1},... | collective-permute-start | bytes 442376 | tf_op jit(solution)/shard_map/ppermute | solution.py:309
  81.1 7.8 %collective-permute-start.8 = (bf16[8,24,384]{2,1,0:T(8,128)(2,1)S(1)}, bf16[8,24,384]{2,1,0:T(8,128)(2,1)S(1)}, u32[]{:S(2)}, u32[]{:S(2)}) collective-permute-start(bf16[8,24,384]{2,1,0:T(8,128)(2,1)S(1)} %get-tuple-element.52), channel_id=1, source_target_pairs={{0,12},{1,13},{2,14},{3,15},{4,0},{5,1},{6,2},{7,3},{8,4},{9,5},{1... | collective-permute-start | bytes 442376 | tf_op jit(solution)/shard_map/ppermute | solution.py:309

commit v13 on v9

--- a/solution.py
+++ b/solution.py
@@ -28,8 +28,8 @@
     return lax.shift_right_logical(member, 2), lax.bitwise_and(member, 3)
 
 
-def wrap(index):
-    return lax.bitwise_and(index, 3)
+def swap(index, k):
+    return lax.bitwise_xor(index, k)
 
 
 def column_of(row, first, count):
@@ -48,7 +48,7 @@
     copies = [pltpu.make_async_copy(residual_hbm, residual_ref, sems.at[0]),
               pltpu.make_async_copy(diag_hbm, diag_ref, sems.at[1])]
     for k, part in enumerate((part0, part1, part2, part3)):
-        at = pl.multiple_of(wrap(q + k) * SHARE, SHARE)
+        at = pl.multiple_of(swap(q, k) * SHARE, SHARE)
         copies.append(pltpu.make_async_copy(tiles_hbm.at[:, pl.ds(at, SHARE)], part, sems.at[2 + k]))
     for copy in copies:
         copy.start()
@@ -89,13 +89,13 @@
     for s in range(SIDE):
         at = slice(SLAB * s, SLAB * (s + 1))
         tail = jnp.concatenate([thirds(high[at]), thirds(low[at]), line_ref[...]], axis=0)
-        held_ref[wrap(s - x), 192:PIECE] = tail.astype(BF16)
+        held_ref[swap(x, s), 192:PIECE] = tail.astype(BF16)
     for k in range(SIDE):
         tiles = [parts[k][j].astype(F32) for j in range(2)]
-        to = pl.multiple_of(48 * wrap(q - k), 48)
+        to = pl.multiple_of(48 * swap(q, k), 48)
         for s in range(SIDE):
             pair = jnp.concatenate([tile[SLAB * s:SLAB * (s + 1)] for tile in tiles], axis=0)
-            held_ref[wrap(s - x), pl.ds(to, 48)] = pair.astype(BF16)
+            held_ref[swap(x, s), pl.ds(to, 48)] = pair.astype(BF16)
     for k in range(SIDE):
         outs[k][...] = held_ref[k]
 
@@ -135,7 +135,7 @@
 
 
 def slot_of(slot_ref, x, k, i):
-    return slot_ref[0, 8 * wrap(x - k) + i]
+    return slot_ref[0, 8 * swap(x, k) + i]
 
 
 def order_kernel(slot_ref, *refs):
@@ -145,7 +145,7 @@
         for y in range(SIDE):
             pair = parts[k][48 * y:48 * (y + 1)].astype(F32)
             for j in range(2):
-                to = lax.bitwise_and(slot_of(slot_ref, x, k, 2 * y + j) - 8 * x, TILES - 1)
+                to = lax.bitwise_xor(slot_of(slot_ref, x, k, 2 * y + j), 8 * x)
                 held_ref[to] = pair[SLAB * j:SLAB * (j + 1)].astype(BF16)
     for k in range(SIDE):
         outs[k][...] = held_ref[8 * k:8 * k + 8]
@@ -190,7 +190,7 @@
         row = tail[16:17, 0:128] + (tail[16:17, 128:256] + tail[16:17, 256:384])
         start = unthirds(tail[0:8]) + unthirds(tail[8:16])
         scale = jnp.broadcast_to(column_of(row, x * SLAB, SLAB), (SLAB, NRHS))
-        r = wrap(x - k)
+        r = swap(x, k)
         start_ref[r] = start
         scale_ref[r] = scale
         first_ref[r] = GAIN * (start - scale * total_ref[r])
@@ -228,7 +228,7 @@
         left = jnp.concatenate([part[k] for part in parts], axis=0)
         total += jnp.dot(left, ext_ref[cols_ref[x, k]], preferred_element_type=F32)
     for k in range(SIDE):
-        line_ref[pl.ds(pl.multiple_of(wrap(x - k) * SLAB, 8), SLAB), :] = total[SLAB * k:SLAB * (k + 1)]
+        line_ref[pl.ds(pl.multiple_of(swap(x, k) * SLAB, 8), SLAB), :] = total[SLAB * k:SLAB * (k + 1)]
     mine = pl.ds(pl.multiple_of(q * SHARE, SHARE), SHARE)
     rest = jnp.concatenate([got_ref[SIDE * s + q, SHARE:120].astype(F32) for s in range(SIDE)], axis=0)
     second = own_ref[x, mine].astype(F32) - scale_ref[...] * line_ref[...]
@@ -281,11 +281,11 @@
         return call(kernel, [rows] + near(got), [OWN] + HALVES, 1)
 
     def along_x(values):
-        pairs = [[(m, (m + SIDE * k) % GROUP) for m in range(GROUP)] for k in range(SIDE)]
+        pairs = [[(m, m ^ (SIDE * k)) for m in range(GROUP)] for k in range(SIDE)]
         return exchange(values, pairs)
 
     def along_y(values):
-        pairs = [[(m, m - m % SIDE + (m + k) % SIDE) for m in range(GROUP)] for k in range(SIDE)]
+        pairs = [[(m, m ^ k) for m in range(GROUP)] for k in range(SIDE)]
         return exchange(values, pairs)
 
     def exchange(values, pairs):

time: 88.3 us -> 88.5 us (level)
  waiting for transfers between devices: 20.5 us -> 25.1 us
  blocking collectives: 27.7 us -> 23.8 us
    all_to_all x2, blocking collectives: 27.7 us -> 23.8 us  [gather(): return lax.all_to_all(wide, 'grp', 0, 0)]
    ppermute x9, waiting for transfers between devices: 12.2 us -> 15.7 us  [exchange(): out.append(lax.ppermute(values[k], 'grp', pairs[k]))]
    all_to_all x1, waiting for transfers between devices: 2.53 us -> 3.62 us  [gather(): return lax.all_to_all(wide, 'grp', 0, 0)]
    ppermute x9, starting transfers between devices: 12.8 us -> 11.8 us  [exchange(): out.append(lax.ppermute(values[k], 'grp', pairs[k]))]
  transfers between devices with their start and end apart: 16 -> 16, of which waited for: 9 -> 11; matrix products, arithmetic and copies ran while one was open for 0% -> 0% of each run, Pallas kernels for 3% -> 3%
where the time goes in v13:
time: 88.5 us; the launch traced here: 88.2 us
  starting transfers between devices  32.1 us (36%)
  waiting for transfers between devices  25.1 us (28%)
  blocking collectives  23.8 us (27%)
  Pallas kernels  7.07 us (8%)
    all_to_all x2, blocking collectives, gather(): return lax.all_to_all(wide, 'grp', 0, 0)  23.8 us
    ppermute x9, waiting for transfers between devices, exchange(): out.append(lax.ppermute(values[k], 'grp', pairs[k]))  15.7 us
    ppermute x9, starting transfers between devices, exchange(): out.append(lax.ppermute(values[k], 'grp', pairs[k]))  11.8 us
    ppermute x3, starting transfers between devices, halo(): lax.ppermute(up, 'lead', [(i, (i + 1) % leads) for i in range(leads)])  11.1 us
    all_to_all x1, starting transfers between devices, gather(): return lax.all_to_all(wide, 'grp', 0, 0)  6.77 us
    pallas_call x11, Pallas kernels, call(): pl.pallas_call(kernel, in_specs=specs, out_specs=[VMEM] * len(outs), out_...  6.27 us
    ppermute x3, waiting for transfers between devices, halo(): lax.ppermute(down, 'lead', [(i, (i - 1) % leads) for i in range(leads)])  3.7 us
    all_to_all x1, waiting for transfers between devices, gather(): return lax.all_to_all(wide, 'grp', 0, 0)  3.62 us
  transfers between devices with their start and end apart: 16, of which 11 were waited for; matrix products, arithmetic and copies ran while one was open for 0% of the time, Pallas kernels for 3%

profile of v13, /device:TPU:97, one launch (start us, length us, event | category | flops | bytes accessed | tf_op | source)
XLA Modules:
  0.0 88.2 jit_solution(10149772879324621593)
XLA Ops:
  0.0 2.0 %shard_map.64 = (bf16[2,96,384]{2,1,0:T(8,128)(2,1)S(1)}, bf16[2,96,384]{2,1,0:T(8,128)(2,1)S(1)}, bf16[2,96,384]{2,1,0:T(8,128)(2,1)S(1)}, bf16[2,96,384]{2,1,0...) custom-call(bf16[2,384,384]{2,1,0:T(8,128)(2,1)} %tiles_hbm.1, ...), custom_call_target="tpu_custom_call" | custom-call | tf_op jit(solution)/shard_map/pallas_call | solution.py:248
  2.0 6.8 %all-to-all-start = ((bf16[16,96,128]{2,1,0:T(8,128)(2,1)}), bf16[16,96,128]{2,1,0:T(8,128)(2,1)S(1)}, u32[]{:S(2)}, u32[]{:S(2)}) async-start(bf16[16,96,128]{2,1,0:T(8,128)(2,1)} %get-tuple-element.54), calls=%async_computation | async-start | bytes 786432 | tf_op jit(solution)/shard_map/all_to_all | solution.py:278
  8.8 1.4 %collective-permute-start = (bf16[2,96,384]{2,1,0:T(8,128)(2,1)S(1)}, bf16[2,96,384]{2,1,0:T(8,128)(2,1)S(1)}, u32[]{:S(2)}, u32[]{:S(2)}) collective-permute-start(bf16[2,96,384]{2,1,0:T(8,128)(2,1)S(1)} %get-tuple-element.40), channel_id=1, source_target_pairs={{0,1},{1,0},{2,3},{3,2},{4,5},{5,4},{6,7},{7,6},{8,9},{9,8},{10,11... | collective-permute-start | bytes 442376 | tf_op jit(solution)/shard_map/ppermute | solution.py:294
  10.1 2.4 %collective-permute-start.1 = (bf16[2,96,384]{2,1,0:T(8,128)(2,1)S(1)}, bf16[2,96,384]{2,1,0:T(8,128)(2,1)S(1)}, u32[]{:S(2)}, u32[]{:S(2)}) collective-permute-start(bf16[2,96,384]{2,1,0:T(8,128)(2,1)S(1)} %get-tuple-element.41), channel_id=1, source_target_pairs={{0,2},{1,3},{2,0},{3,1},{4,6},{5,7},{6,4},{7,5},{8,10},{9,11},{10,... | collective-permute-start | bytes 442376 | tf_op jit(solution)/shard_map/ppermute | solution.py:294
  12.5 0.2 collective-permute-start.2
  12.7 0.8 tables.1
  13.5 3.6 %all-to-all-done.got_ref = bf16[16,96,128]{2,1,0:T(8,128)(2,1)S(1)} async-done(((bf16[16,96,128]{2,1,0:T(8,128)(2,1)}), bf16[16,96,128]{2,1,0:T(8,128)(2,1)S(1)}, u32[]{:S(2)}, u32[]{:S(2)}) %all-to-all-start) | async-done | bytes 393248 | tf_op jit(solution)/shard_map/all_to_all | solution.py:278
  17.1 0.1 shard_map.67
  17.2 2.4 %collective-permute-start.10 = (bf16[2,384,128]{2,1,0:T(8,128)(2,1)S(1)}, bf16[2,384,128]{2,1,0:T(8,128)(2,1)S(1)}, u32[]{:S(2)}, u32[]{:S(2)}) collective-permute-start(bf16[2,384,128]{2,1,0:T(8,128)(2,1)S(1)} %get-tuple-element.57), channel_id=1, source_target_pairs={{0,240},{16,0},{32,16},{48,32},{64,48},{80,64},{96,80},{112,96},{1... | collective-permute-start | bytes 589832 | tf_op jit(solution)/shard_map/ppermute | solution.py:274
  19.6 2.8 %collective-permute-start.9 = (bf16[2,384,128]{2,1,0:T(8,128)(2,1)S(1)}, bf16[2,384,128]{2,1,0:T(8,128)(2,1)S(1)}, u32[]{:S(2)}, u32[]{:S(2)}) collective-permute-start(bf16[2,384,128]{2,1,0:T(8,128)(2,1)S(1)} %get-tuple-element.56), channel_id=1, source_target_pairs={{0,16},{16,32},{32,48},{48,64},{64,80},{80,96},{96,112},{112,128},... | collective-permute-start | bytes 589832 | tf_op jit(solution)/shard_map/ppermute | solution.py:273
  22.4 0.0 collective-permute-done.refs_1_
  22.4 0.1 collective-permute-done.1.refs_2_
  22.5 1.8 %collective-permute-done.2.refs_3_ = bf16[2,96,384]{2,1,0:T(8,128)(2,1)S(1)} collective-permute-done((bf16[2,96,384]{2,1,0:T(8,128)(2,1)S(1)}, bf16[2,96,384]{2,1,0:T(8,128)(2,1)S(1)}, u32[]{:S(2)}, u32[]{:S(2)}) %collective-permute-start.2) | collective-permute-done | bytes 147488 | tf_op jit(solution)/shard_map/ppermute | solution.py:294
  24.3 0.1 shard_map.65
  24.4 0.1 collective-permute-start.3
  24.5 2.3 %collective-permute-start.4 = (bf16[216,384]{1,0:T(8,128)(2,1)S(1)}, bf16[216,384]{1,0:T(8,128)(2,1)S(1)}, u32[]{:S(2)}, u32[]{:S(2)}) collective-permute-start(bf16[216,384]{1,0:T(8,128)(2,1)S(1)} %get-tuple-element.47), channel_id=1, source_target_pairs={{0,8},{1,9},{2,10},{3,11},{4,12},{5,13},{6,14},{7,15},{8,0},{9,1},... | collective-permute-start | bytes 497672 | tf_op jit(solution)/shard_map/ppermute | solution.py:294
  26.8 1.6 %collective-permute-start.5 = (bf16[216,384]{1,0:T(8,128)(2,1)S(1)}, bf16[216,384]{1,0:T(8,128)(2,1)S(1)}, u32[]{:S(2)}, u32[]{:S(2)}) collective-permute-start(bf16[216,384]{1,0:T(8,128)(2,1)S(1)} %get-tuple-element.48), channel_id=1, source_target_pairs={{0,12},{1,13},{2,14},{3,15},{4,8},{5,9},{6,10},{7,11},{8,4},{9,5},... | collective-permute-start | bytes 497672 | tf_op jit(solution)/shard_map/ppermute | solution.py:294
  28.3 0.9 %collective-permute-done.3.refs_1_ = bf16[216,384]{1,0:T(8,128)(2,1)S(1)} collective-permute-done((bf16[216,384]{1,0:T(8,128)(2,1)S(1)}, bf16[216,384]{1,0:T(8,128)(2,1)S(1)}, u32[]{:S(2)}, u32[]{:S(2)}) %collective-permute-start.3) | collective-permute-done | bytes 165920 | tf_op jit(solution)/shard_map/ppermute | solution.py:294
  29.3 4.4 %collective-permute-done.4.refs_2_ = bf16[216,384]{1,0:T(8,128)(2,1)S(1)} collective-permute-done((bf16[216,384]{1,0:T(8,128)(2,1)S(1)}, bf16[216,384]{1,0:T(8,128)(2,1)S(1)}, u32[]{:S(2)}, u32[]{:S(2)}) %collective-permute-start.4) | collective-permute-done | bytes 165920 | tf_op jit(solution)/shard_map/ppermute | solution.py:294
  33.6 2.8 %collective-permute-done.5.refs_3_ = bf16[216,384]{1,0:T(8,128)(2,1)S(1)} collective-permute-done((bf16[216,384]{1,0:T(8,128)(2,1)S(1)}, bf16[216,384]{1,0:T(8,128)(2,1)S(1)}, u32[]{:S(2)}, u32[]{:S(2)}) %collective-permute-start.5) | collective-permute-done | bytes 165920 | tf_op jit(solution)/shard_map/ppermute | solution.py:294
  36.5 0.6 shard_map.68.refs_4_
  37.1 0.0 collective-permute-done.10.refs_6_
  37.1 0.0 collective-permute-done.9.refs_5_
  37.1 0.8 shard_map.69
  37.9 11.8 %all_to_all.15.got_ref = bf16[16,96,128]{2,1,0:T(8,128)(2,1)S(1)} all-to-all(bf16[16,96,128]{2,1,0:T(8,128)(2,1)S(1)} %get-tuple-element.58), channel_id=1, replica_groups=mesh['lead'=16,'grp'=16] {'grp'}, dimensions={0} | all-to-all | bytes 786432 | tf_op jit(solution)/shard_map/all_to_all | solution.py:278
  49.7 0.1 shard_map.70
  49.8 5.4 %collective-permute-start.11 = (bf16[2,384,128]{2,1,0:T(8,128)(2,1)S(1)}, bf16[2,384,128]{2,1,0:T(8,128)(2,1)S(1)}, u32[]{:S(2)}, u32[]{:S(2)}) collective-permute-start(bf16[2,384,128]{2,1,0:T(8,128)(2,1)S(1)} %get-tuple-element.60), channel_id=1, source_target_pairs={{0,16},{16,32},{32,48},{48,64},{64,80},{80,96},{96,112},{112,128},... | collective-permute-start | bytes 589832 | tf_op jit(solution)/shard_map/ppermute | solution.py:273
  55.2 0.0 collective-permute-start.12
  55.2 0.6 shard_map.71.refs_4_
  55.8 2.0 %collective-permute-done.11.refs_5_ = bf16[2,384,128]{2,1,0:T(8,128)(2,1)S(1)} collective-permute-done((bf16[2,384,128]{2,1,0:T(8,128)(2,1)S(1)}, bf16[2,384,128]{2,1,0:T(8,128)(2,1)S(1)}, u32[]{:S(2)}, u32[]{:S(2)}) %collective-permute-start.11) | collective-permute-done | bytes 196640 | tf_op jit(solution)/shard_map/ppermute | solution.py:273
  57.8 3.7 %collective-permute-done.12.refs_6_ = bf16[2,384,128]{2,1,0:T(8,128)(2,1)S(1)} collective-permute-done((bf16[2,384,128]{2,1,0:T(8,128)(2,1)S(1)}, bf16[2,384,128]{2,1,0:T(8,128)(2,1)S(1)}, u32[]{:S(2)}, u32[]{:S(2)}) %collective-permute-start.12) | collective-permute-done | bytes 196640 | tf_op jit(solution)/shard_map/ppermute | solution.py:274
  61.5 0.8 shard_map.72
  62.3 12.0 %all_to_all.16.got_ref.refs_7_ = bf16[16,120,128]{2,1,0:T(8,128)(2,1)S(1)} all-to-all(bf16[16,120,128]{2,1,0:T(8,128)(2,1)S(1)} %shard_map.72), channel_id=1, replica_groups=mesh['lead'=16,'grp'=16] {'grp'}, dimensions={0} | all-to-all | bytes 983040 | tf_op jit(solution)/shard_map/all_to_all | solution.py:278
  74.4 0.1 shard_map.73
  74.5 2.9 %collective-permute-start.13 = (bf16[2,384,128]{2,1,0:T(8,128)(2,1)S(1)}, bf16[2,384,128]{2,1,0:T(8,128)(2,1)S(1)}, u32[]{:S(2)}, u32[]{:S(2)}) collective-permute-start(bf16[2,384,128]{2,1,0:T(8,128)(2,1)S(1)} %get-tuple-element.66), channel_id=1, source_target_pairs={{0,16},{16,32},{32,48},{48,64},{64,80},{80,96},{96,112},{112,128},... | collective-permute-start | bytes 589832 | tf_op jit(solution)/shard_map/ppermute | solution.py:273
  77.4 0.0 collective-permute-start.14
  77.4 0.1 shard_map.66
  77.5 0.1 collective-permute-start.6
  77.6 2.0 %collective-permute-start.7 = (bf16[8,24,384]{2,1,0:T(8,128)(2,1)S(1)}, bf16[8,24,384]{2,1,0:T(8,128)(2,1)S(1)}, u32[]{:S(2)}, u32[]{:S(2)}) collective-permute-start(bf16[8,24,384]{2,1,0:T(8,128)(2,1)S(1)} %get-tuple-element.51), channel_id=1, source_target_pairs={{0,8},{1,9},{2,10},{3,11},{4,12},{5,13},{6,14},{7,15},{8,0},{9,1},... | collective-permute-start | bytes 442376 | tf_op jit(solution)/shard_map/ppermute | solution.py:294
  79.6 1.8 %collective-permute-start.8 = (bf16[8,24,384]{2,1,0:T(8,128)(2,1)S(1)}, bf16[8,24,384]{2,1,0:T(8,128)(2,1)S(1)}, u32[]{:S(2)}, u32[]{:S(2)}) collective-permute-start(bf16[8,24,384]{2,1,0:T(8,128)(2,1)S(1)} %get-tuple-element.52), channel_id=1, source_target_pairs={{0,12},{1,13},{2,14},{3,15},{4,8},{5,9},{6,10},{7,11},{8,4},{9,5},... | collective-permute-start | bytes 442376 | tf_op jit(solution)/shard_map/ppermute | solution.py:294
  81.5 1.6 %collective-permute-done.6.refs_1_ = bf16[8,24,384]{2,1,0:T(8,128)(2,1)S(1)} collective-permute-done((bf16[8,24,384]{2,1,0:T(8,128)(2,1)S(1)}, bf16[8,24,384]{2,1,0:T(8,128)(2,1)S(1)}, u32[]{:S(2)}, u32[]{:S(2)}) %collective-permute-start.6) | collective-permute-done | bytes 147488 | tf_op jit(solution)/shard_map/ppermute | solution.py:294
  83.1 2.0 %collective-permute-done.7.refs_2_ = bf16[8,24,384]{2,1,0:T(8,128)(2,1)S(1)} collective-permute-done((bf16[8,24,384]{2,1,0:T(8,128)(2,1)S(1)}, bf16[8,24,384]{2,1,0:T(8,128)(2,1)S(1)}, u32[]{:S(2)}, u32[]{:S(2)}) %collective-permute-start.7) | collective-permute-done | bytes 147488 | tf_op jit(solution)/shard_map/ppermute | solution.py:294
  85.1 2.1 %collective-permute-done.8.refs_3_ = bf16[8,24,384]{2,1,0:T(8,128)(2,1)S(1)} collective-permute-done((bf16[8,24,384]{2,1,0:T(8,128)(2,1)S(1)}, bf16[8,24,384]{2,1,0:T(8,128)(2,1)S(1)}, u32[]{:S(2)}, u32[]{:S(2)}) %collective-permute-start.8) | collective-permute-done | bytes 147488 | tf_op jit(solution)/shard_map/ppermute | solution.py:294
  87.2 0.0 collective-permute-done.13.refs_5_
  87.2 0.0 collective-permute-done.14.refs_6_
  87.2 1.0 %shard_map.74 = f32[96,128]{1,0:T(8,128)} custom-call(s32[4,8]{1,0:T(4,128)S(4)} %get-tuple-element.37.cols_ref, bf16[8,24,384]{2,1,0:T(8,128)(2,1)S(1)} %get-tuple-element.49.refs_0_, bf16[8,24,384]{2,1,0:T(8,128)(2,1)S(1)} %collective-permute-done.6.refs_1_, bf16[8,24,384]{2,1,0:T(8,128)(2,1)S(1)} %collective-permute-done.7.refs_2_, ...), custom_call_target="tpu_custom_call" | custom-call | tf_op jit(solution)/shard_map/pallas_call | solution.py:248
Async XLA Ops:
  2.0 15.1 %all-to-all-start = ((bf16[16,96,128]{2,1,0:T(8,128)(2,1)}), bf16[16,96,128]{2,1,0:T(8,128)(2,1)S(1)}, u32[]{:S(2)}, u32[]{:S(2)}) async-start(bf16[16,96,128]{2,1,0:T(8,128)(2,1)} %get-tuple-element.54), calls=%async_computation | async-start | bytes 786432 | tf_op jit(solution)/shard_map/all_to_all | solution.py:278
  8.8 13.6 %collective-permute-start = (bf16[2,96,384]{2,1,0:T(8,128)(2,1)S(1)}, bf16[2,96,384]{2,1,0:T(8,128)(2,1)S(1)}, u32[]{:S(2)}, u32[]{:S(2)}) collective-permute-start(bf16[2,96,384]{2,1,0:T(8,128)(2,1)S(1)} %get-tuple-element.40), channel_id=1, source_target_pairs={{0,1},{1,0},{2,3},{3,2},{4,5},{5,4},{6,7},{7,6},{8,9},{9,8},{10,11... | collective-permute-start | bytes 442376 | tf_op jit(solution)/shard_map/ppermute | solution.py:294
  10.1 12.4 %collective-permute-start.1 = (bf16[2,96,384]{2,1,0:T(8,128)(2,1)S(1)}, bf16[2,96,384]{2,1,0:T(8,128)(2,1)S(1)}, u32[]{:S(2)}, u32[]{:S(2)}) collective-permute-start(bf16[2,96,384]{2,1,0:T(8,128)(2,1)S(1)} %get-tuple-element.41), channel_id=1, source_target_pairs={{0,2},{1,3},{2,0},{3,1},{4,6},{5,7},{6,4},{7,5},{8,10},{9,11},{10,... | collective-permute-start | bytes 442376 | tf_op jit(solution)/shard_map/ppermute | solution.py:294
  12.5 11.7 %collective-permute-start.2 = (bf16[2,96,384]{2,1,0:T(8,128)(2,1)S(1)}, bf16[2,96,384]{2,1,0:T(8,128)(2,1)S(1)}, u32[]{:S(2)}, u32[]{:S(2)}) collective-permute-start(bf16[2,96,384]{2,1,0:T(8,128)(2,1)S(1)} %get-tuple-element.42), channel_id=1, source_target_pairs={{0,3},{1,2},{2,1},{3,0},{4,7},{5,6},{6,5},{7,4},{8,11},{9,10},{10,... | collective-permute-start | bytes 442376 | tf_op jit(solution)/shard_map/ppermute | solution.py:294
  17.2 19.9 %collective-permute-start.10 = (bf16[2,384,128]{2,1,0:T(8,128)(2,1)S(1)}, bf16[2,384,128]{2,1,0:T(8,128)(2,1)S(1)}, u32[]{:S(2)}, u32[]{:S(2)}) collective-permute-start(bf16[2,384,128]{2,1,0:T(8,128)(2,1)S(1)} %get-tuple-element.57), channel_id=1, source_target_pairs={{0,240},{16,0},{32,16},{48,32},{64,48},{80,64},{96,80},{112,96},{1... | collective-permute-start | bytes 589832 | tf_op jit(solution)/shard_map/ppermute | solution.py:274
  19.6 17.5 %collective-permute-start.9 = (bf16[2,384,128]{2,1,0:T(8,128)(2,1)S(1)}, bf16[2,384,128]{2,1,0:T(8,128)(2,1)S(1)}, u32[]{:S(2)}, u32[]{:S(2)}) collective-permute-start(bf16[2,384,128]{2,1,0:T(8,128)(2,1)S(1)} %get-tuple-element.56), channel_id=1, source_target_pairs={{0,16},{16,32},{32,48},{48,64},{64,80},{80,96},{96,112},{112,128},... | collective-permute-start | bytes 589832 | tf_op jit(solution)/shard_map/ppermute | solution.py:273
  24.4 4.9 %collective-permute-start.3 = (bf16[216,384]{1,0:T(8,128)(2,1)S(1)}, bf16[216,384]{1,0:T(8,128)(2,1)S(1)}, u32[]{:S(2)}, u32[]{:S(2)}) collective-permute-start(bf16[216,384]{1,0:T(8,128)(2,1)S(1)} %get-tuple-element.46), channel_id=1, source_target_pairs={{0,4},{1,5},{2,6},{3,7},{4,0},{5,1},{6,2},{7,3},{8,12},{9,13},{10,... | collective-permute-start | bytes 497672 | tf_op jit(solution)/shard_map/ppermute | solution.py:294
  24.5 9.2 %collective-permute-start.4 = (bf16[216,384]{1,0:T(8,128)(2,1)S(1)}, bf16[216,384]{1,0:T(8,128)(2,1)S(1)}, u32[]{:S(2)}, u32[]{:S(2)}) collective-permute-start(bf16[216,384]{1,0:T(8,128)(2,1)S(1)} %get-tuple-element.47), channel_id=1, source_target_pairs={{0,8},{1,9},{2,10},{3,11},{4,12},{5,13},{6,14},{7,15},{8,0},{9,1},... | collective-permute-start | bytes 497672 | tf_op jit(solution)/shard_map/ppermute | solution.py:294
  26.8 9.7 %collective-permute-start.5 = (bf16[216,384]{1,0:T(8,128)(2,1)S(1)}, bf16[216,384]{1,0:T(8,128)(2,1)S(1)}, u32[]{:S(2)}, u32[]{:S(2)}) collective-permute-start(bf16[216,384]{1,0:T(8,128)(2,1)S(1)} %get-tuple-element.48), channel_id=1, source_target_pairs={{0,12},{1,13},{2,14},{3,15},{4,8},{5,9},{6,10},{7,11},{8,4},{9,5},... | collective-permute-start | bytes 497672 | tf_op jit(solution)/shard_map/ppermute | solution.py:294
  49.8 8.0 %collective-permute-start.11 = (bf16[2,384,128]{2,1,0:T(8,128)(2,1)S(1)}, bf16[2,384,128]{2,1,0:T(8,128)(2,1)S(1)}, u32[]{:S(2)}, u32[]{:S(2)}) collective-permute-start(bf16[2,384,128]{2,1,0:T(8,128)(2,1)S(1)} %get-tuple-element.60), channel_id=1, source_target_pairs={{0,16},{16,32},{32,48},{48,64},{64,80},{80,96},{96,112},{112,128},... | collective-permute-start | bytes 589832 | tf_op jit(solution)/shard_map/ppermute | solution.py:273
  55.2 6.3 %collective-permute-start.12 = (bf16[2,384,128]{2,1,0:T(8,128)(2,1)S(1)}, bf16[2,384,128]{2,1,0:T(8,128)(2,1)S(1)}, u32[]{:S(2)}, u32[]{:S(2)}) collective-permute-start(bf16[2,384,128]{2,1,0:T(8,128)(2,1)S(1)} %get-tuple-element.61), channel_id=1, source_target_pairs={{0,240},{16,0},{32,16},{48,32},{64,48},{80,64},{96,80},{112,96},{1... | collective-permute-start | bytes 589832 | tf_op jit(solution)/shard_map/ppermute | solution.py:274
  74.5 12.7 %collective-permute-start.13 = (bf16[2,384,128]{2,1,0:T(8,128)(2,1)S(1)}, bf16[2,384,128]{2,1,0:T(8,128)(2,1)S(1)}, u32[]{:S(2)}, u32[]{:S(2)}) collective-permute-start(bf16[2,384,128]{2,1,0:T(8,128)(2,1)S(1)} %get-tuple-element.66), channel_id=1, source_target_pairs={{0,16},{16,32},{32,48},{48,64},{64,80},{80,96},{96,112},{112,128},... | collective-permute-start | bytes 589832 | tf_op jit(solution)/shard_map/ppermute | solution.py:273
  77.4 9.8 %collective-permute-start.14 = (bf16[2,384,128]{2,1,0:T(8,128)(2,1)S(1)}, bf16[2,384,128]{2,1,0:T(8,128)(2,1)S(1)}, u32[]{:S(2)}, u32[]{:S(2)}) collective-permute-start(bf16[2,384,128]{2,1,0:T(8,128)(2,1)S(1)} %get-tuple-element.67), channel_id=1, source_target_pairs={{0,240},{16,0},{32,16},{48,32},{64,48},{80,64},{96,80},{112,96},{1... | collective-permute-start | bytes 589832 | tf_op jit(solution)/shard_map/ppermute | solution.py:274
  77.5 5.6 %collective-permute-start.6 = (bf16[8,24,384]{2,1,0:T(8,128)(2,1)S(1)}, bf16[8,24,384]{2,1,0:T(8,128)(2,1)S(1)}, u32[]{:S(2)}, u32[]{:S(2)}) collective-permute-start(bf16[8,24,384]{2,1,0:T(8,128)(2,1)S(1)} %get-tuple-element.50), channel_id=1, source_target_pairs={{0,4},{1,5},{2,6},{3,7},{4,0},{5,1},{6,2},{7,3},{8,12},{9,13},{10,... | collective-permute-start | bytes 442376 | tf_op jit(solution)/shard_map/ppermute | solution.py:294
  77.6 7.4 %collective-permute-start.7 = (bf16[8,24,384]{2,1,0:T(8,128)(2,1)S(1)}, bf16[8,24,384]{2,1,0:T(8,128)(2,1)S(1)}, u32[]{:S(2)}, u32[]{:S(2)}) collective-permute-start(bf16[8,24,384]{2,1,0:T(8,128)(2,1)S(1)} %get-tuple-element.51), channel_id=1, source_target_pairs={{0,8},{1,9},{2,10},{3,11},{4,12},{5,13},{6,14},{7,15},{8,0},{9,1},... | collective-permute-start | bytes 442376 | tf_op jit(solution)/shard_map/ppermute | solution.py:294
  79.6 7.5 %collective-permute-start.8 = (bf16[8,24,384]{2,1,0:T(8,128)(2,1)S(1)}, bf16[8,24,384]{2,1,0:T(8,128)(2,1)S(1)}, u32[]{:S(2)}, u32[]{:S(2)}) collective-permute-start(bf16[8,24,384]{2,1,0:T(8,128)(2,1)S(1)} %get-tuple-element.52), channel_id=1, source_target_pairs={{0,12},{1,13},{2,14},{3,15},{4,8},{5,9},{6,10},{7,11},{8,4},{9,5},... | collective-permute-start | bytes 442376 | tf_op jit(solution)/shard_map/ppermute | solution.py:294

commit v14 on v9

--- a/solution.py
+++ b/solution.py
@@ -43,7 +43,7 @@
 
 
 def start_kernel(tiles_hbm, residual_hbm, diag_hbm, part0, part1, part2, part3, wide_ref, start_ref, scale_ref,
-                 line_ref, residual_ref, diag_ref, sems):
+                 line_ref, residual_ref, diag_ref, high_ref, sems):
     _, q = place()
     copies = [pltpu.make_async_copy(residual_hbm, residual_ref, sems.at[0]),
               pltpu.make_async_copy(diag_hbm, diag_ref, sems.at[1])]
@@ -62,8 +62,11 @@
     scaled = residual_ref[...] * scale
     scale_ref[...] = scale
     start_ref[...] = scaled
-    spread(scaled, wide_ref)
-    for copy in copies[2:]:
+    high_ref[...] = scaled.astype(BF16)
+    pieces = [pltpu.make_async_copy(high_ref, wide_ref.at[m], sems.at[6 + m]) for m in range(GROUP)]
+    for piece in pieces:
+        piece.start()
+    for copy in copies[2:] + pieces:
         copy.wait()
 
 
@@ -239,13 +242,14 @@
     return pltpu.VMEM(shape, dtype)
 
 
-def call(kernel, args, outs, scalars=0, scratch=(), far=0):
+def call(kernel, args, outs, scalars=0, scratch=(), far=0, away=()):
     vectors = args[scalars:]
     space = pltpu.HBM if far else pltpu.VMEM
     vectors = [pltpu.with_memory_space_constraint(a, space) for a in vectors]
     specs = [SMEM] * scalars + [pl.BlockSpec(memory_space=space)] * len(vectors)
     tables = [pltpu.with_memory_space_constraint(a, pltpu.SMEM) for a in args[:scalars]]
-    return pl.pallas_call(kernel, in_specs=specs, out_specs=[VMEM] * len(outs),
+    return pl.pallas_call(kernel, in_specs=specs,
+                          out_specs=[pl.BlockSpec(memory_space=pltpu.HBM) if n in away else VMEM for n in range(len(outs))],
                           out_shape=outs, scratch_shapes=list(scratch),
                           compiler_params=pltpu.CompilerParams(vmem_limit_bytes=GRANT))(*tables, *vectors)
 
@@ -296,8 +300,9 @@
 
     *quarters, wide, start, scale, line = call(
         start_kernel, [matrix_tiles, residual, diag],
-        [arr((2, SHARE, TILE), BF16)] * 4 + [WIDE, ROWS, ROWS, arr((8, TILE), F32)],
-        scratch=(ROWS, arr((1, SHARE), F32), pltpu.SemaphoreType.DMA((6,))), far=1)
+        [arr((2, SHARE, TILE), BF16)] * 4 + [pltpu.HBM((GROUP, SHARE, NRHS), BF16), ROWS, ROWS, arr((8, TILE), F32)],
+        scratch=(ROWS, arr((1, SHARE), F32), arr((SHARE, NRHS), BF16), pltpu.SemaphoreType.DMA((6 + GROUP,))), far=1,
+        away=(4,))
     tables = [pltpu.SMEM((1, TILES), jnp.int32), pltpu.SMEM((SIDE, 8), jnp.int32), pltpu.SMEM((2, 2), jnp.int32)]
     tile_slot, tile_cols, rows = pl.pallas_call(
         table_kernel, name="tables", in_specs=[SMEM] * 3, out_specs=[SMEM] * 3, out_shape=tables)(

time: 88.3 us -> 88.2 us (level)
  no operation moved by 1% of the time
where the time goes in v14:
time: 88.2 us; the launch traced here: 87.5 us
  starting transfers between devices  32.3 us (37%)
  blocking collectives  27.7 us (31%)
  waiting for transfers between devices  20.5 us (23%)
  Pallas kernels  6.96 us (8%)
    all_to_all x2, blocking collectives, gather(): return lax.all_to_all(wide, 'grp', 0, 0)  27.7 us
    ppermute x9, starting transfers between devices, exchange(): out.append(lax.ppermute(values[k], 'grp', pairs[k]))  12.8 us
    ppermute x9, waiting for transfers between devices, exchange(): out.append(lax.ppermute(values[k], 'grp', pairs[k]))  12.2 us
    ppermute x3, starting transfers between devices, halo(): lax.ppermute(up, 'lead', [(i, (i + 1) % leads) for i in range(leads)])  10.2 us
    all_to_all x1, starting transfers between devices, gather(): return lax.all_to_all(wide, 'grp', 0, 0)  6.77 us
    pallas_call x11, Pallas kernels, call(): pl.pallas_call(kernel, in_specs=specs, out_specs=[pl.BlockSpec(memory_spa...  6.16 us
    ppermute x3, waiting for transfers between devices, halo(): lax.ppermute(down, 'lead', [(i, (i - 1) % leads) for i in range(leads)])  3.7 us
    all_to_all x1, waiting for transfers between devices, gather(): return lax.all_to_all(wide, 'grp', 0, 0)  2.53 us
  transfers between devices with their start and end apart: 16, of which 9 were waited for; matrix products, arithmetic and copies ran while one was open for 0% of the time, Pallas kernels for 3%

profile of v14, /device:TPU:97, one launch (start us, length us, event | category | flops | bytes accessed | tf_op | source)
XLA Modules:
  0.0 87.5 jit_solution(14384180370324397790)
XLA Ops:
  0.0 1.8 %shard_map.64 = (bf16[2,96,384]{2,1,0:T(8,128)(2,1)S(1)}, bf16[2,96,384]{2,1,0:T(8,128)(2,1)S(1)}, bf16[2,96,384]{2,1,0:T(8,128)(2,1)S(1)}, bf16[2,96,384]{2,1,0...) custom-call(bf16[2,384,384]{2,1,0:T(8,128)(2,1)} %tiles_hbm.1, ...), custom_call_target="tpu_custom_call" | custom-call | tf_op jit(solution)/shard_map/pallas_call | solution.py:251
  1.8 6.8 %all-to-all-start = ((bf16[16,96,128]{2,1,0:T(8,128)(2,1)}), bf16[16,96,128]{2,1,0:T(8,128)(2,1)S(1)}, u32[]{:S(2)}, u32[]{:S(2)}) async-start(bf16[16,96,128]{2,1,0:T(8,128)(2,1)} %get-tuple-element.54), calls=%async_computation | async-start | bytes 786432 | tf_op jit(solution)/shard_map/all_to_all | solution.py:282
  8.6 1.4 %collective-permute-start = (bf16[2,96,384]{2,1,0:T(8,128)(2,1)S(1)}, bf16[2,96,384]{2,1,0:T(8,128)(2,1)S(1)}, u32[]{:S(2)}, u32[]{:S(2)}) collective-permute-start(bf16[2,96,384]{2,1,0:T(8,128)(2,1)S(1)} %get-tuple-element.40), channel_id=1, source_target_pairs={{0,1},{1,2},{2,3},{3,0},{4,5},{5,6},{6,7},{7,4},{8,9},{9,10},{10,1... | collective-permute-start | bytes 442376 | tf_op jit(solution)/shard_map/ppermute | solution.py:298
  10.0 2.4 %collective-permute-start.1 = (bf16[2,96,384]{2,1,0:T(8,128)(2,1)S(1)}, bf16[2,96,384]{2,1,0:T(8,128)(2,1)S(1)}, u32[]{:S(2)}, u32[]{:S(2)}) collective-permute-start(bf16[2,96,384]{2,1,0:T(8,128)(2,1)S(1)} %get-tuple-element.41), channel_id=1, source_target_pairs={{0,2},{1,3},{2,0},{3,1},{4,6},{5,7},{6,4},{7,5},{8,10},{9,11},{10,... | collective-permute-start | bytes 442376 | tf_op jit(solution)/shard_map/ppermute | solution.py:298
  12.4 1.2 %collective-permute-start.2 = (bf16[2,96,384]{2,1,0:T(8,128)(2,1)S(1)}, bf16[2,96,384]{2,1,0:T(8,128)(2,1)S(1)}, u32[]{:S(2)}, u32[]{:S(2)}) collective-permute-start(bf16[2,96,384]{2,1,0:T(8,128)(2,1)S(1)} %get-tuple-element.42), channel_id=1, source_target_pairs={{0,3},{1,0},{2,1},{3,2},{4,7},{5,4},{6,5},{7,6},{8,11},{9,8},{10,9... | collective-permute-start | bytes 442376 | tf_op jit(solution)/shard_map/ppermute | solution.py:298
  13.6 0.8 tables.1
  14.4 2.5 %all-to-all-done.got_ref = bf16[16,96,128]{2,1,0:T(8,128)(2,1)S(1)} async-done(((bf16[16,96,128]{2,1,0:T(8,128)(2,1)}), bf16[16,96,128]{2,1,0:T(8,128)(2,1)S(1)}, u32[]{:S(2)}, u32[]{:S(2)}) %all-to-all-start) | async-done | bytes 393248 | tf_op jit(solution)/shard_map/all_to_all | solution.py:282
  16.9 0.1 shard_map.67
  17.0 2.5 %collective-permute-start.10 = (bf16[2,384,128]{2,1,0:T(8,128)(2,1)S(1)}, bf16[2,384,128]{2,1,0:T(8,128)(2,1)S(1)}, u32[]{:S(2)}, u32[]{:S(2)}) collective-permute-start(bf16[2,384,128]{2,1,0:T(8,128)(2,1)S(1)} %get-tuple-element.57), channel_id=1, source_target_pairs={{0,240},{16,0},{32,16},{48,32},{64,48},{80,64},{96,80},{112,96},{1... | collective-permute-start | bytes 589832 | tf_op jit(solution)/shard_map/ppermute | solution.py:278
  19.5 2.8 %collective-permute-start.9 = (bf16[2,384,128]{2,1,0:T(8,128)(2,1)S(1)}, bf16[2,384,128]{2,1,0:T(8,128)(2,1)S(1)}, u32[]{:S(2)}, u32[]{:S(2)}) collective-permute-start(bf16[2,384,128]{2,1,0:T(8,128)(2,1)S(1)} %get-tuple-element.56), channel_id=1, source_target_pairs={{0,16},{16,32},{32,48},{48,64},{64,80},{80,96},{96,112},{112,128},... | collective-permute-start | bytes 589832 | tf_op jit(solution)/shard_map/ppermute | solution.py:277
  22.2 0.0 collective-permute-done.refs_1_
  22.2 0.1 collective-permute-done.1.refs_2_
  22.4 0.2 collective-permute-done.2.refs_3_
  22.6 0.1 shard_map.65
  22.7 1.4 %collective-permute-start.3 = (bf16[216,384]{1,0:T(8,128)(2,1)S(1)}, bf16[216,384]{1,0:T(8,128)(2,1)S(1)}, u32[]{:S(2)}, u32[]{:S(2)}) collective-permute-start(bf16[216,384]{1,0:T(8,128)(2,1)S(1)} %get-tuple-element.46), channel_id=1, source_target_pairs={{0,4},{1,5},{2,6},{3,7},{4,8},{5,9},{6,10},{7,11},{8,12},{9,13},{1... | collective-permute-start | bytes 497672 | tf_op jit(solution)/shard_map/ppermute | solution.py:298
  24.2 2.5 %collective-permute-start.4 = (bf16[216,384]{1,0:T(8,128)(2,1)S(1)}, bf16[216,384]{1,0:T(8,128)(2,1)S(1)}, u32[]{:S(2)}, u32[]{:S(2)}) collective-permute-start(bf16[216,384]{1,0:T(8,128)(2,1)S(1)} %get-tuple-element.47), channel_id=1, source_target_pairs={{0,8},{1,9},{2,10},{3,11},{4,12},{5,13},{6,14},{7,15},{8,0},{9,1},... | collective-permute-start | bytes 497672 | tf_op jit(solution)/shard_map/ppermute | solution.py:298
  26.6 1.0 %collective-permute-start.5 = (bf16[216,384]{1,0:T(8,128)(2,1)S(1)}, bf16[216,384]{1,0:T(8,128)(2,1)S(1)}, u32[]{:S(2)}, u32[]{:S(2)}) collective-permute-start(bf16[216,384]{1,0:T(8,128)(2,1)S(1)} %get-tuple-element.48), channel_id=1, source_target_pairs={{0,12},{1,13},{2,14},{3,15},{4,0},{5,1},{6,2},{7,3},{8,4},{9,5},{1... | collective-permute-start | bytes 497672 | tf_op jit(solution)/shard_map/ppermute | solution.py:298
  27.7 0.6 collective-permute-done.3.refs_1_
  28.2 5.3 %collective-permute-done.4.refs_2_ = bf16[216,384]{1,0:T(8,128)(2,1)S(1)} collective-permute-done((bf16[216,384]{1,0:T(8,128)(2,1)S(1)}, bf16[216,384]{1,0:T(8,128)(2,1)S(1)}, u32[]{:S(2)}, u32[]{:S(2)}) %collective-permute-start.4) | collective-permute-done | bytes 165920 | tf_op jit(solution)/shard_map/ppermute | solution.py:298
  33.5 0.0 collective-permute-done.5.refs_3_
  33.5 0.6 shard_map.68.refs_4_
  34.1 0.0 collective-permute-done.10.refs_6_
  34.1 0.0 collective-permute-done.9.refs_5_
  34.1 0.8 shard_map.69
  35.0 15.7 %all_to_all.15.got_ref = bf16[16,96,128]{2,1,0:T(8,128)(2,1)S(1)} all-to-all(bf16[16,96,128]{2,1,0:T(8,128)(2,1)S(1)} %get-tuple-element.58), channel_id=1, replica_groups=mesh['lead'=16,'grp'=16] {'grp'}, dimensions={0} | all-to-all | bytes 786432 | tf_op jit(solution)/shard_map/all_to_all | solution.py:282
  50.6 0.1 shard_map.70
  50.7 4.5 %collective-permute-start.11 = (bf16[2,384,128]{2,1,0:T(8,128)(2,1)S(1)}, bf16[2,384,128]{2,1,0:T(8,128)(2,1)S(1)}, u32[]{:S(2)}, u32[]{:S(2)}) collective-permute-start(bf16[2,384,128]{2,1,0:T(8,128)(2,1)S(1)} %get-tuple-element.60), channel_id=1, source_target_pairs={{0,16},{16,32},{32,48},{48,64},{64,80},{80,96},{96,112},{112,128},... | collective-permute-start | bytes 589832 | tf_op jit(solution)/shard_map/ppermute | solution.py:277
  55.2 0.0 collective-permute-start.12
  55.2 0.6 shard_map.71.refs_4_
  55.8 2.0 %collective-permute-done.11.refs_5_ = bf16[2,384,128]{2,1,0:T(8,128)(2,1)S(1)} collective-permute-done((bf16[2,384,128]{2,1,0:T(8,128)(2,1)S(1)}, bf16[2,384,128]{2,1,0:T(8,128)(2,1)S(1)}, u32[]{:S(2)}, u32[]{:S(2)}) %collective-permute-start.11) | collective-permute-done | bytes 196640 | tf_op jit(solution)/shard_map/ppermute | solution.py:277
  57.9 3.7 %collective-permute-done.12.refs_6_ = bf16[2,384,128]{2,1,0:T(8,128)(2,1)S(1)} collective-permute-done((bf16[2,384,128]{2,1,0:T(8,128)(2,1)S(1)}, bf16[2,384,128]{2,1,0:T(8,128)(2,1)S(1)}, u32[]{:S(2)}, u32[]{:S(2)}) %collective-permute-start.12) | collective-permute-done | bytes 196640 | tf_op jit(solution)/shard_map/ppermute | solution.py:278
  61.5 0.8 shard_map.72
  62.4 12.0 %all_to_all.16.got_ref.refs_7_ = bf16[16,120,128]{2,1,0:T(8,128)(2,1)S(1)} all-to-all(bf16[16,120,128]{2,1,0:T(8,128)(2,1)S(1)} %shard_map.72), channel_id=1, replica_groups=mesh['lead'=16,'grp'=16] {'grp'}, dimensions={0} | all-to-all | bytes 983040 | tf_op jit(solution)/shard_map/all_to_all | solution.py:282
  74.4 0.1 shard_map.73
  74.5 2.9 %collective-permute-start.13 = (bf16[2,384,128]{2,1,0:T(8,128)(2,1)S(1)}, bf16[2,384,128]{2,1,0:T(8,128)(2,1)S(1)}, u32[]{:S(2)}, u32[]{:S(2)}) collective-permute-start(bf16[2,384,128]{2,1,0:T(8,128)(2,1)S(1)} %get-tuple-element.66), channel_id=1, source_target_pairs={{0,16},{16,32},{32,48},{48,64},{64,80},{80,96},{96,112},{112,128},... | collective-permute-start | bytes 589832 | tf_op jit(solution)/shard_map/ppermute | solution.py:277
  77.4 0.0 collective-permute-start.14
  77.4 0.1 shard_map.66
  77.6 0.1 collective-permute-start.6
  77.7 2.0 %collective-permute-start.7 = (bf16[8,24,384]{2,1,0:T(8,128)(2,1)S(1)}, bf16[8,24,384]{2,1,0:T(8,128)(2,1)S(1)}, u32[]{:S(2)}, u32[]{:S(2)}) collective-permute-start(bf16[8,24,384]{2,1,0:T(8,128)(2,1)S(1)} %get-tuple-element.51), channel_id=1, source_target_pairs={{0,8},{1,9},{2,10},{3,11},{4,12},{5,13},{6,14},{7,15},{8,0},{9,1},... | collective-permute-start | bytes 442376 | tf_op jit(solution)/shard_map/ppermute | solution.py:298
  79.7 0.8 collective-permute-start.8
  80.5 5.2 %collective-permute-done.6.refs_1_ = bf16[8,24,384]{2,1,0:T(8,128)(2,1)S(1)} collective-permute-done((bf16[8,24,384]{2,1,0:T(8,128)(2,1)S(1)}, bf16[8,24,384]{2,1,0:T(8,128)(2,1)S(1)}, u32[]{:S(2)}, u32[]{:S(2)}) %collective-permute-start.6) | collective-permute-done | bytes 147488 | tf_op jit(solution)/shard_map/ppermute | solution.py:298
  85.6 0.0 collective-permute-done.7.refs_2_
  85.6 0.9 collective-permute-done.8.refs_3_
  86.5 0.0 collective-permute-done.13.refs_5_
  86.5 0.0 collective-permute-done.14.refs_6_
  86.5 1.0 %shard_map.74 = f32[96,128]{1,0:T(8,128)} custom-call(s32[4,8]{1,0:T(4,128)S(4)} %get-tuple-element.37.cols_ref, bf16[8,24,384]{2,1,0:T(8,128)(2,1)S(1)} %get-tuple-element.49.refs_0_, bf16[8,24,384]{2,1,0:T(8,128)(2,1)S(1)} %collective-permute-done.6.refs_1_, bf16[8,24,384]{2,1,0:T(8,128)(2,1)S(1)} %collective-permute-done.7.refs_2_, ...), custom_call_target="tpu_custom_call" | custom-call | tf_op jit(solution)/shard_map/pallas_call | solution.py:251
Async XLA Ops:
  1.8 15.1 %all-to-all-start = ((bf16[16,96,128]{2,1,0:T(8,128)(2,1)}), bf16[16,96,128]{2,1,0:T(8,128)(2,1)S(1)}, u32[]{:S(2)}, u32[]{:S(2)}) async-start(bf16[16,96,128]{2,1,0:T(8,128)(2,1)} %get-tuple-element.54), calls=%async_computation | async-start | bytes 786432 | tf_op jit(solution)/shard_map/all_to_all | solution.py:282
  8.6 13.6 %collective-permute-start = (bf16[2,96,384]{2,1,0:T(8,128)(2,1)S(1)}, bf16[2,96,384]{2,1,0:T(8,128)(2,1)S(1)}, u32[]{:S(2)}, u32[]{:S(2)}) collective-permute-start(bf16[2,96,384]{2,1,0:T(8,128)(2,1)S(1)} %get-tuple-element.40), channel_id=1, source_target_pairs={{0,1},{1,2},{2,3},{3,0},{4,5},{5,6},{6,7},{7,4},{8,9},{9,10},{10,1... | collective-permute-start | bytes 442376 | tf_op jit(solution)/shard_map/ppermute | solution.py:298
  10.0 12.4 %collective-permute-start.1 = (bf16[2,96,384]{2,1,0:T(8,128)(2,1)S(1)}, bf16[2,96,384]{2,1,0:T(8,128)(2,1)S(1)}, u32[]{:S(2)}, u32[]{:S(2)}) collective-permute-start(bf16[2,96,384]{2,1,0:T(8,128)(2,1)S(1)} %get-tuple-element.41), channel_id=1, source_target_pairs={{0,2},{1,3},{2,0},{3,1},{4,6},{5,7},{6,4},{7,5},{8,10},{9,11},{10,... | collective-permute-start | bytes 442376 | tf_op jit(solution)/shard_map/ppermute | solution.py:298
  12.4 10.2 %collective-permute-start.2 = (bf16[2,96,384]{2,1,0:T(8,128)(2,1)S(1)}, bf16[2,96,384]{2,1,0:T(8,128)(2,1)S(1)}, u32[]{:S(2)}, u32[]{:S(2)}) collective-permute-start(bf16[2,96,384]{2,1,0:T(8,128)(2,1)S(1)} %get-tuple-element.42), channel_id=1, source_target_pairs={{0,3},{1,0},{2,1},{3,2},{4,7},{5,4},{6,5},{7,6},{8,11},{9,8},{10,9... | collective-permute-start | bytes 442376 | tf_op jit(solution)/shard_map/ppermute | solution.py:298
  17.0 17.1 %collective-permute-start.10 = (bf16[2,384,128]{2,1,0:T(8,128)(2,1)S(1)}, bf16[2,384,128]{2,1,0:T(8,128)(2,1)S(1)}, u32[]{:S(2)}, u32[]{:S(2)}) collective-permute-start(bf16[2,384,128]{2,1,0:T(8,128)(2,1)S(1)} %get-tuple-element.57), channel_id=1, source_target_pairs={{0,240},{16,0},{32,16},{48,32},{64,48},{80,64},{96,80},{112,96},{1... | collective-permute-start | bytes 589832 | tf_op jit(solution)/shard_map/ppermute | solution.py:278
  19.5 14.6 %collective-permute-start.9 = (bf16[2,384,128]{2,1,0:T(8,128)(2,1)S(1)}, bf16[2,384,128]{2,1,0:T(8,128)(2,1)S(1)}, u32[]{:S(2)}, u32[]{:S(2)}) collective-permute-start(bf16[2,384,128]{2,1,0:T(8,128)(2,1)S(1)} %get-tuple-element.56), channel_id=1, source_target_pairs={{0,16},{16,32},{32,48},{48,64},{64,80},{80,96},{96,112},{112,128},... | collective-permute-start | bytes 589832 | tf_op jit(solution)/shard_map/ppermute | solution.py:277
  22.7 5.5 %collective-permute-start.3 = (bf16[216,384]{1,0:T(8,128)(2,1)S(1)}, bf16[216,384]{1,0:T(8,128)(2,1)S(1)}, u32[]{:S(2)}, u32[]{:S(2)}) collective-permute-start(bf16[216,384]{1,0:T(8,128)(2,1)S(1)} %get-tuple-element.46), channel_id=1, source_target_pairs={{0,4},{1,5},{2,6},{3,7},{4,8},{5,9},{6,10},{7,11},{8,12},{9,13},{1... | collective-permute-start | bytes 497672 | tf_op jit(solution)/shard_map/ppermute | solution.py:298
  24.2 9.3 %collective-permute-start.4 = (bf16[216,384]{1,0:T(8,128)(2,1)S(1)}, bf16[216,384]{1,0:T(8,128)(2,1)S(1)}, u32[]{:S(2)}, u32[]{:S(2)}) collective-permute-start(bf16[216,384]{1,0:T(8,128)(2,1)S(1)} %get-tuple-element.47), channel_id=1, source_target_pairs={{0,8},{1,9},{2,10},{3,11},{4,12},{5,13},{6,14},{7,15},{8,0},{9,1},... | collective-permute-start | bytes 497672 | tf_op jit(solution)/shard_map/ppermute | solution.py:298
  26.6 6.9 %collective-permute-start.5 = (bf16[216,384]{1,0:T(8,128)(2,1)S(1)}, bf16[216,384]{1,0:T(8,128)(2,1)S(1)}, u32[]{:S(2)}, u32[]{:S(2)}) collective-permute-start(bf16[216,384]{1,0:T(8,128)(2,1)S(1)} %get-tuple-element.48), channel_id=1, source_target_pairs={{0,12},{1,13},{2,14},{3,15},{4,0},{5,1},{6,2},{7,3},{8,4},{9,5},{1... | collective-permute-start | bytes 497672 | tf_op jit(solution)/shard_map/ppermute | solution.py:298
  50.7 7.1 %collective-permute-start.11 = (bf16[2,384,128]{2,1,0:T(8,128)(2,1)S(1)}, bf16[2,384,128]{2,1,0:T(8,128)(2,1)S(1)}, u32[]{:S(2)}, u32[]{:S(2)}) collective-permute-start(bf16[2,384,128]{2,1,0:T(8,128)(2,1)S(1)} %get-tuple-element.60), channel_id=1, source_target_pairs={{0,16},{16,32},{32,48},{48,64},{64,80},{80,96},{96,112},{112,128},... | collective-permute-start | bytes 589832 | tf_op jit(solution)/shard_map/ppermute | solution.py:277
  55.2 6.3 %collective-permute-start.12 = (bf16[2,384,128]{2,1,0:T(8,128)(2,1)S(1)}, bf16[2,384,128]{2,1,0:T(8,128)(2,1)S(1)}, u32[]{:S(2)}, u32[]{:S(2)}) collective-permute-start(bf16[2,384,128]{2,1,0:T(8,128)(2,1)S(1)} %get-tuple-element.61), channel_id=1, source_target_pairs={{0,240},{16,0},{32,16},{48,32},{64,48},{80,64},{96,80},{112,96},{1... | collective-permute-start | bytes 589832 | tf_op jit(solution)/shard_map/ppermute | solution.py:278
  74.5 12.0 %collective-permute-start.13 = (bf16[2,384,128]{2,1,0:T(8,128)(2,1)S(1)}, bf16[2,384,128]{2,1,0:T(8,128)(2,1)S(1)}, u32[]{:S(2)}, u32[]{:S(2)}) collective-permute-start(bf16[2,384,128]{2,1,0:T(8,128)(2,1)S(1)} %get-tuple-element.66), channel_id=1, source_target_pairs={{0,16},{16,32},{32,48},{48,64},{64,80},{80,96},{96,112},{112,128},... | collective-permute-start | bytes 589832 | tf_op jit(solution)/shard_map/ppermute | solution.py:277
  77.4 9.1 %collective-permute-start.14 = (bf16[2,384,128]{2,1,0:T(8,128)(2,1)S(1)}, bf16[2,384,128]{2,1,0:T(8,128)(2,1)S(1)}, u32[]{:S(2)}, u32[]{:S(2)}) collective-permute-start(bf16[2,384,128]{2,1,0:T(8,128)(2,1)S(1)} %get-tuple-element.67), channel_id=1, source_target_pairs={{0,240},{16,0},{32,16},{48,32},{64,48},{80,64},{96,80},{112,96},{1... | collective-permute-start | bytes 589832 | tf_op jit(solution)/shard_map/ppermute | solution.py:278
  77.6 8.1 %collective-permute-start.6 = (bf16[8,24,384]{2,1,0:T(8,128)(2,1)S(1)}, bf16[8,24,384]{2,1,0:T(8,128)(2,1)S(1)}, u32[]{:S(2)}, u32[]{:S(2)}) collective-permute-start(bf16[8,24,384]{2,1,0:T(8,128)(2,1)S(1)} %get-tuple-element.50), channel_id=1, source_target_pairs={{0,4},{1,5},{2,6},{3,7},{4,8},{5,9},{6,10},{7,11},{8,12},{9,13},{1... | collective-permute-start | bytes 442376 | tf_op jit(solution)/shard_map/ppermute | solution.py:298
  77.7 8.0 %collective-permute-start.7 = (bf16[8,24,384]{2,1,0:T(8,128)(2,1)S(1)}, bf16[8,24,384]{2,1,0:T(8,128)(2,1)S(1)}, u32[]{:S(2)}, u32[]{:S(2)}) collective-permute-start(bf16[8,24,384]{2,1,0:T(8,128)(2,1)S(1)} %get-tuple-element.51), channel_id=1, source_target_pairs={{0,8},{1,9},{2,10},{3,11},{4,12},{5,13},{6,14},{7,15},{8,0},{9,1},... | collective-permute-start | bytes 442376 | tf_op jit(solution)/shard_map/ppermute | solution.py:298
  79.7 6.8 %collective-permute-start.8 = (bf16[8,24,384]{2,1,0:T(8,128)(2,1)S(1)}, bf16[8,24,384]{2,1,0:T(8,128)(2,1)S(1)}, u32[]{:S(2)}, u32[]{:S(2)}) collective-permute-start(bf16[8,24,384]{2,1,0:T(8,128)(2,1)S(1)} %get-tuple-element.52), channel_id=1, source_target_pairs={{0,12},{1,13},{2,14},{3,15},{4,0},{5,1},{6,2},{7,3},{8,4},{9,5},{1... | collective-permute-start | bytes 442376 | tf_op jit(solution)/shard_map/ppermute | solution.py:298

commit v15 on v9

--- a/solution.py
+++ b/solution.py
@@ -103,13 +103,15 @@
 def table_kernel(slot_ref, cols_ref, rows_ref, slot_out, cols_out, rows_out):
     for t in range(TILES):
         slot_out[0, t] = slot_ref[0, t]
+    lead = lax.axis_index("lead")
+    odd = lax.bitwise_and(lead, 1)
     for r in range(SIDE):
         for k in range(8):
-            cols_out[r, k] = cols_ref[r, k]
-    lead = lax.axis_index("lead")
-    for side in range(2):
-        for h in range(2):
-            rows_out[side, h] = rows_ref[side, h, lead]
+            col = cols_ref[r, k]
+            cols_out[r, k] = jnp.where(col >= 4, lax.bitwise_xor(col, 2 * odd), col)
+    for h in range(2):
+        rows_out[0, h] = rows_ref[1 - odd, h, lead]
+        rows_out[1, h] = rows_ref[odd, h, lead]
 
 
 def send_halves(rows_ref, own_ref, up_ref, down_ref):
@@ -270,8 +272,8 @@
     diag = diag_inv.reshape(1, SHARE)
 
     def halo(up, down):
-        lower = lax.ppermute(up, "lead", [(i, (i + 1) % leads) for i in range(leads)])
-        upper = lax.ppermute(down, "lead", [(i, (i - 1) % leads) for i in range(leads)])
+        lower = lax.ppermute(up, "lead", [(i, (i + 2 * (i % 2) - 1) % leads) for i in range(leads)])
+        upper = lax.ppermute(down, "lead", [(i, i ^ 1) for i in range(leads)])
         return lower, upper
 
     def gather(wide):

time: 88.3 us -> 90.1 us (1.020)
  the two profiles are of different devices: /device:TPU:97 before, /device:TPU:1 now
where the time goes in v15:
time: 90.1 us; the launch traced here: 89.9 us
  starting transfers between devices  38.7 us (43%)
  blocking collectives  27.2 us (30%)
  waiting for transfers between devices  16.7 us (19%)
  Pallas kernels  7.1 us (8%)
    all_to_all x2, blocking collectives, gather(): return lax.all_to_all(wide, 'grp', 0, 0)  27.2 us
    ppermute x9, waiting for transfers between devices, exchange(): out.append(lax.ppermute(values[k], 'grp', pairs[k]))  13.7 us
    ppermute x9, starting transfers between devices, exchange(): out.append(lax.ppermute(values[k], 'grp', pairs[k]))  13 us
    ppermute x3, starting transfers between devices, halo(): lax.ppermute(up, 'lead', [(i, (i + 2 * (i % 2) - 1) % leads) for i in ran...  10.6 us
    all_to_all x1, starting transfers between devices, gather(): return lax.all_to_all(wide, 'grp', 0, 0)  7.58 us
    ppermute x3, starting transfers between devices, halo(): upper = lax.ppermute(down, 'lead', [(i, i ^ 1) for i in range(leads)])  7.51 us
    pallas_call x11, Pallas kernels, call(): pl.pallas_call(kernel, in_specs=specs, out_specs=[VMEM] * len(outs), out_...  6.28 us
    all_to_all x1, waiting for transfers between devices, gather(): return lax.all_to_all(wide, 'grp', 0, 0)  2.5 us
  transfers between devices with their start and end apart: 16, of which 10 were waited for; matrix products, arithmetic and copies ran while one was open for 0% of the time, Pallas kernels for 3%

profile of v15, /device:TPU:1, one launch (start us, length us, event | category | flops | bytes accessed | tf_op | source)
XLA Modules:
  0.0 89.9 jit_solution(14230422545819560204)
XLA Ops:
  0.0 2.0 %shard_map.64 = (bf16[2,96,384]{2,1,0:T(8,128)(2,1)S(1)}, bf16[2,96,384]{2,1,0:T(8,128)(2,1)S(1)}, bf16[2,96,384]{2,1,0:T(8,128)(2,1)S(1)}, bf16[2,96,384]{2,1,0...) custom-call(bf16[2,384,384]{2,1,0:T(8,128)(2,1)} %tiles_hbm.1, ...), custom_call_target="tpu_custom_call" | custom-call | tf_op jit(solution)/shard_map/pallas_call | solution.py:250
  2.0 7.6 %all-to-all-start = ((bf16[16,96,128]{2,1,0:T(8,128)(2,1)}), bf16[16,96,128]{2,1,0:T(8,128)(2,1)S(1)}, u32[]{:S(2)}, u32[]{:S(2)}) async-start(bf16[16,96,128]{2,1,0:T(8,128)(2,1)} %get-tuple-element.54), calls=%async_computation | async-start | bytes 786432 | tf_op jit(solution)/shard_map/all_to_all | solution.py:280
  9.6 1.4 %collective-permute-start = (bf16[2,96,384]{2,1,0:T(8,128)(2,1)S(1)}, bf16[2,96,384]{2,1,0:T(8,128)(2,1)S(1)}, u32[]{:S(2)}, u32[]{:S(2)}) collective-permute-start(bf16[2,96,384]{2,1,0:T(8,128)(2,1)S(1)} %get-tuple-element.40), channel_id=1, source_target_pairs={{0,1},{1,2},{2,3},{3,0},{4,5},{5,6},{6,7},{7,4},{8,9},{9,10},{10,1... | collective-permute-start | bytes 442376 | tf_op jit(solution)/shard_map/ppermute | solution.py:296
  10.9 2.4 %collective-permute-start.1 = (bf16[2,96,384]{2,1,0:T(8,128)(2,1)S(1)}, bf16[2,96,384]{2,1,0:T(8,128)(2,1)S(1)}, u32[]{:S(2)}, u32[]{:S(2)}) collective-permute-start(bf16[2,96,384]{2,1,0:T(8,128)(2,1)S(1)} %get-tuple-element.41), channel_id=1, source_target_pairs={{0,2},{1,3},{2,0},{3,1},{4,6},{5,7},{6,4},{7,5},{8,10},{9,11},{10,... | collective-permute-start | bytes 442376 | tf_op jit(solution)/shard_map/ppermute | solution.py:296
  13.3 1.2 %collective-permute-start.2 = (bf16[2,96,384]{2,1,0:T(8,128)(2,1)S(1)}, bf16[2,96,384]{2,1,0:T(8,128)(2,1)S(1)}, u32[]{:S(2)}, u32[]{:S(2)}) collective-permute-start(bf16[2,96,384]{2,1,0:T(8,128)(2,1)S(1)} %get-tuple-element.42), channel_id=1, source_target_pairs={{0,3},{1,0},{2,1},{3,2},{4,7},{5,4},{6,5},{7,6},{8,11},{9,8},{10,9... | collective-permute-start | bytes 442376 | tf_op jit(solution)/shard_map/ppermute | solution.py:296
  14.5 0.8 tables.1
  15.3 2.5 %all-to-all-done.got_ref = bf16[16,96,128]{2,1,0:T(8,128)(2,1)S(1)} async-done(((bf16[16,96,128]{2,1,0:T(8,128)(2,1)}), bf16[16,96,128]{2,1,0:T(8,128)(2,1)S(1)}, u32[]{:S(2)}, u32[]{:S(2)}) %all-to-all-start) | async-done | bytes 393248 | tf_op jit(solution)/shard_map/all_to_all | solution.py:280
  17.8 0.1 shard_map.67
  17.9 2.6 %collective-permute-start.10 = (bf16[2,384,128]{2,1,0:T(8,128)(2,1)S(1)}, bf16[2,384,128]{2,1,0:T(8,128)(2,1)S(1)}, u32[]{:S(2)}, u32[]{:S(2)}) collective-permute-start(bf16[2,384,128]{2,1,0:T(8,128)(2,1)S(1)} %get-tuple-element.57), channel_id=1, source_target_pairs={{0,16},{16,0},{32,48},{48,32},{64,80},{80,64},{96,112},{112,96},{1... | collective-permute-start | bytes 589832 | tf_op jit(solution)/shard_map/ppermute | solution.py:276
  20.5 1.6 %collective-permute-start.9 = (bf16[2,384,128]{2,1,0:T(8,128)(2,1)S(1)}, bf16[2,384,128]{2,1,0:T(8,128)(2,1)S(1)}, u32[]{:S(2)}, u32[]{:S(2)}) collective-permute-start(bf16[2,384,128]{2,1,0:T(8,128)(2,1)S(1)} %get-tuple-element.56), channel_id=1, source_target_pairs={{0,240},{16,32},{32,16},{48,64},{64,48},{80,96},{96,80},{112,128},... | collective-permute-start | bytes 589832 | tf_op jit(solution)/shard_map/ppermute | solution.py:275
  22.1 0.0 collective-permute-done.refs_1_
  22.1 1.2 %collective-permute-done.1.refs_2_ = bf16[2,96,384]{2,1,0:T(8,128)(2,1)S(1)} collective-permute-done((bf16[2,96,384]{2,1,0:T(8,128)(2,1)S(1)}, bf16[2,96,384]{2,1,0:T(8,128)(2,1)S(1)}, u32[]{:S(2)}, u32[]{:S(2)}) %collective-permute-start.1) | collective-permute-done | bytes 147488 | tf_op jit(solution)/shard_map/ppermute | solution.py:296
  23.3 0.2 collective-permute-done.2.refs_3_
  23.6 0.1 shard_map.65
  23.7 1.4 %collective-permute-start.3 = (bf16[216,384]{1,0:T(8,128)(2,1)S(1)}, bf16[216,384]{1,0:T(8,128)(2,1)S(1)}, u32[]{:S(2)}, u32[]{:S(2)}) collective-permute-start(bf16[216,384]{1,0:T(8,128)(2,1)S(1)} %get-tuple-element.46), channel_id=1, source_target_pairs={{0,4},{1,5},{2,6},{3,7},{4,8},{5,9},{6,10},{7,11},{8,12},{9,13},{1... | collective-permute-start | bytes 497672 | tf_op jit(solution)/shard_map/ppermute | solution.py:296
  25.1 2.5 %collective-permute-start.4 = (bf16[216,384]{1,0:T(8,128)(2,1)S(1)}, bf16[216,384]{1,0:T(8,128)(2,1)S(1)}, u32[]{:S(2)}, u32[]{:S(2)}) collective-permute-start(bf16[216,384]{1,0:T(8,128)(2,1)S(1)} %get-tuple-element.47), channel_id=1, source_target_pairs={{0,8},{1,9},{2,10},{3,11},{4,12},{5,13},{6,14},{7,15},{8,0},{9,1},... | collective-permute-start | bytes 497672 | tf_op jit(solution)/shard_map/ppermute | solution.py:296
  27.6 1.0 %collective-permute-start.5 = (bf16[216,384]{1,0:T(8,128)(2,1)S(1)}, bf16[216,384]{1,0:T(8,128)(2,1)S(1)}, u32[]{:S(2)}, u32[]{:S(2)}) collective-permute-start(bf16[216,384]{1,0:T(8,128)(2,1)S(1)} %get-tuple-element.48), channel_id=1, source_target_pairs={{0,12},{1,13},{2,14},{3,15},{4,0},{5,1},{6,2},{7,3},{8,4},{9,5},{1... | collective-permute-start | bytes 497672 | tf_op jit(solution)/shard_map/ppermute | solution.py:296
  28.6 0.8 collective-permute-done.3.refs_1_
  29.4 4.4 %collective-permute-done.4.refs_2_ = bf16[216,384]{1,0:T(8,128)(2,1)S(1)} collective-permute-done((bf16[216,384]{1,0:T(8,128)(2,1)S(1)}, bf16[216,384]{1,0:T(8,128)(2,1)S(1)}, u32[]{:S(2)}, u32[]{:S(2)}) %collective-permute-start.4) | collective-permute-done | bytes 165920 | tf_op jit(solution)/shard_map/ppermute | solution.py:296
  33.9 0.0 collective-permute-done.5.refs_3_
  33.9 0.6 shard_map.68.refs_4_
  34.4 0.0 collective-permute-done.10.refs_6_
  34.4 0.0 collective-permute-done.9.refs_5_
  34.5 0.8 shard_map.69
  35.3 14.9 %all_to_all.15.got_ref = bf16[16,96,128]{2,1,0:T(8,128)(2,1)S(1)} all-to-all(bf16[16,96,128]{2,1,0:T(8,128)(2,1)S(1)} %get-tuple-element.58), channel_id=1, replica_groups=mesh['lead'=16,'grp'=16] {'grp'}, dimensions={0} | all-to-all | bytes 786432 | tf_op jit(solution)/shard_map/all_to_all | solution.py:280
  50.2 0.1 shard_map.70
  50.3 4.7 %collective-permute-start.11 = (bf16[2,384,128]{2,1,0:T(8,128)(2,1)S(1)}, bf16[2,384,128]{2,1,0:T(8,128)(2,1)S(1)}, u32[]{:S(2)}, u32[]{:S(2)}) collective-permute-start(bf16[2,384,128]{2,1,0:T(8,128)(2,1)S(1)} %get-tuple-element.60), channel_id=1, source_target_pairs={{0,240},{16,32},{32,16},{48,64},{64,48},{80,96},{96,80},{112,128},... | collective-permute-start | bytes 589832 | tf_op jit(solution)/shard_map/ppermute | solution.py:275
  55.0 2.7 %collective-permute-start.12 = (bf16[2,384,128]{2,1,0:T(8,128)(2,1)S(1)}, bf16[2,384,128]{2,1,0:T(8,128)(2,1)S(1)}, u32[]{:S(2)}, u32[]{:S(2)}) collective-permute-start(bf16[2,384,128]{2,1,0:T(8,128)(2,1)S(1)} %get-tuple-element.61), channel_id=1, source_target_pairs={{0,16},{16,0},{32,48},{48,32},{64,80},{80,64},{96,112},{112,96},{1... | collective-permute-start | bytes 589832 | tf_op jit(solution)/shard_map/ppermute | solution.py:276
  57.7 0.6 shard_map.71.refs_4_
  58.3 0.4 collective-permute-done.11.refs_5_
  58.7 0.1 collective-permute-done.12.refs_6_
  58.8 0.8 shard_map.72
  59.6 12.3 %all_to_all.16.got_ref.refs_7_ = bf16[16,120,128]{2,1,0:T(8,128)(2,1)S(1)} all-to-all(bf16[16,120,128]{2,1,0:T(8,128)(2,1)S(1)} %shard_map.72), channel_id=1, replica_groups=mesh['lead'=16,'grp'=16] {'grp'}, dimensions={0} | all-to-all | bytes 983040 | tf_op jit(solution)/shard_map/all_to_all | solution.py:280
  71.9 0.1 shard_map.73
  72.0 4.3 %collective-permute-start.13 = (bf16[2,384,128]{2,1,0:T(8,128)(2,1)S(1)}, bf16[2,384,128]{2,1,0:T(8,128)(2,1)S(1)}, u32[]{:S(2)}, u32[]{:S(2)}) collective-permute-start(bf16[2,384,128]{2,1,0:T(8,128)(2,1)S(1)} %get-tuple-element.66), channel_id=1, source_target_pairs={{0,240},{16,32},{32,16},{48,64},{64,48},{80,96},{96,80},{112,128},... | collective-permute-start | bytes 589832 | tf_op jit(solution)/shard_map/ppermute | solution.py:275
  76.3 2.2 %collective-permute-start.14 = (bf16[2,384,128]{2,1,0:T(8,128)(2,1)S(1)}, bf16[2,384,128]{2,1,0:T(8,128)(2,1)S(1)}, u32[]{:S(2)}, u32[]{:S(2)}) collective-permute-start(bf16[2,384,128]{2,1,0:T(8,128)(2,1)S(1)} %get-tuple-element.67), channel_id=1, source_target_pairs={{0,16},{16,0},{32,48},{48,32},{64,80},{80,64},{96,112},{112,96},{1... | collective-permute-start | bytes 589832 | tf_op jit(solution)/shard_map/ppermute | solution.py:276
  78.5 0.1 shard_map.66
  78.6 0.1 collective-permute-start.6
  78.7 2.2 %collective-permute-start.7 = (bf16[8,24,384]{2,1,0:T(8,128)(2,1)S(1)}, bf16[8,24,384]{2,1,0:T(8,128)(2,1)S(1)}, u32[]{:S(2)}, u32[]{:S(2)}) collective-permute-start(bf16[8,24,384]{2,1,0:T(8,128)(2,1)S(1)} %get-tuple-element.51), channel_id=1, source_target_pairs={{0,8},{1,9},{2,10},{3,11},{4,12},{5,13},{6,14},{7,15},{8,0},{9,1},... | collective-permute-start | bytes 442376 | tf_op jit(solution)/shard_map/ppermute | solution.py:296
  80.9 0.9 collective-permute-start.8
  81.8 4.0 %collective-permute-done.6.refs_1_ = bf16[8,24,384]{2,1,0:T(8,128)(2,1)S(1)} collective-permute-done((bf16[8,24,384]{2,1,0:T(8,128)(2,1)S(1)}, bf16[8,24,384]{2,1,0:T(8,128)(2,1)S(1)}, u32[]{:S(2)}, u32[]{:S(2)}) %collective-permute-start.6) | collective-permute-done | bytes 147488 | tf_op jit(solution)/shard_map/ppermute | solution.py:296
  85.8 2.2 %collective-permute-done.7.refs_2_ = bf16[8,24,384]{2,1,0:T(8,128)(2,1)S(1)} collective-permute-done((bf16[8,24,384]{2,1,0:T(8,128)(2,1)S(1)}, bf16[8,24,384]{2,1,0:T(8,128)(2,1)S(1)}, u32[]{:S(2)}, u32[]{:S(2)}) %collective-permute-start.7) | collective-permute-done | bytes 147488 | tf_op jit(solution)/shard_map/ppermute | solution.py:296
  88.0 0.8 collective-permute-done.8.refs_3_
  88.8 0.0 collective-permute-done.13.refs_5_
  88.8 0.0 collective-permute-done.14.refs_6_
  88.8 1.0 %shard_map.74 = f32[96,128]{1,0:T(8,128)} custom-call(s32[4,8]{1,0:T(4,128)S(4)} %get-tuple-element.37.cols_ref, bf16[8,24,384]{2,1,0:T(8,128)(2,1)S(1)} %get-tuple-element.49.refs_0_, bf16[8,24,384]{2,1,0:T(8,128)(2,1)S(1)} %collective-permute-done.6.refs_1_, bf16[8,24,384]{2,1,0:T(8,128)(2,1)S(1)} %collective-permute-done.7.refs_2_, ...), custom_call_target="tpu_custom_call" | custom-call | tf_op jit(solution)/shard_map/pallas_call | solution.py:250
Async XLA Ops:
  2.0 15.9 %all-to-all-start = ((bf16[16,96,128]{2,1,0:T(8,128)(2,1)}), bf16[16,96,128]{2,1,0:T(8,128)(2,1)S(1)}, u32[]{:S(2)}, u32[]{:S(2)}) async-start(bf16[16,96,128]{2,1,0:T(8,128)(2,1)} %get-tuple-element.54), calls=%async_computation | async-start | bytes 786432 | tf_op jit(solution)/shard_map/all_to_all | solution.py:280
  9.6 12.5 %collective-permute-start = (bf16[2,96,384]{2,1,0:T(8,128)(2,1)S(1)}, bf16[2,96,384]{2,1,0:T(8,128)(2,1)S(1)}, u32[]{:S(2)}, u32[]{:S(2)}) collective-permute-start(bf16[2,96,384]{2,1,0:T(8,128)(2,1)S(1)} %get-tuple-element.40), channel_id=1, source_target_pairs={{0,1},{1,2},{2,3},{3,0},{4,5},{5,6},{6,7},{7,4},{8,9},{9,10},{10,1... | collective-permute-start | bytes 442376 | tf_op jit(solution)/shard_map/ppermute | solution.py:296
  10.9 12.4 %collective-permute-start.1 = (bf16[2,96,384]{2,1,0:T(8,128)(2,1)S(1)}, bf16[2,96,384]{2,1,0:T(8,128)(2,1)S(1)}, u32[]{:S(2)}, u32[]{:S(2)}) collective-permute-start(bf16[2,96,384]{2,1,0:T(8,128)(2,1)S(1)} %get-tuple-element.41), channel_id=1, source_target_pairs={{0,2},{1,3},{2,0},{3,1},{4,6},{5,7},{6,4},{7,5},{8,10},{9,11},{10,... | collective-permute-start | bytes 442376 | tf_op jit(solution)/shard_map/ppermute | solution.py:296
  13.3 10.2 %collective-permute-start.2 = (bf16[2,96,384]{2,1,0:T(8,128)(2,1)S(1)}, bf16[2,96,384]{2,1,0:T(8,128)(2,1)S(1)}, u32[]{:S(2)}, u32[]{:S(2)}) collective-permute-start(bf16[2,96,384]{2,1,0:T(8,128)(2,1)S(1)} %get-tuple-element.42), channel_id=1, source_target_pairs={{0,3},{1,0},{2,1},{3,2},{4,7},{5,4},{6,5},{7,6},{8,11},{9,8},{10,9... | collective-permute-start | bytes 442376 | tf_op jit(solution)/shard_map/ppermute | solution.py:296
  17.9 16.5 %collective-permute-start.10 = (bf16[2,384,128]{2,1,0:T(8,128)(2,1)S(1)}, bf16[2,384,128]{2,1,0:T(8,128)(2,1)S(1)}, u32[]{:S(2)}, u32[]{:S(2)}) collective-permute-start(bf16[2,384,128]{2,1,0:T(8,128)(2,1)S(1)} %get-tuple-element.57), channel_id=1, source_target_pairs={{0,16},{16,0},{32,48},{48,32},{64,80},{80,64},{96,112},{112,96},{1... | collective-permute-start | bytes 589832 | tf_op jit(solution)/shard_map/ppermute | solution.py:276
  20.5 14.0 %collective-permute-start.9 = (bf16[2,384,128]{2,1,0:T(8,128)(2,1)S(1)}, bf16[2,384,128]{2,1,0:T(8,128)(2,1)S(1)}, u32[]{:S(2)}, u32[]{:S(2)}) collective-permute-start(bf16[2,384,128]{2,1,0:T(8,128)(2,1)S(1)} %get-tuple-element.56), channel_id=1, source_target_pairs={{0,240},{16,32},{32,16},{48,64},{64,48},{80,96},{96,80},{112,128},... | collective-permute-start | bytes 589832 | tf_op jit(solution)/shard_map/ppermute | solution.py:275
  23.7 5.7 %collective-permute-start.3 = (bf16[216,384]{1,0:T(8,128)(2,1)S(1)}, bf16[216,384]{1,0:T(8,128)(2,1)S(1)}, u32[]{:S(2)}, u32[]{:S(2)}) collective-permute-start(bf16[216,384]{1,0:T(8,128)(2,1)S(1)} %get-tuple-element.46), channel_id=1, source_target_pairs={{0,4},{1,5},{2,6},{3,7},{4,8},{5,9},{6,10},{7,11},{8,12},{9,13},{1... | collective-permute-start | bytes 497672 | tf_op jit(solution)/shard_map/ppermute | solution.py:296
  25.1 8.7 %collective-permute-start.4 = (bf16[216,384]{1,0:T(8,128)(2,1)S(1)}, bf16[216,384]{1,0:T(8,128)(2,1)S(1)}, u32[]{:S(2)}, u32[]{:S(2)}) collective-permute-start(bf16[216,384]{1,0:T(8,128)(2,1)S(1)} %get-tuple-element.47), channel_id=1, source_target_pairs={{0,8},{1,9},{2,10},{3,11},{4,12},{5,13},{6,14},{7,15},{8,0},{9,1},... | collective-permute-start | bytes 497672 | tf_op jit(solution)/shard_map/ppermute | solution.py:296
  27.6 6.3 %collective-permute-start.5 = (bf16[216,384]{1,0:T(8,128)(2,1)S(1)}, bf16[216,384]{1,0:T(8,128)(2,1)S(1)}, u32[]{:S(2)}, u32[]{:S(2)}) collective-permute-start(bf16[216,384]{1,0:T(8,128)(2,1)S(1)} %get-tuple-element.48), channel_id=1, source_target_pairs={{0,12},{1,13},{2,14},{3,15},{4,0},{5,1},{6,2},{7,3},{8,4},{9,5},{1... | collective-permute-start | bytes 497672 | tf_op jit(solution)/shard_map/ppermute | solution.py:296
  50.3 8.4 %collective-permute-start.11 = (bf16[2,384,128]{2,1,0:T(8,128)(2,1)S(1)}, bf16[2,384,128]{2,1,0:T(8,128)(2,1)S(1)}, u32[]{:S(2)}, u32[]{:S(2)}) collective-permute-start(bf16[2,384,128]{2,1,0:T(8,128)(2,1)S(1)} %get-tuple-element.60), channel_id=1, source_target_pairs={{0,240},{16,32},{32,16},{48,64},{64,48},{80,96},{96,80},{112,128},... | collective-permute-start | bytes 589832 | tf_op jit(solution)/shard_map/ppermute | solution.py:275
  55.0 3.8 %collective-permute-start.12 = (bf16[2,384,128]{2,1,0:T(8,128)(2,1)S(1)}, bf16[2,384,128]{2,1,0:T(8,128)(2,1)S(1)}, u32[]{:S(2)}, u32[]{:S(2)}) collective-permute-start(bf16[2,384,128]{2,1,0:T(8,128)(2,1)S(1)} %get-tuple-element.61), channel_id=1, source_target_pairs={{0,16},{16,0},{32,48},{48,32},{64,80},{80,64},{96,112},{112,96},{1... | collective-permute-start | bytes 589832 | tf_op jit(solution)/shard_map/ppermute | solution.py:276
  72.0 16.8 %collective-permute-start.13 = (bf16[2,384,128]{2,1,0:T(8,128)(2,1)S(1)}, bf16[2,384,128]{2,1,0:T(8,128)(2,1)S(1)}, u32[]{:S(2)}, u32[]{:S(2)}) collective-permute-start(bf16[2,384,128]{2,1,0:T(8,128)(2,1)S(1)} %get-tuple-element.66), channel_id=1, source_target_pairs={{0,240},{16,32},{32,16},{48,64},{64,48},{80,96},{96,80},{112,128},... | collective-permute-start | bytes 589832 | tf_op jit(solution)/shard_map/ppermute | solution.py:275
  76.3 12.6 %collective-permute-start.14 = (bf16[2,384,128]{2,1,0:T(8,128)(2,1)S(1)}, bf16[2,384,128]{2,1,0:T(8,128)(2,1)S(1)}, u32[]{:S(2)}, u32[]{:S(2)}) collective-permute-start(bf16[2,384,128]{2,1,0:T(8,128)(2,1)S(1)} %get-tuple-element.67), channel_id=1, source_target_pairs={{0,16},{16,0},{32,48},{48,32},{64,80},{80,64},{96,112},{112,96},{1... | collective-permute-start | bytes 589832 | tf_op jit(solution)/shard_map/ppermute | solution.py:276
  78.6 7.2 %collective-permute-start.6 = (bf16[8,24,384]{2,1,0:T(8,128)(2,1)S(1)}, bf16[8,24,384]{2,1,0:T(8,128)(2,1)S(1)}, u32[]{:S(2)}, u32[]{:S(2)}) collective-permute-start(bf16[8,24,384]{2,1,0:T(8,128)(2,1)S(1)} %get-tuple-element.50), channel_id=1, source_target_pairs={{0,4},{1,5},{2,6},{3,7},{4,8},{5,9},{6,10},{7,11},{8,12},{9,13},{1... | collective-permute-start | bytes 442376 | tf_op jit(solution)/shard_map/ppermute | solution.py:296
  78.7 9.3 %collective-permute-start.7 = (bf16[8,24,384]{2,1,0:T(8,128)(2,1)S(1)}, bf16[8,24,384]{2,1,0:T(8,128)(2,1)S(1)}, u32[]{:S(2)}, u32[]{:S(2)}) collective-permute-start(bf16[8,24,384]{2,1,0:T(8,128)(2,1)S(1)} %get-tuple-element.51), channel_id=1, source_target_pairs={{0,8},{1,9},{2,10},{3,11},{4,12},{5,13},{6,14},{7,15},{8,0},{9,1},... | collective-permute-start | bytes 442376 | tf_op jit(solution)/shard_map/ppermute | solution.py:296
  80.9 7.9 %collective-permute-start.8 = (bf16[8,24,384]{2,1,0:T(8,128)(2,1)S(1)}, bf16[8,24,384]{2,1,0:T(8,128)(2,1)S(1)}, u32[]{:S(2)}, u32[]{:S(2)}) collective-permute-start(bf16[8,24,384]{2,1,0:T(8,128)(2,1)S(1)} %get-tuple-element.52), channel_id=1, source_target_pairs={{0,12},{1,13},{2,14},{3,15},{4,0},{5,1},{6,2},{7,3},{8,4},{9,5},{1... | collective-permute-start | bytes 442376 | tf_op jit(solution)/shard_map/ppermute | solution.py:296

commit v16 on v14

--- a/solution.py
+++ b/solution.py
@@ -106,13 +106,15 @@
 def table_kernel(slot_ref, cols_ref, rows_ref, slot_out, cols_out, rows_out):
     for t in range(TILES):
         slot_out[0, t] = slot_ref[0, t]
+    lead = lax.axis_index("lead")
+    odd = lax.bitwise_and(lead, 1)
     for r in range(SIDE):
         for k in range(8):
-            cols_out[r, k] = cols_ref[r, k]
-    lead = lax.axis_index("lead")
-    for side in range(2):
-        for h in range(2):
-            rows_out[side, h] = rows_ref[side, h, lead]
+            col = cols_ref[r, k]
+            cols_out[r, k] = jnp.where(col >= 4, lax.bitwise_xor(col, 2 * odd), col)
+    for h in range(2):
+        rows_out[0, h] = rows_ref[1 - odd, h, lead]
+        rows_out[1, h] = rows_ref[odd, h, lead]
 
 
 def send_halves(rows_ref, own_ref, up_ref, down_ref):
@@ -274,8 +276,8 @@
     diag = diag_inv.reshape(1, SHARE)
 
     def halo(up, down):
-        lower = lax.ppermute(up, "lead", [(i, (i + 1) % leads) for i in range(leads)])
-        upper = lax.ppermute(down, "lead", [(i, (i - 1) % leads) for i in range(leads)])
+        lower = lax.ppermute(up, "lead", [(i, (i + 2 * (i % 2) - 1) % leads) for i in range(leads)])
+        upper = lax.ppermute(down, "lead", [(i, i ^ 1) for i in range(leads)])
         return lower, upper
 
     def gather(wide):

time: 88.2 us -> 90 us (1.020)
  the two profiles are of different devices: /device:TPU:97 before, /device:TPU:1 now
where the time goes in v16:
time: 90 us; the launch traced here: 89.7 us
  starting transfers between devices  38.7 us (43%)
  blocking collectives  27.2 us (30%)
  waiting for transfers between devices  16.7 us (19%)
  Pallas kernels  6.97 us (8%)
    all_to_all x2, blocking collectives, gather(): return lax.all_to_all(wide, 'grp', 0, 0)  27.2 us
    ppermute x9, waiting for transfers between devices, exchange(): out.append(lax.ppermute(values[k], 'grp', pairs[k]))  13.7 us
    ppermute x9, starting transfers between devices, exchange(): out.append(lax.ppermute(values[k], 'grp', pairs[k]))  13 us
    ppermute x3, starting transfers between devices, halo(): lax.ppermute(up, 'lead', [(i, (i + 2 * (i % 2) - 1) % leads) for i in ran...  10.6 us
    all_to_all x1, starting transfers between devices, gather(): return lax.all_to_all(wide, 'grp', 0, 0)  7.58 us
    ppermute x3, starting transfers between devices, halo(): upper = lax.ppermute(down, 'lead', [(i, i ^ 1) for i in range(leads)])  7.52 us
    pallas_call x11, Pallas kernels, call(): pl.pallas_call(kernel, in_specs=specs, out_specs=[pl.BlockSpec(memory_spa...  6.15 us
    all_to_all x1, waiting for transfers between devices, gather(): return lax.all_to_all(wide, 'grp', 0, 0)  2.5 us
  transfers between devices with their start and end apart: 16, of which 10 were waited for; matrix products, arithmetic and copies ran while one was open for 0% of the time, Pallas kernels for 3%

profile of v16, /device:TPU:1, one launch (start us, length us, event | category | flops | bytes accessed | tf_op | source)
XLA Modules:
  0.0 89.7 jit_solution(6488826440958510688)
XLA Ops:
  0.0 1.8 %shard_map.64 = (bf16[2,96,384]{2,1,0:T(8,128)(2,1)S(1)}, bf16[2,96,384]{2,1,0:T(8,128)(2,1)S(1)}, bf16[2,96,384]{2,1,0:T(8,128)(2,1)S(1)}, bf16[2,96,384]{2,1,0...) custom-call(bf16[2,384,384]{2,1,0:T(8,128)(2,1)} %tiles_hbm.1, ...), custom_call_target="tpu_custom_call" | custom-call | tf_op jit(solution)/shard_map/pallas_call | solution.py:253
  1.8 7.6 %all-to-all-start = ((bf16[16,96,128]{2,1,0:T(8,128)(2,1)}), bf16[16,96,128]{2,1,0:T(8,128)(2,1)S(1)}, u32[]{:S(2)}, u32[]{:S(2)}) async-start(bf16[16,96,128]{2,1,0:T(8,128)(2,1)} %get-tuple-element.54), calls=%async_computation | async-start | bytes 786432 | tf_op jit(solution)/shard_map/all_to_all | solution.py:284
  9.4 1.4 %collective-permute-start = (bf16[2,96,384]{2,1,0:T(8,128)(2,1)S(1)}, bf16[2,96,384]{2,1,0:T(8,128)(2,1)S(1)}, u32[]{:S(2)}, u32[]{:S(2)}) collective-permute-start(bf16[2,96,384]{2,1,0:T(8,128)(2,1)S(1)} %get-tuple-element.40), channel_id=1, source_target_pairs={{0,1},{1,2},{2,3},{3,0},{4,5},{5,6},{6,7},{7,4},{8,9},{9,10},{10,1... | collective-permute-start | bytes 442376 | tf_op jit(solution)/shard_map/ppermute | solution.py:300
  10.8 2.4 %collective-permute-start.1 = (bf16[2,96,384]{2,1,0:T(8,128)(2,1)S(1)}, bf16[2,96,384]{2,1,0:T(8,128)(2,1)S(1)}, u32[]{:S(2)}, u32[]{:S(2)}) collective-permute-start(bf16[2,96,384]{2,1,0:T(8,128)(2,1)S(1)} %get-tuple-element.41), channel_id=1, source_target_pairs={{0,2},{1,3},{2,0},{3,1},{4,6},{5,7},{6,4},{7,5},{8,10},{9,11},{10,... | collective-permute-start | bytes 442376 | tf_op jit(solution)/shard_map/ppermute | solution.py:300
  13.2 1.2 %collective-permute-start.2 = (bf16[2,96,384]{2,1,0:T(8,128)(2,1)S(1)}, bf16[2,96,384]{2,1,0:T(8,128)(2,1)S(1)}, u32[]{:S(2)}, u32[]{:S(2)}) collective-permute-start(bf16[2,96,384]{2,1,0:T(8,128)(2,1)S(1)} %get-tuple-element.42), channel_id=1, source_target_pairs={{0,3},{1,0},{2,1},{3,2},{4,7},{5,4},{6,5},{7,6},{8,11},{9,8},{10,9... | collective-permute-start | bytes 442376 | tf_op jit(solution)/shard_map/ppermute | solution.py:300
  14.4 0.8 tables.1
  15.2 2.5 %all-to-all-done.got_ref = bf16[16,96,128]{2,1,0:T(8,128)(2,1)S(1)} async-done(((bf16[16,96,128]{2,1,0:T(8,128)(2,1)}), bf16[16,96,128]{2,1,0:T(8,128)(2,1)S(1)}, u32[]{:S(2)}, u32[]{:S(2)}) %all-to-all-start) | async-done | bytes 393248 | tf_op jit(solution)/shard_map/all_to_all | solution.py:284
  17.7 0.1 shard_map.67
  17.8 2.6 %collective-permute-start.10 = (bf16[2,384,128]{2,1,0:T(8,128)(2,1)S(1)}, bf16[2,384,128]{2,1,0:T(8,128)(2,1)S(1)}, u32[]{:S(2)}, u32[]{:S(2)}) collective-permute-start(bf16[2,384,128]{2,1,0:T(8,128)(2,1)S(1)} %get-tuple-element.57), channel_id=1, source_target_pairs={{0,16},{16,0},{32,48},{48,32},{64,80},{80,64},{96,112},{112,96},{1... | collective-permute-start | bytes 589832 | tf_op jit(solution)/shard_map/ppermute | solution.py:280
  20.4 1.6 %collective-permute-start.9 = (bf16[2,384,128]{2,1,0:T(8,128)(2,1)S(1)}, bf16[2,384,128]{2,1,0:T(8,128)(2,1)S(1)}, u32[]{:S(2)}, u32[]{:S(2)}) collective-permute-start(bf16[2,384,128]{2,1,0:T(8,128)(2,1)S(1)} %get-tuple-element.56), channel_id=1, source_target_pairs={{0,240},{16,32},{32,16},{48,64},{64,48},{80,96},{96,80},{112,128},... | collective-permute-start | bytes 589832 | tf_op jit(solution)/shard_map/ppermute | solution.py:279
  22.0 0.0 collective-permute-done.refs_1_
  22.0 1.2 %collective-permute-done.1.refs_2_ = bf16[2,96,384]{2,1,0:T(8,128)(2,1)S(1)} collective-permute-done((bf16[2,96,384]{2,1,0:T(8,128)(2,1)S(1)}, bf16[2,96,384]{2,1,0:T(8,128)(2,1)S(1)}, u32[]{:S(2)}, u32[]{:S(2)}) %collective-permute-start.1) | collective-permute-done | bytes 147488 | tf_op jit(solution)/shard_map/ppermute | solution.py:300
  23.2 0.2 collective-permute-done.2.refs_3_
  23.4 0.1 shard_map.65
  23.5 1.4 %collective-permute-start.3 = (bf16[216,384]{1,0:T(8,128)(2,1)S(1)}, bf16[216,384]{1,0:T(8,128)(2,1)S(1)}, u32[]{:S(2)}, u32[]{:S(2)}) collective-permute-start(bf16[216,384]{1,0:T(8,128)(2,1)S(1)} %get-tuple-element.46), channel_id=1, source_target_pairs={{0,4},{1,5},{2,6},{3,7},{4,8},{5,9},{6,10},{7,11},{8,12},{9,13},{1... | collective-permute-start | bytes 497672 | tf_op jit(solution)/shard_map/ppermute | solution.py:300
  25.0 2.5 %collective-permute-start.4 = (bf16[216,384]{1,0:T(8,128)(2,1)S(1)}, bf16[216,384]{1,0:T(8,128)(2,1)S(1)}, u32[]{:S(2)}, u32[]{:S(2)}) collective-permute-start(bf16[216,384]{1,0:T(8,128)(2,1)S(1)} %get-tuple-element.47), channel_id=1, source_target_pairs={{0,8},{1,9},{2,10},{3,11},{4,12},{5,13},{6,14},{7,15},{8,0},{9,1},... | collective-permute-start | bytes 497672 | tf_op jit(solution)/shard_map/ppermute | solution.py:300
  27.4 1.0 %collective-permute-start.5 = (bf16[216,384]{1,0:T(8,128)(2,1)S(1)}, bf16[216,384]{1,0:T(8,128)(2,1)S(1)}, u32[]{:S(2)}, u32[]{:S(2)}) collective-permute-start(bf16[216,384]{1,0:T(8,128)(2,1)S(1)} %get-tuple-element.48), channel_id=1, source_target_pairs={{0,12},{1,13},{2,14},{3,15},{4,0},{5,1},{6,2},{7,3},{8,4},{9,5},{1... | collective-permute-start | bytes 497672 | tf_op jit(solution)/shard_map/ppermute | solution.py:300
  28.5 0.8 collective-permute-done.3.refs_1_
  29.3 4.4 %collective-permute-done.4.refs_2_ = bf16[216,384]{1,0:T(8,128)(2,1)S(1)} collective-permute-done((bf16[216,384]{1,0:T(8,128)(2,1)S(1)}, bf16[216,384]{1,0:T(8,128)(2,1)S(1)}, u32[]{:S(2)}, u32[]{:S(2)}) %collective-permute-start.4) | collective-permute-done | bytes 165920 | tf_op jit(solution)/shard_map/ppermute | solution.py:300
  33.7 0.0 collective-permute-done.5.refs_3_
  33.7 0.6 shard_map.68.refs_4_
  34.3 0.0 collective-permute-done.10.refs_6_
  34.3 0.0 collective-permute-done.9.refs_5_
  34.3 0.8 shard_map.69
  35.2 14.9 %all_to_all.15.got_ref = bf16[16,96,128]{2,1,0:T(8,128)(2,1)S(1)} all-to-all(bf16[16,96,128]{2,1,0:T(8,128)(2,1)S(1)} %get-tuple-element.58), channel_id=1, replica_groups=mesh['lead'=16,'grp'=16] {'grp'}, dimensions={0} | all-to-all | bytes 786432 | tf_op jit(solution)/shard_map/all_to_all | solution.py:284
  50.1 0.1 shard_map.70
  50.2 4.7 %collective-permute-start.11 = (bf16[2,384,128]{2,1,0:T(8,128)(2,1)S(1)}, bf16[2,384,128]{2,1,0:T(8,128)(2,1)S(1)}, u32[]{:S(2)}, u32[]{:S(2)}) collective-permute-start(bf16[2,384,128]{2,1,0:T(8,128)(2,1)S(1)} %get-tuple-element.60), channel_id=1, source_target_pairs={{0,240},{16,32},{32,16},{48,64},{64,48},{80,96},{96,80},{112,128},... | collective-permute-start | bytes 589832 | tf_op jit(solution)/shard_map/ppermute | solution.py:279
  54.9 2.7 %collective-permute-start.12 = (bf16[2,384,128]{2,1,0:T(8,128)(2,1)S(1)}, bf16[2,384,128]{2,1,0:T(8,128)(2,1)S(1)}, u32[]{:S(2)}, u32[]{:S(2)}) collective-permute-start(bf16[2,384,128]{2,1,0:T(8,128)(2,1)S(1)} %get-tuple-element.61), channel_id=1, source_target_pairs={{0,16},{16,0},{32,48},{48,32},{64,80},{80,64},{96,112},{112,96},{1... | collective-permute-start | bytes 589832 | tf_op jit(solution)/shard_map/ppermute | solution.py:280
  57.6 0.6 shard_map.71.refs_4_
  58.2 0.4 collective-permute-done.11.refs_5_
  58.6 0.1 collective-permute-done.12.refs_6_
  58.7 0.8 shard_map.72
  59.5 12.3 %all_to_all.16.got_ref.refs_7_ = bf16[16,120,128]{2,1,0:T(8,128)(2,1)S(1)} all-to-all(bf16[16,120,128]{2,1,0:T(8,128)(2,1)S(1)} %shard_map.72), channel_id=1, replica_groups=mesh['lead'=16,'grp'=16] {'grp'}, dimensions={0} | all-to-all | bytes 983040 | tf_op jit(solution)/shard_map/all_to_all | solution.py:284
  71.8 0.1 shard_map.73
  71.9 4.3 %collective-permute-start.13 = (bf16[2,384,128]{2,1,0:T(8,128)(2,1)S(1)}, bf16[2,384,128]{2,1,0:T(8,128)(2,1)S(1)}, u32[]{:S(2)}, u32[]{:S(2)}) collective-permute-start(bf16[2,384,128]{2,1,0:T(8,128)(2,1)S(1)} %get-tuple-element.66), channel_id=1, source_target_pairs={{0,240},{16,32},{32,16},{48,64},{64,48},{80,96},{96,80},{112,128},... | collective-permute-start | bytes 589832 | tf_op jit(solution)/shard_map/ppermute | solution.py:279
  76.1 2.3 %collective-permute-start.14 = (bf16[2,384,128]{2,1,0:T(8,128)(2,1)S(1)}, bf16[2,384,128]{2,1,0:T(8,128)(2,1)S(1)}, u32[]{:S(2)}, u32[]{:S(2)}) collective-permute-start(bf16[2,384,128]{2,1,0:T(8,128)(2,1)S(1)} %get-tuple-element.67), channel_id=1, source_target_pairs={{0,16},{16,0},{32,48},{48,32},{64,80},{80,64},{96,112},{112,96},{1... | collective-permute-start | bytes 589832 | tf_op jit(solution)/shard_map/ppermute | solution.py:280
  78.4 0.1 shard_map.66
  78.5 0.1 collective-permute-start.6
  78.6 2.2 %collective-permute-start.7 = (bf16[8,24,384]{2,1,0:T(8,128)(2,1)S(1)}, bf16[8,24,384]{2,1,0:T(8,128)(2,1)S(1)}, u32[]{:S(2)}, u32[]{:S(2)}) collective-permute-start(bf16[8,24,384]{2,1,0:T(8,128)(2,1)S(1)} %get-tuple-element.51), channel_id=1, source_target_pairs={{0,8},{1,9},{2,10},{3,11},{4,12},{5,13},{6,14},{7,15},{8,0},{9,1},... | collective-permute-start | bytes 442376 | tf_op jit(solution)/shard_map/ppermute | solution.py:300
  80.8 0.9 collective-permute-start.8
  81.7 4.0 %collective-permute-done.6.refs_1_ = bf16[8,24,384]{2,1,0:T(8,128)(2,1)S(1)} collective-permute-done((bf16[8,24,384]{2,1,0:T(8,128)(2,1)S(1)}, bf16[8,24,384]{2,1,0:T(8,128)(2,1)S(1)}, u32[]{:S(2)}, u32[]{:S(2)}) %collective-permute-start.6) | collective-permute-done | bytes 147488 | tf_op jit(solution)/shard_map/ppermute | solution.py:300
  85.7 2.2 %collective-permute-done.7.refs_2_ = bf16[8,24,384]{2,1,0:T(8,128)(2,1)S(1)} collective-permute-done((bf16[8,24,384]{2,1,0:T(8,128)(2,1)S(1)}, bf16[8,24,384]{2,1,0:T(8,128)(2,1)S(1)}, u32[]{:S(2)}, u32[]{:S(2)}) %collective-permute-start.7) | collective-permute-done | bytes 147488 | tf_op jit(solution)/shard_map/ppermute | solution.py:300
  87.9 0.8 collective-permute-done.8.refs_3_
  88.7 0.0 collective-permute-done.13.refs_5_
  88.7 0.0 collective-permute-done.14.refs_6_
  88.7 1.0 %shard_map.74 = f32[96,128]{1,0:T(8,128)} custom-call(s32[4,8]{1,0:T(4,128)S(4)} %get-tuple-element.37.cols_ref, bf16[8,24,384]{2,1,0:T(8,128)(2,1)S(1)} %get-tuple-element.49.refs_0_, bf16[8,24,384]{2,1,0:T(8,128)(2,1)S(1)} %collective-permute-done.6.refs_1_, bf16[8,24,384]{2,1,0:T(8,128)(2,1)S(1)} %collective-permute-done.7.refs_2_, ...), custom_call_target="tpu_custom_call" | custom-call | tf_op jit(solution)/shard_map/pallas_call | solution.py:253
Async XLA Ops:
  1.8 15.9 %all-to-all-start = ((bf16[16,96,128]{2,1,0:T(8,128)(2,1)}), bf16[16,96,128]{2,1,0:T(8,128)(2,1)S(1)}, u32[]{:S(2)}, u32[]{:S(2)}) async-start(bf16[16,96,128]{2,1,0:T(8,128)(2,1)} %get-tuple-element.54), calls=%async_computation | async-start | bytes 786432 | tf_op jit(solution)/shard_map/all_to_all | solution.py:284
  9.4 12.5 %collective-permute-start = (bf16[2,96,384]{2,1,0:T(8,128)(2,1)S(1)}, bf16[2,96,384]{2,1,0:T(8,128)(2,1)S(1)}, u32[]{:S(2)}, u32[]{:S(2)}) collective-permute-start(bf16[2,96,384]{2,1,0:T(8,128)(2,1)S(1)} %get-tuple-element.40), channel_id=1, source_target_pairs={{0,1},{1,2},{2,3},{3,0},{4,5},{5,6},{6,7},{7,4},{8,9},{9,10},{10,1... | collective-permute-start | bytes 442376 | tf_op jit(solution)/shard_map/ppermute | solution.py:300
  10.8 12.4 %collective-permute-start.1 = (bf16[2,96,384]{2,1,0:T(8,128)(2,1)S(1)}, bf16[2,96,384]{2,1,0:T(8,128)(2,1)S(1)}, u32[]{:S(2)}, u32[]{:S(2)}) collective-permute-start(bf16[2,96,384]{2,1,0:T(8,128)(2,1)S(1)} %get-tuple-element.41), channel_id=1, source_target_pairs={{0,2},{1,3},{2,0},{3,1},{4,6},{5,7},{6,4},{7,5},{8,10},{9,11},{10,... | collective-permute-start | bytes 442376 | tf_op jit(solution)/shard_map/ppermute | solution.py:300
  13.2 10.2 %collective-permute-start.2 = (bf16[2,96,384]{2,1,0:T(8,128)(2,1)S(1)}, bf16[2,96,384]{2,1,0:T(8,128)(2,1)S(1)}, u32[]{:S(2)}, u32[]{:S(2)}) collective-permute-start(bf16[2,96,384]{2,1,0:T(8,128)(2,1)S(1)} %get-tuple-element.42), channel_id=1, source_target_pairs={{0,3},{1,0},{2,1},{3,2},{4,7},{5,4},{6,5},{7,6},{8,11},{9,8},{10,9... | collective-permute-start | bytes 442376 | tf_op jit(solution)/shard_map/ppermute | solution.py:300
  17.8 16.5 %collective-permute-start.10 = (bf16[2,384,128]{2,1,0:T(8,128)(2,1)S(1)}, bf16[2,384,128]{2,1,0:T(8,128)(2,1)S(1)}, u32[]{:S(2)}, u32[]{:S(2)}) collective-permute-start(bf16[2,384,128]{2,1,0:T(8,128)(2,1)S(1)} %get-tuple-element.57), channel_id=1, source_target_pairs={{0,16},{16,0},{32,48},{48,32},{64,80},{80,64},{96,112},{112,96},{1... | collective-permute-start | bytes 589832 | tf_op jit(solution)/shard_map/ppermute | solution.py:280
  20.4 14.0 %collective-permute-start.9 = (bf16[2,384,128]{2,1,0:T(8,128)(2,1)S(1)}, bf16[2,384,128]{2,1,0:T(8,128)(2,1)S(1)}, u32[]{:S(2)}, u32[]{:S(2)}) collective-permute-start(bf16[2,384,128]{2,1,0:T(8,128)(2,1)S(1)} %get-tuple-element.56), channel_id=1, source_target_pairs={{0,240},{16,32},{32,16},{48,64},{64,48},{80,96},{96,80},{112,128},... | collective-permute-start | bytes 589832 | tf_op jit(solution)/shard_map/ppermute | solution.py:279
  23.5 5.7 %collective-permute-start.3 = (bf16[216,384]{1,0:T(8,128)(2,1)S(1)}, bf16[216,384]{1,0:T(8,128)(2,1)S(1)}, u32[]{:S(2)}, u32[]{:S(2)}) collective-permute-start(bf16[216,384]{1,0:T(8,128)(2,1)S(1)} %get-tuple-element.46), channel_id=1, source_target_pairs={{0,4},{1,5},{2,6},{3,7},{4,8},{5,9},{6,10},{7,11},{8,12},{9,13},{1... | collective-permute-start | bytes 497672 | tf_op jit(solution)/shard_map/ppermute | solution.py:300
  25.0 8.7 %collective-permute-start.4 = (bf16[216,384]{1,0:T(8,128)(2,1)S(1)}, bf16[216,384]{1,0:T(8,128)(2,1)S(1)}, u32[]{:S(2)}, u32[]{:S(2)}) collective-permute-start(bf16[216,384]{1,0:T(8,128)(2,1)S(1)} %get-tuple-element.47), channel_id=1, source_target_pairs={{0,8},{1,9},{2,10},{3,11},{4,12},{5,13},{6,14},{7,15},{8,0},{9,1},... | collective-permute-start | bytes 497672 | tf_op jit(solution)/shard_map/ppermute | solution.py:300
  27.4 6.3 %collective-permute-start.5 = (bf16[216,384]{1,0:T(8,128)(2,1)S(1)}, bf16[216,384]{1,0:T(8,128)(2,1)S(1)}, u32[]{:S(2)}, u32[]{:S(2)}) collective-permute-start(bf16[216,384]{1,0:T(8,128)(2,1)S(1)} %get-tuple-element.48), channel_id=1, source_target_pairs={{0,12},{1,13},{2,14},{3,15},{4,0},{5,1},{6,2},{7,3},{8,4},{9,5},{1... | collective-permute-start | bytes 497672 | tf_op jit(solution)/shard_map/ppermute | solution.py:300
  50.2 8.4 %collective-permute-start.11 = (bf16[2,384,128]{2,1,0:T(8,128)(2,1)S(1)}, bf16[2,384,128]{2,1,0:T(8,128)(2,1)S(1)}, u32[]{:S(2)}, u32[]{:S(2)}) collective-permute-start(bf16[2,384,128]{2,1,0:T(8,128)(2,1)S(1)} %get-tuple-element.60), channel_id=1, source_target_pairs={{0,240},{16,32},{32,16},{48,64},{64,48},{80,96},{96,80},{112,128},... | collective-permute-start | bytes 589832 | tf_op jit(solution)/shard_map/ppermute | solution.py:279
  54.9 3.8 %collective-permute-start.12 = (bf16[2,384,128]{2,1,0:T(8,128)(2,1)S(1)}, bf16[2,384,128]{2,1,0:T(8,128)(2,1)S(1)}, u32[]{:S(2)}, u32[]{:S(2)}) collective-permute-start(bf16[2,384,128]{2,1,0:T(8,128)(2,1)S(1)} %get-tuple-element.61), channel_id=1, source_target_pairs={{0,16},{16,0},{32,48},{48,32},{64,80},{80,64},{96,112},{112,96},{1... | collective-permute-start | bytes 589832 | tf_op jit(solution)/shard_map/ppermute | solution.py:280
  71.9 16.8 %collective-permute-start.13 = (bf16[2,384,128]{2,1,0:T(8,128)(2,1)S(1)}, bf16[2,384,128]{2,1,0:T(8,128)(2,1)S(1)}, u32[]{:S(2)}, u32[]{:S(2)}) collective-permute-start(bf16[2,384,128]{2,1,0:T(8,128)(2,1)S(1)} %get-tuple-element.66), channel_id=1, source_target_pairs={{0,240},{16,32},{32,16},{48,64},{64,48},{80,96},{96,80},{112,128},... | collective-permute-start | bytes 589832 | tf_op jit(solution)/shard_map/ppermute | solution.py:279
  76.1 12.6 %collective-permute-start.14 = (bf16[2,384,128]{2,1,0:T(8,128)(2,1)S(1)}, bf16[2,384,128]{2,1,0:T(8,128)(2,1)S(1)}, u32[]{:S(2)}, u32[]{:S(2)}) collective-permute-start(bf16[2,384,128]{2,1,0:T(8,128)(2,1)S(1)} %get-tuple-element.67), channel_id=1, source_target_pairs={{0,16},{16,0},{32,48},{48,32},{64,80},{80,64},{96,112},{112,96},{1... | collective-permute-start | bytes 589832 | tf_op jit(solution)/shard_map/ppermute | solution.py:280
  78.5 7.2 %collective-permute-start.6 = (bf16[8,24,384]{2,1,0:T(8,128)(2,1)S(1)}, bf16[8,24,384]{2,1,0:T(8,128)(2,1)S(1)}, u32[]{:S(2)}, u32[]{:S(2)}) collective-permute-start(bf16[8,24,384]{2,1,0:T(8,128)(2,1)S(1)} %get-tuple-element.50), channel_id=1, source_target_pairs={{0,4},{1,5},{2,6},{3,7},{4,8},{5,9},{6,10},{7,11},{8,12},{9,13},{1... | collective-permute-start | bytes 442376 | tf_op jit(solution)/shard_map/ppermute | solution.py:300
  78.6 9.3 %collective-permute-start.7 = (bf16[8,24,384]{2,1,0:T(8,128)(2,1)S(1)}, bf16[8,24,384]{2,1,0:T(8,128)(2,1)S(1)}, u32[]{:S(2)}, u32[]{:S(2)}) collective-permute-start(bf16[8,24,384]{2,1,0:T(8,128)(2,1)S(1)} %get-tuple-element.51), channel_id=1, source_target_pairs={{0,8},{1,9},{2,10},{3,11},{4,12},{5,13},{6,14},{7,15},{8,0},{9,1},... | collective-permute-start | bytes 442376 | tf_op jit(solution)/shard_map/ppermute | solution.py:300
  80.8 7.9 %collective-permute-start.8 = (bf16[8,24,384]{2,1,0:T(8,128)(2,1)S(1)}, bf16[8,24,384]{2,1,0:T(8,128)(2,1)S(1)}, u32[]{:S(2)}, u32[]{:S(2)}) collective-permute-start(bf16[8,24,384]{2,1,0:T(8,128)(2,1)S(1)} %get-tuple-element.52), channel_id=1, source_target_pairs={{0,12},{1,13},{2,14},{3,15},{4,0},{5,1},{6,2},{7,3},{8,4},{9,5},{1... | collective-permute-start | bytes 442376 | tf_op jit(solution)/shard_map/ppermute | solution.py:300

commit v17 on v12

--- a/solution.py
+++ b/solution.py
@@ -106,13 +106,15 @@
 def table_kernel(slot_ref, cols_ref, rows_ref, slot_out, cols_out, rows_out):
     for t in range(TILES):
         slot_out[0, t] = slot_ref[0, t]
+    lead = lax.axis_index("lead")
+    odd = lax.bitwise_and(lead, 1)
     for r in range(SIDE):
         for k in range(8):
-            cols_out[r, k] = cols_ref[r, k]
-    lead = lax.axis_index("lead")
-    for side in range(2):
-        for h in range(2):
-            rows_out[side, h] = rows_ref[side, h, lead]
+            col = cols_ref[r, k]
+            cols_out[r, k] = jnp.where(col >= 4, lax.bitwise_xor(col, 2 * odd), col)
+    for h in range(2):
+        rows_out[0, h] = rows_ref[1 - odd, h, lead]
+        rows_out[1, h] = rows_ref[odd, h, lead]
 
 
 def send_halves(rows_ref, own_ref, up_ref, down_ref):
@@ -285,8 +287,8 @@
     diag = diag_inv.reshape(1, SHARE)
 
     def halo(up, down):
-        lower = lax.ppermute(up, "lead", [(i, (i + 1) % leads) for i in range(leads)])
-        upper = lax.ppermute(down, "lead", [(i, (i - 1) % leads) for i in range(leads)])
+        lower = lax.ppermute(up, "lead", [(i, (i + 2 * (i % 2) - 1) % leads) for i in range(leads)])
+        upper = lax.ppermute(down, "lead", [(i, i ^ 1) for i in range(leads)])
         return lower, upper
 
     def gather(wide):

time: 90.2 us -> 92.8 us (1.029)
  the two profiles are of different devices: /device:TPU:6 before, /device:TPU:1 now
where the time goes in v17:
time: 92.8 us; the launch traced here: 92.5 us
  starting transfers between devices  39.1 us (42%)
  blocking collectives  26.9 us (29%)
  waiting for transfers between devices  18.5 us (20%)
  Pallas kernels  7.86 us (8%)
    all_to_all x2, blocking collectives, gather(): return lax.all_to_all(wide, 'grp', 0, 0)  26.9 us
    ppermute x9, waiting for transfers between devices, exchange(): out.append(lax.ppermute(values[k], 'grp', pairs[k]))  13.9 us
    ppermute x9, starting transfers between devices, exchange(): out.append(lax.ppermute(values[k], 'grp', pairs[k]))  12.8 us
    ppermute x3, starting transfers between devices, halo(): upper = lax.ppermute(down, 'lead', [(i, i ^ 1) for i in range(leads)])  9.91 us
    ppermute x3, starting transfers between devices, halo(): lax.ppermute(up, 'lead', [(i, (i + 2 * (i % 2) - 1) % leads) for i in ran...  8.77 us
    all_to_all x1, starting transfers between devices, gather(): return lax.all_to_all(wide, 'grp', 0, 0)  7.58 us
    pallas_call x13, Pallas kernels, call(): pl.pallas_call(kernel, in_specs=specs, out_specs=[pl.BlockSpec(memory_spa...  7.04 us
    all_to_all x1, waiting for transfers between devices, gather(): return lax.all_to_all(wide, 'grp', 0, 0)  2.5 us
  transfers between devices with their start and end apart: 16, of which 8 were waited for; matrix products, arithmetic and copies ran while one was open for 0% of the time, Pallas kernels for 4%

profile of v17, /device:TPU:1, one launch (start us, length us, event | category | flops | bytes accessed | tf_op | source)
XLA Modules:
  0.0 92.5 jit_solution(8944173767596086463)
XLA Ops:
  0.0 1.8 %shard_map.64 = (bf16[2,96,384]{2,1,0:T(8,128)(2,1)S(1)}, bf16[2,96,384]{2,1,0:T(8,128)(2,1)S(1)}, bf16[2,96,384]{2,1,0:T(8,128)(2,1)S(1)}, bf16[2,96,384]{2,1,0...) custom-call(bf16[2,384,384]{2,1,0:T(8,128)(2,1)} %tiles_hbm.1, ...), custom_call_target="tpu_custom_call" | custom-call | tf_op jit(solution)/shard_map/pallas_call | solution.py:265
  1.8 7.6 %all-to-all-start = ((bf16[16,96,128]{2,1,0:T(8,128)(2,1)}), bf16[16,96,128]{2,1,0:T(8,128)(2,1)S(1)}, u32[]{:S(2)}, u32[]{:S(2)}) async-start(bf16[16,96,128]{2,1,0:T(8,128)(2,1)} %get-tuple-element.54), calls=%async_computation | async-start | bytes 786432 | tf_op jit(solution)/shard_map/all_to_all | solution.py:295
  9.4 1.4 %collective-permute-start = (bf16[2,96,384]{2,1,0:T(8,128)(2,1)S(1)}, bf16[2,96,384]{2,1,0:T(8,128)(2,1)S(1)}, u32[]{:S(2)}, u32[]{:S(2)}) collective-permute-start(bf16[2,96,384]{2,1,0:T(8,128)(2,1)S(1)} %get-tuple-element.40), channel_id=1, source_target_pairs={{0,1},{1,2},{2,3},{3,0},{4,5},{5,6},{6,7},{7,4},{8,9},{9,10},{10,1... | collective-permute-start | bytes 442376 | tf_op jit(solution)/shard_map/ppermute | solution.py:311
  10.8 2.4 %collective-permute-start.1 = (bf16[2,96,384]{2,1,0:T(8,128)(2,1)S(1)}, bf16[2,96,384]{2,1,0:T(8,128)(2,1)S(1)}, u32[]{:S(2)}, u32[]{:S(2)}) collective-permute-start(bf16[2,96,384]{2,1,0:T(8,128)(2,1)S(1)} %get-tuple-element.41), channel_id=1, source_target_pairs={{0,2},{1,3},{2,0},{3,1},{4,6},{5,7},{6,4},{7,5},{8,10},{9,11},{10,... | collective-permute-start | bytes 442376 | tf_op jit(solution)/shard_map/ppermute | solution.py:311
  13.2 1.2 %collective-permute-start.2 = (bf16[2,96,384]{2,1,0:T(8,128)(2,1)S(1)}, bf16[2,96,384]{2,1,0:T(8,128)(2,1)S(1)}, u32[]{:S(2)}, u32[]{:S(2)}) collective-permute-start(bf16[2,96,384]{2,1,0:T(8,128)(2,1)S(1)} %get-tuple-element.42), channel_id=1, source_target_pairs={{0,3},{1,0},{2,1},{3,2},{4,7},{5,4},{6,5},{7,6},{8,11},{9,8},{10,9... | collective-permute-start | bytes 442376 | tf_op jit(solution)/shard_map/ppermute | solution.py:311
  14.4 0.8 tables.1
  15.2 2.5 %all-to-all-done.got_ref = bf16[16,96,128]{2,1,0:T(8,128)(2,1)S(1)} async-done(((bf16[16,96,128]{2,1,0:T(8,128)(2,1)}), bf16[16,96,128]{2,1,0:T(8,128)(2,1)S(1)}, u32[]{:S(2)}, u32[]{:S(2)}) %all-to-all-start) | async-done | bytes 393248 | tf_op jit(solution)/shard_map/all_to_all | solution.py:295
  17.7 0.1 shard_map.67
  17.8 2.6 %collective-permute-start.9 = (bf16[2,384,128]{2,1,0:T(8,128)(2,1)S(1)}, bf16[2,384,128]{2,1,0:T(8,128)(2,1)S(1)}, u32[]{:S(2)}, u32[]{:S(2)}) collective-permute-start(bf16[2,384,128]{2,1,0:T(8,128)(2,1)S(1)} %get-tuple-element.56), channel_id=1, source_target_pairs={{0,16},{16,0},{32,48},{48,32},{64,80},{80,64},{96,112},{112,96},{1... | collective-permute-start | bytes 589832 | tf_op jit(solution)/shard_map/ppermute | solution.py:291
  20.4 1.6 %collective-permute-start.10 = (bf16[2,384,128]{2,1,0:T(8,128)(2,1)S(1)}, bf16[2,384,128]{2,1,0:T(8,128)(2,1)S(1)}, u32[]{:S(2)}, u32[]{:S(2)}) collective-permute-start(bf16[2,384,128]{2,1,0:T(8,128)(2,1)S(1)} %get-tuple-element.57), channel_id=1, source_target_pairs={{0,240},{16,32},{32,16},{48,64},{64,48},{80,96},{96,80},{112,128},... | collective-permute-start | bytes 589832 | tf_op jit(solution)/shard_map/ppermute | solution.py:290
  22.0 0.0 collective-permute-done.refs_1_
  22.0 1.2 %collective-permute-done.1.refs_2_ = bf16[2,96,384]{2,1,0:T(8,128)(2,1)S(1)} collective-permute-done((bf16[2,96,384]{2,1,0:T(8,128)(2,1)S(1)}, bf16[2,96,384]{2,1,0:T(8,128)(2,1)S(1)}, u32[]{:S(2)}, u32[]{:S(2)}) %collective-permute-start.1) | collective-permute-done | bytes 147488 | tf_op jit(solution)/shard_map/ppermute | solution.py:311
  23.2 0.2 collective-permute-done.2.refs_3_
  23.4 0.1 shard_map.65
  23.5 1.4 %collective-permute-start.3 = (bf16[216,384]{1,0:T(8,128)(2,1)S(1)}, bf16[216,384]{1,0:T(8,128)(2,1)S(1)}, u32[]{:S(2)}, u32[]{:S(2)}) collective-permute-start(bf16[216,384]{1,0:T(8,128)(2,1)S(1)} %get-tuple-element.46), channel_id=1, source_target_pairs={{0,4},{1,5},{2,6},{3,7},{4,8},{5,9},{6,10},{7,11},{8,12},{9,13},{1... | collective-permute-start | bytes 497672 | tf_op jit(solution)/shard_map/ppermute | solution.py:311
  25.0 2.5 %collective-permute-start.4 = (bf16[216,384]{1,0:T(8,128)(2,1)S(1)}, bf16[216,384]{1,0:T(8,128)(2,1)S(1)}, u32[]{:S(2)}, u32[]{:S(2)}) collective-permute-start(bf16[216,384]{1,0:T(8,128)(2,1)S(1)} %get-tuple-element.47), channel_id=1, source_target_pairs={{0,8},{1,9},{2,10},{3,11},{4,12},{5,13},{6,14},{7,15},{8,0},{9,1},... | collective-permute-start | bytes 497672 | tf_op jit(solution)/shard_map/ppermute | solution.py:311
  27.4 1.0 %collective-permute-start.5 = (bf16[216,384]{1,0:T(8,128)(2,1)S(1)}, bf16[216,384]{1,0:T(8,128)(2,1)S(1)}, u32[]{:S(2)}, u32[]{:S(2)}) collective-permute-start(bf16[216,384]{1,0:T(8,128)(2,1)S(1)} %get-tuple-element.48), channel_id=1, source_target_pairs={{0,12},{1,13},{2,14},{3,15},{4,0},{5,1},{6,2},{7,3},{8,4},{9,5},{1... | collective-permute-start | bytes 497672 | tf_op jit(solution)/shard_map/ppermute | solution.py:311
  28.5 0.8 collective-permute-done.3.refs_1_
  29.3 4.4 %collective-permute-done.4.refs_2_ = bf16[216,384]{1,0:T(8,128)(2,1)S(1)} collective-permute-done((bf16[216,384]{1,0:T(8,128)(2,1)S(1)}, bf16[216,384]{1,0:T(8,128)(2,1)S(1)}, u32[]{:S(2)}, u32[]{:S(2)}) %collective-permute-start.4) | collective-permute-done | bytes 165920 | tf_op jit(solution)/shard_map/ppermute | solution.py:311
  33.7 0.0 collective-permute-done.5.refs_3_
  33.7 0.7 shard_map.68.refs_4_
  34.5 0.0 collective-permute-done.9.refs_5_
  34.5 0.5 shard_map.69.refs_4_
  35.0 0.0 collective-permute-done.10.refs_5_
  35.0 0.6 shard_map.70
  35.6 14.9 %all_to_all.15.got_ref = bf16[16,96,128]{2,1,0:T(8,128)(2,1)S(1)} all-to-all(bf16[16,96,128]{2,1,0:T(8,128)(2,1)S(1)} %get-tuple-element.58), channel_id=1, replica_groups=mesh['lead'=16,'grp'=16] {'grp'}, dimensions={0} | all-to-all | bytes 786432 | tf_op jit(solution)/shard_map/all_to_all | solution.py:295
  50.5 0.1 shard_map.71
  50.6 2.7 %collective-permute-start.11 = (bf16[2,384,128]{2,1,0:T(8,128)(2,1)S(1)}, bf16[2,384,128]{2,1,0:T(8,128)(2,1)S(1)}, u32[]{:S(2)}, u32[]{:S(2)}) collective-permute-start(bf16[2,384,128]{2,1,0:T(8,128)(2,1)S(1)} %get-tuple-element.60), channel_id=1, source_target_pairs={{0,16},{16,0},{32,48},{48,32},{64,80},{80,64},{96,112},{112,96},{1... | collective-permute-start | bytes 589832 | tf_op jit(solution)/shard_map/ppermute | solution.py:291
  53.3 2.1 %collective-permute-start.12 = (bf16[2,384,128]{2,1,0:T(8,128)(2,1)S(1)}, bf16[2,384,128]{2,1,0:T(8,128)(2,1)S(1)}, u32[]{:S(2)}, u32[]{:S(2)}) collective-permute-start(bf16[2,384,128]{2,1,0:T(8,128)(2,1)S(1)} %get-tuple-element.61), channel_id=1, source_target_pairs={{0,240},{16,32},{32,16},{48,64},{64,48},{80,96},{96,80},{112,128},... | collective-permute-start | bytes 589832 | tf_op jit(solution)/shard_map/ppermute | solution.py:290
  55.4 0.7 shard_map.72.refs_4_
  56.2 0.0 collective-permute-done.11.refs_5_
  56.2 0.5 shard_map.73.refs_4_
  56.7 2.1 %collective-permute-done.12.refs_5_ = bf16[2,384,128]{2,1,0:T(8,128)(2,1)S(1)} collective-permute-done((bf16[2,384,128]{2,1,0:T(8,128)(2,1)S(1)}, bf16[2,384,128]{2,1,0:T(8,128)(2,1)S(1)}, u32[]{:S(2)}, u32[]{:S(2)}) %collective-permute-start.12) | collective-permute-done | bytes 196640 | tf_op jit(solution)/shard_map/ppermute | solution.py:290
  58.8 0.6 shard_map.74
  59.4 12.0 %all_to_all.16.got_ref.refs_7_ = bf16[16,120,128]{2,1,0:T(8,128)(2,1)S(1)} all-to-all(bf16[16,120,128]{2,1,0:T(8,128)(2,1)S(1)} %shard_map.74), channel_id=1, replica_groups=mesh['lead'=16,'grp'=16] {'grp'}, dimensions={0} | all-to-all | bytes 983040 | tf_op jit(solution)/shard_map/all_to_all | solution.py:295
  71.4 0.1 shard_map.75
  71.5 5.0 %collective-permute-start.13 = (bf16[2,384,128]{2,1,0:T(8,128)(2,1)S(1)}, bf16[2,384,128]{2,1,0:T(8,128)(2,1)S(1)}, u32[]{:S(2)}, u32[]{:S(2)}) collective-permute-start(bf16[2,384,128]{2,1,0:T(8,128)(2,1)S(1)} %get-tuple-element.66), channel_id=1, source_target_pairs={{0,240},{16,32},{32,16},{48,64},{64,48},{80,96},{96,80},{112,128},... | collective-permute-start | bytes 589832 | tf_op jit(solution)/shard_map/ppermute | solution.py:290
  76.5 4.6 %collective-permute-start.14 = (bf16[2,384,128]{2,1,0:T(8,128)(2,1)S(1)}, bf16[2,384,128]{2,1,0:T(8,128)(2,1)S(1)}, u32[]{:S(2)}, u32[]{:S(2)}) collective-permute-start(bf16[2,384,128]{2,1,0:T(8,128)(2,1)S(1)} %get-tuple-element.67), channel_id=1, source_target_pairs={{0,16},{16,0},{32,48},{48,32},{64,80},{80,64},{96,112},{112,96},{1... | collective-permute-start | bytes 589832 | tf_op jit(solution)/shard_map/ppermute | solution.py:291
  81.1 0.1 shard_map.66
  81.3 0.1 collective-permute-start.6
  81.3 2.1 %collective-permute-start.7 = (bf16[8,24,384]{2,1,0:T(8,128)(2,1)S(1)}, bf16[8,24,384]{2,1,0:T(8,128)(2,1)S(1)}, u32[]{:S(2)}, u32[]{:S(2)}) collective-permute-start(bf16[8,24,384]{2,1,0:T(8,128)(2,1)S(1)} %get-tuple-element.51), channel_id=1, source_target_pairs={{0,8},{1,9},{2,10},{3,11},{4,12},{5,13},{6,14},{7,15},{8,0},{9,1},... | collective-permute-start | bytes 442376 | tf_op jit(solution)/shard_map/ppermute | solution.py:311
  83.4 0.8 collective-permute-start.8
  84.2 6.9 %collective-permute-done.6.refs_1_ = bf16[8,24,384]{2,1,0:T(8,128)(2,1)S(1)} collective-permute-done((bf16[8,24,384]{2,1,0:T(8,128)(2,1)S(1)}, bf16[8,24,384]{2,1,0:T(8,128)(2,1)S(1)}, u32[]{:S(2)}, u32[]{:S(2)}) %collective-permute-start.6) | collective-permute-done | bytes 147488 | tf_op jit(solution)/shard_map/ppermute | solution.py:311
  91.1 0.0 collective-permute-done.7.refs_2_
  91.1 0.3 collective-permute-done.8.refs_3_
  91.4 0.0 collective-permute-done.13.refs_5_
  91.5 0.0 collective-permute-done.14.refs_6_
  91.5 1.0 %shard_map.76 = f32[96,128]{1,0:T(8,128)} custom-call(s32[4,8]{1,0:T(4,128)S(4)} %get-tuple-element.37.cols_ref, bf16[8,24,384]{2,1,0:T(8,128)(2,1)S(1)} %get-tuple-element.49.refs_0_, bf16[8,24,384]{2,1,0:T(8,128)(2,1)S(1)} %collective-permute-done.6.refs_1_, bf16[8,24,384]{2,1,0:T(8,128)(2,1)S(1)} %collective-permute-done.7.refs_2_, ...), custom_call_target="tpu_custom_call" | custom-call | tf_op jit(solution)/shard_map/pallas_call | solution.py:265
Async XLA Ops:
  1.8 15.9 %all-to-all-start = ((bf16[16,96,128]{2,1,0:T(8,128)(2,1)}), bf16[16,96,128]{2,1,0:T(8,128)(2,1)S(1)}, u32[]{:S(2)}, u32[]{:S(2)}) async-start(bf16[16,96,128]{2,1,0:T(8,128)(2,1)} %get-tuple-element.54), calls=%async_computation | async-start | bytes 786432 | tf_op jit(solution)/shard_map/all_to_all | solution.py:295
  9.4 12.5 %collective-permute-start = (bf16[2,96,384]{2,1,0:T(8,128)(2,1)S(1)}, bf16[2,96,384]{2,1,0:T(8,128)(2,1)S(1)}, u32[]{:S(2)}, u32[]{:S(2)}) collective-permute-start(bf16[2,96,384]{2,1,0:T(8,128)(2,1)S(1)} %get-tuple-element.40), channel_id=1, source_target_pairs={{0,1},{1,2},{2,3},{3,0},{4,5},{5,6},{6,7},{7,4},{8,9},{9,10},{10,1... | collective-permute-start | bytes 442376 | tf_op jit(solution)/shard_map/ppermute | solution.py:311
  10.8 12.4 %collective-permute-start.1 = (bf16[2,96,384]{2,1,0:T(8,128)(2,1)S(1)}, bf16[2,96,384]{2,1,0:T(8,128)(2,1)S(1)}, u32[]{:S(2)}, u32[]{:S(2)}) collective-permute-start(bf16[2,96,384]{2,1,0:T(8,128)(2,1)S(1)} %get-tuple-element.41), channel_id=1, source_target_pairs={{0,2},{1,3},{2,0},{3,1},{4,6},{5,7},{6,4},{7,5},{8,10},{9,11},{10,... | collective-permute-start | bytes 442376 | tf_op jit(solution)/shard_map/ppermute | solution.py:311
  13.2 10.2 %collective-permute-start.2 = (bf16[2,96,384]{2,1,0:T(8,128)(2,1)S(1)}, bf16[2,96,384]{2,1,0:T(8,128)(2,1)S(1)}, u32[]{:S(2)}, u32[]{:S(2)}) collective-permute-start(bf16[2,96,384]{2,1,0:T(8,128)(2,1)S(1)} %get-tuple-element.42), channel_id=1, source_target_pairs={{0,3},{1,0},{2,1},{3,2},{4,7},{5,4},{6,5},{7,6},{8,11},{9,8},{10,9... | collective-permute-start | bytes 442376 | tf_op jit(solution)/shard_map/ppermute | solution.py:311
  17.8 16.7 %collective-permute-start.9 = (bf16[2,384,128]{2,1,0:T(8,128)(2,1)S(1)}, bf16[2,384,128]{2,1,0:T(8,128)(2,1)S(1)}, u32[]{:S(2)}, u32[]{:S(2)}) collective-permute-start(bf16[2,384,128]{2,1,0:T(8,128)(2,1)S(1)} %get-tuple-element.56), channel_id=1, source_target_pairs={{0,16},{16,0},{32,48},{48,32},{64,80},{80,64},{96,112},{112,96},{1... | collective-permute-start | bytes 589832 | tf_op jit(solution)/shard_map/ppermute | solution.py:291
  20.4 14.7 %collective-permute-start.10 = (bf16[2,384,128]{2,1,0:T(8,128)(2,1)S(1)}, bf16[2,384,128]{2,1,0:T(8,128)(2,1)S(1)}, u32[]{:S(2)}, u32[]{:S(2)}) collective-permute-start(bf16[2,384,128]{2,1,0:T(8,128)(2,1)S(1)} %get-tuple-element.57), channel_id=1, source_target_pairs={{0,240},{16,32},{32,16},{48,64},{64,48},{80,96},{96,80},{112,128},... | collective-permute-start | bytes 589832 | tf_op jit(solution)/shard_map/ppermute | solution.py:290
  23.5 5.7 %collective-permute-start.3 = (bf16[216,384]{1,0:T(8,128)(2,1)S(1)}, bf16[216,384]{1,0:T(8,128)(2,1)S(1)}, u32[]{:S(2)}, u32[]{:S(2)}) collective-permute-start(bf16[216,384]{1,0:T(8,128)(2,1)S(1)} %get-tuple-element.46), channel_id=1, source_target_pairs={{0,4},{1,5},{2,6},{3,7},{4,8},{5,9},{6,10},{7,11},{8,12},{9,13},{1... | collective-permute-start | bytes 497672 | tf_op jit(solution)/shard_map/ppermute | solution.py:311
  25.0 8.7 %collective-permute-start.4 = (bf16[216,384]{1,0:T(8,128)(2,1)S(1)}, bf16[216,384]{1,0:T(8,128)(2,1)S(1)}, u32[]{:S(2)}, u32[]{:S(2)}) collective-permute-start(bf16[216,384]{1,0:T(8,128)(2,1)S(1)} %get-tuple-element.47), channel_id=1, source_target_pairs={{0,8},{1,9},{2,10},{3,11},{4,12},{5,13},{6,14},{7,15},{8,0},{9,1},... | collective-permute-start | bytes 497672 | tf_op jit(solution)/shard_map/ppermute | solution.py:311
  27.4 6.3 %collective-permute-start.5 = (bf16[216,384]{1,0:T(8,128)(2,1)S(1)}, bf16[216,384]{1,0:T(8,128)(2,1)S(1)}, u32[]{:S(2)}, u32[]{:S(2)}) collective-permute-start(bf16[216,384]{1,0:T(8,128)(2,1)S(1)} %get-tuple-element.48), channel_id=1, source_target_pairs={{0,12},{1,13},{2,14},{3,15},{4,0},{5,1},{6,2},{7,3},{8,4},{9,5},{1... | collective-permute-start | bytes 497672 | tf_op jit(solution)/shard_map/ppermute | solution.py:311
  50.6 5.6 %collective-permute-start.11 = (bf16[2,384,128]{2,1,0:T(8,128)(2,1)S(1)}, bf16[2,384,128]{2,1,0:T(8,128)(2,1)S(1)}, u32[]{:S(2)}, u32[]{:S(2)}) collective-permute-start(bf16[2,384,128]{2,1,0:T(8,128)(2,1)S(1)} %get-tuple-element.60), channel_id=1, source_target_pairs={{0,16},{16,0},{32,48},{48,32},{64,80},{80,64},{96,112},{112,96},{1... | collective-permute-start | bytes 589832 | tf_op jit(solution)/shard_map/ppermute | solution.py:291
  53.3 5.5 %collective-permute-start.12 = (bf16[2,384,128]{2,1,0:T(8,128)(2,1)S(1)}, bf16[2,384,128]{2,1,0:T(8,128)(2,1)S(1)}, u32[]{:S(2)}, u32[]{:S(2)}) collective-permute-start(bf16[2,384,128]{2,1,0:T(8,128)(2,1)S(1)} %get-tuple-element.61), channel_id=1, source_target_pairs={{0,240},{16,32},{32,16},{48,64},{64,48},{80,96},{96,80},{112,128},... | collective-permute-start | bytes 589832 | tf_op jit(solution)/shard_map/ppermute | solution.py:290
  71.5 20.0 %collective-permute-start.13 = (bf16[2,384,128]{2,1,0:T(8,128)(2,1)S(1)}, bf16[2,384,128]{2,1,0:T(8,128)(2,1)S(1)}, u32[]{:S(2)}, u32[]{:S(2)}) collective-permute-start(bf16[2,384,128]{2,1,0:T(8,128)(2,1)S(1)} %get-tuple-element.66), channel_id=1, source_target_pairs={{0,240},{16,32},{32,16},{48,64},{64,48},{80,96},{96,80},{112,128},... | collective-permute-start | bytes 589832 | tf_op jit(solution)/shard_map/ppermute | solution.py:290
  76.5 14.9 %collective-permute-start.14 = (bf16[2,384,128]{2,1,0:T(8,128)(2,1)S(1)}, bf16[2,384,128]{2,1,0:T(8,128)(2,1)S(1)}, u32[]{:S(2)}, u32[]{:S(2)}) collective-permute-start(bf16[2,384,128]{2,1,0:T(8,128)(2,1)S(1)} %get-tuple-element.67), channel_id=1, source_target_pairs={{0,16},{16,0},{32,48},{48,32},{64,80},{80,64},{96,112},{112,96},{1... | collective-permute-start | bytes 589832 | tf_op jit(solution)/shard_map/ppermute | solution.py:291
  81.3 9.8 %collective-permute-start.6 = (bf16[8,24,384]{2,1,0:T(8,128)(2,1)S(1)}, bf16[8,24,384]{2,1,0:T(8,128)(2,1)S(1)}, u32[]{:S(2)}, u32[]{:S(2)}) collective-permute-start(bf16[8,24,384]{2,1,0:T(8,128)(2,1)S(1)} %get-tuple-element.50), channel_id=1, source_target_pairs={{0,4},{1,5},{2,6},{3,7},{4,8},{5,9},{6,10},{7,11},{8,12},{9,13},{1... | collective-permute-start | bytes 442376 | tf_op jit(solution)/shard_map/ppermute | solution.py:311
  81.3 9.8 %collective-permute-start.7 = (bf16[8,24,384]{2,1,0:T(8,128)(2,1)S(1)}, bf16[8,24,384]{2,1,0:T(8,128)(2,1)S(1)}, u32[]{:S(2)}, u32[]{:S(2)}) collective-permute-start(bf16[8,24,384]{2,1,0:T(8,128)(2,1)S(1)} %get-tuple-element.51), channel_id=1, source_target_pairs={{0,8},{1,9},{2,10},{3,11},{4,12},{5,13},{6,14},{7,15},{8,0},{9,1},... | collective-permute-start | bytes 442376 | tf_op jit(solution)/shard_map/ppermute | solution.py:311
  83.4 8.0 %collective-permute-start.8 = (bf16[8,24,384]{2,1,0:T(8,128)(2,1)S(1)}, bf16[8,24,384]{2,1,0:T(8,128)(2,1)S(1)}, u32[]{:S(2)}, u32[]{:S(2)}) collective-permute-start(bf16[8,24,384]{2,1,0:T(8,128)(2,1)S(1)} %get-tuple-element.52), channel_id=1, source_target_pairs={{0,12},{1,13},{2,14},{3,15},{4,0},{5,1},{6,2},{7,3},{8,4},{9,5},{1... | collective-permute-start | bytes 442376 | tf_op jit(solution)/shard_map/ppermute | solution.py:311
